TPU v7x, 32 devices: a whole 2x2x4 slice. The times are simulated.
32 devices in a mesh: dp: 8 (over y, x, core), tensor: 4 (over z).
Axes of the slice: x: 2, y: 2, z: 4, core: 2. Of those that a mesh axis runs over, the one named last changes fastest.
Arguments:
- tokens: bfloat16 [8, 2048, 768], P('dp', 'tensor'), may hold values from -6 to 6
- lengths: int32 [8, 24], P('dp'), may hold values from 1 to 1024, 2048 in all within a row
- w_qkv: bfloat16 [768, 3, 768], P(None, None, 'tensor'), may hold values from -0.21875 to 0.21875
- w_out: bfloat16 [768, 768], P('tensor'), may hold values from -1.25 to 1.25
- norm1_scale: float32 [768], replicated, may hold values from 0.25 to 1.75
- norm1_shift: float32 [768], replicated, may hold values from -3 to 3
- w_gate_up: bfloat16 [768, 2, 3072], P(None, None, 'tensor'), may hold values from -0.21875 to 0.21875
- w_down: bfloat16 [3072, 768], P('tensor'), may hold values from -0.109375 to 0.109375
- norm2_scale: float32 [768], replicated, may hold values from 0.25 to 1.75
- norm2_shift: float32 [768], replicated, may hold values from -3 to 3
- cotangent: bfloat16 [8, 2048, 768], P('dp', 'tensor'), may hold values from -15 to 15
Outputs:
- layer_out: bfloat16 [8, 2048, 768], P('dp', 'tensor')
- grad_tokens: float32 [8, 2048, 768], P('dp', 'tensor')
- grad_w_qkv: float32 [768, 3, 768], P(None, None, 'tensor')
- grad_w_out: float32 [768, 768], P('tensor')
- grad_norm1_scale: float32 [768], replicated
- grad_norm1_shift: float32 [768], replicated
- grad_w_gate_up: float32 [768, 2, 3072], P(None, None, 'tensor')
- grad_w_down: float32 [3072, 768], P('tensor')
- grad_norm2_scale: float32 [768], replicated
- grad_norm2_shift: float32 [768], replicated
Inputs may be any that keep to these rules, and one draw needn't show every extreme that they name: Each row holds 24 lengths that sum to 2048: the first 23 are the row's documents in order, the last is the padding at its end.
All inputs are finite; a program needn't handle non-finite values.
Results may differ from a plain program's by a relative error of at most 0.019.
Values may be sent and summed in bfloat16 or wider, within the bound.
No kernel may reach another device: no remote copies, remote signals or barrier semaphores. Data moves between devices by JAX's collectives and lax.ppermute only.
A program may use at most 192 MiB of HBM per device.

v0:
```python
import jax
import jax.numpy as jnp
from jax import lax
from jax.sharding import PartitionSpec as P

HD = 64
SEQ = 2048
DOCS = 24


EPSILON = 1e-05
ROPE_BASE = 1000.0
MASKED = -1e30


def doc_layout(row_lengths, seq_len, doc_slots):
    doc_ends = jnp.cumsum(row_lengths)
    starts = doc_ends - row_lengths
    places = jnp.arange(seq_len, dtype=jnp.int32)
    segment = jnp.sum((places[:, None] >= doc_ends[None, :]).astype(jnp.int32), axis=1)
    member = segment[:, None] == jnp.arange(doc_slots, dtype=jnp.int32)[None, :]
    offset = jnp.sum(jnp.where(member, starts[None, :], 0), axis=1)
    position = (places - offset).astype(jnp.float32)
    valid_row = (segment < doc_slots - 1).astype(jnp.float32)
    return (segment, position, valid_row)


def rope_tables(position, head_dim):
    half_dim = head_dim // 2
    inverse = ROPE_BASE ** (-2.0 * jnp.arange(half_dim, dtype=jnp.float32) / head_dim)
    angles = position[:, None] * inverse[None, :]
    return (jnp.cos(angles), jnp.sin(angles))


def rotate(heads_values, cosine_table, sine_table):
    half_dim = heads_values.shape[-1] // 2
    first_half = heads_values[..., :half_dim]
    second_half = heads_values[..., half_dim:]
    cos_part = cosine_table[:, None, :]
    sin_part = sine_table[:, None, :]
    return jnp.concatenate(
        [
            first_half * cos_part - second_half * sin_part,
            second_half * cos_part + first_half * sin_part,
        ],
        axis=-1,
    )


def unrotate(heads_grads, cosine_table, sine_table):
    half_dim = heads_grads.shape[-1] // 2
    first_half = heads_grads[..., :half_dim]
    second_half = heads_grads[..., half_dim:]
    cos_part = cosine_table[:, None, :]
    sin_part = sine_table[:, None, :]
    return jnp.concatenate(
        [
            first_half * cos_part + second_half * sin_part,
            second_half * cos_part - first_half * sin_part,
        ],
        axis=-1,
    )


def norm_forward(values, scale_vec, shift_vec):
    centered = values - jnp.mean(values, axis=-1, keepdims=True)
    inv_std = lax.rsqrt(jnp.mean(centered * centered, axis=-1, keepdims=True) + EPSILON)
    unit_rows = centered * inv_std
    return (unit_rows * scale_vec + shift_vec, unit_rows, inv_std)


def norm_backward(upstream, unit_rows, inv_std, scale_vec):
    scaled = upstream * scale_vec
    result = inv_std * (
        scaled
        - jnp.mean(scaled, axis=-1, keepdims=True)
        - unit_rows * jnp.mean(scaled * unit_rows, axis=-1, keepdims=True)
    )
    return (result, jnp.sum(upstream * unit_rows, axis=0), jnp.sum(upstream, axis=0))


def contract_rows(left, right):
    return lax.dot_general(
        left, right, (((0,), (0,)), ((), ())), preferred_element_type=jnp.float32
    )


def contract_cols(left, right):
    return lax.dot_general(
        left, right, (((1,), (1,)), ((), ())), preferred_element_type=jnp.float32
    )


def attend_forward(queries, keys_all, values, segment):
    seq_len, heads_here, head_dim = queries.shape
    block_rows = min(512, seq_len)
    scale_factor = head_dim ** (-0.5)

    def one_block(block_index):
        first_row = block_index * block_rows
        query_block = lax.dynamic_slice_in_dim(queries, first_row, block_rows, 0)
        seg_block = lax.dynamic_slice_in_dim(segment, first_row, block_rows, 0)
        scores = (
            jnp.einsum("qhe,khe->hqk", query_block, keys_all, preferred_element_type=jnp.float32)
            * scale_factor
        )
        same_doc = seg_block[:, None] == segment[None, :]
        scores = jnp.where(same_doc[None], scores, MASKED)
        row_peak = jnp.max(scores, axis=-1, keepdims=True)
        exp_scores = jnp.exp(scores - row_peak)
        totals = jnp.sum(exp_scores, axis=-1, keepdims=True)
        prob_rows = (exp_scores / totals).astype(jnp.bfloat16)
        outputs = jnp.einsum("hqk,khe->qhe", prob_rows, values, preferred_element_type=jnp.float32)
        return (outputs, row_peak[..., 0] + jnp.log(totals[..., 0]))

    block_outs, lse_blocks = lax.map(one_block, jnp.arange(seq_len // block_rows, dtype=jnp.int32))
    return (block_outs.reshape(seq_len, heads_here, head_dim), lse_blocks)


def attend_backward(queries, keys_all, values, segment, lse_blocks, grad_heads):
    seq_len, heads_here, head_dim = queries.shape
    block_rows = min(512, seq_len)
    scale_factor = head_dim ** (-0.5)

    def one_block(carries, block_index):
        key_grad, value_grad = carries
        first_row = block_index * block_rows
        query_block = lax.dynamic_slice_in_dim(queries, first_row, block_rows, 0)
        grad_block = lax.dynamic_slice_in_dim(grad_heads, first_row, block_rows, 0)
        seg_block = lax.dynamic_slice_in_dim(segment, first_row, block_rows, 0)
        lse_here = lse_blocks[block_index]
        scores = (
            jnp.einsum("qhe,khe->hqk", query_block, keys_all, preferred_element_type=jnp.float32)
            * scale_factor
        )
        same_doc = seg_block[:, None] == segment[None, :]
        scores = jnp.where(same_doc[None], scores, MASKED)
        prob_rows = jnp.exp(scores - lse_here[..., None])
        value_grad = value_grad + jnp.einsum(
            "hqk,qhe->khe",
            prob_rows.astype(jnp.bfloat16),
            grad_block,
            preferred_element_type=jnp.float32,
        )
        prob_grad = jnp.einsum(
            "qhe,khe->hqk", grad_block, values, preferred_element_type=jnp.float32
        )
        score_grad = (
            prob_rows * (prob_grad - jnp.sum(prob_rows * prob_grad, axis=-1, keepdims=True))
        ).astype(jnp.bfloat16)
        query_grad = (
            jnp.einsum("hqk,khe->qhe", score_grad, keys_all, preferred_element_type=jnp.float32)
            * scale_factor
        )
        key_grad = (
            key_grad
            + jnp.einsum(
                "hqk,qhe->khe", score_grad, query_block, preferred_element_type=jnp.float32
            )
            * scale_factor
        )
        return ((key_grad, value_grad), query_grad)

    empty = jnp.zeros((seq_len, heads_here, head_dim), jnp.float32)
    (key_grad, value_grad), query_grads = lax.scan(
        one_block, (empty, empty), jnp.arange(seq_len // block_rows, dtype=jnp.int32)
    )
    return (query_grads.reshape(seq_len, heads_here, head_dim), key_grad, value_grad)


def body(
    tokens,
    lengths,
    w_qkv,
    w_out,
    norm1_scale,
    norm1_shift,
    w_gate_up,
    w_down,
    norm2_scale,
    norm2_shift,
    cotangent,
):
    tok_piece = tokens[0]
    piece_rows, model_width = tok_piece.shape
    heads_cols = w_qkv.shape[2]
    hidden_cols = w_gate_up.shape[2]
    head_dim = HD
    heads_here = heads_cols // head_dim
    seq_len = SEQ
    segment, position, valid_row = doc_layout(lengths[0], seq_len, DOCS)
    cosine_table, sine_table = rope_tables(position, head_dim)
    qkv_flat = w_qkv.reshape(model_width, 3 * heads_cols)
    gate_up_flat = w_gate_up.reshape(model_width, 2 * hidden_cols)
    gathered = lax.all_gather(tok_piece, "tensor", axis=0, tiled=True)
    projected = jnp.dot(gathered, qkv_flat, preferred_element_type=jnp.float32).reshape(
        seq_len, 3, heads_here, head_dim
    )
    queries = rotate(projected[:, 0], cosine_table, sine_table).astype(jnp.bfloat16)
    keys_all = rotate(projected[:, 1], cosine_table, sine_table).astype(jnp.bfloat16)
    values = projected[:, 2].astype(jnp.bfloat16)
    attended, lse_blocks = attend_forward(queries, keys_all, values, segment)
    mixed_heads = (
        (attended * valid_row[:, None, None]).astype(jnp.bfloat16).reshape(seq_len, heads_cols)
    )
    attn_piece = lax.psum_scatter(
        jnp.dot(mixed_heads, w_out, preferred_element_type=jnp.float32).astype(jnp.bfloat16),
        "tensor",
        scatter_dimension=0,
        tiled=True,
    ).astype(jnp.float32)
    normed, unit_one, inv_one = norm_forward(
        tok_piece.astype(jnp.float32) + attn_piece, norm1_scale, norm1_shift
    )
    normed_low = normed.astype(jnp.bfloat16)
    normed_all = lax.all_gather(normed_low, "tensor", axis=0, tiled=True)
    hidden_pre = jnp.dot(normed_all, gate_up_flat, preferred_element_type=jnp.float32)
    gate_part = hidden_pre[:, :hidden_cols]
    up_part = hidden_pre[:, hidden_cols:]
    gate_sigmoid = jax.nn.sigmoid(gate_part)
    active = (gate_part * gate_sigmoid * up_part).astype(jnp.bfloat16)
    feed_piece = lax.psum_scatter(
        jnp.dot(active, w_down, preferred_element_type=jnp.float32).astype(jnp.bfloat16),
        "tensor",
        scatter_dimension=0,
        tiled=True,
    ).astype(jnp.float32)
    result, unit_two, inv_two = norm_forward(normed + feed_piece, norm2_scale, norm2_shift)
    layer_out = result.astype(jnp.bfloat16)[None]
    upstream = cotangent[0].astype(jnp.float32)
    grad_two, scale2_grad, shift2_grad = norm_backward(upstream, unit_two, inv_two, norm2_scale)
    feed_grad_all = lax.all_gather(grad_two.astype(jnp.bfloat16), "tensor", axis=0, tiled=True)
    down_grad = contract_rows(active, feed_grad_all)
    active_grad = contract_cols(feed_grad_all, w_down)
    gate_grad = active_grad * up_part * gate_sigmoid * (1.0 + gate_part * (1.0 - gate_sigmoid))
    up_grad = active_grad * gate_part * gate_sigmoid
    hidden_grad = jnp.concatenate([gate_grad, up_grad], axis=1).astype(jnp.bfloat16)
    gate_up_grad = contract_rows(normed_all, hidden_grad)
    gate_up_grad = gate_up_grad.reshape(model_width, 2, hidden_cols)
    normed_grad = (
        lax.psum_scatter(
            contract_cols(hidden_grad, gate_up_flat).astype(jnp.bfloat16),
            "tensor",
            scatter_dimension=0,
            tiled=True,
        ).astype(jnp.float32)
        + grad_two
    )
    grad_one, scale1_grad, shift1_grad = norm_backward(normed_grad, unit_one, inv_one, norm1_scale)
    branch_grad_all = lax.all_gather(grad_one.astype(jnp.bfloat16), "tensor", axis=0, tiled=True)
    out_grad = contract_rows(mixed_heads, branch_grad_all)
    mixed_grad = contract_cols(branch_grad_all, w_out).astype(jnp.bfloat16) * valid_row[
        :, None
    ].astype(jnp.bfloat16)
    mixed_grad = mixed_grad.reshape(seq_len, heads_here, head_dim)
    query_grad, key_grad, value_grad = attend_backward(
        queries, keys_all, values, segment, lse_blocks, mixed_grad
    )
    query_low = lax.optimization_barrier(query_grad.astype(jnp.bfloat16)).astype(jnp.float32)
    key_low = lax.optimization_barrier(key_grad.astype(jnp.bfloat16)).astype(jnp.float32)
    query_pre = unrotate(query_low, cosine_table, sine_table)
    key_pre = unrotate(key_low, cosine_table, sine_table)
    projected_grad = (
        jnp.stack([query_pre, key_pre, value_grad], axis=1)
        .astype(jnp.bfloat16)
        .reshape(seq_len, 3 * heads_cols)
    )
    qkv_grad = contract_rows(gathered, projected_grad)
    qkv_grad = qkv_grad.reshape(model_width, 3, heads_cols)
    input_grad = (
        lax.psum_scatter(
            contract_cols(projected_grad, qkv_flat).astype(jnp.bfloat16),
            "tensor",
            scatter_dimension=0,
            tiled=True,
        ).astype(jnp.float32)
        + grad_one
    )
    qkv_sum, out_sum, gate_up_sum, down_sum = lax.psum(
        (qkv_grad, out_grad, gate_up_grad, down_grad), "dp"
    )
    scale1_sum, shift1_sum, scale2_sum, shift2_sum = lax.psum(
        (scale1_grad, shift1_grad, scale2_grad, shift2_grad), ("dp", "tensor")
    )
    return (
        layer_out,
        input_grad[None],
        qkv_sum,
        out_sum,
        scale1_sum,
        shift1_sum,
        gate_up_sum,
        down_sum,
        scale2_sum,
        shift2_sum,
    )


def solution(mesh):
    in_specs = (
        P("dp", "tensor", None),
        P("dp", None),
        P(None, None, "tensor"),
        P("tensor", None),
        P(),
        P(),
        P(None, None, "tensor"),
        P("tensor", None),
        P(),
        P(),
        P("dp", "tensor", None),
    )
    out_specs = (
        P("dp", "tensor", None),
        P("dp", "tensor", None),
        P(None, None, "tensor"),
        P("tensor", None),
        P(),
        P(),
        P(None, None, "tensor"),
        P("tensor", None),
        P(),
        P(),
    )
    return jax.shard_map(body, mesh=mesh, in_specs=in_specs, out_specs=out_specs, check_vma=False)
```

profile of v0, /device:TPU:0, one launch (start us, length us, event | category | flops | bytes accessed | tf_op | source)
XLA Modules:
  0.0 1021.2 jit_solution(4878535570187811052)
XLA Ops:
  11.4 64.4 %all-gather.12.cloned.1.call-done = bf16[1,2048,768]{2,1,0:T(8,128)(2,1)} async-done(((bf16[1,512,768]{2,1,0:T(8,128)(2,1)}), bf16[1,2048,768]{2,1,0:T(8,128)(2,1)}) %all-gather.12.cloned.1.call-update) | async-done | bytes 3145744 | tf_op jit(solution)/shard_map/all_gather | solution.py:195
  75.8 4.1 fusion.38
  81.9 127.4 %while.27 = (s32[]{:T(128)}, f32[4,512,3,64]{1,0,3,2:T(4,128)}, f32[4,3,512]{2,1,0:T(4,128)}, s32[4]{0:T(128)S(1)}, s32[2048]{0:T(1024)S(1)}, /*index=5*/bf16[20...) while((s32[]{:T(128)}, f32[4,512,3,64]{1,0,3,2:T(4,128)}, ...), condition=%wide.region_6.7_spmd, body=%wide.region_3.6_spmd.sunk | while | flops 844102144 | bytes 45744328 | solution.py:116
  83.9 6.8 fusion.115
  90.7 6.8 fusion.116
  97.5 6.7 fusion.117
  105.2 8.6 dynamic_update_slice.18
  115.8 6.8 fusion.115
  122.6 6.8 fusion.116
  129.4 6.7 fusion.117
  137.0 8.6 dynamic_update_slice.18
  147.6 6.8 fusion.115
  154.4 6.8 fusion.116
  161.2 6.7 fusion.117
  168.9 8.6 dynamic_update_slice.18
  179.5 6.8 fusion.115
  186.3 6.8 fusion.116
  193.1 6.7 fusion.117
  200.8 8.6 dynamic_update_slice.18
  215.6 58.7 %reduce-scatter.5.cloned.1.call-done = bf16[512,768]{1,0:T(8,128)(2,1)} async-done(((bf16[2048,768]{1,0:T(8,128)(2,1)}), bf16[512,768]{1,0:T(8,128)(2,1)}) %reduce-scatter.5.cloned.1.call-update) | async-done | bytes 786448 | tf_op jit(solution)/shard_map/reduce_scatter | solution.py:206
  280.1 3.5 copy.46
  283.6 60.1 %all-gather.6.cloned.1.call-done = bf16[2048,768]{1,0:T(8,128)(2,1)} async-done(((bf16[512,768]{1,0:T(8,128)(2,1)}), bf16[2048,768]{1,0:T(8,128)(2,1)}) %all-gather.6.cloned.1.call-update) | async-done | bytes 3145744 | tf_op jit(solution)/shard_map/all_gather | solution.py:216
  343.7 8.2 fusion.68
  358.1 4.0 convolution_convert_fusion
  362.2 59.0 %reduce-scatter.7.cloned.1.call-done = bf16[512,768]{1,0:T(8,128)(2,1)} async-done(((bf16[2048,768]{1,0:T(8,128)(2,1)}), bf16[512,768]{1,0:T(8,128)(2,1)}) %reduce-scatter.7.cloned.1.call-update) | async-done | bytes 786448 | tf_op jit(solution)/shard_map/reduce_scatter | solution.py:222
  427.3 63.6 %all-gather.8.cloned.1.call-done = bf16[2048,768]{1,0:T(8,128)(2,1)} async-done(((bf16[512,768]{1,0:T(8,128)(2,1)}), bf16[2048,768]{1,0:T(8,128)(2,1)}) %all-gather.8.cloned.1.call-update) | async-done | bytes 3145744 | tf_op jit(solution)/shard_map/all_gather | solution.py:232
  491.0 8.0 multiply_convert_fusion.2
  501.6 6.5 fusion.37
  508.1 59.0 %reduce-scatter.9.cloned.1.call-done = bf16[512,768]{1,0:T(8,128)(2,1)} async-done(((bf16[2048,768]{1,0:T(8,128)(2,1)}), bf16[512,768]{1,0:T(8,128)(2,1)}) %reduce-scatter.9.cloned.1.call-update) | async-done | bytes 786448 | tf_op jit(solution)/shard_map/reduce_scatter | solution.py:241
  567.2 3.3 multiply_reduce_fusion.1
  572.7 63.6 %all-gather.10.cloned.1.call-done = bf16[2048,768]{1,0:T(8,128)(2,1)} async-done(((bf16[512,768]{1,0:T(8,128)(2,1)}), bf16[2048,768]{1,0:T(8,128)(2,1)}) %all-gather.10.cloned.1.call-update) | async-done | bytes 3145744 | tf_op jit(solution)/shard_map/all_gather | solution.py:250
  636.3 3.1 fusion.42
  639.3 151.0 %while.28 = (s32[]{:T(128)}, f32[2048,3,64]{0,2,1:T(8,128)}, f32[2048,3,64]{0,2,1:T(8,128)}, bf16[4,512,3,64]{1,3,2,0:T(8,128)(2,1)}, s32[4]{0:T(128)S(1)}, /*in...) while((s32[]{:T(128)}, f32[2048,3,64]{0,2,1:T(8,128)}, ...), condition=%wide.region_20.21_spmd.clone, body=%wide.region_18.20_spmd.clone.sunk | while | flops 2063563264 | bytes 156690960 | solution.py:165
  653.9 3.0 fusion.127
  656.9 4.7 fusion.129
  661.6 5.8 multiply_reduce_fusion.7
  667.4 6.1 multiply_convert_fusion.8
  673.5 5.8 fusion.130
  679.3 3.5 fusion.128
  687.7 3.0 fusion.127
  690.7 6.1 fusion.129
  696.8 5.8 multiply_reduce_fusion.7
  702.6 6.1 multiply_convert_fusion.8
  708.7 5.8 fusion.130
  714.5 4.1 fusion.128
  723.4 3.0 fusion.127
  726.5 6.1 fusion.129
  732.5 5.8 multiply_reduce_fusion.7
  738.3 6.1 multiply_convert_fusion.8
  744.4 5.8 fusion.130
  750.2 4.1 fusion.128
  759.1 3.0 fusion.127
  762.2 6.1 fusion.129
  768.3 5.8 multiply_reduce_fusion.7
  774.1 6.1 multiply_convert_fusion.8
  780.2 5.8 fusion.130
  786.0 4.1 fusion.128
  796.9 4.0 convolution_convert_fusion.1
  802.8 10.1 fusion.35
  813.0 7.1 reshape.263
  820.0 6.0 fusion.69
  827.8 3.2 fusion.40
  832.3 41.9 %all-reduce = (f32[768]{0:T(1024)}, f32[768]{0:T(1024)}, f32[768]{0:T(1024)}, f32[768]{0:T(1024)}) all-reduce(f32[768]{0:T(1024)S(1)} %copy-done.42, f32[768]{0:T(1024)S(1)} %copy-done.43, f32[768]{0:T(1024)S(1)} %copy-done.41, f32[768]{0:T(1024)S(1)} %convert_reduce_fusion), channel_id=1, replica_groups=mesh['dp'=8,'tensor'=4] {'dp','tensor'}, use_global_device_ids=true, to_apply=%region_25.26 | all-reduce | flops 3072 | bytes 24576 | tf_op jit(solution)/shard_map/psum | solution.py:282
  876.7 127.9 %all-reduce.4.cloned.1.call-done = (f32[768,3,192]{0,2,1:T(8,128)}, f32[192,768]{1,0:T(8,128)}, f32[768,2,768]{2,1,0:T(2,128)}, f32[768,768]{1,0:T(8,128)}) async-done(((f32[768,3,192]{0,2,1:T(8,128)}, f32[192,768]{1,0:T(8,128)}, f32[768,2,768]{2,1,0:T(2,128)}, f32[768,768]{1,0:T(8,128)}), (f32[768,3,192]{0,2,1:T(8,128)}, f32[192,768]{1,0:T(8,128)}, f32[768,2,768]{2,1,0:T(2,128)}, ...) | async-done | bytes 9437200 | tf_op jit(solution)/shard_map/psum | solution.py:279
  (262 shorter events, 76.5 us)
Async XLA Ops:
  7.2 350.9 %copy-start = (bf16[768,768]{1,0:T(8,128)(2,1)S(1)}, bf16[768,768]{1,0:T(8,128)(2,1)}, u32[]{:S(2)}) copy-start(bf16[768,768]{1,0:T(8,128)(2,1)} %param.22) | copy-start | bytes 3538948
  7.2 68.6 %all-gather.12.cloned.1.call-start = ((), (), s32[]{:S(2)}) async-start(), calls=%async_computation.11 | async-start | bytes 3932160 | tf_op jit(solution)/shard_map/all_gather | solution.py:195
  7.9 266.5 %reduce-scatter.5.cloned.1.call-start = ((), (), s32[]{:S(2)}) async-start(), calls=%async_computation.4 | async-start | bytes 3932160 | tf_op jit(solution)/shard_map/reduce_scatter | solution.py:206
  10.4 201.0 %copy-start.36 = (f32[2048]{0:T(1024)}, f32[2048]{0:T(1024)S(1)}, u32[]{:S(2)}) copy-start(f32[2048]{0:T(1024)S(1)} %get-tuple-element.236) | copy-start | bytes 24580
  11.4 69.0 %copy-start.24 = (f32[2048,32]{0,1:T(8,128)}, f32[2048,32]{0,1:T(8,128)S(1)}, u32[]{:S(2)}) copy-start(f32[2048,32]{0,1:T(8,128)S(1)} %get-tuple-element.233) | copy-start | bytes 786436
  11.4 69.0 %copy-start.26 = (f32[2048,32]{0,1:T(8,128)}, f32[2048,32]{0,1:T(8,128)S(1)}, u32[]{:S(2)}) copy-start(f32[2048,32]{0,1:T(8,128)S(1)} %get-tuple-element.234) | copy-start | bytes 786436
  209.4 3.2 copy-start.34
  215.3 59.1 %copy-start.9 = (bf16[1,512,768]{2,1,0:T(8,128)(2,1)S(1)}, bf16[1,512,768]{2,1,0:T(8,128)(2,1)}, u32[]{:S(2)}) copy-start(bf16[1,512,768]{2,1,0:T(8,128)(2,1)} %param.15) | copy-start | bytes 2359300
  215.3 62.7 %copy-start.38 = (f32[768]{0:T(1024)S(1)}, f32[768]{0:T(1024)}, u32[]{:S(2)}) copy-start(f32[768]{0:T(1024)} %param.19) | copy-start | bytes 9220
  215.3 128.4 %all-gather.6.cloned.1.call-start = ((), (), s32[]{:S(2)}) async-start(), calls=%async_computation.5 | async-start | bytes 3932160 | tf_op jit(solution)/shard_map/all_gather | solution.py:216
  274.4 3.6 copy-start.10
  280.0 141.1 %reduce-scatter.7.cloned.1.call-start = ((), (), s32[]{:S(2)}) async-start(), calls=%async_computation.6 | async-start | bytes 3932160 | tf_op jit(solution)/shard_map/reduce_scatter | solution.py:222
  351.9 4.5 copy-start.15
  362.1 128.9 %all-gather.8.cloned.1.call-start = ((), (), s32[]{:S(2)}) async-start(), calls=%async_computation.7 | async-start | bytes 3932160 | tf_op jit(solution)/shard_map/all_gather | solution.py:232
  427.3 139.9 %reduce-scatter.9.cloned.1.call-start = ((), (), s32[]{:S(2)}) async-start(), calls=%async_computation.8 | async-start | bytes 3932160 | tf_op jit(solution)/shard_map/reduce_scatter | solution.py:241
  491.0 10.6 %copy-start.28 = (bf16[96,8,2,768]{3,1,2,0:T(8,128)(2,1)S(1)}, bf16[96,8,2,768]{3,1,2,0:T(8,128)(2,1)}, u32[]{:S(2)}) copy-start(bf16[96,8,2,768]{3,1,2,0:T(8,128)(2,1)} %copy.46) | copy-start | bytes 7077892
  508.1 59.1 %copy-start.11 = (bf16[512,768]{1,0:T(8,128)(2,1)S(1)}, bf16[512,768]{1,0:T(8,128)(2,1)}, u32[]{:S(2)}) copy-start(bf16[512,768]{1,0:T(8,128)(2,1)} %reduce-scatter.5.cloned.1.call-done) | copy-start | bytes 2359300
  508.1 59.1 %copy-start.40 = (f32[512]{0:T(512)S(1)}, f32[512]{0:T(512)}, u32[]{:S(2)}) copy-start(f32[512]{0:T(512)} %copy-done.39) | copy-start | bytes 6148
  508.1 128.2 %all-gather.10.cloned.1.call-start = ((), (), s32[]{:S(2)}) async-start(), calls=%async_computation.9 | async-start | bytes 3932160 | tf_op jit(solution)/shard_map/all_gather | solution.py:250
  567.2 3.3 copy-start.14
  567.2 3.3 copy-start.21
  570.5 65.8 %copy-start.35 = (bf16[192,768]{1,0:T(8,128)(2,1)S(1)}, bf16[192,768]{1,0:T(8,128)(2,1)}, u32[]{:S(2)}) copy-start(bf16[192,768]{1,0:T(8,128)(2,1)} %param.18) | copy-start | bytes 884740
  570.5 65.8 %copy-start.45 = (bf16[2048]{0:T(1024)(128)(2,1)S(1)}, bf16[2048]{0:T(1024)(128)(2,1)}, u32[]{:S(2)}) copy-start(bf16[2048]{0:T(1024)(128)(2,1)} %get-tuple-element.235) | copy-start | bytes 12292
  572.6 301.7 %reduce-scatter.11.cloned.1.call-start = ((), (), s32[]{:S(2)}) async-start(), calls=%async_computation.10 | async-start | bytes 3932160 | tf_op jit(solution)/shard_map/reduce_scatter | solution.py:271
  649.1 7.8 copy-start.4
  649.1 7.8 copy-start.7
  649.1 7.8 copy-start.32
  653.9 3.0 copy-start.3
  673.5 5.8 copy-start.2
  679.3 3.5 copy-start.5
  679.3 3.5 copy-start.8
  679.3 3.5 copy-start.33
  682.9 7.8 copy-start.4
  682.9 7.8 copy-start.7
  682.9 7.8 copy-start.32
  708.7 5.8 copy-start.2
  714.5 4.1 copy-start.5
  714.5 4.1 copy-start.8
  714.5 4.1 copy-start.33
  718.6 7.8 copy-start.4
  718.6 7.8 copy-start.7
  718.6 7.8 copy-start.32
  744.4 5.8 copy-start.2
  750.2 4.1 copy-start.5
  750.2 4.1 copy-start.8
  750.2 4.1 copy-start.33
  754.3 7.8 copy-start.4
  754.4 7.8 copy-start.7
  754.4 7.8 copy-start.32
  780.2 5.8 copy-start.2
  786.0 4.1 copy-start.5
  786.0 4.1 copy-start.8
  786.0 4.1 copy-start.33
  793.6 3.3 copy-start.49
  801.0 203.6 %all-reduce.4.cloned.1.call-start = ((), (), s32[]{:S(2)}) async-start(), calls=%async_computation.12 | async-start | bytes 18874368 | tf_op jit(solution)/shard_map/psum | solution.py:279
  812.9 7.1 copy-start.23
  820.0 6.1 copy-start.13
  820.0 6.1 copy-start.20
  820.0 6.1 copy-start.37
  820.0 7.7 copy-start.47
  831.0 43.2 %copy-start.18 = (f32[512,768]{1,0:T(8,128)S(1)}, f32[512,768]{1,0:T(8,128)}, u32[]{:S(2)}) copy-start(f32[512,768]{1,0:T(8,128)} %get-tuple-element.207) | copy-start | bytes 4718596
  1004.6 4.9 copy-start.19
  1009.5 3.4 copy-start.29
  1009.5 4.8 copy-start.1
  (21 other events, 37.1 us)
Sparse Core Ops, SparseCore 0:
  9.6 66.1 all-gather.11
  215.4 58.8 reduce-scatter.4
  280.2 63.5 all-gather.5
  362.2 58.8 reduce-scatter.6
  427.4 63.5 all-gather.7
  508.2 58.8 reduce-scatter.8
  572.7 63.5 all-gather.9
  801.1 59.5 reduce-scatter.10
  865.2 139.3 all-reduce.3
where the time goes:
time: 1030 us; the launch traced here: 1020 us
  waiting for transfers between devices  557 us (54%)
  matrix products  213 us (21%)
  other arithmetic  87.2 us (8%)
  local copies, waits for them, and re-layouts  83.2 us (8%)
  blocking collectives  41.9 us (4%)
  loops' own time  23.7 us (2%)
  between operations  14.8 us (1%)
    psum x1, waiting for transfers between devices, body(): lax.psum((qkv_grad, out_grad, gate_up_grad, down_grad), 'dp')  128 us
    all_gather x1, waiting for transfers between devices, body(): gathered = lax.all_gather(tok_piece, 'tensor', axis=0, tiled=True)  64.4 us
    all_gather x1, waiting for transfers between devices, body(): lax.all_gather(grad_two.astype(jnp.bfloat16), 'tensor', axis=0, tiled=True)  63.6 us
    all_gather x1, waiting for transfers between devices, body(): lax.all_gather(grad_one.astype(jnp.bfloat16), 'tensor', axis=0, tiled=True)  63.6 us
    all_gather x1, waiting for transfers between devices, body(): normed_all = lax.all_gather(normed_low, 'tensor', axis=0, tiled=True)  60.1 us
    reduce_scatter x1, waiting for transfers between devices, body(): lax.psum_scatter(jnp.dot(active, w_down, preferred_element_type=jnp.float...  59 us
    reduce_scatter x1, waiting for transfers between devices, body(): lax.psum_scatter(contract_cols(hidden_grad, gate_up_flat).astype(jnp.bflo...  59 us
    reduce_scatter x1, waiting for transfers between devices, body(): lax.psum_scatter(jnp.dot(mixed_heads, w_out, preferred_element_type=jnp.f...  58.7 us
  transfers between devices with their start and end apart: 9, of which 8 were waited for; matrix products, arithmetic and copies ran while one was open for 4% of the time, Pallas kernels for 0%

commit v1 on v0

v1 whole, which is shorter than its diff:
```python
import functools

import jax
import jax.numpy as jnp
from jax import lax
from jax.experimental import pallas as pl
from jax.experimental.pallas import tpu as pltpu
from jax.sharding import PartitionSpec as P

TILE = 256
HALF = 32
BIG = 1e30
f32, bf16 = jnp.float32, jnp.bfloat16

def nt(a, b):
    return lax.dot_general(a, b, (((1,), (1,)), ((), ())), preferred_element_type=f32)

def nn(a, b):
    return jnp.dot(a, b, preferred_element_type=f32)

def attn_fwd_kernel(info, tok, wqk, wv, wvt, cos, sin, seg, qh, ka, va, mixed, lse, vt, acc, top, *, docs, heads):
    seq = tok.shape[0]
    nt_ = seq // TILE
    lane = lax.broadcasted_iota(jnp.int32, (TILE, 128), 1)
    used = heads * HALF

    def project(c, _):
        rows = pl.ds(pl.multiple_of(c * TILE, TILE), TILE)
        x = tok[rows, :]
        p = nn(x, wqk[...])
        co, si = cos[rows, :], sin[rows, :]
        qa, qb, k_a, k_b = p[:, :128], p[:, 128:256], p[:, 256:384], p[:, 384:]
        hit = (lane - used) == seg[rows, :]
        aug = (lane >= used) & (lane < used + docs)
        ra = (qa * co - qb * si).astype(bf16).astype(f32) * 0.125
        rb = (qb * co + qa * si).astype(bf16).astype(f32) * 0.125
        for h in range(heads):
            keep = (lane >= HALF * h) & (lane < HALF * (h + 1))
            qh[h, rows, :128] = jnp.where(keep, ra, jnp.where(hit, -BIG, 0.0)).astype(bf16)
            qh[h, rows, 128:] = jnp.where(keep, rb, 0.0).astype(bf16)
        ka[rows, :128] = jnp.where(lane < used, k_a * co - k_b * si, jnp.where(aug & ~hit, 1.0, 0.0)).astype(bf16)
        ka[rows, 128:] = (k_b * co + k_a * si).astype(bf16)
        va[rows, :] = nn(x, wv[...]).astype(bf16)
        t = nt(wvt[...], x)
        r = lax.broadcasted_iota(jnp.int32, t.shape, 0)
        one = r == 64
        for h in range(1, heads):
            one = one | (r == 80 * h + 64)
        vt[:, rows] = jnp.where(one, 1.0, t).astype(bf16)
        return 0

    lax.fori_loop(0, nt_, project, 0)
    base = info[2 * nt_]

    def q_tile(c, _):
        a = lax.rem(c + base, nt_)
        lo, hi = info[a], info[nt_ + a]
        rows = pl.ds(pl.multiple_of(c * TILE, TILE), TILE)
        acc[...] = jnp.zeros_like(acc)
        top[...] = jnp.full_like(top, -3e38)

        def k_tile(t, _):
            cols = pl.ds(pl.multiple_of(lax.rem(t - base + nt_, nt_) * TILE, TILE), TILE)
            kk = ka[cols, :]
            for h in range(heads):
                s = nt(kk, qh[h, rows, :])
                old = top[h:h + 1, :]
                new = jnp.maximum(old, jnp.max(s, axis=0, keepdims=True))
                p = jnp.exp(s - new).astype(bf16)
                top[h:h + 1, :] = new
                acc[h] = acc[h] * jnp.exp(old - new) + nn(vt[80 * h:80 * h + 80, cols], p)
            return 0

        lax.fori_loop(lo, hi, k_tile, 0)
        live = hi > lo
        col = lax.broadcasted_iota(jnp.int32, (TILE, 1), 0)
        good = (seg[rows, :] < docs - 1) & live
        outs, stats = [], []
        for h in range(heads):
            total = jnp.where(live, acc[h, 64:65, :], 1.0)
            outs.append(acc[h, :64, :] / total)
            stats.append(top[h:h + 1, :] + jnp.log(total))
        o = jnp.concatenate(outs, axis=0).T
        mixed[rows, :] = jnp.where(good, o, 0.0).astype(bf16)
        lse[:, rows] = jnp.concatenate(stats + [jnp.zeros((8 - heads, TILE), f32)], axis=0)
        return 0

    lax.fori_loop(0, nt_, q_tile, 0)

def attn_fwd(info, tok, wqk, wv, wvt, cos, sin, seg, docs, heads):
    seq = tok.shape[0]
    vm = pl.BlockSpec(memory_space=pltpu.VMEM)
    return pl.pallas_call(
        functools.partial(attn_fwd_kernel, docs=docs, heads=heads),
        out_shape=(jax.ShapeDtypeStruct((heads, seq, 256), bf16), jax.ShapeDtypeStruct((seq, 256), bf16),
                   jax.ShapeDtypeStruct((seq, 64 * heads), bf16), jax.ShapeDtypeStruct((seq, 64 * heads), bf16),
                   jax.ShapeDtypeStruct((8, seq), f32)),
        in_specs=[pl.BlockSpec(memory_space=pltpu.SMEM)] + [vm] * 7,
        out_specs=(vm,) * 5,
        scratch_shapes=[pltpu.VMEM((80 * heads, seq), bf16), pltpu.VMEM((heads, 80, TILE), f32), pltpu.VMEM((8, TILE), f32)],
        compiler_params=pltpu.CompilerParams(vmem_limit_bytes=40 << 20),
        cost_estimate=pl.CostEstimate(flops=8 << 30, bytes_accessed=14 << 20, transcendentals=4 << 20),
        name="attn_fwd",
    )(info, tok, wqk, wv, wvt, cos, sin, seg)

def attn_bwd_kernel(info, qh, ka, va, mixed, do, lse, cos, sin, seg, out, doh, kt, dqt, delta, dk, dv, *, docs, heads):
    seq = ka.shape[0]
    nt_ = seq // TILE
    width = 64 * heads
    used = heads * HALF
    base = info[2 * nt_]
    ones = jnp.ones((8, width), f32)
    wlane = lax.broadcasted_iota(jnp.int32, (TILE, width), 1)
    lane = lax.broadcasted_iota(jnp.int32, (TILE, 128), 1)
    dqt[...] = jnp.zeros_like(dqt)

    def prepare(c, _):
        rows = pl.ds(pl.multiple_of(c * TILE, TILE), TILE)
        d = jnp.where(seg[rows, :] < docs - 1, do[rows, :].astype(f32), 0.0)
        o = mixed[rows, :].astype(f32)
        for h in range(heads):
            m = jnp.where((wlane >= 64 * h) & (wlane < 64 * h + 64), d, 0.0)
            doh[h, rows, :] = m.astype(bf16)
            delta[h:h + 1, rows] = lax.dot_general(ones, m * o, (((1,), (1,)), ((), ())), precision=lax.Precision.HIGHEST, preferred_element_type=f32)[:1]
        t = ka[rows, :].astype(f32).T
        for h in range(heads):
            kt[h, :, rows] = jnp.concatenate([t[HALF * h:HALF * h + HALF], t[128 + HALF * h:128 + HALF * h + HALF]], axis=0).astype(bf16)
        return 0

    lax.fori_loop(0, nt_, prepare, 0)

    def unrotate(a, b, rows):
        a, b = a.astype(bf16).astype(f32), b.astype(bf16).astype(f32)
        co, si = cos[rows, :], sin[rows, :]
        keep = lane < used
        return (jnp.where(keep, a * co + b * si, 0.0).astype(bf16), jnp.where(keep, b * co - a * si, 0.0).astype(bf16))

    def k_tile(c, _):
        t = lax.rem(c + base, nt_)
        rows = pl.ds(pl.multiple_of(c * TILE, TILE), TILE)
        dk[...] = jnp.zeros_like(dk)
        dv[...] = jnp.zeros_like(dv)
        kk, vv = ka[rows, :], va[rows, :]

        def q_tile(u, _):
            cols = pl.ds(pl.multiple_of(lax.rem(u - base + nt_, nt_) * TILE, TILE), TILE)
            for h in range(heads):
                q, d = qh[h, cols, :], doh[h, cols, :]
                p = jnp.exp(nt(kk, q) - lse[h:h + 1, cols])
                ds = (p * (nt(vv, d) - delta[h:h + 1, cols])).astype(bf16)
                dv[...] += nn(p.astype(bf16), d)
                dk[...] += nn(ds, q)
                g = nn(kt[h, :, rows], ds)
                dqt[HALF * h:HALF * h + HALF, cols] += g[:HALF]
                dqt[128 + HALF * h:128 + HALF * h + HALF, cols] += g[HALF:]
            return 0

        lax.fori_loop(info[t], info[nt_ + t], q_tile, 0)
        a, b = unrotate(dk[:, :128], dk[:, 128:], rows)
        out[rows, 256:384] = a
        out[rows, 384:512] = b
        out[rows, 512:512 + width] = dv[...].astype(bf16)
        out[rows, 512 + width:] = jnp.zeros((TILE, 256 - width), bf16)
        return 0

    lax.fori_loop(0, nt_, k_tile, 0)

    def finish(c, _):
        rows = pl.ds(pl.multiple_of(c * TILE, TILE), TILE)
        g = dqt[:, rows].T * 0.125
        a, b = unrotate(g[:, :128], g[:, 128:], rows)
        out[rows, :128] = a
        out[rows, 128:256] = b
        return 0

    lax.fori_loop(0, nt_, finish, 0)

def attn_bwd(info, qh, ka, va, mixed, do, lse, cos, sin, seg, docs):
    heads, seq = qh.shape[:2]
    width = 64 * heads
    vm = pl.BlockSpec(memory_space=pltpu.VMEM)
    return pl.pallas_call(
        functools.partial(attn_bwd_kernel, docs=docs, heads=heads),
        out_shape=jax.ShapeDtypeStruct((seq, 768), bf16),
        in_specs=[pl.BlockSpec(memory_space=pltpu.SMEM)] + [vm] * 9,
        out_specs=vm,
        scratch_shapes=[pltpu.VMEM((heads, seq, width), bf16), pltpu.VMEM((heads, 64, seq), bf16), pltpu.VMEM((256, seq), f32),
                        pltpu.VMEM((8, seq), f32), pltpu.VMEM((TILE, 256), f32), pltpu.VMEM((TILE, width), f32)],
        compiler_params=pltpu.CompilerParams(vmem_limit_bytes=40 << 20),
        cost_estimate=pl.CostEstimate(flops=16 << 30, bytes_accessed=14 << 20, transcendentals=4 << 20),
        name="attn_bwd",
    )(info, qh, ka, va, mixed, do, lse, cos, sin, seg)

def doc_tables(lengths, seq, base_row):
    docs = lengths.shape[0]
    ends = jnp.cumsum(lengths)
    starts = ends - lengths
    place = lax.rem(jnp.arange(seq, dtype=jnp.int32) + base_row, seq)
    segment = jnp.sum((place[:, None] >= ends[None, :]).astype(jnp.int32), axis=1)
    member = segment[:, None] == jnp.arange(docs, dtype=jnp.int32)[None, :]
    offset = jnp.sum(jnp.where(member, starts[None, :], 0), axis=1)
    position = (place - offset).astype(f32)
    n = seq // TILE
    first = jnp.arange(n, dtype=jnp.int32) * TILE
    live = ends[docs - 2]
    last = jnp.minimum(first + TILE, live) - 1
    lo = jnp.max(jnp.where(starts[None, :] <= first[:, None], starts[None, :], 0), axis=1)
    hi = jnp.min(jnp.where(ends[None, :] > last[:, None], ends[None, :], seq), axis=1)
    lo = lo // TILE
    hi = (jnp.minimum(hi, live) + TILE - 1) // TILE
    hi = jnp.where(first < live, hi, lo)
    info = jnp.concatenate([lo, hi, jnp.reshape(base_row // TILE, (1,))]).astype(jnp.int32)
    return segment, position, info

HD = 64
EPSILON = 1e-05
ROPE_BASE = 1000.0


def rotate_axis(size, step):
    return [(i, (i + step) % size) for i in range(size)]


def flip_axis(size, bit):
    return [(i, i ^ bit) for i in range(size)]


def norm_forward(values, scale_vec, shift_vec):
    centered = values - jnp.mean(values, axis=-1, keepdims=True)
    inv_std = lax.rsqrt(jnp.mean(centered * centered, axis=-1, keepdims=True) + EPSILON)
    unit_rows = centered * inv_std
    return (unit_rows * scale_vec + shift_vec, unit_rows, inv_std)


def norm_backward(upstream, unit_rows, inv_std, scale_vec):
    scaled = upstream * scale_vec
    result = inv_std * (
        scaled
        - jnp.mean(scaled, axis=-1, keepdims=True)
        - unit_rows * jnp.mean(scaled * unit_rows, axis=-1, keepdims=True)
    )
    return (result, jnp.sum(upstream * unit_rows, axis=0), jnp.sum(upstream, axis=0))


def tn(left, right):
    return lax.dot_general(left, right, (((0,), (0,)), ((), ())), preferred_element_type=f32)


def take(array, index, axis):
    return lax.dynamic_index_in_dim(array, index, axis, keepdims=False)


def reduce_over_dp(parts, me, size):
    bits = size.bit_length() - 1
    blocks, rows, cols = parts.shape[1:]
    if bits == 0:
        return parts[0]
    view = parts.reshape(size // 2, 2, blocks, rows, cols)
    mine = me & 1
    got = lax.ppermute(take(view, 1 - mine, 1), "dp", flip_axis(size, 1))
    kept = (take(view, mine, 1).astype(f32) + got.astype(f32)).astype(bf16)
    kept = kept.reshape((2,) * (bits - 1) + (blocks, rows, cols))
    half = blocks // 2 if blocks > 1 else 0
    pieces = []
    if half:
        todo = [(kept[..., :half, :, :], False), (kept[..., half:, :, :], True)]
    else:
        todo = [(kept[..., : rows // 2, :], False), (kept[..., rows // 2 :, :], True)]
    for piece, low_first in todo:
        left = list(range(bits - 1, 0, -1))
        order = list(range(1, bits)) if not low_first else list(range(bits - 1, 0, -1))
        for bit in order:
            axis = left.index(bit)
            left.remove(bit)
            own = (me >> bit) & 1
            got = lax.ppermute(take(piece, 1 - own, axis), "dp", flip_axis(size, 1 << bit))
            piece = (take(piece, own, axis).astype(f32) + got.astype(f32)).astype(bf16)
        pieces.append(piece)
    return jnp.concatenate(pieces, axis=0 if half else 1)


def reduce_over_tensor(parts, z, size):
    total = take(parts, z, 0).astype(f32)
    for step in range(1, size):
        sent = take(parts, lax.rem(z + step, size), 0)
        total = total + lax.ppermute(sent, "tensor", rotate_axis(size, step)).astype(f32)
    return total


def body(
    dp_size,
    tp_size,
    tokens,
    lengths,
    w_qkv,
    w_out,
    norm1_scale,
    norm1_shift,
    w_gate_up,
    w_down,
    norm2_scale,
    norm2_shift,
    cotangent,
):
    own = tokens[0]
    rows_here, width = own.shape
    docs = lengths.shape[1]
    seq = rows_here * tp_size
    cols_here = w_qkv.shape[2]
    heads = cols_here // HD
    units = w_gate_up.shape[2]
    share = units // dp_size
    me = lax.axis_index("dp")
    z = lax.axis_index("tensor")

    gate_slice = lax.dynamic_slice_in_dim(w_gate_up, me * share, share, 2)
    down_slice = lax.dynamic_slice_in_dim(w_down, me * share, share, 0)
    out_slice = lax.dynamic_slice_in_dim(w_out, me * (width // dp_size), width // dp_size, 1)
    piece = jnp.concatenate([gate_slice[:, 0].T, gate_slice[:, 1].T, down_slice, out_slice.T], axis=1)
    weights = lax.all_gather(piece, ("dp", "tensor"), axis=0, tiled=True)

    slots = [own]
    for step in range(1, tp_size):
        slots.append(lax.ppermute(own, "tensor", rotate_axis(tp_size, -step)))
    row_tokens = jnp.concatenate(slots, axis=0)

    segment, position, info = doc_tables(lengths[0], seq, z * rows_here)
    inverse = ROPE_BASE ** (-2.0 * jnp.arange(HALF, dtype=f32) / HD)
    angles = position[:, None] * inverse[None, :]
    cosine, sine = jnp.tile(jnp.cos(angles), (1, 4)), jnp.tile(jnp.sin(angles), (1, 4))
    seg_col = segment[:, None]

    def rope_order(matrix):
        halves = matrix.reshape(width, heads, 2, HALF).transpose(0, 2, 1, 3).reshape(width, 2, heads * HALF)
        return jnp.pad(halves, ((0, 0), (0, 0), (0, 128 - heads * HALF))).reshape(width, 256)

    w_qk = jnp.concatenate([rope_order(w_qkv[:, 0]), rope_order(w_qkv[:, 1])], axis=1)
    w_v = w_qkv[:, 2]
    w_vt = jnp.pad(w_v.T.reshape(heads, HD, width), ((0, 0), (0, 16), (0, 0))).reshape(heads * 80, width)
    w_all = jnp.concatenate([w_qk, jnp.pad(w_v, ((0, 0), (0, 256 - cols_here)))], axis=1)

    qh, ka, va, mixed, lse = attn_fwd(info, row_tokens, w_qk, w_v, w_vt, cosine, sine, seg_col, docs, heads)

    mixed_slots = mixed.reshape(tp_size, rows_here, cols_here)
    mixed_rel = [mixed_slots[0]]
    for step in range(1, tp_size):
        mixed_rel.append(lax.ppermute(mixed_slots[step], "tensor", rotate_axis(tp_size, step)))
    mixed_here = jnp.concatenate(mixed_rel, axis=1)

    out_abs = weights[:, 3 * width :].reshape(dp_size, tp_size, width // dp_size, cols_here)
    out_abs = out_abs.transpose(1, 3, 0, 2).reshape(tp_size, cols_here, width)
    out_rel = jnp.concatenate([take(out_abs, lax.rem(z - s + tp_size, tp_size), 0) for s in range(tp_size)], axis=0)
    branch = jnp.dot(mixed_here, out_rel, preferred_element_type=f32)
    normed, unit_one, inv_one = norm_forward(own.astype(f32) + branch, norm1_scale, norm1_shift)
    normed_low = normed.astype(bf16)

    w_gate, w_up, w_dn = weights[:, :width], weights[:, width : 2 * width], weights[:, 2 * width : 3 * width]
    gate = nt(normed_low, w_gate)
    up = nt(normed_low, w_up)
    sigma = jax.nn.sigmoid(gate)
    active = (gate * sigma * up).astype(bf16)
    feed = nn(active, w_dn)
    result, unit_two, inv_two = norm_forward(normed + feed, norm2_scale, norm2_shift)
    layer_out = result.astype(bf16)[None]
    upstream = cotangent[0].astype(f32)
    grad_two, scale2_grad, shift2_grad = norm_backward(upstream, unit_two, inv_two, norm2_scale)
    feed_low = grad_two.astype(bf16)
    down_grad = tn(active, feed_low).astype(bf16)
    active_grad = nt(feed_low, w_dn)
    gate_grad = (active_grad * up * sigma * (1.0 + gate * (1.0 - sigma))).astype(bf16)
    up_grad = (active_grad * gate * sigma).astype(bf16)
    gate_w_grad = tn(gate_grad, normed_low).astype(bf16)
    up_w_grad = tn(up_grad, normed_low).astype(bf16)
    normed_grad = nn(gate_grad, w_gate) + nn(up_grad, w_up) + grad_two
    grad_one, scale1_grad, shift1_grad = norm_backward(normed_grad, unit_one, inv_one, norm1_scale)
    branch_low = grad_one.astype(bf16)

    small = jnp.concatenate([scale1_grad, shift1_grad, scale2_grad, shift2_grad])
    small_high = small.astype(bf16)
    small_low = (small - small_high.astype(f32)).astype(bf16)
    small_rows = jnp.concatenate([small_high, small_low]).reshape(-1, cols_here)
    mixed_grad = nt(branch_low, out_rel).astype(bf16)
    back = [mixed_grad[:, :cols_here]]
    small_sum = small
    count = small.shape[0]
    for step in range(1, tp_size):
        block = (tp_size - step) % tp_size
        sent = jnp.concatenate([mixed_grad[:, block * cols_here : (block + 1) * cols_here], small_rows], axis=0)
        got = lax.ppermute(sent, "tensor", rotate_axis(tp_size, step))
        back.append(got[:rows_here])
        extra = got[rows_here:].reshape(-1).astype(f32)
        small_sum = small_sum + (extra[:count] + extra[count:])
    mixed_back = jnp.concatenate([back[(tp_size - s) % tp_size] for s in range(tp_size)], axis=0)

    out_grads = tn(branch_low, mixed_here).astype(bf16).reshape(width, tp_size, cols_here)
    out_grads = jnp.stack([take(out_grads, lax.rem(z - t + tp_size, tp_size), 1) for t in range(tp_size)], axis=0)
    out_grads = out_grads.reshape(tp_size, dp_size, width // dp_size, cols_here).transpose(1, 0, 2, 3)

    shape4 = (dp_size, tp_size, share)
    group_one = jnp.concatenate([down_grad.reshape(shape4 + (width,)), out_grads], axis=-1)
    group_two = jnp.concatenate([gate_w_grad.reshape(shape4 + (width,)), up_w_grad.reshape(shape4 + (width,))], axis=-1)
    share_one = reduce_over_tensor(reduce_over_dp(group_one, me, dp_size), z, tp_size).astype(bf16)
    share_two = reduce_over_tensor(reduce_over_dp(group_two, me, dp_size), z, tp_size).astype(bf16)

    dqkv = attn_bwd(info, qh, ka, va, mixed, mixed_back, lse, cosine, sine, seg_col, docs)
    qkv_grad = tn(row_tokens, dqkv).astype(bf16)
    rows_share = width // dp_size
    small_share = small_sum.reshape(dp_size, 1, 1, count // dp_size)
    small_share = jnp.pad(small_share.astype(bf16), ((0, 0), (0, 0), (0, 15), (0, width - count // dp_size)))
    group_three = jnp.concatenate([qkv_grad.reshape(dp_size, 1, rows_share, width), small_share], axis=2)
    share_three = reduce_over_dp(group_three, me, dp_size)[0]

    input_part = nt(dqkv, w_all).astype(bf16).reshape(tp_size, rows_here, width)
    input_grad = grad_one + input_part[0].astype(f32)
    for step in range(1, tp_size):
        input_grad = input_grad + lax.ppermute(input_part[step], "tensor", rotate_axis(tp_size, step)).astype(f32)

    final = jnp.concatenate([share_one, share_two, share_three[:rows_share]], axis=1)
    final = jnp.concatenate([final, jnp.pad(share_three[rows_share:], ((0, 0), (0, final.shape[1] - width)))], axis=0)
    final = lax.all_gather(final, "dp", axis=0, tiled=False)
    main = final[:, :share].reshape(units, -1).astype(f32)
    small_out = final[:, share, : count // dp_size].astype(f32).reshape(4, width)
    down_sum = main[:, :width]
    out_sum = main[:, width : width + cols_here].T
    start = width + cols_here
    gate_up_sum = jnp.stack([main[:, start : start + width].T, main[:, start + width : start + 2 * width].T], axis=1)
    q3 = main[:, start + 2 * width :]

    def rope_back(matrix):
        halves = matrix.reshape(width, 2, 128)[:, :, : heads * HALF].reshape(width, 2, heads, HALF)
        return halves.transpose(0, 2, 1, 3).reshape(width, cols_here)

    qkv_sum = jnp.stack([rope_back(q3[:, :256]), rope_back(q3[:, 256:512]), q3[:, 512 : 512 + cols_here]], axis=1)
    return (
        layer_out,
        input_grad[None],
        qkv_sum,
        out_sum,
        small_out[0],
        small_out[1],
        gate_up_sum,
        down_sum,
        small_out[2],
        small_out[3],
    )


def solution(mesh):
    in_specs = (
        P("dp", "tensor", None),
        P("dp", None),
        P(None, None, "tensor"),
        P("tensor", None),
        P(),
        P(),
        P(None, None, "tensor"),
        P("tensor", None),
        P(),
        P(),
        P("dp", "tensor", None),
    )
    out_specs = (
        P("dp", "tensor", None),
        P("dp", "tensor", None),
        P(None, None, "tensor"),
        P("tensor", None),
        P(),
        P(),
        P(None, None, "tensor"),
        P("tensor", None),
        P(),
        P(),
    )
    return jax.shard_map(
        functools.partial(body, mesh.shape["dp"], mesh.shape["tensor"]),
        mesh=mesh,
        in_specs=in_specs,
        out_specs=out_specs,
        check_vma=False,
    )
```

time: 1030 us -> 606 us (0.59)
  the two profiles are of different devices: /device:TPU:0 before, /device:TPU:17 now
where the time goes in v1:
time: 606 us; the launch traced here: 599 us
  waiting for transfers between devices  257 us (42%)
  local copies, waits for them, and re-layouts  95 us (16%)
  matrix products  70.8 us (12%)
  Pallas kernels  69.5 us (11%)
  other arithmetic  53.8 us (9%)
  starting transfers between devices  37.1 us (6%)
  between operations  16.1 us (3%)
    ppermute x3, waiting for transfers between devices, body(): slots.append(lax.ppermute(own, 'tensor', rotate_axis(tp_size, -step)))  85.1 us
    ppermute x3, waiting for transfers between devices, body(): lax.ppermute(input_part[step], 'tensor', rotate_axis(tp_size, step))  67.6 us
    ppermute x12, waiting for transfers between devices, reduce_over_dp(): lax.ppermute(take(piece, 1 - own, axis), 'dp', flip_axis(size, 1 << bit))  53.8 us
    pallas_call x1, Pallas kernels, attn_bwd(): pl.pallas_call(functools.partial(attn_bwd_kernel, docs=docs, heads=heads)...  43.3 us
    dot_general x5, matrix products, nt(): lax.dot_general(a, b, (((1,), (1,)), ((), ())), preferred_element_type=f32)  27.1 us
    ppermute x6, waiting for transfers between devices, reduce_over_tensor(): lax.ppermute(sent, 'tensor', rotate_axis(size, step)).astype(f32)  26.4 us
    pallas_call x1, Pallas kernels, attn_fwd(): pl.pallas_call(functools.partial(attn_fwd_kernel, docs=docs, heads=heads)...  26.2 us
    unnamed x172, local copies, waits for them, and re-layouts  23.6 us
  transfers between devices with their start and end apart: 35, of which 16 were waited for; matrix products, arithmetic and copies ran while one was open for 16% of the time, Pallas kernels for 12%

profile of v1, /device:TPU:17, one launch (start us, length us, event | category | flops | bytes accessed | tf_op | source)
XLA Modules:
  0.0 599.1 jit_solution(5402490626676418598)
XLA Ops:
  7.2 3.0 constant_dynamic-slice_fusion
  13.1 3.2 collective-permute-start.1
  19.6 2.0 fusion.114
  25.7 1.7 pad.25
  30.3 6.5 %collective-permute-done = bf16[512,768]{1,0:T(8,128)(2,1)} collective-permute-done((bf16[512,768]{1,0:T(8,128)(2,1)}, bf16[512,768]{1,0:T(8,128)(2,1)}, u32[]{:S(2)}, u32[]{:S(2)}) %collective-permute-start) | collective-permute-done | bytes 786464 | tf_op jit(solution)/shard_map/ppermute | solution.py:324
  36.8 75.1 %collective-permute-done.1 = bf16[512,768]{1,0:T(8,128)(2,1)} collective-permute-done((bf16[512,768]{1,0:T(8,128)(2,1)}, bf16[512,768]{1,0:T(8,128)(2,1)}, u32[]{:S(2)}, u32[]{:S(2)}) %collective-permute-start.1) | collective-permute-done | bytes 786464 | tf_op jit(solution)/shard_map/ppermute | solution.py:324
  111.8 3.5 collective-permute-done.2
  115.3 2.9 pad_maximum_fusion.1.tok
  118.2 26.2 %attn_fwd.1 = (bf16[3,2048,256]{2,1,0:T(8,128)(2,1)S(1)}, bf16[2048,256]{1,0:T(8,128)(2,1)S(1)}, bf16[2048,192]{1,0:T(8,128)(2,1)S(1)}, bf16[2048,192]{1,0:T(8,128)(2,1)S(1)}, f32[8,2048]{1,0:T(8,128)S(1)}) custom-call(s32[17]{0:T(128)S(1)} %pad_add_fusion.info, bf16[2048,768]{1,0:T(8,128)(2,1)S(1)} %pad_maximum_fusion.1.tok, ...), custom_call_target="tpu_custom_call" | custom-call | flops 8589934592 | bytes 14680064 | tf_op jit(solution)/shard_map/attn_fwd/pallas_call | solution.py:93
  149.6 1.7 collective-permute-start.5
  152.2 22.2 %all-gather.4.cloned.1.call-done = bf16[3072,2496]{1,0:T(8,128)(2,1)} async-done(((bf16[96,2496]{1,0:T(8,128)(2,1)}), bf16[3072,2496]{1,0:T(8,128)(2,1)}) %all-gather.4.cloned.1.call-update) | async-done | bytes 15335440 | tf_op jit(solution)/shard_map/all_gather | solution.py:320
  174.4 2.7 slice.283
  177.1 2.8 copy.187
  179.9 3.8 reshape.450
  185.1 2.6 fusion.117
  188.9 4.8 fusion.16
  193.8 8.0 %multiply_convert_fusion.2 = (bf16[512,3072]{1,0:T(8,128)(2,1)S(1)}, f32[512,3072]{1,0:T(8,128)}) fusion(f32[512,3072]{1,0:T(8,128)S(1)} %fusion.16, bf16[512,768]{1,0:T(8,128)(2,1)S(1)} %fusion.42, bf16[3072,2496]{1,0:T(8,128)(2,1)} %all-gather.4.cloned.1.call-done), kind=kOutput, calls=%fused_computation.14 | convolution fusion | flops 2425356288 | bytes 21233664 | tf_op jit(solution)/shard_map/dot_general | solution.py:16
  201.8 6.2 %fusion.118 = (f32[512]{0:T(512)S(1)}, f32[512,768]{1,0:T(8,128)S(1)}) fusion(bf16[512,3072]{1,0:T(8,128)(2,1)S(1)} %get-tuple-element.156, bf16[3072,2496]{1,0:T(8,128)(2,1)} %all-gather.4.cloned.1.call-done, f32[768]{0:T(1024)S(1)} %copy-done.62, f32[768]{0:T(1024)S(1)} %copy-done.54, f32[512]{0:T(512)S(1)} %add_rsqrt_fusion.1, ...), kind=kOutput, calls=%fused_computation.276 | convolution fusion | flops 2418277888 | bytes 11022336 | tf_op jit(solution)/shard_map/dot_general | solution.py:19
  211.3 9.4 %multiply_convert_fusion.1 = (bf16[512,3072]{1,0:T(8,128)(2,1)}, bf16[512,3072]{1,0:T(8,128)(2,1)S(1)}) fusion(f32[512,3072]{1,0:T(8,128)S(1)} %fusion.16, f32[512,3072]{1,0:T(8,128)} %get-tuple-element.157, bf16[3072,2496]{1,0:T(8,128)(2,1)} %all-gather.4.cloned.1.call-done, f32[512]{0:T(512)S(1)} %broadcast_multiply_fusion.2, ...), kind=kOutput, calls=%fused_computation.13 | convolution fusion | flops 2439905280 | bytes 25963520 | tf_op jit(solution)/shard_map/dot_general | solution.py:16
  220.8 6.2 %fusion.10 = f32[512,768]{1,0:T(8,128)S(1)} fusion(bf16[512,3072]{1,0:T(8,128)(2,1)S(1)} %get-tuple-element.104, bf16[3072,2496]{1,0:T(8,128)(2,1)} %all-gather.4.cloned.1.call-done), kind=kOutput, calls=%fused_computation.29 | convolution fusion | flops 2415919104 | bytes 9437184 | tf_op jit(solution)/shard_map/dot_general | solution.py:19
  227.0 7.5 %multiply_reduce_fusion.1 = (f32[512]{0:T(512)}, f32[768]{0:T(1024)}, f32[512]{0:T(512)}, f32[768]{0:T(1024)}, f32[512,768]{1,0:T(8,128)}) fusion(f32[512,768]{1,0:T(8,128)S(1)} %get-tuple-element.155, f32[768]{0:T(1024)S(1)} %copy-done.54, f32[512]{0:T(512)S(1)} %add_rsqrt_fusion.1, f32[512]{0:T(512)S(1)} %broadcast_multiply_fusion.5, ...), kind=kOutput, calls=%fused_computation.81 | convolution fusion | flops 2423387648 | bytes 14970880 | tf_op jit(solution)/shard_map/dot_general | solution.py:19
  243.0 4.9 convolution_convert_fusion.1
  248.0 3.1 convolution_convert_fusion
  252.4 5.1 convolution_convert_fusion.2
  261.5 6.8 %collective-permute-start.7 = (bf16[544,192]{1,0:T(8,128)(2,1)}, bf16[544,192]{1,0:T(8,128)(2,1)}, u32[]{:S(2)}, u32[]{:S(2)}) collective-permute-start(bf16[544,192]{1,0:T(8,128)(2,1)} %get-tuple-element.150), channel_id=1, source_target_pairs={{0,2},{1,3},{2,0},{3,1},{4,6},{5,7},{6,4},{7,5},{8,10},{9,11},{10,... | collective-permute-start | bytes 626696 | tf_op jit(solution)/shard_map/ppermute | solution.py:389
  268.3 2.4 collective-permute-start.6
  270.7 2.5 fusion.3
  274.2 2.4 convolution_convert_fusion.5
  277.7 2.2 stack.30
  279.8 2.1 stack.31
  282.0 2.2 stack.32
  284.1 2.2 stack.33
  286.3 2.9 pad_maximum_fusion.3
  289.2 5.9 copy.191
  295.1 4.1 fusion.19
  307.4 1.9 copy-done.8
  309.3 43.3 %attn_bwd.1 = bf16[2048,768]{1,0:T(8,128)(2,1)S(1)} custom-call(s32[17]{0:T(128)S(1)} %pad_add_fusion.info, bf16[3,2048,256]{2,1,0:T(8,128)(2,1)S(1)} %copy-done.8, bf16[2048,256]{1,0:T(8,128)(2,1)S(1)} %copy-done.10, bf16[2048,192]{1,0:T(8,128)(2,1)S(1)} %copy-done.12, bf16[2048,192]{1,0:T(8,128)(2,1)S(1)} %copy-done.3, ...), custom_call_target="tpu_custom_call" | custom-call | flops 17179869184 | bytes 14680064 | tf_op jit(solution)/shard_map/attn_bwd/pallas_call | solution.py:182
  352.7 5.7 convolution_convert_fusion.4
  359.9 1.8 collective-permute-done.28
  364.2 4.3 collective-permute-done.29
  371.3 4.0 fusion.1
  379.8 13.7 %collective-permute-done.15 = bf16[2,2,96,960]{3,2,1,0:T(8,128)(2,1)S(1)} collective-permute-done((bf16[2,2,96,960]{3,2,1,0:T(8,128)(2,1)S(1)}, bf16[2,2,96,960]{3,2,1,0:T(8,128)(2,1)S(1)}, u32[]{:S(2)}, u32[]{:S(2)}) %collective-permute-start.15) | collective-permute-done | bytes 737312 | tf_op jit(solution)/shard_map/ppermute | solution.py:276
  394.7 3.8 fusion
  404.7 3.9 collective-permute-done.16
  408.8 23.8 %collective-permute-done.14 = bf16[2,96,960]{2,1,0:T(8,128)(2,1)S(1)} collective-permute-done((bf16[2,96,960]{2,1,0:T(8,128)(2,1)S(1)}, bf16[2,96,960]{2,1,0:T(8,128)(2,1)S(1)}, u32[]{:S(2)}, u32[]{:S(2)}) %collective-permute-start.14) | collective-permute-done | bytes 368672 | tf_op jit(solution)/shard_map/ppermute | solution.py:276
  436.7 2.1 collective-permute-start.19
  438.8 8.2 %collective-permute-done.24 = bf16[2,96,1536]{2,1,0:T(8,128)(2,1)S(1)} collective-permute-done((bf16[2,96,1536]{2,1,0:T(8,128)(2,1)S(1)}, bf16[2,96,1536]{2,1,0:T(8,128)(2,1)S(1)}, u32[]{:S(2)}, u32[]{:S(2)}) %collective-permute-start.24) | collective-permute-done | bytes 589856 | tf_op jit(solution)/shard_map/ppermute | solution.py:276
  448.6 2.1 collective-permute-start.27
  451.4 13.6 %collective-permute-done.19 = bf16[96,960]{1,0:T(8,128)(2,1)S(1)} collective-permute-done((bf16[96,960]{1,0:T(8,128)(2,1)S(1)}, bf16[96,960]{1,0:T(8,128)(2,1)S(1)}, u32[]{:S(2)}, u32[]{:S(2)}) %collective-permute-start.19) | collective-permute-done | bytes 184352 | tf_op jit(solution)/shard_map/ppermute | solution.py:286
  465.9 6.6 %collective-permute-done.25 = bf16[96,1536]{1,0:T(8,128)(2,1)S(1)} collective-permute-done((bf16[96,1536]{1,0:T(8,128)(2,1)S(1)}, bf16[96,1536]{1,0:T(8,128)(2,1)S(1)}, u32[]{:S(2)}, u32[]{:S(2)}) %collective-permute-start.25) | collective-permute-done | bytes 294944 | tf_op jit(solution)/shard_map/ppermute | solution.py:286
  472.5 6.2 %collective-permute-done.27 = bf16[96,1536]{1,0:T(8,128)(2,1)S(1)} collective-permute-done((bf16[96,1536]{1,0:T(8,128)(2,1)S(1)}, bf16[96,1536]{1,0:T(8,128)(2,1)S(1)}, u32[]{:S(2)}, u32[]{:S(2)}) %collective-permute-start.27) | collective-permute-done | bytes 294944 | tf_op jit(solution)/shard_map/ppermute | solution.py:286
  479.6 2.5 concatenate.136
  482.1 2.0 fusion.56
  484.2 4.0 convolution_convert_fusion.3
  488.5 2.5 collective-permute-start.11
  491.8 29.4 %collective-permute-done.10 = bf16[512,768]{1,0:T(8,128)(2,1)S(1)} collective-permute-done((bf16[512,768]{1,0:T(8,128)(2,1)S(1)}, bf16[512,768]{1,0:T(8,128)(2,1)S(1)}, u32[]{:S(2)}, u32[]{:S(2)}) %collective-permute-start.10) | collective-permute-done | bytes 786464 | tf_op jit(solution)/shard_map/ppermute | solution.py:416
  521.3 33.7 %collective-permute-done.11 = bf16[512,768]{1,0:T(8,128)(2,1)S(1)} collective-permute-done((bf16[512,768]{1,0:T(8,128)(2,1)S(1)}, bf16[512,768]{1,0:T(8,128)(2,1)S(1)}, u32[]{:S(2)}, u32[]{:S(2)}) %collective-permute-start.11) | collective-permute-done | bytes 786464 | tf_op jit(solution)/shard_map/ppermute | solution.py:416
  555.0 4.4 collective-permute-done.9
  561.1 2.8 slice.314
  564.9 2.8 fusion.108
  570.1 2.5 pad_maximum_fusion
  572.6 8.2 %copy.204 = f32[768,2,768]{2,1,0:T(2,128)} copy(f32[768,2,768]{0,2,1:T(8,128)} %pad_maximum_fusion) | data formatting | bytes 9437184
  585.4 1.8 copy.202
  587.2 2.2 copy.203
  (350 shorter events, 88.8 us)
Async XLA Ops:
  7.2 167.2 %all-gather.4.cloned.1.call-start = ((), (), s32[]{:S(2)}) async-start(), calls=%async_computation | async-start | bytes 16220160 | tf_op jit(solution)/shard_map/all_gather | solution.py:320
  10.2 6.1 %copy-start.72 = (s32[1,24]{1,0:T(1,128)S(1)}, s32[1,24]{1,0:T(1,128)}, u32[]{:S(2)}) copy-start(s32[1,24]{1,0:T(1,128)} %param.12) | copy-start | bytes 292
  12.8 548.2 %all-gather.6.cloned.1.call-start = ((), (), s32[]{:S(2)}) async-start(), calls=%async_computation.1 | async-start | bytes 6709248 | tf_op jit(solution)/shard_map/all_gather | solution.py:420
  12.9 23.9 %collective-permute-start = (bf16[512,768]{1,0:T(8,128)(2,1)}, bf16[512,768]{1,0:T(8,128)(2,1)}, u32[]{:S(2)}, u32[]{:S(2)}) collective-permute-start(bf16[512,768]{1,0:T(8,128)(2,1)} %bitcast), channel_id=1, source_target_pairs={{0,3},{1,0},{2,1},{3,2},{4,7},{5,4},{6,5},{7,6},{8,11},{9,8},{10,9... | collective-permute-start | bytes 2359304 | tf_op jit(solution)/shard_map/ppermute | solution.py:324
  13.1 98.7 %collective-permute-start.1 = (bf16[512,768]{1,0:T(8,128)(2,1)}, bf16[512,768]{1,0:T(8,128)(2,1)}, u32[]{:S(2)}, u32[]{:S(2)}) collective-permute-start(bf16[512,768]{1,0:T(8,128)(2,1)} %bitcast), channel_id=1, source_target_pairs={{0,2},{1,3},{2,0},{3,1},{4,6},{5,7},{6,4},{7,5},{8,10},{9,11},{10,... | collective-permute-start | bytes 2359304 | tf_op jit(solution)/shard_map/ppermute | solution.py:324
  16.3 99.0 %collective-permute-start.2 = (bf16[512,768]{1,0:T(8,128)(2,1)}, bf16[512,768]{1,0:T(8,128)(2,1)}, u32[]{:S(2)}, u32[]{:S(2)}) collective-permute-start(bf16[512,768]{1,0:T(8,128)(2,1)} %bitcast), channel_id=1, source_target_pairs={{0,1},{1,2},{2,3},{3,0},{4,5},{5,6},{6,7},{7,4},{8,9},{9,10},{10,1... | collective-permute-start | bytes 2359304 | tf_op jit(solution)/shard_map/ppermute | solution.py:324
  30.3 88.0 %copy-start.4 = (bf16[3,80,768]{2,1,0:T(8,128)(2,1)S(1)}, bf16[3,80,768]{2,1,0:T(8,128)(2,1)}, u32[]{:S(2)}) copy-start(bf16[3,80,768]{2,1,0:T(8,128)(2,1)} %pad.25) | copy-start | bytes 1105924
  149.1 35.9 %collective-permute-start.3 = (bf16[512,192]{1,0:T(8,128)(2,1)}, bf16[512,192]{1,0:T(8,128)(2,1)}, u32[]{:S(2)}, u32[]{:S(2)}) collective-permute-start(bf16[512,192]{1,0:T(8,128)(2,1)} %get-tuple-element.136), channel_id=1, source_target_pairs={{0,1},{1,2},{2,3},{3,0},{4,5},{5,6},{6,7},{7,4},{8,9},{9,10},{10,1... | collective-permute-start | bytes 589832 | tf_op jit(solution)/shard_map/ppermute | solution.py:347
  149.1 35.9 %collective-permute-start.4 = (bf16[512,192]{1,0:T(8,128)(2,1)}, bf16[512,192]{1,0:T(8,128)(2,1)}, u32[]{:S(2)}, u32[]{:S(2)}) collective-permute-start(bf16[512,192]{1,0:T(8,128)(2,1)} %get-tuple-element.135), channel_id=1, source_target_pairs={{0,2},{1,3},{2,0},{3,1},{4,6},{5,7},{6,4},{7,5},{8,10},{9,11},{10,... | collective-permute-start | bytes 589832 | tf_op jit(solution)/shard_map/ppermute | solution.py:347
  149.6 35.5 %collective-permute-start.5 = (bf16[512,192]{1,0:T(8,128)(2,1)}, bf16[512,192]{1,0:T(8,128)(2,1)}, u32[]{:S(2)}, u32[]{:S(2)}) collective-permute-start(bf16[512,192]{1,0:T(8,128)(2,1)} %get-tuple-element.134), channel_id=1, source_target_pairs={{0,3},{1,0},{2,1},{3,2},{4,7},{5,4},{6,5},{7,6},{8,11},{9,8},{10,9... | collective-permute-start | bytes 589832 | tf_op jit(solution)/shard_map/ppermute | solution.py:347
  187.8 39.2 %copy-start.17 = (f32[512,768]{1,0:T(8,128)}, f32[512,768]{1,0:T(8,128)S(1)}, u32[]{:S(2)}) copy-start(f32[512,768]{1,0:T(8,128)S(1)} %get-tuple-element.155) | copy-start | bytes 4718596
  187.8 39.1 %copy-start.46 = (f32[512]{0:T(512)}, f32[512]{0:T(512)S(1)}, u32[]{:S(2)}) copy-start(f32[512]{0:T(512)S(1)} %broadcast_multiply_fusion.5) | copy-start | bytes 6148
  188.6 38.4 %copy-start.50 = (f32[512]{0:T(512)}, f32[512]{0:T(512)S(1)}, u32[]{:S(2)}) copy-start(f32[512]{0:T(512)S(1)} %add_rsqrt_fusion.1) | copy-start | bytes 6148
  201.8 6.2 %copy-start.76 = (bf16[512,3072]{1,0:T(8,128)(2,1)}, bf16[512,3072]{1,0:T(8,128)(2,1)S(1)}, u32[]{:S(2)}) copy-start(bf16[512,3072]{1,0:T(8,128)(2,1)S(1)} %get-tuple-element.156) | copy-start | bytes 9437188
  208.0 19.0 %copy-start.21 = (f32[512,768]{1,0:T(8,128)}, f32[512,768]{1,0:T(8,128)S(1)}, u32[]{:S(2)}) copy-start(f32[512,768]{1,0:T(8,128)S(1)} %get-tuple-element.159) | copy-start | bytes 4718596
  208.1 18.9 %copy-start.52 = (f32[512]{0:T(512)}, f32[512]{0:T(512)S(1)}, u32[]{:S(2)}) copy-start(f32[512]{0:T(512)S(1)} %broadcast_multiply_fusion.4) | copy-start | bytes 6148
  209.7 17.3 %copy-start.60 = (f32[512]{0:T(512)}, f32[512]{0:T(512)S(1)}, u32[]{:S(2)}) copy-start(f32[512]{0:T(512)S(1)} %add_rsqrt_fusion) | copy-start | bytes 6148
  211.3 15.7 %copy-start.66 = (f32[512]{0:T(512)}, f32[512]{0:T(512)S(1)}, u32[]{:S(2)}) copy-start(f32[512]{0:T(512)S(1)} %broadcast_multiply_fusion.2) | copy-start | bytes 6148
  211.3 15.7 %copy-start.68 = (f32[512]{0:T(512)}, f32[512]{0:T(512)S(1)}, u32[]{:S(2)}) copy-start(f32[512]{0:T(512)S(1)} %broadcast_multiply_fusion.3) | copy-start | bytes 6148
  220.8 6.2 %copy-start.73 = (bf16[512,3072]{1,0:T(8,128)(2,1)}, bf16[512,3072]{1,0:T(8,128)(2,1)S(1)}, u32[]{:S(2)}) copy-start(bf16[512,3072]{1,0:T(8,128)(2,1)S(1)} %get-tuple-element.104) | copy-start | bytes 9437188
  220.8 6.3 %copy-start.75 = (bf16[512,3072]{1,0:T(8,128)(2,1)S(1)}, bf16[512,3072]{1,0:T(8,128)(2,1)}, u32[]{:S(2)}) copy-start(bf16[512,3072]{1,0:T(8,128)(2,1)} %get-tuple-element.103) | copy-start | bytes 9437188
  247.9 22.7 %copy-start.15 = (bf16[3072,768]{1,0:T(8,128)(2,1)}, bf16[3072,768]{1,0:T(8,128)(2,1)S(1)}, u32[]{:S(2)}) copy-start(bf16[3072,768]{1,0:T(8,128)(2,1)S(1)} %convolution_convert_fusion.1) | copy-start | bytes 14155780
  252.3 18.4 %copy-start.16 = (bf16[3072,768]{1,0:T(8,128)(2,1)}, bf16[3072,768]{1,0:T(8,128)(2,1)S(1)}, u32[]{:S(2)}) copy-start(bf16[3072,768]{1,0:T(8,128)(2,1)S(1)} %convolution_convert_fusion) | copy-start | bytes 14155780
  252.3 5.2 copy-start.29
  258.8 15.5 %copy-start.23 = (f32[512,768]{1,0:T(8,128)}, f32[512,768]{1,0:T(8,128)S(1)}, u32[]{:S(2)}) copy-start(f32[512,768]{1,0:T(8,128)S(1)} %subtract_multiply_fusion) | copy-start | bytes 4718596
  261.5 37.7 %collective-permute-start.8 = (bf16[544,192]{1,0:T(8,128)(2,1)}, bf16[544,192]{1,0:T(8,128)(2,1)}, u32[]{:S(2)}, u32[]{:S(2)}) collective-permute-start(bf16[544,192]{1,0:T(8,128)(2,1)} %get-tuple-element.151), channel_id=1, source_target_pairs={{0,1},{1,2},{2,3},{3,0},{4,5},{5,6},{6,7},{7,4},{8,9},{9,10},{10,1... | collective-permute-start | bytes 626696 | tf_op jit(solution)/shard_map/ppermute | solution.py:389
  261.5 39.8 %collective-permute-start.7 = (bf16[544,192]{1,0:T(8,128)(2,1)}, bf16[544,192]{1,0:T(8,128)(2,1)}, u32[]{:S(2)}, u32[]{:S(2)}) collective-permute-start(bf16[544,192]{1,0:T(8,128)(2,1)} %get-tuple-element.150), channel_id=1, source_target_pairs={{0,2},{1,3},{2,0},{3,1},{4,6},{5,7},{6,4},{7,5},{8,10},{9,11},{10,... | collective-permute-start | bytes 626696 | tf_op jit(solution)/shard_map/ppermute | solution.py:389
  268.3 37.9 %collective-permute-start.6 = (bf16[544,192]{1,0:T(8,128)(2,1)}, bf16[544,192]{1,0:T(8,128)(2,1)}, u32[]{:S(2)}, u32[]{:S(2)}) collective-permute-start(bf16[544,192]{1,0:T(8,128)(2,1)} %get-tuple-element.149), channel_id=1, source_target_pairs={{0,3},{1,0},{2,1},{3,2},{4,7},{5,4},{6,5},{7,6},{8,11},{9,8},{10,9... | collective-permute-start | bytes 626696 | tf_op jit(solution)/shard_map/ppermute | solution.py:389
  273.1 121.5 %collective-permute-start.20 = (bf16[4,4,96,1536]{3,2,1,0:T(8,128)(2,1)}, bf16[4,4,96,1536]{3,2,1,0:T(8,128)(2,1)}, u32[]{:S(2)}, u32[]{:S(2)}) collective-permute-start(bf16[4,4,96,1536]{3,2,1,0:T(8,128)(2,1)} %fusion.3), channel_id=1, source_target_pairs={{0,4},{4,0},{8,12},{12,8},{16,20},{20,16},{24,28},{28,24},{1,5},{5... | collective-permute-start | bytes 14155784 | tf_op jit(solution)/shard_map/ppermute | solution.py:260
  299.2 72.1 %collective-permute-start.12 = (bf16[4,4,96,960]{3,2,1,0:T(8,128)(2,1)}, bf16[4,4,96,960]{3,2,1,0:T(8,128)(2,1)}, u32[]{:S(2)}, u32[]{:S(2)}) collective-permute-start(bf16[4,4,96,960]{3,2,1,0:T(8,128)(2,1)} %fusion.19), channel_id=1, source_target_pairs={{0,4},{4,0},{8,12},{12,8},{16,20},{20,16},{24,28},{28,24},{1,5},{5... | collective-permute-start | bytes 8847368 | tf_op jit(solution)/shard_map/ppermute | solution.py:260
  352.7 5.7 copy-start.5
  352.7 6.5 %copy-start.45 = (f32[8,384]{1,0:T(8,128)S(1)}, f32[8,384]{1,0:T(8,128)}, u32[]{:S(2)}) copy-start(f32[8,384]{1,0:T(8,128)} %add.377) | copy-start | bytes 36868
  352.7 6.5 %copy-start.56 = (f32[2,384]{1,0:T(2,128)S(1)}, f32[2,384]{1,0:T(2,128)}, u32[]{:S(2)}) copy-start(f32[2,384]{1,0:T(2,128)} %concatenate.131) | copy-start | bytes 9220
  352.7 6.5 %copy-start.57 = (f32[2,384]{1,0:T(2,128)S(1)}, f32[2,384]{1,0:T(2,128)}, u32[]{:S(2)}) copy-start(f32[2,384]{1,0:T(2,128)} %concatenate.128) | copy-start | bytes 9220
  352.7 6.5 %copy-start.58 = (f32[2,384]{1,0:T(2,128)S(1)}, f32[2,384]{1,0:T(2,128)}, u32[]{:S(2)}) copy-start(f32[2,384]{1,0:T(2,128)} %concatenate.129) | copy-start | bytes 9220
  352.7 6.5 %copy-start.59 = (f32[2,384]{1,0:T(2,128)S(1)}, f32[2,384]{1,0:T(2,128)}, u32[]{:S(2)}) copy-start(f32[2,384]{1,0:T(2,128)} %concatenate.130) | copy-start | bytes 9220
  359.4 2.3 collective-permute-start.28
  362.7 5.8 collective-permute-start.29
  364.0 30.7 %slice-start = ((s8[4718592]{0:T(1024)(128)(4,1)}), s8[4194304]{0:T(1024)(128)(4,1)S(1)}, s32[]{:S(2)}) async-start(s8[4718592]{0:T(1024)(128)(4,1)} %bitcast.266), calls=%async_computation.2 | async-start | bytes 8388608
  364.0 30.7 %slice-start.2 = ((s8[4718592]{0:T(1024)(128)(4,1)}), s8[4194304]{0:T(1024)(128)(4,1)S(1)}, s32[]{:S(2)}) async-start(s8[4718592]{0:T(1024)(128)(4,1)} %bitcast.270), calls=%async_computation.4 | async-start | bytes 8388608
  364.0 7.0 %collective-permute-start.31 = (bf16[2,1,56,768]{3,2,0,1:T(8,128)(2,1)S(1)}, bf16[2,1,56,768]{3,2,0,1:T(8,128)(2,1)S(1)}, u32[]{:S(2)}, u32[]{:S(2)}) collective-permute-start(bf16[2,1,56,768]{3,2,0,1:T(8,128)(2,1)S(1)} %dynamic-slice_bitcast_fusion.12), channel_id=1, source_target_pairs={{0,16},{4,20},{8,24},{12,28},{16,0},{20,4},{24,8},{28,12},{1,17},{... | collective-permute-start | bytes 516104 | tf_op jit(solution)/shard_map/ppermute | solution.py:276
  369.5 8.4 %collective-permute-start.30 = (bf16[1,56,768]{2,1,0:T(8,128)(2,1)S(1)}, bf16[1,56,768]{2,1,0:T(8,128)(2,1)S(1)}, u32[]{:S(2)}, u32[]{:S(2)}) collective-permute-start(bf16[1,56,768]{2,1,0:T(8,128)(2,1)S(1)} %dynamic-slice_bitcast_fusion.15), channel_id=1, source_target_pairs={{0,16},{4,20},{8,24},{12,28},{16,0},{20,4},{24,8},{28,12},{1,17},{... | collective-permute-start | bytes 258056 | tf_op jit(solution)/shard_map/ppermute | solution.py:276
  371.1 23.5 %slice-start.1 = ((s8[4718592]{0:T(1024)(128)(4,1)}), s8[524288]{0:T(1024)(128)(4,1)S(1)}, s32[]{:S(2)}) async-start(s8[4718592]{0:T(1024)(128)(4,1)} %bitcast.266), calls=%async_computation.3 | async-start | bytes 1048576
  371.1 23.5 %slice-start.3 = ((s8[4718592]{0:T(1024)(128)(4,1)}), s8[524288]{0:T(1024)(128)(4,1)S(1)}, s32[]{:S(2)}) async-start(s8[4718592]{0:T(1024)(128)(4,1)} %bitcast.270), calls=%async_computation.5 | async-start | bytes 1048576
  371.2 6.1 %collective-permute-start.32 = (bf16[1,56,768]{2,1,0:T(8,128)(2,1)S(1)}, bf16[1,56,768]{2,1,0:T(8,128)(2,1)S(1)}, u32[]{:S(2)}, u32[]{:S(2)}) collective-permute-start(bf16[1,56,768]{2,1,0:T(8,128)(2,1)S(1)} %dynamic-slice_bitcast_fusion.14), channel_id=1, source_target_pairs={{0,8},{4,12},{8,0},{12,4},{16,24},{20,28},{24,16},{28,20},{1,9},{5... | collective-permute-start | bytes 258056 | tf_op jit(solution)/shard_map/ppermute | solution.py:276
  375.8 17.6 %collective-permute-start.15 = (bf16[2,2,96,960]{3,2,1,0:T(8,128)(2,1)S(1)}, bf16[2,2,96,960]{3,2,1,0:T(8,128)(2,1)S(1)}, u32[]{:S(2)}, u32[]{:S(2)}) collective-permute-start(bf16[2,2,96,960]{3,2,1,0:T(8,128)(2,1)S(1)} %dynamic-slice_bitcast_fusion.2), channel_id=1, source_target_pairs={{0,16},{4,20},{8,24},{12,28},{16,0},{20,4},{24,8},{28,12},{1,17},{... | collective-permute-start | bytes 2211848 | tf_op jit(solution)/shard_map/ppermute | solution.py:276
  379.5 22.0 %collective-permute-start.13 = (bf16[2,2,96,960]{3,2,1,0:T(8,128)(2,1)}, bf16[2,2,96,960]{3,2,1,0:T(8,128)(2,1)}, u32[]{:S(2)}, u32[]{:S(2)}) collective-permute-start(bf16[2,2,96,960]{3,2,1,0:T(8,128)(2,1)} %dynamic-slice_bitcast_fusion.3), channel_id=1, source_target_pairs={{0,8},{4,12},{8,0},{12,4},{16,24},{20,28},{24,16},{28,20},{1,9},{5... | collective-permute-start | bytes 2211848 | tf_op jit(solution)/shard_map/ppermute | solution.py:276
  399.0 33.7 %collective-permute-start.23 = (bf16[2,2,96,1536]{3,2,1,0:T(8,128)(2,1)S(1)}, bf16[2,2,96,1536]{3,2,1,0:T(8,128)(2,1)S(1)}, u32[]{:S(2)}, u32[]{:S(2)}) collective-permute-start(bf16[2,2,96,1536]{3,2,1,0:T(8,128)(2,1)S(1)} %dynamic-slice_bitcast_fusion), channel_id=1, source_target_pairs={{0,16},{4,20},{8,24},{12,28},{16,0},{20,4},{24,8},{28,12},{1,17},{... | collective-permute-start | bytes 3538952 | tf_op jit(solution)/shard_map/ppermute | solution.py:276
  400.6 8.1 %collective-permute-start.16 = (bf16[2,96,960]{2,1,0:T(8,128)(2,1)S(1)}, bf16[2,96,960]{2,1,0:T(8,128)(2,1)S(1)}, u32[]{:S(2)}, u32[]{:S(2)}) collective-permute-start(bf16[2,96,960]{2,1,0:T(8,128)(2,1)S(1)} %dynamic-slice_bitcast_fusion.6), channel_id=1, source_target_pairs={{0,8},{4,12},{8,0},{12,4},{16,24},{20,28},{24,16},{28,20},{1,9},{5... | collective-permute-start | bytes 1105928 | tf_op jit(solution)/shard_map/ppermute | solution.py:276
  403.0 29.6 %collective-permute-start.14 = (bf16[2,96,960]{2,1,0:T(8,128)(2,1)S(1)}, bf16[2,96,960]{2,1,0:T(8,128)(2,1)S(1)}, u32[]{:S(2)}, u32[]{:S(2)}) collective-permute-start(bf16[2,96,960]{2,1,0:T(8,128)(2,1)S(1)} %dynamic-slice_bitcast_fusion.7), channel_id=1, source_target_pairs={{0,16},{4,20},{8,24},{12,28},{16,0},{20,4},{24,8},{28,12},{1,17},{... | collective-permute-start | bytes 1105928 | tf_op jit(solution)/shard_map/ppermute | solution.py:276
  403.7 30.9 %collective-permute-start.21 = (bf16[2,2,96,1536]{3,2,1,0:T(8,128)(2,1)S(1)}, bf16[2,2,96,1536]{3,2,1,0:T(8,128)(2,1)S(1)}, u32[]{:S(2)}, u32[]{:S(2)}) collective-permute-start(bf16[2,2,96,1536]{3,2,1,0:T(8,128)(2,1)S(1)} %dynamic-slice_bitcast_fusion.1), channel_id=1, source_target_pairs={{0,8},{4,12},{8,0},{12,4},{16,24},{20,28},{24,16},{28,20},{1,9},{5... | collective-permute-start | bytes 3538952 | tf_op jit(solution)/shard_map/ppermute | solution.py:276
  433.1 13.9 %collective-permute-start.24 = (bf16[2,96,1536]{2,1,0:T(8,128)(2,1)S(1)}, bf16[2,96,1536]{2,1,0:T(8,128)(2,1)S(1)}, u32[]{:S(2)}, u32[]{:S(2)}) collective-permute-start(bf16[2,96,1536]{2,1,0:T(8,128)(2,1)S(1)} %dynamic-slice_bitcast_fusion.4), channel_id=1, source_target_pairs={{0,8},{4,12},{8,0},{12,4},{16,24},{20,28},{24,16},{28,20},{1,9},{5... | collective-permute-start | bytes 1769480 | tf_op jit(solution)/shard_map/ppermute | solution.py:276
  435.0 12.2 %collective-permute-start.22 = (bf16[2,96,1536]{2,1,0:T(8,128)(2,1)S(1)}, bf16[2,96,1536]{2,1,0:T(8,128)(2,1)S(1)}, u32[]{:S(2)}, u32[]{:S(2)}) collective-permute-start(bf16[2,96,1536]{2,1,0:T(8,128)(2,1)S(1)} %dynamic-slice_bitcast_fusion.5), channel_id=1, source_target_pairs={{0,16},{4,20},{8,24},{12,28},{16,0},{20,4},{24,8},{28,12},{1,17},{... | collective-permute-start | bytes 1769480 | tf_op jit(solution)/shard_map/ppermute | solution.py:276
  435.8 12.8 %collective-permute-start.17 = (bf16[96,960]{1,0:T(8,128)(2,1)S(1)}, bf16[96,960]{1,0:T(8,128)(2,1)S(1)}, u32[]{:S(2)}, u32[]{:S(2)}) collective-permute-start(bf16[96,960]{1,0:T(8,128)(2,1)S(1)} %get-tuple-element.140), channel_id=1, source_target_pairs={{0,1},{1,2},{2,3},{3,0},{4,5},{5,6},{6,7},{7,4},{8,9},{9,10},{10,1... | collective-permute-start | bytes 552968 | tf_op jit(solution)/shard_map/ppermute | solution.py:286
  435.8 15.5 %collective-permute-start.18 = (bf16[96,960]{1,0:T(8,128)(2,1)S(1)}, bf16[96,960]{1,0:T(8,128)(2,1)S(1)}, u32[]{:S(2)}, u32[]{:S(2)}) collective-permute-start(bf16[96,960]{1,0:T(8,128)(2,1)S(1)} %get-tuple-element.141), channel_id=1, source_target_pairs={{0,2},{1,3},{2,0},{3,1},{4,6},{5,7},{6,4},{7,5},{8,10},{9,11},{10,... | collective-permute-start | bytes 552968 | tf_op jit(solution)/shard_map/ppermute | solution.py:286
  436.7 28.3 %collective-permute-start.19 = (bf16[96,960]{1,0:T(8,128)(2,1)S(1)}, bf16[96,960]{1,0:T(8,128)(2,1)S(1)}, u32[]{:S(2)}, u32[]{:S(2)}) collective-permute-start(bf16[96,960]{1,0:T(8,128)(2,1)S(1)} %get-tuple-element.142), channel_id=1, source_target_pairs={{0,3},{1,0},{2,1},{3,2},{4,7},{5,4},{6,5},{7,6},{8,11},{9,8},{10,9... | collective-permute-start | bytes 552968 | tf_op jit(solution)/shard_map/ppermute | solution.py:286
  447.7 24.8 %collective-permute-start.25 = (bf16[96,1536]{1,0:T(8,128)(2,1)S(1)}, bf16[96,1536]{1,0:T(8,128)(2,1)S(1)}, u32[]{:S(2)}, u32[]{:S(2)}) collective-permute-start(bf16[96,1536]{1,0:T(8,128)(2,1)S(1)} %get-tuple-element.122), channel_id=1, source_target_pairs={{0,1},{1,2},{2,3},{3,0},{4,5},{5,6},{6,7},{7,4},{8,9},{9,10},{10,1... | collective-permute-start | bytes 884744 | tf_op jit(solution)/shard_map/ppermute | solution.py:286
  447.7 24.7 %collective-permute-start.26 = (bf16[96,1536]{1,0:T(8,128)(2,1)S(1)}, bf16[96,1536]{1,0:T(8,128)(2,1)S(1)}, u32[]{:S(2)}, u32[]{:S(2)}) collective-permute-start(bf16[96,1536]{1,0:T(8,128)(2,1)S(1)} %get-tuple-element.123), channel_id=1, source_target_pairs={{0,2},{1,3},{2,0},{3,1},{4,6},{5,7},{6,4},{7,5},{8,10},{9,11},{10,... | collective-permute-start | bytes 884744 | tf_op jit(solution)/shard_map/ppermute | solution.py:286
  448.6 30.1 %collective-permute-start.27 = (bf16[96,1536]{1,0:T(8,128)(2,1)S(1)}, bf16[96,1536]{1,0:T(8,128)(2,1)S(1)}, u32[]{:S(2)}, u32[]{:S(2)}) collective-permute-start(bf16[96,1536]{1,0:T(8,128)(2,1)S(1)} %get-tuple-element.124), channel_id=1, source_target_pairs={{0,3},{1,0},{2,1},{3,2},{4,7},{5,4},{6,5},{7,6},{8,11},{9,8},{10,9... | collective-permute-start | bytes 884744 | tf_op jit(solution)/shard_map/ppermute | solution.py:286
  488.2 71.2 %copy-start.24 = (f32[512,768]{1,0:T(8,128)S(1)}, f32[512,768]{1,0:T(8,128)}, u32[]{:S(2)}) copy-start(f32[512,768]{1,0:T(8,128)} %copy-done.23) | copy-start | bytes 4718596
  488.4 32.9 %collective-permute-start.10 = (bf16[512,768]{1,0:T(8,128)(2,1)S(1)}, bf16[512,768]{1,0:T(8,128)(2,1)S(1)}, u32[]{:S(2)}, u32[]{:S(2)}) collective-permute-start(bf16[512,768]{1,0:T(8,128)(2,1)S(1)} %get-tuple-element.118), channel_id=1, source_target_pairs={{0,2},{1,3},{2,0},{3,1},{4,6},{5,7},{6,4},{7,5},{8,10},{9,11},{10,... | collective-permute-start | bytes 2359304 | tf_op jit(solution)/shard_map/ppermute | solution.py:416
  488.5 66.5 %collective-permute-start.11 = (bf16[512,768]{1,0:T(8,128)(2,1)S(1)}, bf16[512,768]{1,0:T(8,128)(2,1)S(1)}, u32[]{:S(2)}, u32[]{:S(2)}) collective-permute-start(bf16[512,768]{1,0:T(8,128)(2,1)S(1)} %get-tuple-element.117), channel_id=1, source_target_pairs={{0,3},{1,0},{2,1},{3,2},{4,7},{5,4},{6,5},{7,6},{8,11},{9,8},{10,9... | collective-permute-start | bytes 2359304 | tf_op jit(solution)/shard_map/ppermute | solution.py:416
  490.9 68.5 %collective-permute-start.9 = (bf16[512,768]{1,0:T(8,128)(2,1)S(1)}, bf16[512,768]{1,0:T(8,128)(2,1)S(1)}, u32[]{:S(2)}, u32[]{:S(2)}) collective-permute-start(bf16[512,768]{1,0:T(8,128)(2,1)S(1)} %get-tuple-element.116), channel_id=1, source_target_pairs={{0,1},{1,2},{2,3},{3,0},{4,5},{5,6},{6,7},{7,4},{8,9},{9,10},{10,1... | collective-permute-start | bytes 2359304 | tf_op jit(solution)/shard_map/ppermute | solution.py:416
  585.4 6.5 %copy-start.1 = (bf16[768,768]{1,0:T(8,128)(2,1)S(1)}, bf16[768,768]{1,0:T(8,128)(2,1)}, u32[]{:S(2)}) copy-start(bf16[768,768]{1,0:T(8,128)(2,1)} %param.18) | copy-start | bytes 3538948
  (53 other events, 150.4 us)
Sparse Core Ops, SparseCore 0:
  13.0 161.3 all-gather.3
  484.3 46.2 all-gather.5

commit v2 on v1

v2 whole, which is shorter than its diff:
```python
import functools

import jax
import jax.numpy as jnp
from jax import lax
from jax.experimental import pallas as pl
from jax.experimental.pallas import tpu as pltpu
from jax.sharding import PartitionSpec as P

TILE = 256
HALF = 32
HD = 64
BIG = 1e30
f32, bf16 = jnp.float32, jnp.bfloat16


def nt(a, b):
    return lax.dot_general(a, b, (((1,), (1,)), ((), ())), preferred_element_type=f32)


def nn(a, b):
    return jnp.dot(a, b, preferred_element_type=f32)


def tile_rows(tile, base, count):
    return pl.ds(pl.multiple_of(lax.rem(tile - base + count, count) * TILE, TILE), TILE)


def attn_fwd_kernel(info, *refs, docs, heads, slots):
    toks = refs[:slots]
    w, cos, sin, seg, qh, ka, va, lse, mixed, tok, vt, acc, top = refs[slots:]
    here, width = toks[0].shape
    seq = here * slots
    count = seq // TILE
    used = heads * HALF
    cols = heads * HD
    lo, hi, base = info[0], info[1], info[2]

    @pl.when(pl.program_id(0) == 0)
    def _():
        for s in range(slots):
            tok[s * here : (s + 1) * here, :] = toks[s][...]
        r = lax.broadcasted_iota(jnp.int32, vt.shape, 0)
        one = r == HD
        for h in range(1, heads):
            one = one | (r == 80 * h + HD)
        vt[...] = jnp.where(one, 1.0, 0.0).astype(bf16)

    def weight(start, stop):
        return w[:, 0, :, start:stop].reshape(width, stop - start)

    lane = lax.broadcasted_iota(jnp.int32, (TILE, 128), 1)

    def queries(c, _):
        rows = pl.ds(pl.multiple_of(c * TILE, TILE), TILE)
        p = nn(tok[rows, :], weight(0, 256))
        co, si = cos[rows, :], sin[rows, :]
        hit = (lane - used) == seg[rows, :]
        ra = (p[:, :128] * co - p[:, 128:] * si).astype(bf16).astype(f32) * HD**-0.5
        rb = (p[:, 128:] * co + p[:, :128] * si).astype(bf16).astype(f32) * HD**-0.5
        for h in range(heads):
            keep = (lane >= HALF * h) & (lane < HALF * (h + 1))
            qh[0, h, rows, :128] = jnp.where(keep, ra, jnp.where(hit, -BIG, 0.0)).astype(bf16)
            qh[0, h, rows, 128:] = jnp.where(keep, rb, 0.0).astype(bf16)
        return 0

    lax.fori_loop(0, here // TILE, queries, 0)

    def keys(t, _):
        rows = tile_rows(t, base, count)
        x = tok[rows, :]
        p = nn(x, weight(256, 512))
        co, si = cos[rows, :], sin[rows, :]
        other = (lane >= used) & (lane < used + docs) & ((lane - used) != seg[rows, :])
        ra, rb = p[:, :128] * co - p[:, 128:] * si, p[:, 128:] * co + p[:, :128] * si
        ka[0, rows, :128] = jnp.where(lane < used, ra, jnp.where(other, 1.0, 0.0)).astype(bf16)
        ka[0, rows, 128:] = rb.astype(bf16)
        v = nn(x, weight(512 + cols, 512 + 2 * cols))
        va[0, rows, :] = v.astype(bf16)
        vtt = v.T.astype(bf16)
        for h in range(heads):
            vt[80 * h : 80 * h + HD, rows] = vtt[HD * h : HD * (h + 1), :]
        return 0

    lax.fori_loop(lo, hi, keys, 0)
    acc[...] = jnp.zeros_like(acc)
    top[...] = jnp.full_like(top, -3e38)

    def k_tile(t, _):
        rows = tile_rows(t, base, count)
        kk = ka[0, rows, :]
        for h in range(heads):
            s = nt(kk, qh[0, h])
            old = top[h : h + 1, :]
            new = jnp.maximum(old, jnp.max(s, axis=0, keepdims=True))
            p = jnp.exp(s - new).astype(bf16)
            top[h : h + 1, :] = new
            acc[h] = acc[h] * jnp.exp(old - new) + nn(vt[80 * h : 80 * h + 80, rows], p)
        return 0

    lax.fori_loop(lo, hi, k_tile, 0)
    good = seg[:here, :] < docs - 1
    total = [jnp.where(top[h : h + 1, :] > -1e29, acc[h, HD : HD + 1, :], 1.0) for h in range(heads)]
    outs = jnp.concatenate([acc[h, :HD, :] / total[h] for h in range(heads)], axis=0).T
    mixed[0] = jnp.where(good, outs, 0.0).astype(bf16)
    stats = [top[h : h + 1, :] + jnp.log(total[h]) for h in range(heads)]
    lse[0] = jnp.concatenate(stats + [jnp.zeros((8 - heads, here), f32)], axis=0)


def attn_fwd(info, toks, w, cos, sin, seg, docs, heads):
    slots = len(toks)
    here, width = toks[0].shape
    seq = here * slots
    cols = heads * HD

    def whole(shape):
        return pl.BlockSpec(shape, lambda g: (0,) * len(shape))

    def part(shape):
        return pl.BlockSpec((1,) + shape, lambda g: (g,) + (0,) * len(shape))

    shapes = [((heads, here, 256), bf16), ((seq, 256), bf16), ((seq, cols), bf16), ((8, here), f32), ((here, cols), bf16)]
    return pl.pallas_call(
        functools.partial(attn_fwd_kernel, docs=docs, heads=heads, slots=slots),
        grid=(slots,),
        out_shape=tuple(jax.ShapeDtypeStruct((slots,) + s, d) for s, d in shapes),
        in_specs=[pl.BlockSpec(memory_space=pltpu.SMEM)]
        + [whole((here, width))] * slots
        + [pl.BlockSpec((w.shape[0], 1) + w.shape[2:], lambda g: (0, g, 0, 0)), whole(cos.shape), whole(sin.shape), whole(seg.shape)],
        out_specs=tuple(part(s) for s, _ in shapes),
        scratch_shapes=[
            pltpu.VMEM((seq, width), bf16),
            pltpu.VMEM((80 * heads, seq), bf16),
            pltpu.VMEM((heads, 80, here), f32),
            pltpu.VMEM((8, here), f32),
        ],
        compiler_params=pltpu.CompilerParams(vmem_limit_bytes=50 << 20),
        cost_estimate=pl.CostEstimate(flops=20 << 30, bytes_accessed=20 << 20, transcendentals=4 << 20),
        name="attn_fwd",
    )(info, *toks, w, cos, sin, seg)


def attn_bwd_kernel(info, *refs, docs, heads, slots, pieces):
    toks = refs[:slots]
    w, cos, sin, seg, qh, ka, va, lse, mixed, do = refs[slots : slots + 10]
    dw, dx_out = refs[slots + 10], refs[slots + 11 : 2 * slots + 11]
    tokt, dx, dqt, dwa, doh, delta = refs[2 * slots + 11 :]
    here, width = toks[0].shape
    seq = here * slots
    count = seq // TILE
    used = heads * HALF
    cols = heads * HD
    lo, hi, base, me = info[0], info[1], info[2], info[3]

    @pl.when(pl.program_id(0) == 0)
    def _():
        dx[...] = jnp.zeros_like(dx)
        for s in range(slots):
            for c in range(here // TILE):
                start = s * here + c * TILE
                tokt[:, start : start + TILE] = toks[s][c * TILE : (c + 1) * TILE, :].astype(f32).T.astype(bf16)

    def weight(start, stop):
        return w[:, 0, :, start:stop].reshape(width, stop - start)

    wlane = lax.broadcasted_iota(jnp.int32, (here, cols), 1)
    lane = lax.broadcasted_iota(jnp.int32, (TILE, 128), 1)
    ones = jnp.ones((8, cols), f32)
    dqt[...] = jnp.zeros_like(dqt)
    dwa[...] = jnp.zeros_like(dwa)
    d = jnp.where(seg[:here, :] < docs - 1, do[0].astype(f32), 0.0)
    o = mixed[0].astype(f32)
    for h in range(heads):
        m = jnp.where((wlane >= HD * h) & (wlane < HD * (h + 1)), d, 0.0)
        doh[h] = m.astype(bf16)
        sums = lax.dot_general(ones, m * o, (((1,), (1,)), ((), ())), precision=lax.Precision.HIGHEST, preferred_element_type=f32)
        delta[h : h + 1, :] = sums[:1]

    def unrotate(a, b, rows):
        a, b = a.astype(bf16).astype(f32), b.astype(bf16).astype(f32)
        co, si = cos[rows, :], sin[rows, :]
        keep = lane < used
        both = [jnp.where(keep, a * co + b * si, 0.0), jnp.where(keep, b * co - a * si, 0.0)]
        return jnp.concatenate(both, axis=1).astype(bf16)

    def k_tile(t, _):
        rows = tile_rows(t, base, count)
        kk, vv = ka[0, rows, :], va[0, rows, :]
        kt = kk.astype(f32).T.astype(bf16)
        dk = jnp.zeros((TILE, 256), f32)
        dv = jnp.zeros((TILE, cols), f32)
        for h in range(heads):
            q, dd = qh[0, h], doh[h]
            p = jnp.exp(nt(kk, q) - lse[0, h : h + 1, :])
            ds = (p * (nt(vv, dd) - delta[h : h + 1, :])).astype(bf16)
            dv = dv + nn(p.astype(bf16), dd)
            dk = dk + nn(ds, q)
            kth = jnp.concatenate([kt[HALF * h : HALF * (h + 1)], kt[128 + HALF * h : 128 + HALF * (h + 1)]], axis=0)
            g = nn(kth, ds)
            dqt[HALF * h : HALF * (h + 1), :] += g[:HALF]
            dqt[128 + HALF * h : 128 + HALF * (h + 1), :] += g[HALF:]
        dkl = unrotate(dk[:, :128], dk[:, 128:], rows)
        dvl = dv.astype(bf16)
        dx[rows, :] += nt(dkl, weight(256, 512)) + nt(dvl, weight(512 + cols, 512 + 2 * cols))
        dwa[:, 256:512] += nn(tokt[:, rows], dkl)
        dwa[:, 512 : 512 + cols] += nn(tokt[:, rows], dvl)
        return 0

    lax.fori_loop(lo, hi, k_tile, 0)
    for c in range(here // TILE):
        rows = slice(c * TILE, (c + 1) * TILE)
        g = dqt[:, rows].T * HD**-0.5
        dql = unrotate(g[:, :128], g[:, 128:], rows)
        dx[rows, :] += nt(dql, weight(0, 256))
        dwa[:, :256] += nn(tokt[:, rows], dql)
    share = width // pieces
    for r in range(pieces):
        p = jnp.bitwise_xor(me, r)
        dw[r, 0] = dwa[pl.ds(pl.multiple_of(p * share, 8), share), :].astype(bf16)

    @pl.when(pl.program_id(0) == slots - 1)
    def _():
        for s in range(slots):
            dx_out[s][...] = dx[s * here : (s + 1) * here, :].astype(dx_out[s].dtype)


def attn_bwd(info, toks, w, cos, sin, seg, saved, do, docs, heads, pieces):
    slots = len(toks)
    here, width = toks[0].shape
    seq = here * slots
    cols = heads * HD
    span = -(-(512 + cols) // 128) * 128

    def whole(shape):
        return pl.BlockSpec(shape, lambda g: (0,) * len(shape))

    def part(array):
        return pl.BlockSpec((1,) + array.shape[1:], lambda g: (g,) + (0,) * (array.ndim - 1))

    return pl.pallas_call(
        functools.partial(attn_bwd_kernel, docs=docs, heads=heads, slots=slots, pieces=pieces),
        grid=(slots,),
        out_shape=(jax.ShapeDtypeStruct((pieces, slots, width // pieces, span), bf16), jax.ShapeDtypeStruct((here, width), f32))
        + (jax.ShapeDtypeStruct((here, width), bf16),) * (slots - 1),
        in_specs=[pl.BlockSpec(memory_space=pltpu.SMEM)]
        + [whole((here, width))] * slots
        + [pl.BlockSpec((w.shape[0], 1) + w.shape[2:], lambda g: (0, g, 0, 0)), whole(cos.shape), whole(sin.shape), whole(seg.shape)]
        + [part(a) for a in (*saved, do)],
        out_specs=(pl.BlockSpec((pieces, 1, width // pieces, span), lambda g: (0, g, 0, 0)),) + (whole((here, width)),) * slots,
        scratch_shapes=[
            pltpu.VMEM((width, seq), bf16),
            pltpu.VMEM((seq, width), f32),
            pltpu.VMEM((256, here), f32),
            pltpu.VMEM((width, span), f32),
            pltpu.VMEM((heads, here, cols), bf16),
            pltpu.VMEM((8, here), f32),
        ],
        compiler_params=pltpu.CompilerParams(vmem_limit_bytes=56 << 20),
        cost_estimate=pl.CostEstimate(flops=40 << 30, bytes_accessed=24 << 20, transcendentals=4 << 20),
        name="attn_bwd",
    )(info, *toks, w, cos, sin, seg, *saved, do)


def doc_tables(lengths, seq, first, here):
    docs = lengths.shape[0]
    ends = jnp.cumsum(lengths)
    starts = ends - lengths
    place = lax.rem(jnp.arange(seq, dtype=jnp.int32) + first, seq)
    segment = jnp.sum((place[:, None] >= ends[None, :]).astype(jnp.int32), axis=1)
    member = segment[:, None] == jnp.arange(docs, dtype=jnp.int32)[None, :]
    offset = jnp.sum(jnp.where(member, starts[None, :], 0), axis=1)
    position = (place - offset).astype(f32)
    live = ends[docs - 2]
    last = jnp.minimum(first + here, live) - 1
    lo = jnp.max(jnp.where(starts <= first, starts, 0))
    hi = jnp.minimum(jnp.min(jnp.where(ends > last, ends, seq)), live)
    lo = lo // TILE
    hi = jnp.where(first < live, (hi + TILE - 1) // TILE, lo)
    return segment, position, lo, hi, first // TILE


EPSILON = 1e-05
ROWS = 256


def tn(left, right):
    return lax.dot_general(left, right, (((0,), (0,)), ((), ())), preferred_element_type=f32)


def row_mean(values):
    return jnp.mean(values, axis=-1, keepdims=True)


def normalise(values):
    centered = values - row_mean(values)
    inv = lax.rsqrt(row_mean(centered * centered) + EPSILON)
    return centered * inv, inv


def norm_back(upstream, unit, inv, scale):
    scaled = upstream * scale
    return inv * (scaled - row_mean(scaled) - unit * row_mean(scaled * unit))


def ffn_kernel(*refs, slots, pieces, share):
    own, cot, s1, b1, s2, b2, rel, w1_hbm, wown_hbm, w2_hbm = refs[:10]
    layer_out, grad_one, nlow, flow, brt, back, small, act_hbm, gg_hbm, ug_hbm = refs[10:20]
    w, wo, ws, g, u, normed, unit1, inv1, acc, stage, wsem, psem, osem, ssem = refs[20:]
    tokens, width = own.shape
    heads_cols = rel.shape[2]
    blk = slots * share
    rows_share = width // pieces

    def load_own(p):
        return pltpu.make_async_copy(wown_hbm.at[p], w.at[p, pl.ds(0, share)], psem.at[p])

    def load(p):
        return pltpu.make_async_copy(w2_hbm.at[p], w.at[p, pl.ds(share, blk - share)], wsem.at[p])

    first = pltpu.make_async_copy(w1_hbm.at[:, :, :, pl.ds(512, wo.shape[3])], wo, osem)
    first.start()
    for p in range(pieces):
        load_own(p).start()
        load(p).start()
    first.wait()
    for s in range(slots):
        for p in range(pieces):
            ws[s, p * rows_share : (p + 1) * rows_share, :] = wo[p, s, :, :heads_cols]
    small[...] = jnp.zeros_like(small)

    def head(c, _):
        rows = pl.ds(pl.multiple_of(c * ROWS, ROWS), ROWS)
        h = own[rows, :].astype(f32)
        for s in range(slots):
            h = h + nt(rel[s, rows, :], ws[s])
        unit, inv = normalise(h)
        n = unit * s1[...] + b1[...]
        unit1[rows, :] = unit
        inv1[rows, :] = inv
        normed[rows, :] = n
        nlow[rows, :] = n.astype(bf16)
        acc[rows, :] = n
        return 0

    lax.fori_loop(0, tokens // ROWS, head, 0)

    def out_copy(which, target, p, slot):
        return pltpu.make_async_copy(stage.at[which, slot], target.at[:, pl.ds(pl.multiple_of(p * blk, 128), blk)], ssem.at[which, slot])

    def forward(p, _):
        slot = lax.rem(p, 2)
        cols = pl.ds(pl.multiple_of(p * blk, 128), blk)
        load_own(p).wait()
        load(p).wait()

        @pl.when(p >= 2)
        def _():
            out_copy(0, act_hbm, p - 2, slot).wait()

        x = nlow[...]
        gp = nt(x, w[p, :, :width])
        up = nt(x, w[p, :, width : 2 * width])
        g[:, cols] = gp
        u[:, cols] = up
        a = (gp * jax.nn.sigmoid(gp) * up).astype(bf16)
        stage[0, slot] = a
        out_copy(0, act_hbm, p, slot).start()
        acc[...] += nn(a, w[p, :, 2 * width :])
        return 0

    lax.fori_loop(0, pieces, forward, 0)

    def middle(c, _):
        rows = pl.ds(pl.multiple_of(c * ROWS, ROWS), ROWS)
        unit, inv = normalise(acc[rows, :])
        layer_out[rows, :] = (unit * s2[...] + b2[...]).astype(bf16)
        up = cot[rows, :].astype(f32)
        d = norm_back(up, unit, inv, s2[...])
        small[2:3, :] += jnp.sum(up * unit, axis=0, keepdims=True)
        small[3:4, :] += jnp.sum(up, axis=0, keepdims=True)
        flow[rows, :] = d.astype(bf16)
        acc[rows, :] = d
        return 0

    lax.fori_loop(0, tokens // ROWS, middle, 0)
    for p in range(max(pieces - 2, 0), pieces):
        out_copy(0, act_hbm, p, p % 2).wait()

    def backward(p, _):
        slot = lax.rem(p, 2)
        cols = pl.ds(pl.multiple_of(p * blk, 128), blk)

        @pl.when(p >= 2)
        def _():
            out_copy(0, gg_hbm, p - 2, slot).wait()
            out_copy(1, ug_hbm, p - 2, slot).wait()

        da = nt(flow[...], w[p, :, 2 * width :])
        gp, up = g[:, cols], u[:, cols]
        sig = jax.nn.sigmoid(gp)
        dg = (da * up * sig * (1.0 + gp * (1.0 - sig))).astype(bf16)
        du = (da * gp * sig).astype(bf16)
        stage[0, slot] = dg
        stage[1, slot] = du
        out_copy(0, gg_hbm, p, slot).start()
        out_copy(1, ug_hbm, p, slot).start()
        acc[...] += nn(dg, w[p, :, :width]) + nn(du, w[p, :, width : 2 * width])
        return 0

    lax.fori_loop(0, pieces, backward, 0)

    def tail(c, _):
        rows = pl.ds(pl.multiple_of(c * ROWS, ROWS), ROWS)
        up, unit = acc[rows, :], unit1[rows, :]
        d = norm_back(up, unit, inv1[rows, :], s1[...])
        small[0:1, :] += jnp.sum(up * unit, axis=0, keepdims=True)
        small[1:2, :] += jnp.sum(up, axis=0, keepdims=True)
        grad_one[rows, :] = d
        low = d.astype(bf16)
        brt[:, rows] = d.T.astype(bf16)
        for s in range(slots):
            back[s, rows, :] = nn(low, ws[s]).astype(bf16)
        return 0

    lax.fori_loop(0, tokens // ROWS, tail, 0)
    for p in range(max(pieces - 2, 0), pieces):
        out_copy(0, gg_hbm, p, p % 2).wait()
        out_copy(1, ug_hbm, p, p % 2).wait()


def ffn_layer(own, cot, norms, rel, w1, w_own, w2):
    slots, tokens, cols = rel.shape
    width = own.shape[1]
    pieces, share = w_own.shape[:2]
    units = pieces * slots * share
    vm, hbm = pl.BlockSpec(memory_space=pltpu.VMEM), pl.BlockSpec(memory_space=pl.ANY)
    wide = jax.ShapeDtypeStruct((tokens, width), bf16)
    hidden = jax.ShapeDtypeStruct((tokens, units), bf16)
    return pl.pallas_call(
        functools.partial(ffn_kernel, slots=slots, pieces=pieces, share=share),
        out_shape=(wide, jax.ShapeDtypeStruct((tokens, width), f32), wide, wide, jax.ShapeDtypeStruct((width, tokens), bf16))
        + (jax.ShapeDtypeStruct((slots, tokens, cols), bf16), jax.ShapeDtypeStruct((8, width), f32), hidden, hidden, hidden),
        in_specs=[vm] * 7 + [hbm] * 3,
        out_specs=(vm,) * 7 + (hbm,) * 3,
        scratch_shapes=[
            pltpu.VMEM((pieces, slots * share, 3 * width), bf16),
            pltpu.VMEM((pieces, slots, width // pieces, 256), bf16),
            pltpu.VMEM((slots, width, cols), bf16),
            pltpu.VMEM((tokens, units), f32),
            pltpu.VMEM((tokens, units), f32),
            pltpu.VMEM((tokens, width), f32),
            pltpu.VMEM((tokens, width), f32),
            pltpu.VMEM((tokens, 1), f32),
            pltpu.VMEM((tokens, width), f32),
            pltpu.VMEM((2, 2, tokens, slots * share), bf16),
            pltpu.SemaphoreType.DMA((pieces,)),
            pltpu.SemaphoreType.DMA((pieces,)),
            pltpu.SemaphoreType.DMA,
            pltpu.SemaphoreType.DMA((2, 2)),
        ],
        compiler_params=pltpu.CompilerParams(vmem_limit_bytes=60 << 20),
        cost_estimate=pl.CostEstimate(flops=16 << 30, bytes_accessed=30 << 20, transcendentals=3 << 20),
        name="ffn_layer",
    )(own, cot, *norms, rel, w1, w_own, w2)


def wgrad_kernel(*refs, slots, share, add):
    gg, ug, act, brt, nlow, flow, rel, small = refs[1:9]
    got = refs[9] if add else None
    out = refs[-1]
    width = nlow.shape[1]
    cols = rel.shape[2]
    edge = 3 * width + cols
    room = out.shape[2] - edge

    def put(rows, lanes, value):
        if add:
            value = value + got[0, rows, lanes].astype(f32)
        out[0, rows, lanes] = value.astype(bf16)

    every = slice(0, out.shape[1])
    put(every, slice(0, width), tn(gg[...], nlow[...]))
    put(every, slice(width, 2 * width), tn(ug[...], nlow[...]))
    put(every, slice(2 * width, 3 * width), tn(act[...], flow[...]))
    for s in range(slots):
        put(slice(s * share, (s + 1) * share), slice(3 * width, edge), nn(brt[...], rel[s]))
        put(slice(s * share, (s + 1) * share), slice(edge, edge + room), jnp.concatenate([small[0], jnp.zeros((share - 16, room), f32)], axis=0))


def wgrad(me, first, count, gg, ug, act, brt, nlow, flow, rel, small, got, pieces, share, span):
    slots = rel.shape[0]
    tokens, width = nlow.shape
    blk = slots * share

    def piece(i, me):
        return jnp.bitwise_xor(2 * i + first, me[0])

    out_block = pl.BlockSpec((1, blk, span), lambda i, me: (i, 0, 0))
    in_specs = [pl.BlockSpec((tokens, blk), lambda i, me: (0, piece(i, me)))] * 3
    in_specs += [pl.BlockSpec((width // pieces, tokens), lambda i, me: (piece(i, me), 0))]
    in_specs += [pl.BlockSpec((tokens, width), lambda i, me: (0, 0))] * 2
    in_specs += [pl.BlockSpec(rel.shape, lambda i, me: (0, 0, 0)), pl.BlockSpec((1,) + small.shape[1:], lambda i, me: (piece(i, me), 0, 0))]
    args = [gg, ug, act, brt, nlow, flow, rel, small]
    if got is not None:
        in_specs.append(out_block)
        args.append(got)
    return pl.pallas_call(
        functools.partial(wgrad_kernel, slots=slots, share=share, add=got is not None),
        out_shape=jax.ShapeDtypeStruct((count, blk, span), bf16),
        grid_spec=pltpu.PrefetchScalarGridSpec(num_scalar_prefetch=1, grid=(count,), in_specs=in_specs, out_specs=out_block),
        compiler_params=pltpu.CompilerParams(vmem_limit_bytes=40 << 20),
        cost_estimate=pl.CostEstimate(flops=count << 30, bytes_accessed=count * 5 << 20, transcendentals=0),
        name="wgrad",
    )(me, *args)


ROPE_BASE = 1000.0


def rotate_axis(size, step):
    return [(i, (i + step) % size) for i in range(size)]


def line_axis(size, step):
    return [(i, i + step) for i in range(size) if 0 <= i + step < size]


def flip_axis(size, bit):
    return [(i, i ^ bit) for i in range(size)]


def after(value, *others):
    return lax.optimization_barrier((value, *others))[0]


def low_sum(left, right):
    return (left.astype(f32) + right.astype(f32)).astype(bf16)


def body(
    dp_size,
    tp_size,
    tokens,
    lengths,
    w_qkv,
    w_out,
    norm1_scale,
    norm1_shift,
    w_gate_up,
    w_down,
    norm2_scale,
    norm2_shift,
    cotangent,
):
    own = tokens[0]
    rows_here, width = own.shape
    docs = lengths.shape[1]
    seq = rows_here * tp_size
    cols_here = w_qkv.shape[2]
    heads = cols_here // HD
    units = w_gate_up.shape[2]
    pieces = min(dp_size, 8)
    groups = None if pieces == dp_size else [list(range(i, i + pieces)) for i in range(0, dp_size, pieces)]
    share = units // pieces
    rows_share = width // pieces
    span = -(-(3 * width + cols_here) // 128) * 128
    me = lax.rem(lax.axis_index("dp"), pieces)
    z = lax.axis_index("tensor")

    def flip(array, bit):
        return lax.ppermute(array, "dp", flip_axis(dp_size, bit))

    def shift(array, step):
        return lax.ppermute(array, "tensor", rotate_axis(tp_size, step))

    def along(array, step):
        return lax.ppermute(array, "tensor", line_axis(tp_size, step))

    def gather_dp(array):
        return lax.all_gather(array, "dp", axis=0, axis_index_groups=groups)

    def rope_order(matrix):
        halves = matrix.reshape(rows_share, heads, 2, HALF).transpose(0, 2, 1, 3).reshape(rows_share, 2, heads * HALF)
        return jnp.pad(halves, ((0, 0), (0, 0), (0, 128 - heads * HALF))).reshape(rows_share, 256)

    qkv_slice = lax.dynamic_slice_in_dim(w_qkv, me * rows_share, rows_share, 0)
    out_slice = lax.dynamic_slice_in_dim(w_out, me * rows_share, rows_share, 1)
    piece_one = jnp.concatenate([rope_order(qkv_slice[:, 0]), rope_order(qkv_slice[:, 1]), out_slice.T, qkv_slice[:, 2]], axis=1)
    gate_slice = lax.dynamic_slice_in_dim(w_gate_up, me * share, share, 2)
    down_slice = lax.dynamic_slice_in_dim(w_down, me * share, share, 0)
    piece_two = jnp.concatenate([gate_slice[:, 0].T, gate_slice[:, 1].T, down_slice], axis=1)
    piece_one, piece_two = lax.optimization_barrier((piece_one, piece_two))
    ones = [piece_one] + [shift(piece_one, s) for s in range(1, tp_size)]
    piece_two = after(piece_two, *ones[1:])
    twos = [shift(piece_two, s) for s in range(1, tp_size)]
    w1 = gather_dp(jnp.stack(ones))
    w2 = gather_dp(jnp.concatenate(twos, axis=0))

    own_late = after(own, *ones[1:])
    before, behind = along(own_late, 1), along(own_late, -1)
    before2, behind2 = along(before, 1), along(behind, -1)
    toks = [own, behind, jnp.where(z < tp_size // 2, behind2, before2), before]

    row_lengths, gate_up_late, down_late = after(lengths[0], ones[-1]), after(w_gate_up, ones[-1]), after(w_down, ones[-1])
    w_own = jnp.concatenate([gate_up_late[:, 0].T, gate_up_late[:, 1].T, down_late], axis=1).reshape(pieces, share, 3 * width)

    segment, position, lo, hi, base = doc_tables(row_lengths, seq, z * rows_here, rows_here)
    info = jnp.stack([lo, hi, base, me]).astype(jnp.int32)
    inverse = ROPE_BASE ** (-2.0 * lax.rem(jnp.arange(128), HALF).astype(f32) / HD)
    angles = position[:, None] * inverse[None, :]
    cosine, sine = jnp.cos(angles), jnp.sin(angles)
    seg_col = segment[:, None]

    saved = attn_fwd(info, toks, w1, cosine, sine, seg_col, docs, heads)
    rel = saved[4]
    norms = [v.reshape(1, width) for v in (norm1_scale, norm1_shift, norm2_scale, norm2_shift)]
    layer_out, grad_one, nlow, flow, brt, back, small, act, gg, ug = ffn_layer(own, cotangent[0], norms, rel, w1, w_own, w2)

    half = tp_size // 2

    def meet(one, two, bit):
        return low_sum(one, flip(two, bit))

    def reduce_slots(parts):
        total = parts[0].astype(f32)
        for s in range(1, tp_size):
            total = total + shift(parts[s], -s).astype(f32)
        return total.astype(bf16)

    me_array = me.reshape(1).astype(jnp.int32)
    room = span - 3 * width - cols_here
    chunk = small[:4].reshape(pieces, 4 * width // pieces // room, room)
    chunk = jnp.pad(chunk, ((0, 0), (0, 16 - chunk.shape[1]), (0, 0)))
    fixed = (gg, ug, act, brt, nlow, flow, rel, chunk)
    far_sent = wgrad(me_array, 5, 2, *fixed, None, pieces, share, span)
    near_sent = wgrad(after(me_array, far_sent), 1, 2, *fixed, None, pieces, share, span)
    far = wgrad(after(me_array, near_sent), 4, 2, *fixed, flip(far_sent, 1), pieces, share, span)
    near = wgrad(after(me_array, far), 0, 2, *fixed, flip(near_sent, 1), pieces, share, span)
    far, near = (v.reshape(2, tp_size, share, span) for v in (far, near))
    far_a, far_b, near_a, near_b = far[:, :half], far[:, half:], near[:, :half], near[:, half:]
    out_b, out_a = far_b, jnp.stack([near_a[1], far_a[1]])

    back, out_a, out_b = lax.optimization_barrier((back, out_a, out_b))
    next_b = meet(near_b, out_b, 4)
    next_a = meet(jnp.stack([near_a[0], far_a[0]]), out_a, 2)
    bwd = attn_bwd(info, toks, w1, cosine, sine, seg_col, saved, back, docs, heads, pieces)
    dw, dx = bwd[0], bwd[1:]
    right, left = along(dx[1], 1), along(dx[3], -1)
    across_half = lax.ppermute(dx[2], "tensor", rotate_axis(tp_size, half))
    input_grad = grad_one + dx[0] + right.astype(f32) + left.astype(f32) + across_half.astype(f32)

    last_b = meet(next_b[0], next_b[1], 2)
    last_a = meet(next_a[0], next_a[1], 4)
    last_a, last_b, right, left, across_half = lax.optimization_barrier((last_a, last_b, right, left, across_half))
    share_two = reduce_slots([last_a[i] for i in range(half)] + [last_b[i] for i in range(tp_size - half)])

    pairs = dw.reshape((pieces // 2, 2) + dw.shape[1:])
    pairs = meet(pairs[:, 0], pairs[:, 1], 1).reshape((2, 2) + dw.shape[1:])
    next_a = meet(pairs[:, 0, :half], pairs[:, 1, :half], 2)
    next_b = meet(pairs[0, :, half:], pairs[1, :, half:], 4)
    last_a, last_b = meet(next_a[0], next_a[1], 4), meet(next_b[0], next_b[1], 2)
    last_a, last_b, share_two = lax.optimization_barrier((last_a, last_b, share_two))
    share_one = reduce_slots([last_a[i] for i in range(half)] + [last_b[i] for i in range(tp_size - half)])

    def finish(array):
        if groups is not None:
            across = [[g * pieces + i for g in range(dp_size // pieces)] for i in range(pieces)]
            array = lax.psum(array.astype(f32), "dp", axis_index_groups=across).astype(bf16)
        return gather_dp(array)

    main = finish(share_two).reshape(units, span).astype(f32)
    down_sum = main[:, 2 * width : 3 * width]
    out_sum = main[:, 3 * width : 3 * width + cols_here].T
    gate_up_sum = jnp.stack([main[:, :width].T, main[:, width : 2 * width].T], axis=1)
    q3 = finish(share_one).reshape(width, -1).astype(f32)

    def rope_back(matrix):
        halves = matrix.reshape(width, 2, 128)[:, :, : heads * HALF].reshape(width, 2, heads, HALF)
        return halves.transpose(0, 2, 1, 3).reshape(width, cols_here)

    qkv_sum = jnp.stack([rope_back(q3[:, :256]), rope_back(q3[:, 256:512]), q3[:, 512 : 512 + cols_here]], axis=1)
    small_out = main.reshape(pieces, share, span)[:, : 4 * width // pieces // room, span - room :].reshape(4, width)
    return (
        layer_out[None],
        input_grad[None],
        qkv_sum,
        out_sum,
        small_out[0],
        small_out[1],
        gate_up_sum,
        down_sum,
        small_out[2],
        small_out[3],
    )


def solution(mesh):
    in_specs = (
        P("dp", "tensor", None),
        P("dp", None),
        P(None, None, "tensor"),
        P("tensor", None),
        P(),
        P(),
        P(None, None, "tensor"),
        P("tensor", None),
        P(),
        P(),
        P("dp", "tensor", None),
    )
    out_specs = (
        P("dp", "tensor", None),
        P("dp", "tensor", None),
        P(None, None, "tensor"),
        P("tensor", None),
        P(),
        P(),
        P(None, None, "tensor"),
        P("tensor", None),
        P(),
        P(),
    )
    return jax.shard_map(
        functools.partial(body, mesh.shape["dp"], mesh.shape["tensor"]),
        mesh=mesh,
        in_specs=in_specs,
        out_specs=out_specs,
        check_vma=False,
    )
```

time: 606 us -> 547 us (0.903)
  the two profiles are of different devices: /device:TPU:17 before, /device:TPU:0 now
where the time goes in v2:
time: 547 us; the launch traced here: 544 us
  waiting for transfers between devices  186 us (34%)
  Pallas kernels  132 us (24%)
  starting transfers between devices  110 us (20%)
  local copies, waits for them, and re-layouts  66.2 us (12%)
  other arithmetic  29.7 us (5%)
  between operations  19.8 us (4%)
    ppermute x12, waiting for transfers between devices, shift(): return lax.ppermute(array, 'tensor', rotate_axis(tp_size, step))  92.5 us
    ppermute x11, starting transfers between devices, flip(): return lax.ppermute(array, 'dp', flip_axis(dp_size, bit))  65.5 us
    all_gather x4, waiting for transfers between devices, gather_dp(): return lax.all_gather(array, 'dp', axis=0, axis_index_groups=groups)  46.4 us
    pallas_call x1, Pallas kernels, ffn_layer(): pl.pallas_call(functools.partial(ffn_kernel, slots=slots, pieces=pieces,...  41.7 us
    pallas_call x1, Pallas kernels, attn_bwd(): pl.pallas_call(functools.partial(attn_bwd_kernel, docs=docs, heads=heads,...  40.8 us
    ppermute x11, waiting for transfers between devices, flip(): return lax.ppermute(array, 'dp', flip_axis(dp_size, bit))  33.4 us
    pallas_call x1, Pallas kernels, attn_fwd(): pl.pallas_call(functools.partial(attn_fwd_kernel, docs=docs, heads=heads,...  29.1 us
    unnamed x74, local copies, waits for them, and re-layouts  27.8 us
  transfers between devices with their start and end apart: 34, of which 19 were waited for; matrix products, arithmetic and copies ran while one was open for 8% of the time, Pallas kernels for 15%

profile of v2, /device:TPU:0, one launch (start us, length us, event | category | flops | bytes accessed | tf_op | source)
XLA Modules:
  0.0 543.8 jit_solution(14541900311667942406)
XLA Ops:
  10.8 2.9 constant_dynamic-slice_fusion.2
  14.5 4.1 collective-permute-start.2
  18.6 1.6 collective-permute-start.1
  20.1 2.2 collective-permute-start
  22.4 8.8 %collective-permute-done.2 = bf16[96,896]{1,0:T(8,128)(2,1)S(1)} collective-permute-done((bf16[96,896]{1,0:T(8,128)(2,1)S(1)}, bf16[96,896]{1,0:T(8,128)(2,1)S(1)}, u32[]{:S(2)}, u32[]{:S(2)}) %collective-permute-start.2) | collective-permute-done | bytes 172064 | tf_op jit(solution)/shard_map/ppermute | solution.py:574
  33.0 2.1 collective-permute-start.9
  35.1 2.7 collective-permute-start.8
  37.8 1.9 collective-permute-start.7
  39.8 6.4 %collective-permute-done.9 = bf16[96,2304]{1,0:T(8,128)(2,1)S(1)} collective-permute-done((bf16[96,2304]{1,0:T(8,128)(2,1)S(1)}, bf16[96,2304]{1,0:T(8,128)(2,1)S(1)}, u32[]{:S(2)}, u32[]{:S(2)}) %collective-permute-start.9) | collective-permute-done | bytes 442400 | tf_op jit(solution)/shard_map/ppermute | solution.py:574
  46.2 30.4 %collective-permute-done.8 = bf16[96,2304]{1,0:T(8,128)(2,1)S(1)} collective-permute-done((bf16[96,2304]{1,0:T(8,128)(2,1)S(1)}, bf16[96,2304]{1,0:T(8,128)(2,1)S(1)}, u32[]{:S(2)}, u32[]{:S(2)}) %collective-permute-start.8) | collective-permute-done | bytes 442400 | tf_op jit(solution)/shard_map/ppermute | solution.py:574
  91.0 6.7 %copy.111 = bf16[768,2,768]{0,2,1:T(8,128)(2,1)} copy(bf16[768,2,768]{2,1,0:T(2,128)(2,1)} %param.17) | data formatting | bytes 4718592 | tf_op jit(solution)/shard_map/optimization_barrier | solution.py:533
  97.8 1.9 slice_bitcast_fusion.5
  99.7 1.9 pad_maximum_fusion.1
  101.6 4.6 collective-permute-start.6
  106.3 1.5 collective-permute-start.4
  107.8 5.5 %multiply_sine_fusion = (f32[2048,128]{1,0:T(8,128)}, f32[2048,128]{1,0:T(8,128)}) fusion(f32[128]{0:T(128)S(1)} %multiply_power_fusion, f32[2048]{0:T(1024)S(1)} %subtract_convert_fusion), kind=kLoop, calls=%fused_computation.17 | loop fusion | flops 262144 | bytes 2105856 | tf_op jit(solution)/shard_map/sin | solution.py:611
  113.4 9.0 %collective-permute-done.6 = bf16[512,768]{1,0:T(8,128)(2,1)S(1)} collective-permute-done((bf16[512,768]{1,0:T(8,128)(2,1)S(1)}, bf16[512,768]{1,0:T(8,128)(2,1)S(1)}, u32[]{:S(2)}, u32[]{:S(2)}) %collective-permute-start.6) | collective-permute-done | bytes 786464 | tf_op jit(solution)/shard_map/ppermute | solution.py:577
  122.3 4.2 collective-permute-done.4
  126.7 29.1 %attn_fwd.1 = (bf16[4,3,512,256]{3,2,1,0:T(8,128)(2,1)}, bf16[4,2048,256]{2,1,0:T(8,128)(2,1)}, bf16[4,2048,192]{2,1,0:T(8,128)(2,1)}, f32[4,8,512]{2,1,0:T(8,128)S(1)}, bf16[4,512,192]{2,1,0:T(8,128)(2,1)}) custom-call(s32[4]{0:T(128)S(1)} %pad_add_fusion.info, bf16[512,768]{1,0:T(8,128)(2,1)S(1)} %bitcast.153, ...), custom_call_target="tpu_custom_call" | custom-call | flops 21474836480 | bytes 20971520 | tf_op jit(solution)/shard_map/attn_fwd/pallas_call | solution.py:123
  156.4 41.7 %ffn_layer.1 = (bf16[512,768]{1,0:T(8,128)(2,1)}, f32[512,768]{1,0:T(8,128)}, bf16[512,768]{1,0:T(8,128)(2,1)}, bf16[512,768]{1,0:T(8,128)(2,1)}, bf16[768,512]{...) custom-call(bf16[512,768]{1,0:T(8,128)(2,1)} %bitcast.149, ...), custom_call_target="tpu_custom_call" | custom-call | flops 17179869184 | bytes 31457280 | tf_op jit(solution)/shard_map/ffn_layer/pallas_call | solution.py:439
  199.0 1.9 copy-done.2
  200.9 1.9 copy-done.3
  202.8 1.9 copy-done.4
  208.1 4.1 wgrad.4
  212.2 4.1 wgrad.5
  216.9 2.3 collective-permute-done.10.refs_9_
  219.2 1.9 copy-done.19
  221.1 5.6 %wgrad.6 = bf16[2,384,2560]{2,1,0:T(8,128)(2,1)} custom-call(s32[1]{0:T(128)} %bitcast.22.refs_0_, bf16[512,3072]{1,0:T(8,128)(2,1)S(1)} %copy-done.3, bf16[512,3072]{1,0:T(8,128)(2,1)S(1)} %copy-done.4, bf16[512,3072]{1,0:T(8,128)(2,1)S(1)} %copy-done.2, bf16[768,512]{1,0:T(8,128)(2,1)S(1)} %copy-done.8, bf16[512,768]{1,0:T(8,128)(2,1)S(1)} %copy-done.6, ...), custom_call_target="tpu_custom_call" | custom-call | flops 2147483648 | bytes 10485760 | tf_op jit(solution)/shard_map/wgrad/pallas_call | solution.py:507
  226.7 1.7 slice.221
  228.4 2.0 copy-done.18
  230.4 6.0 %wgrad.7 = bf16[2,384,2560]{2,1,0:T(8,128)(2,1)} custom-call(s32[1]{0:T(128)} %bitcast.22.refs_0_, bf16[512,3072]{1,0:T(8,128)(2,1)S(1)} %copy-done.3, bf16[512,3072]{1,0:T(8,128)(2,1)S(1)} %copy-done.4, bf16[512,3072]{1,0:T(8,128)(2,1)S(1)} %copy-done.2, bf16[768,512]{1,0:T(8,128)(2,1)S(1)} %copy-done.8, bf16[512,768]{1,0:T(8,128)(2,1)S(1)} %copy-done.6, ...), custom_call_target="tpu_custom_call" | custom-call | flops 2147483648 | bytes 10485760 | tf_op jit(solution)/shard_map/wgrad/pallas_call | solution.py:507
  236.4 1.8 fusion.17
  238.2 1.4 pad_maximum_fusion.3
  239.6 1.7 collective-permute-start.20
  241.3 20.7 %collective-permute-start.22 = (bf16[2,2,96,2560]{3,2,1,0:T(8,128)(2,1)S(1)}, bf16[2,2,96,2560]{3,2,1,0:T(8,128)(2,1)S(1)}, u32[]{:S(2)}, u32[]{:S(2)}) collective-permute-start(bf16[2,2,96,2560]{3,2,1,0:T(8,128)(2,1)S(1)} %slice.221), channel_id=1, source_target_pairs={{0,16},{4,20},{8,24},{12,28},{16,0},{20,4},{24,8},{28,12},{1,17},{... | collective-permute-start | bytes 5898248 | tf_op jit(solution)/shard_map/ppermute | solution.py:571
  262.0 40.8 %attn_bwd.1 = (bf16[8,4,96,768]{3,2,1,0:T(8,128)(2,1)}, f32[512,768]{1,0:T(8,128)}, bf16[512,768]{1,0:T(8,128)(2,1)}, bf16[512,768]{1,0:T(8,128)(2,1)}, bf16[512,768]{1,0:T(8,128)(2,1)}) custom-call(s32[4]{0:T(128)} %copy-done.10, bf16[512,768]{1,0:T(8,128)(2,1)} %bitcast.150, bf16[512,768]{1,0:T(8,128)(2,1)} %copy-done.13, bf16[512,768]{1,0:T(8,128)(2,1)} %copy-done.9, ...), custom_call_target="tpu_custom_call" | custom-call | flops 42949672960 | bytes 25165824 | tf_op jit(solution)/shard_map/attn_bwd/pallas_call | solution.py:240
  302.9 9.5 %collective-permute-start.12 = (bf16[512,768]{1,0:T(8,128)(2,1)}, bf16[512,768]{1,0:T(8,128)(2,1)S(1)}, u32[]{:S(2)}, u32[]{:S(2)}) collective-permute-start(bf16[512,768]{1,0:T(8,128)(2,1)} %get-tuple-element.75), channel_id=1, source_target_pairs={{0,1},{1,2},{2,3},{4,5},{5,6},{6,7},{8,9},{9,10},{10,11},{12,13},{... | collective-permute-start | bytes 2359304 | tf_op jit(solution)/shard_map/ppermute | solution.py:577
  313.7 2.1 collective-permute-start.14
  315.8 1.8 slice_bitcast_fusion.2
  317.6 21.4 %collective-permute-start.15 = (bf16[4,4,96,768]{3,2,1,0:T(8,128)(2,1)S(1)}, bf16[4,4,96,768]{3,2,1,0:T(8,128)(2,1)S(1)}, u32[]{:S(2)}, u32[]{:S(2)}) collective-permute-start(bf16[4,4,96,768]{3,2,1,0:T(8,128)(2,1)S(1)} %slice_bitcast_fusion.2), channel_id=1, source_target_pairs={{0,4},{4,0},{8,12},{12,8},{16,20},{20,16},{24,28},{28,24},{1,5},{5... | collective-permute-start | bytes 7077896 | tf_op jit(solution)/shard_map/ppermute | solution.py:571
  339.0 2.1 add_convert_fusion.1
  343.2 8.4 %collective-permute-start.23 = (bf16[2,96,2560]{2,1,0:T(8,128)(2,1)S(1)}, bf16[2,96,2560]{2,1,0:T(8,128)(2,1)S(1)}, u32[]{:S(2)}, u32[]{:S(2)}) collective-permute-start(bf16[2,96,2560]{2,1,0:T(8,128)(2,1)S(1)} %slice_bitcast_fusion.6), channel_id=1, source_target_pairs={{0,8},{4,12},{8,0},{12,4},{16,24},{20,28},{24,16},{28,20},{1,9},{5... | collective-permute-start | bytes 2949128 | tf_op jit(solution)/shard_map/ppermute | solution.py:571
  352.4 12.6 %collective-permute-done.21 = bf16[2,96,2560]{2,1,0:T(8,128)(2,1)S(1)} collective-permute-done((bf16[2,96,2560]{2,1,0:T(8,128)(2,1)S(1)}, bf16[2,96,2560]{2,1,0:T(8,128)(2,1)S(1)}, u32[]{:S(2)}, u32[]{:S(2)}) %collective-permute-start.21) | collective-permute-done | bytes 983072 | tf_op jit(solution)/shard_map/ppermute | solution.py:571
  365.0 8.5 %collective-permute-start.16 = (bf16[2,2,96,768]{3,2,1,0:T(8,128)(2,1)S(1)}, bf16[2,2,96,768]{3,2,1,0:T(8,128)(2,1)S(1)}, u32[]{:S(2)}, u32[]{:S(2)}) collective-permute-start(bf16[2,2,96,768]{3,2,1,0:T(8,128)(2,1)S(1)} %slice_bitcast_fusion.14), channel_id=1, source_target_pairs={{0,8},{4,12},{8,0},{12,4},{16,24},{20,28},{24,16},{28,20},{1,9},{5... | collective-permute-start | bytes 1769480 | tf_op jit(solution)/shard_map/ppermute | solution.py:571
  375.5 11.3 %collective-permute-done.16 = bf16[2,2,96,768]{3,2,1,0:T(8,128)(2,1)S(1)} collective-permute-done((bf16[2,2,96,768]{3,2,1,0:T(8,128)(2,1)S(1)}, bf16[2,2,96,768]{3,2,1,0:T(8,128)(2,1)S(1)}, u32[]{:S(2)}, u32[]{:S(2)}) %collective-permute-start.16) | collective-permute-done | bytes 589856 | tf_op jit(solution)/shard_map/ppermute | solution.py:571
  386.7 1.8 collective-permute-done.18
  388.9 1.4 collective-permute-start.17
  390.3 1.5 collective-permute-start.19
  391.8 2.7 collective-permute-start.24
  396.4 3.3 collective-permute-done.19
  400.6 6.8 %collective-permute-done.24 = bf16[96,2560]{1,0:T(8,128)(2,1)S(1)} collective-permute-done((bf16[96,2560]{1,0:T(8,128)(2,1)S(1)}, bf16[96,2560]{1,0:T(8,128)(2,1)S(1)}, u32[]{:S(2)}, u32[]{:S(2)}) %collective-permute-start.24) | collective-permute-done | bytes 491552 | tf_op jit(solution)/shard_map/ppermute | solution.py:574
  407.3 28.0 %collective-permute-done.25 = bf16[96,2560]{1,0:T(8,128)(2,1)S(1)} collective-permute-done((bf16[96,2560]{1,0:T(8,128)(2,1)S(1)}, bf16[96,2560]{1,0:T(8,128)(2,1)S(1)}, u32[]{:S(2)}, u32[]{:S(2)}) %collective-permute-start.25) | collective-permute-done | bytes 491552 | tf_op jit(solution)/shard_map/ppermute | solution.py:574
  437.4 3.1 collective-permute-start.28
  440.5 1.9 collective-permute-start.29
  442.6 11.4 %collective-permute-done.28 = bf16[96,768]{1,0:T(8,128)(2,1)S(1)} collective-permute-done((bf16[96,768]{1,0:T(8,128)(2,1)S(1)}, bf16[96,768]{1,0:T(8,128)(2,1)S(1)}, u32[]{:S(2)}, u32[]{:S(2)}) %collective-permute-start.28) | collective-permute-done | bytes 147488 | tf_op jit(solution)/shard_map/ppermute | solution.py:574
  455.3 3.1 add_bitcast_fusion
  458.4 16.8 %all-gather.13.cloned.1.call-done = bf16[768,768]{1,0:T(8,128)(2,1)} async-done(((bf16[96,768]{1,0:T(8,128)(2,1)}), bf16[768,768]{1,0:T(8,128)(2,1)}) %all-gather.13.cloned.1.call-update) | async-done | bytes 1179664 | tf_op jit(solution)/shard_map/all_gather | solution.py:580
  481.9 1.8 copy.124
  483.7 29.5 %all-gather.15.cloned.1.call-done = bf16[768,2560]{1,0:T(8,128)(2,1)} async-done(((bf16[96,2560]{1,0:T(8,128)(2,1)}), bf16[768,2560]{1,0:T(8,128)(2,1)}) %all-gather.15.cloned.1.call-update) | async-done | bytes 3932176 | tf_op jit(solution)/shard_map/all_gather | solution.py:580
  513.2 3.2 convert_element_type.254
  516.5 1.8 slice_bitcast_fusion.1
  522.1 4.1 pad_maximum_fusion
  526.2 8.2 %copy.126 = f32[768,2,768]{2,1,0:T(2,128)} copy(f32[768,2,768]{0,2,1:T(8,128)} %pad_maximum_fusion) | data formatting | bytes 9437184
  534.4 2.8 slice.249
  (176 shorter events, 43.8 us)
Async XLA Ops:
  7.2 119.5 %all-gather.9.cloned.1.call-start = ((), (), s32[]{:S(2)}) async-start(), calls=%async_computation | async-start | bytes 6193152 | tf_op jit(solution)/shard_map/all_gather | solution.py:580
  14.5 16.7 %collective-permute-start.2 = (bf16[96,896]{1,0:T(8,128)(2,1)S(1)}, bf16[96,896]{1,0:T(8,128)(2,1)S(1)}, u32[]{:S(2)}, u32[]{:S(2)}) collective-permute-start(bf16[96,896]{1,0:T(8,128)(2,1)S(1)} %pad_maximum_fusion.7), channel_id=1, source_target_pairs={{0,2},{1,3},{2,0},{3,1},{4,6},{5,7},{6,4},{7,5},{8,10},{9,11},{10,... | collective-permute-start | bytes 516104 | tf_op jit(solution)/shard_map/ppermute | solution.py:574
  18.6 12.6 %collective-permute-start.1 = (bf16[96,896]{1,0:T(8,128)(2,1)S(1)}, bf16[96,896]{1,0:T(8,128)(2,1)S(1)}, u32[]{:S(2)}, u32[]{:S(2)}) collective-permute-start(bf16[96,896]{1,0:T(8,128)(2,1)S(1)} %pad_maximum_fusion.7), channel_id=1, source_target_pairs={{0,1},{1,2},{2,3},{3,0},{4,5},{5,6},{6,7},{7,4},{8,9},{9,10},{10,1... | collective-permute-start | bytes 516104 | tf_op jit(solution)/shard_map/ppermute | solution.py:574
  20.1 11.8 %collective-permute-start = (bf16[96,896]{1,0:T(8,128)(2,1)S(1)}, bf16[96,896]{1,0:T(8,128)(2,1)S(1)}, u32[]{:S(2)}, u32[]{:S(2)}) collective-permute-start(bf16[96,896]{1,0:T(8,128)(2,1)S(1)} %pad_maximum_fusion.7), channel_id=1, source_target_pairs={{0,3},{1,0},{2,1},{3,2},{4,7},{5,4},{6,5},{7,6},{8,11},{9,8},{10,9... | collective-permute-start | bytes 516104 | tf_op jit(solution)/shard_map/ppermute | solution.py:574
  32.9 44.9 %copy-start.27 = (f32[768]{0:T(1024)S(1)}, f32[768]{0:T(1024)}, u32[]{:S(2)}) copy-start(f32[768]{0:T(1024)} %param.15) | copy-start | bytes 9220
  32.9 45.5 %copy-start.28 = (f32[768]{0:T(1024)S(1)}, f32[768]{0:T(1024)}, u32[]{:S(2)}) copy-start(f32[768]{0:T(1024)} %param.16) | copy-start | bytes 9220
  32.9 46.1 %copy-start.29 = (f32[768]{0:T(1024)S(1)}, f32[768]{0:T(1024)}, u32[]{:S(2)}) copy-start(f32[768]{0:T(1024)} %param.19) | copy-start | bytes 9220
  32.9 46.7 %copy-start.30 = (f32[768]{0:T(1024)S(1)}, f32[768]{0:T(1024)}, u32[]{:S(2)}) copy-start(f32[768]{0:T(1024)} %param.20) | copy-start | bytes 9220
  32.9 47.3 %copy-start.31 = (s32[1,24]{1,0:T(1,128)S(1)}, s32[1,24]{1,0:T(1,128)}, u32[]{:S(2)}) copy-start(s32[1,24]{1,0:T(1,128)} %param.12) | copy-start | bytes 292
  32.9 48.0 %copy-start.11 = (bf16[1,512,768]{2,1,0:T(8,128)(2,1)S(1)}, bf16[1,512,768]{2,1,0:T(8,128)(2,1)}, u32[]{:S(2)}) copy-start(bf16[1,512,768]{2,1,0:T(8,128)(2,1)} %param.11) | copy-start | bytes 2359300
  32.9 123.5 %all-gather.11.cloned.1.call-start = ((), (), s32[]{:S(2)}) async-start(), calls=%async_computation.1 | async-start | bytes 11943936 | tf_op jit(solution)/shard_map/all_gather | solution.py:580
  33.0 13.2 %collective-permute-start.9 = (bf16[96,2304]{1,0:T(8,128)(2,1)S(1)}, bf16[96,2304]{1,0:T(8,128)(2,1)S(1)}, u32[]{:S(2)}, u32[]{:S(2)}) collective-permute-start(bf16[96,2304]{1,0:T(8,128)(2,1)S(1)} %pad_maximum_fusion.6), channel_id=1, source_target_pairs={{0,3},{1,0},{2,1},{3,2},{4,7},{5,4},{6,5},{7,6},{8,11},{9,8},{10,9... | collective-permute-start | bytes 1327112 | tf_op jit(solution)/shard_map/ppermute | solution.py:574
  35.1 41.4 %collective-permute-start.8 = (bf16[96,2304]{1,0:T(8,128)(2,1)S(1)}, bf16[96,2304]{1,0:T(8,128)(2,1)S(1)}, u32[]{:S(2)}, u32[]{:S(2)}) collective-permute-start(bf16[96,2304]{1,0:T(8,128)(2,1)S(1)} %pad_maximum_fusion.6), channel_id=1, source_target_pairs={{0,2},{1,3},{2,0},{3,1},{4,6},{5,7},{6,4},{7,5},{8,10},{9,11},{10,... | collective-permute-start | bytes 1327112 | tf_op jit(solution)/shard_map/ppermute | solution.py:574
  37.8 38.7 %collective-permute-start.7 = (bf16[96,2304]{1,0:T(8,128)(2,1)S(1)}, bf16[96,2304]{1,0:T(8,128)(2,1)S(1)}, u32[]{:S(2)}, u32[]{:S(2)}) collective-permute-start(bf16[96,2304]{1,0:T(8,128)(2,1)S(1)} %pad_maximum_fusion.6), channel_id=1, source_target_pairs={{0,1},{1,2},{2,3},{3,0},{4,5},{5,6},{6,7},{7,4},{8,9},{9,10},{10,1... | collective-permute-start | bytes 1327112 | tf_op jit(solution)/shard_map/ppermute | solution.py:574
  77.7 397.5 %all-gather.13.cloned.1.call-start = ((), (), s32[]{:S(2)}) async-start(), calls=%async_computation.2 | async-start | bytes 1327104 | tf_op jit(solution)/shard_map/all_gather | solution.py:580
  80.9 20.7 %collective-permute-start.5 = (bf16[512,768]{1,0:T(8,128)(2,1)S(1)}, bf16[512,768]{1,0:T(8,128)(2,1)S(1)}, u32[]{:S(2)}, u32[]{:S(2)}) collective-permute-start(bf16[512,768]{1,0:T(8,128)(2,1)S(1)} %bitcast.151), channel_id=1, source_target_pairs={{0,1},{1,2},{2,3},{4,5},{5,6},{6,7},{8,9},{9,10},{10,11},{12,13},{... | collective-permute-start | bytes 2359304 | tf_op jit(solution)/shard_map/ppermute | solution.py:577
  82.3 24.0 %collective-permute-start.3 = (bf16[512,768]{1,0:T(8,128)(2,1)S(1)}, bf16[512,768]{1,0:T(8,128)(2,1)S(1)}, u32[]{:S(2)}, u32[]{:S(2)}) collective-permute-start(bf16[512,768]{1,0:T(8,128)(2,1)S(1)} %bitcast.152), channel_id=1, source_target_pairs={{1,0},{2,1},{3,2},{5,4},{6,5},{7,6},{9,8},{10,9},{11,10},{13,12},{... | collective-permute-start | bytes 2359304 | tf_op jit(solution)/shard_map/ppermute | solution.py:577
  97.8 2.0 copy-start.23
  101.6 54.1 %copy-start.12 = (bf16[512,768]{1,0:T(8,128)(2,1)}, bf16[512,768]{1,0:T(8,128)(2,1)S(1)}, u32[]{:S(2)}) copy-start(bf16[512,768]{1,0:T(8,128)(2,1)S(1)} %collective-permute-done.5.refs_3_) | copy-start | bytes 2359300
  101.6 20.7 %collective-permute-start.6 = (bf16[512,768]{1,0:T(8,128)(2,1)S(1)}, bf16[512,768]{1,0:T(8,128)(2,1)S(1)}, u32[]{:S(2)}, u32[]{:S(2)}) collective-permute-start(bf16[512,768]{1,0:T(8,128)(2,1)S(1)} %collective-permute-done.5.refs_3_), channel_id=1, source_target_pairs={{0,1},{1,2},{2,3},{4,5},{5,6},{6,7},{8,9},{9,10},{10,11},{12,13},{... | collective-permute-start | bytes 2359304 | tf_op jit(solution)/shard_map/ppermute | solution.py:577
  106.2 49.5 %copy-start.13 = (bf16[512,768]{1,0:T(8,128)(2,1)}, bf16[512,768]{1,0:T(8,128)(2,1)S(1)}, u32[]{:S(2)}) copy-start(bf16[512,768]{1,0:T(8,128)(2,1)S(1)} %collective-permute-done.3.refs_1_) | copy-start | bytes 2359300
  106.3 20.3 %collective-permute-start.4 = (bf16[512,768]{1,0:T(8,128)(2,1)S(1)}, bf16[512,768]{1,0:T(8,128)(2,1)S(1)}, u32[]{:S(2)}, u32[]{:S(2)}) collective-permute-start(bf16[512,768]{1,0:T(8,128)(2,1)S(1)} %collective-permute-done.3.refs_1_), channel_id=1, source_target_pairs={{1,0},{2,1},{3,2},{5,4},{6,5},{7,6},{9,8},{10,9},{11,10},{13,12},{... | collective-permute-start | bytes 2359304 | tf_op jit(solution)/shard_map/ppermute | solution.py:577
  107.8 48.0 %copy-start.10 = (s32[4]{0:T(128)}, s32[4]{0:T(128)S(1)}, u32[]{:S(2)}) copy-start(s32[4]{0:T(128)S(1)} %pad_add_fusion.info) | copy-start | bytes 52
  126.6 29.2 %copy-start.9 = (bf16[512,768]{1,0:T(8,128)(2,1)}, bf16[512,768]{1,0:T(8,128)(2,1)S(1)}, u32[]{:S(2)}) copy-start(bf16[512,768]{1,0:T(8,128)(2,1)S(1)} %broadcast_select_fusion.refs_2_) | copy-start | bytes 2359300
  156.4 42.6 %copy-start.5 = (bf16[4,512,192]{2,1,0:T(8,128)(2,1)S(1)}, bf16[4,512,192]{2,1,0:T(8,128)(2,1)}, u32[]{:S(2)}) copy-start(bf16[4,512,192]{2,1,0:T(8,128)(2,1)} %get-tuple-element.51.refs_6_.refs_7_.refs_12_) | copy-start | bytes 2359300
  199.0 1.9 copy-start.2
  200.9 1.9 copy-start.3
  202.8 1.9 copy-start.4
  204.7 1.1 copy-start.6
  212.2 7.0 %collective-permute-start.10 = (bf16[2,384,2560]{2,1,0:T(8,128)(2,1)}, bf16[2,384,2560]{2,1,0:T(8,128)(2,1)S(1)}, u32[]{:S(2)}, u32[]{:S(2)}) collective-permute-start(bf16[2,384,2560]{2,1,0:T(8,128)(2,1)} %wgrad.4), channel_id=1, source_target_pairs={{0,4},{4,0},{8,12},{12,8},{16,20},{20,16},{24,28},{28,24},{1,5},{5... | collective-permute-start | bytes 11796488 | tf_op jit(solution)/shard_map/ppermute | solution.py:571
  216.3 12.1 %collective-permute-start.11 = (bf16[2,384,2560]{2,1,0:T(8,128)(2,1)}, bf16[2,384,2560]{2,1,0:T(8,128)(2,1)S(1)}, u32[]{:S(2)}, u32[]{:S(2)}) collective-permute-start(bf16[2,384,2560]{2,1,0:T(8,128)(2,1)} %wgrad.5), channel_id=1, source_target_pairs={{0,4},{4,0},{8,12},{12,8},{16,20},{20,16},{24,28},{28,24},{1,5},{5... | collective-permute-start | bytes 11796488 | tf_op jit(solution)/shard_map/ppermute | solution.py:571
  219.2 1.9 copy-start.19
  228.4 8.0 %copy-start.16 = (bf16[2,384,2560]{2,1,0:T(8,128)(2,1)S(1)}, bf16[2,384,2560]{2,1,0:T(8,128)(2,1)}, u32[]{:S(2)}) copy-start(bf16[2,384,2560]{2,1,0:T(8,128)(2,1)} %wgrad.6) | copy-start | bytes 11796484
  228.4 2.0 copy-start.18
  239.6 78.0 %collective-permute-start.20 = (bf16[2,2,96,2560]{3,2,1,0:T(8,128)(2,1)}, bf16[2,2,96,2560]{3,2,1,0:T(8,128)(2,1)}, u32[]{:S(2)}, u32[]{:S(2)}) collective-permute-start(bf16[2,2,96,2560]{3,2,1,0:T(8,128)(2,1)} %pad_maximum_fusion.3), channel_id=1, source_target_pairs={{0,8},{4,12},{8,0},{12,4},{16,24},{20,28},{24,16},{28,20},{1,9},{5... | collective-permute-start | bytes 5898248 | tf_op jit(solution)/shard_map/ppermute | solution.py:571
  241.3 99.9 %collective-permute-start.22 = (bf16[2,2,96,2560]{3,2,1,0:T(8,128)(2,1)S(1)}, bf16[2,2,96,2560]{3,2,1,0:T(8,128)(2,1)S(1)}, u32[]{:S(2)}, u32[]{:S(2)}) collective-permute-start(bf16[2,2,96,2560]{3,2,1,0:T(8,128)(2,1)S(1)} %slice.221), channel_id=1, source_target_pairs={{0,16},{4,20},{8,24},{12,28},{16,0},{20,4},{24,8},{28,12},{1,17},{... | collective-permute-start | bytes 5898248 | tf_op jit(solution)/shard_map/ppermute | solution.py:571
  302.9 72.5 %collective-permute-start.12 = (bf16[512,768]{1,0:T(8,128)(2,1)}, bf16[512,768]{1,0:T(8,128)(2,1)S(1)}, u32[]{:S(2)}, u32[]{:S(2)}) collective-permute-start(bf16[512,768]{1,0:T(8,128)(2,1)} %get-tuple-element.75), channel_id=1, source_target_pairs={{0,1},{1,2},{2,3},{4,5},{5,6},{6,7},{8,9},{9,10},{10,11},{12,13},{... | collective-permute-start | bytes 2359304 | tf_op jit(solution)/shard_map/ppermute | solution.py:577
  312.4 63.0 %collective-permute-start.13 = (bf16[512,768]{1,0:T(8,128)(2,1)}, bf16[512,768]{1,0:T(8,128)(2,1)S(1)}, u32[]{:S(2)}, u32[]{:S(2)}) collective-permute-start(bf16[512,768]{1,0:T(8,128)(2,1)} %get-tuple-element.76), channel_id=1, source_target_pairs={{1,0},{2,1},{3,2},{5,4},{6,5},{7,6},{9,8},{10,9},{11,10},{13,12},{... | collective-permute-start | bytes 2359304 | tf_op jit(solution)/shard_map/ppermute | solution.py:577
  313.7 61.7 %collective-permute-start.14 = (bf16[512,768]{1,0:T(8,128)(2,1)}, bf16[512,768]{1,0:T(8,128)(2,1)S(1)}, u32[]{:S(2)}, u32[]{:S(2)}) collective-permute-start(bf16[512,768]{1,0:T(8,128)(2,1)} %get-tuple-element.77), channel_id=1, source_target_pairs={{0,2},{1,3},{2,0},{3,1},{4,6},{5,7},{6,4},{7,5},{8,10},{9,11},{10,... | collective-permute-start | bytes 2359304 | tf_op jit(solution)/shard_map/ppermute | solution.py:649
  317.6 25.5 %collective-permute-start.15 = (bf16[4,4,96,768]{3,2,1,0:T(8,128)(2,1)S(1)}, bf16[4,4,96,768]{3,2,1,0:T(8,128)(2,1)S(1)}, u32[]{:S(2)}, u32[]{:S(2)}) collective-permute-start(bf16[4,4,96,768]{3,2,1,0:T(8,128)(2,1)S(1)} %slice_bitcast_fusion.2), channel_id=1, source_target_pairs={{0,4},{4,0},{8,12},{12,8},{16,20},{20,16},{24,28},{28,24},{1,5},{5... | collective-permute-start | bytes 7077896 | tf_op jit(solution)/shard_map/ppermute | solution.py:571
  339.0 2.7 copy-start.15
  341.2 10.4 %slice-start = ((s8[4718592]{0:T(1024)(128)(4,1)}), s8[4194304]{0:T(1024)(128)(4,1)S(1)}, s32[]{:S(2)}) async-start(s8[4718592]{0:T(1024)(128)(4,1)} %bitcast.163), calls=%async_computation.4 | async-start | bytes 8388608
  341.2 10.3 %slice-start.1 = ((s8[4718592]{0:T(1024)(128)(4,1)}), s8[524288]{0:T(1024)(128)(4,1)S(1)}, s32[]{:S(2)}) async-start(s8[4718592]{0:T(1024)(128)(4,1)} %bitcast.163), calls=%async_computation.5 | async-start | bytes 1048576
  341.3 23.7 %collective-permute-start.21 = (bf16[2,96,2560]{2,1,0:T(8,128)(2,1)S(1)}, bf16[2,96,2560]{2,1,0:T(8,128)(2,1)S(1)}, u32[]{:S(2)}, u32[]{:S(2)}) collective-permute-start(bf16[2,96,2560]{2,1,0:T(8,128)(2,1)S(1)} %slice_bitcast_fusion.8), channel_id=1, source_target_pairs={{0,16},{4,20},{8,24},{12,28},{16,0},{20,4},{24,8},{28,12},{1,17},{... | collective-permute-start | bytes 2949128 | tf_op jit(solution)/shard_map/ppermute | solution.py:571
  343.2 30.6 %collective-permute-start.23 = (bf16[2,96,2560]{2,1,0:T(8,128)(2,1)S(1)}, bf16[2,96,2560]{2,1,0:T(8,128)(2,1)S(1)}, u32[]{:S(2)}, u32[]{:S(2)}) collective-permute-start(bf16[2,96,2560]{2,1,0:T(8,128)(2,1)S(1)} %slice_bitcast_fusion.6), channel_id=1, source_target_pairs={{0,8},{4,12},{8,0},{12,4},{16,24},{20,28},{24,16},{28,20},{1,9},{5... | collective-permute-start | bytes 2949128 | tf_op jit(solution)/shard_map/ppermute | solution.py:571
  365.0 21.7 %collective-permute-start.16 = (bf16[2,2,96,768]{3,2,1,0:T(8,128)(2,1)S(1)}, bf16[2,2,96,768]{3,2,1,0:T(8,128)(2,1)S(1)}, u32[]{:S(2)}, u32[]{:S(2)}) collective-permute-start(bf16[2,2,96,768]{3,2,1,0:T(8,128)(2,1)S(1)} %slice_bitcast_fusion.14), channel_id=1, source_target_pairs={{0,8},{4,12},{8,0},{12,4},{16,24},{20,28},{24,16},{28,20},{1,9},{5... | collective-permute-start | bytes 1769480 | tf_op jit(solution)/shard_map/ppermute | solution.py:571
  373.8 14.7 %collective-permute-start.18 = (bf16[2,2,96,768]{3,2,1,0:T(8,128)(2,1)S(1)}, bf16[2,2,96,768]{3,2,1,0:T(8,128)(2,1)S(1)}, u32[]{:S(2)}, u32[]{:S(2)}) collective-permute-start(bf16[2,2,96,768]{3,2,1,0:T(8,128)(2,1)S(1)} %slice_bitcast_fusion.12), channel_id=1, source_target_pairs={{0,16},{4,20},{8,24},{12,28},{16,0},{20,4},{24,8},{28,12},{1,17},{... | collective-permute-start | bytes 1769480 | tf_op jit(solution)/shard_map/ppermute | solution.py:571
  375.3 13.4 %copy-start.24 = (bf16[512,768]{1,0:T(8,128)(2,1)}, bf16[512,768]{1,0:T(8,128)(2,1)S(1)}, u32[]{:S(2)}) copy-start(bf16[512,768]{1,0:T(8,128)(2,1)S(1)} %collective-permute-done.12) | copy-start | bytes 2359300
  375.4 13.4 %copy-start.25 = (bf16[512,768]{1,0:T(8,128)(2,1)}, bf16[512,768]{1,0:T(8,128)(2,1)S(1)}, u32[]{:S(2)}) copy-start(bf16[512,768]{1,0:T(8,128)(2,1)S(1)} %collective-permute-done.13) | copy-start | bytes 2359300
  375.4 13.4 %copy-start.26 = (bf16[512,768]{1,0:T(8,128)(2,1)}, bf16[512,768]{1,0:T(8,128)(2,1)S(1)}, u32[]{:S(2)}) copy-start(bf16[512,768]{1,0:T(8,128)(2,1)S(1)} %collective-permute-done.14) | copy-start | bytes 2359300
  388.9 7.5 %collective-permute-start.17 = (bf16[2,96,768]{2,1,0:T(8,128)(2,1)S(1)}, bf16[2,96,768]{2,1,0:T(8,128)(2,1)S(1)}, u32[]{:S(2)}, u32[]{:S(2)}) collective-permute-start(bf16[2,96,768]{2,1,0:T(8,128)(2,1)S(1)} %slice_bitcast_fusion.21), channel_id=1, source_target_pairs={{0,16},{4,20},{8,24},{12,28},{16,0},{20,4},{24,8},{28,12},{1,17},{... | collective-permute-start | bytes 884744 | tf_op jit(solution)/shard_map/ppermute | solution.py:571
  390.3 9.5 %collective-permute-start.19 = (bf16[2,96,768]{2,1,0:T(8,128)(2,1)S(1)}, bf16[2,96,768]{2,1,0:T(8,128)(2,1)S(1)}, u32[]{:S(2)}, u32[]{:S(2)}) collective-permute-start(bf16[2,96,768]{2,1,0:T(8,128)(2,1)S(1)} %slice_bitcast_fusion.19), channel_id=1, source_target_pairs={{0,8},{4,12},{8,0},{12,4},{16,24},{20,28},{24,16},{28,20},{1,9},{5... | collective-permute-start | bytes 884744 | tf_op jit(solution)/shard_map/ppermute | solution.py:571
  391.8 15.5 %collective-permute-start.24 = (bf16[96,2560]{1,0:T(8,128)(2,1)S(1)}, bf16[96,2560]{1,0:T(8,128)(2,1)S(1)}, u32[]{:S(2)}, u32[]{:S(2)}) collective-permute-start(bf16[96,2560]{1,0:T(8,128)(2,1)S(1)} %slice_bitcast_fusion.18), channel_id=1, source_target_pairs={{0,3},{1,0},{2,1},{3,2},{4,7},{5,4},{6,5},{7,6},{8,11},{9,8},{10,9... | collective-permute-start | bytes 1474568 | tf_op jit(solution)/shard_map/ppermute | solution.py:574
  394.5 40.8 %collective-permute-start.25 = (bf16[96,2560]{1,0:T(8,128)(2,1)S(1)}, bf16[96,2560]{1,0:T(8,128)(2,1)S(1)}, u32[]{:S(2)}, u32[]{:S(2)}) collective-permute-start(bf16[96,2560]{1,0:T(8,128)(2,1)S(1)} %get-tuple-element.156), channel_id=1, source_target_pairs={{0,2},{1,3},{2,0},{3,1},{4,6},{5,7},{6,4},{7,5},{8,10},{9,11},{10,... | collective-permute-start | bytes 1474568 | tf_op jit(solution)/shard_map/ppermute | solution.py:574
  394.5 40.8 %collective-permute-start.26 = (bf16[96,2560]{1,0:T(8,128)(2,1)S(1)}, bf16[96,2560]{1,0:T(8,128)(2,1)S(1)}, u32[]{:S(2)}, u32[]{:S(2)}) collective-permute-start(bf16[96,2560]{1,0:T(8,128)(2,1)S(1)} %get-tuple-element.157), channel_id=1, source_target_pairs={{0,1},{1,2},{2,3},{3,0},{4,5},{5,6},{6,7},{7,4},{8,9},{9,10},{10,1... | collective-permute-start | bytes 1474568 | tf_op jit(solution)/shard_map/ppermute | solution.py:574
  400.6 54.8 %copy-start.21 = (f32[512,768]{1,0:T(8,128)S(1)}, f32[512,768]{1,0:T(8,128)}, u32[]{:S(2)}) copy-start(f32[512,768]{1,0:T(8,128)} %get-tuple-element.57) | copy-start | bytes 4718596
  400.6 54.8 %copy-start.22 = (f32[512,768]{1,0:T(8,128)S(1)}, f32[512,768]{1,0:T(8,128)}, u32[]{:S(2)}) copy-start(f32[512,768]{1,0:T(8,128)} %get-tuple-element.74) | copy-start | bytes 4718596
  437.4 5.2 collective-permute-start.27
  437.4 16.5 %collective-permute-start.28 = (bf16[96,768]{1,0:T(8,128)(2,1)S(1)}, bf16[96,768]{1,0:T(8,128)(2,1)S(1)}, u32[]{:S(2)}, u32[]{:S(2)}) collective-permute-start(bf16[96,768]{1,0:T(8,128)(2,1)S(1)} %get-tuple-element.161), channel_id=1, source_target_pairs={{0,2},{1,3},{2,0},{3,1},{4,6},{5,7},{6,4},{7,5},{8,10},{9,11},{10,... | collective-permute-start | bytes 442376 | tf_op jit(solution)/shard_map/ppermute | solution.py:574
  440.5 13.4 %collective-permute-start.29 = (bf16[96,768]{1,0:T(8,128)(2,1)S(1)}, bf16[96,768]{1,0:T(8,128)(2,1)S(1)}, u32[]{:S(2)}, u32[]{:S(2)}) collective-permute-start(bf16[96,768]{1,0:T(8,128)(2,1)S(1)} %get-tuple-element.162), channel_id=1, source_target_pairs={{0,1},{1,2},{2,3},{3,0},{4,5},{5,6},{6,7},{7,4},{8,9},{9,10},{10,1... | collective-permute-start | bytes 442376 | tf_op jit(solution)/shard_map/ppermute | solution.py:574
  454.7 58.5 %all-gather.15.cloned.1.call-start = ((), (), s32[]{:S(2)}) async-start(), calls=%async_computation.3 | async-start | bytes 4423680 | tf_op jit(solution)/shard_map/all_gather | solution.py:580
  477.1 3.5 copy-start.17
  480.6 1.1 copy-start.20
  526.2 11.1 %copy-start.1 = (bf16[192,768]{1,0:T(8,128)(2,1)S(1)}, bf16[192,768]{1,0:T(8,128)(2,1)}, u32[]{:S(2)}) copy-start(bf16[192,768]{1,0:T(8,128)(2,1)} %param.14) | copy-start | bytes 884740
  (4 other events, 3.9 us)
Sparse Core Ops, SparseCore 0:
  33.0 44.2 all-gather.8
  79.8 63.8 all-gather.10
  454.9 20.3 all-gather.12
  477.6 35.6 all-gather.14

commit v3 on v2

--- a/solution.py
+++ b/solution.py
@@ -24,6 +24,31 @@
 
 def tile_rows(tile, base, count):
     return pl.ds(pl.multiple_of(lax.rem(tile - base + count, count) * TILE, TILE), TILE)
+
+
+def over_tiles(info, lo, hi, tiles, scan):
+    def one(t, _):
+        live = [(t >= info[3 + u]) & (t < info[3 + tiles + u]) for u in range(tiles)]
+        every = functools.reduce(jnp.logical_and, live)
+
+        @pl.when(every)
+        def _():
+            scan(t, slice(0, tiles * TILE))
+
+        @pl.when(jnp.logical_not(every))
+        def _():
+            def single(u, _):
+                @pl.when((t >= info[3 + u]) & (t < info[3 + tiles + u]))
+                def _():
+                    scan(t, pl.ds(pl.multiple_of(u * TILE, TILE), TILE))
+
+                return 0
+
+            lax.fori_loop(0, tiles, single, 0)
+
+        return 0
+
+    lax.fori_loop(lo, hi, one, 0)
 
 
 def attn_fwd_kernel(info, *refs, docs, heads, slots):
@@ -35,6 +60,7 @@
     used = heads * HALF
     cols = heads * HD
     lo, hi, base = info[0], info[1], info[2]
+    tiles = here // TILE
 
     @pl.when(pl.program_id(0) == 0)
     def _():
@@ -86,19 +112,19 @@
     acc[...] = jnp.zeros_like(acc)
     top[...] = jnp.full_like(top, -3e38)
 
-    def k_tile(t, _):
+    def scan(t, mine):
         rows = tile_rows(t, base, count)
         kk = ka[0, rows, :]
+        scores = [nt(kk, qh[0, h, mine, :]) for h in range(heads)]
+        olds = [top[h : h + 1, mine] for h in range(heads)]
+        news = [jnp.maximum(olds[h], jnp.max(scores[h], axis=0, keepdims=True)) for h in range(heads)]
+        probs = [jnp.exp(scores[h] - news[h]).astype(bf16) for h in range(heads)]
+        adds = [nn(vt[80 * h : 80 * h + 80, rows], probs[h]) for h in range(heads)]
         for h in range(heads):
-            s = nt(kk, qh[0, h])
-            old = top[h : h + 1, :]
-            new = jnp.maximum(old, jnp.max(s, axis=0, keepdims=True))
-            p = jnp.exp(s - new).astype(bf16)
-            top[h : h + 1, :] = new
-            acc[h] = acc[h] * jnp.exp(old - new) + nn(vt[80 * h : 80 * h + 80, rows], p)
-        return 0
-
-    lax.fori_loop(lo, hi, k_tile, 0)
+            top[h : h + 1, mine] = news[h]
+            acc[h, :, mine] = acc[h, :, mine] * jnp.exp(olds[h] - news[h]) + adds[h]
+
+    over_tiles(info, lo, hi, tiles, scan)
     good = seg[:here, :] < docs - 1
     total = [jnp.where(top[h : h + 1, :] > -1e29, acc[h, HD : HD + 1, :], 1.0) for h in range(heads)]
     outs = jnp.concatenate([acc[h, :HD, :] / total[h] for h in range(heads)], axis=0).T
@@ -144,37 +170,40 @@
     toks = refs[:slots]
     w, cos, sin, seg, qh, ka, va, lse, mixed, do = refs[slots : slots + 10]
     dw, dx_out = refs[slots + 10], refs[slots + 11 : 2 * slots + 11]
-    tokt, dx, dqt, dwa, doh, delta = refs[2 * slots + 11 :]
+    tokt, dkv, dq, dqt, dwa, doh, delta, dka, dva = refs[2 * slots + 11 :]
     here, width = toks[0].shape
     seq = here * slots
     count = seq // TILE
     used = heads * HALF
     cols = heads * HD
-    lo, hi, base, me = info[0], info[1], info[2], info[3]
+    tiles = here // TILE
+    lo, hi, base, me = info[0], info[1], info[2], info[3 + 2 * tiles]
 
     @pl.when(pl.program_id(0) == 0)
     def _():
-        dx[...] = jnp.zeros_like(dx)
+        dkv[...] = jnp.zeros_like(dkv)
+        dwa[:, 512 + cols :] = jnp.zeros((width, dwa.shape[1] - 512 - cols), f32)
         for s in range(slots):
             for c in range(here // TILE):
                 start = s * here + c * TILE
                 tokt[:, start : start + TILE] = toks[s][c * TILE : (c + 1) * TILE, :].astype(f32).T.astype(bf16)
 
-    def weight(start, stop):
-        return w[:, 0, :, start:stop].reshape(width, stop - start)
+    g = pl.program_id(0)
+
+    def weight(group, start, stop):
+        return w[:, group, :, start:stop].reshape(width, stop - start)
 
     wlane = lax.broadcasted_iota(jnp.int32, (here, cols), 1)
     lane = lax.broadcasted_iota(jnp.int32, (TILE, 128), 1)
-    ones = jnp.ones((8, cols), f32)
     dqt[...] = jnp.zeros_like(dqt)
-    dwa[...] = jnp.zeros_like(dwa)
     d = jnp.where(seg[:here, :] < docs - 1, do[0].astype(f32), 0.0)
-    o = mixed[0].astype(f32)
+    prod = d * mixed[0].astype(f32)
+    prod_high = prod.astype(bf16)
+    prod_low = (prod - prod_high.astype(f32)).astype(bf16)
+    pick = (lax.broadcasted_iota(jnp.int32, (8, cols), 1) // HD == lax.broadcasted_iota(jnp.int32, (8, cols), 0)).astype(bf16)
+    delta[...] = nt(pick, prod_high) + nt(pick, prod_low)
     for h in range(heads):
-        m = jnp.where((wlane >= HD * h) & (wlane < HD * (h + 1)), d, 0.0)
-        doh[h] = m.astype(bf16)
-        sums = lax.dot_general(ones, m * o, (((1,), (1,)), ((), ())), precision=lax.Precision.HIGHEST, preferred_element_type=f32)
-        delta[h : h + 1, :] = sums[:1]
+        doh[h] = jnp.where((wlane >= HD * h) & (wlane < HD * (h + 1)), d, 0.0).astype(bf16)
 
     def unrotate(a, b, rows):
         a, b = a.astype(bf16).astype(f32), b.astype(bf16).astype(f32)
@@ -183,45 +212,59 @@
         both = [jnp.where(keep, a * co + b * si, 0.0), jnp.where(keep, b * co - a * si, 0.0)]
         return jnp.concatenate(both, axis=1).astype(bf16)
 
-    def k_tile(t, _):
+    def scan(t, mine):
         rows = tile_rows(t, base, count)
         kk, vv = ka[0, rows, :], va[0, rows, :]
         kt = kk.astype(f32).T.astype(bf16)
-        dk = jnp.zeros((TILE, 256), f32)
-        dv = jnp.zeros((TILE, cols), f32)
+        qs, dd = [qh[0, h, mine, :] for h in range(heads)], [doh[h, mine, :] for h in range(heads)]
+        probs = [jnp.exp(nt(kk, qs[h]) - lse[0, h : h + 1, mine]) for h in range(heads)]
+        ds = [(probs[h] * (nt(vv, dd[h]) - delta[h : h + 1, mine])).astype(bf16) for h in range(heads)]
+        dva[...] += sum(nn(probs[h].astype(bf16), dd[h]) for h in range(heads))
+        dka[...] += sum(nn(ds[h], qs[h]) for h in range(heads))
         for h in range(heads):
-            q, dd = qh[0, h], doh[h]
-            p = jnp.exp(nt(kk, q) - lse[0, h : h + 1, :])
-            ds = (p * (nt(vv, dd) - delta[h : h + 1, :])).astype(bf16)
-            dv = dv + nn(p.astype(bf16), dd)
-            dk = dk + nn(ds, q)
             kth = jnp.concatenate([kt[HALF * h : HALF * (h + 1)], kt[128 + HALF * h : 128 + HALF * (h + 1)]], axis=0)
-            g = nn(kth, ds)
-            dqt[HALF * h : HALF * (h + 1), :] += g[:HALF]
-            dqt[128 + HALF * h : 128 + HALF * (h + 1), :] += g[HALF:]
-        dkl = unrotate(dk[:, :128], dk[:, 128:], rows)
-        dvl = dv.astype(bf16)
-        dx[rows, :] += nt(dkl, weight(256, 512)) + nt(dvl, weight(512 + cols, 512 + 2 * cols))
-        dwa[:, 256:512] += nn(tokt[:, rows], dkl)
-        dwa[:, 512 : 512 + cols] += nn(tokt[:, rows], dvl)
+            g = nn(kth, ds[h])
+            dqt[HALF * h : HALF * (h + 1), mine] += g[:HALF]
+            dqt[128 + HALF * h : 128 + HALF * (h + 1), mine] += g[HALF:]
+
+    def k_tile(t, _):
+        rows = tile_rows(t, base, count)
+        dka[...] = jnp.zeros_like(dka)
+        dva[...] = jnp.zeros_like(dva)
+        over_tiles(info, t, t + 1, tiles, scan)
+        dkv[g, rows, :256] = unrotate(dka[:, :128], dka[:, 128:], rows)
+        dkv[g, rows, 256:] = dva[...].astype(bf16)
         return 0
 
     lax.fori_loop(lo, hi, k_tile, 0)
     for c in range(here // TILE):
         rows = slice(c * TILE, (c + 1) * TILE)
-        g = dqt[:, rows].T * HD**-0.5
-        dql = unrotate(g[:, :128], g[:, 128:], rows)
-        dx[rows, :] += nt(dql, weight(0, 256))
-        dwa[:, :256] += nn(tokt[:, rows], dql)
+        gq = dqt[:, rows].T * HD**-0.5
+        dq[g, rows, :] = unrotate(gq[:, :128], gq[:, 128:], rows)
+    dwa[:, :256] = nn(tokt[:, :here], dq[g])
+    dwa[:, 256 : 512 + cols] = nn(tokt[...], dkv[g])
     share = width // pieces
     for r in range(pieces):
         p = jnp.bitwise_xor(me, r)
         dw[r, 0] = dwa[pl.ds(pl.multiple_of(p * share, 8), share), :].astype(bf16)
 
-    @pl.when(pl.program_id(0) == slots - 1)
+    @pl.when(g == slots - 1)
     def _():
         for s in range(slots):
-            dx_out[s][...] = dx[s * here : (s + 1) * here, :].astype(dx_out[s].dtype)
+            dx_out[s][...] = jnp.zeros_like(dx_out[s])
+        for s in range(slots):
+            begin = lax.rem(base + s * tiles, count)
+
+            @pl.when((begin + tiles > lo) & (begin < hi))
+            def _(s=s):
+                rows = slice(s * here, (s + 1) * here)
+                total = sum(
+                    nt(dkv[group, rows, :256], weight(group, 256, 512)) + nt(dkv[group, rows, 256:], weight(group, 512 + cols, 512 + 2 * cols))
+                    for group in range(slots)
+                )
+                if s == 0:
+                    total = total + sum(nt(dq[group], weight(group, 0, 256)) for group in range(slots))
+                dx_out[s][...] = total.astype(dx_out[s].dtype)
 
 
 def attn_bwd(info, toks, w, cos, sin, seg, saved, do, docs, heads, pieces):
@@ -244,16 +287,19 @@
         + (jax.ShapeDtypeStruct((here, width), bf16),) * (slots - 1),
         in_specs=[pl.BlockSpec(memory_space=pltpu.SMEM)]
         + [whole((here, width))] * slots
-        + [pl.BlockSpec((w.shape[0], 1) + w.shape[2:], lambda g: (0, g, 0, 0)), whole(cos.shape), whole(sin.shape), whole(seg.shape)]
+        + [whole(w.shape), whole(cos.shape), whole(sin.shape), whole(seg.shape)]
         + [part(a) for a in (*saved, do)],
         out_specs=(pl.BlockSpec((pieces, 1, width // pieces, span), lambda g: (0, g, 0, 0)),) + (whole((here, width)),) * slots,
         scratch_shapes=[
             pltpu.VMEM((width, seq), bf16),
-            pltpu.VMEM((seq, width), f32),
+            pltpu.VMEM((slots, seq, 256 + cols), bf16),
+            pltpu.VMEM((slots, here, 256), bf16),
             pltpu.VMEM((256, here), f32),
             pltpu.VMEM((width, span), f32),
             pltpu.VMEM((heads, here, cols), bf16),
             pltpu.VMEM((8, here), f32),
+            pltpu.VMEM((TILE, 256), f32),
+            pltpu.VMEM((TILE, cols), f32),
         ],
         compiler_params=pltpu.CompilerParams(vmem_limit_bytes=56 << 20),
         cost_estimate=pl.CostEstimate(flops=40 << 30, bytes_accessed=24 << 20, transcendentals=4 << 20),
@@ -271,12 +317,17 @@
     offset = jnp.sum(jnp.where(member, starts[None, :], 0), axis=1)
     position = (place - offset).astype(f32)
     live = ends[docs - 2]
-    last = jnp.minimum(first + here, live) - 1
-    lo = jnp.max(jnp.where(starts <= first, starts, 0))
-    hi = jnp.minimum(jnp.min(jnp.where(ends > last, ends, seq)), live)
-    lo = lo // TILE
-    hi = jnp.where(first < live, (hi + TILE - 1) // TILE, lo)
-    return segment, position, lo, hi, first // TILE
+    tops = first + TILE * jnp.arange(here // TILE, dtype=jnp.int32)
+    last = jnp.minimum(tops + TILE, live) - 1
+    lo = jnp.max(jnp.where(starts[None, :] <= tops[:, None], starts[None, :], 0), axis=1) // TILE
+    hi = jnp.minimum(jnp.min(jnp.where(ends[None, :] > last[:, None], ends[None, :], seq), axis=1), live)
+    hi = jnp.where(tops < live, (hi + TILE - 1) // TILE, lo)
+    span = [jnp.min(jnp.where(hi > lo, lo, seq), keepdims=True), jnp.max(jnp.where(hi > lo, hi, 0), keepdims=True)]
+    return segment, position, jnp.concatenate([*span, jnp.reshape(first // TILE, (1,)), lo, hi])
+
+
+def make_info(tables, me):
+    return jnp.concatenate([tables[2], jnp.reshape(me, (1,))]).astype(jnp.int32)
 
 
 EPSILON = 1e-05
@@ -304,18 +355,20 @@
 
 def ffn_kernel(*refs, slots, pieces, share):
     own, cot, s1, b1, s2, b2, rel, w1_hbm, wown_hbm, w2_hbm = refs[:10]
-    layer_out, grad_one, nlow, flow, brt, back, small, act_hbm, gg_hbm, ug_hbm = refs[10:20]
-    w, wo, ws, g, u, normed, unit1, inv1, acc, stage, wsem, psem, osem, ssem = refs[20:]
+    layer_out, grad_one, nlow, flow, brt, back, chunk, act_hbm, gg_hbm, ug_hbm = refs[10:20]
+    w, wo, ws, g, u, normed, unit1, inv1, acc, small, stage, wsem, psem, osem, ssem = refs[20:]
     tokens, width = own.shape
     heads_cols = rel.shape[2]
     blk = slots * share
+    pair = 2 if pieces % 2 == 0 else 1
+    steps, wide = pieces // pair, pair * blk
     rows_share = width // pieces
 
     def load_own(p):
-        return pltpu.make_async_copy(wown_hbm.at[p], w.at[p, pl.ds(0, share)], psem.at[p])
+        return pltpu.make_async_copy(wown_hbm.at[p], w.at[p // pair, pl.ds(p % pair * blk, share)], psem.at[p])
 
     def load(p):
-        return pltpu.make_async_copy(w2_hbm.at[p], w.at[p, pl.ds(share, blk - share)], wsem.at[p])
+        return pltpu.make_async_copy(w2_hbm.at[p], w.at[p // pair, pl.ds(p % pair * blk + share, blk - share)], wsem.at[p])
 
     first = pltpu.make_async_copy(w1_hbm.at[:, :, :, pl.ds(512, wo.shape[3])], wo, osem)
     first.start()
@@ -345,30 +398,32 @@
     lax.fori_loop(0, tokens // ROWS, head, 0)
 
     def out_copy(which, target, p, slot):
-        return pltpu.make_async_copy(stage.at[which, slot], target.at[:, pl.ds(pl.multiple_of(p * blk, 128), blk)], ssem.at[which, slot])
+        return pltpu.make_async_copy(stage.at[which, slot], target.at[:, pl.ds(pl.multiple_of(p * wide, 128), wide)], ssem.at[which, slot])
 
     def forward(p, _):
         slot = lax.rem(p, 2)
-        cols = pl.ds(pl.multiple_of(p * blk, 128), blk)
-        load_own(p).wait()
-        load(p).wait()
+        cols = pl.ds(pl.multiple_of(p * wide, 128), wide)
+        for i in range(pair):
+            load_own(p * pair + i).wait()
+            load(p * pair + i).wait()
 
         @pl.when(p >= 2)
         def _():
             out_copy(0, act_hbm, p - 2, slot).wait()
 
-        x = nlow[...]
-        gp = nt(x, w[p, :, :width])
-        up = nt(x, w[p, :, width : 2 * width])
-        g[:, cols] = gp
-        u[:, cols] = up
-        a = (gp * jax.nn.sigmoid(gp) * up).astype(bf16)
-        stage[0, slot] = a
+        halves = [slice(i, i + tokens // 2) for i in range(0, tokens, tokens // 2)]
+        gates = [nt(nlow[r, :], w[p, :, :width]) for r in halves]
+        ups = [nt(nlow[r, :], w[p, :, width : 2 * width]) for r in halves]
+        for r, gp, up in zip(halves, gates, ups):
+            g[r, cols] = gp
+            u[r, cols] = up
+            a = (gp * jax.nn.sigmoid(gp) * up).astype(bf16)
+            stage[0, slot, r, :] = a
+            acc[r, :] += nn(a, w[p, :, 2 * width :])
         out_copy(0, act_hbm, p, slot).start()
-        acc[...] += nn(a, w[p, :, 2 * width :])
         return 0
 
-    lax.fori_loop(0, pieces, forward, 0)
+    lax.fori_loop(0, steps, forward, 0)
 
     def middle(c, _):
         rows = pl.ds(pl.multiple_of(c * ROWS, ROWS), ROWS)
@@ -383,31 +438,34 @@
         return 0
 
     lax.fori_loop(0, tokens // ROWS, middle, 0)
-    for p in range(max(pieces - 2, 0), pieces):
+    for p in range(max(steps - 2, 0), steps):
         out_copy(0, act_hbm, p, p % 2).wait()
 
     def backward(p, _):
         slot = lax.rem(p, 2)
-        cols = pl.ds(pl.multiple_of(p * blk, 128), blk)
+        cols = pl.ds(pl.multiple_of(p * wide, 128), wide)
 
         @pl.when(p >= 2)
         def _():
             out_copy(0, gg_hbm, p - 2, slot).wait()
             out_copy(1, ug_hbm, p - 2, slot).wait()
 
-        da = nt(flow[...], w[p, :, 2 * width :])
-        gp, up = g[:, cols], u[:, cols]
-        sig = jax.nn.sigmoid(gp)
-        dg = (da * up * sig * (1.0 + gp * (1.0 - sig))).astype(bf16)
-        du = (da * gp * sig).astype(bf16)
-        stage[0, slot] = dg
-        stage[1, slot] = du
+        halves = [slice(i, i + tokens // 2) for i in range(0, tokens, tokens // 2)]
+        outer = [nt(flow[r, :], w[p, :, 2 * width :]) for r in halves]
+        for r, da in zip(halves, outer):
+            gp, up = g[r, cols], u[r, cols]
+            sig = jax.nn.sigmoid(gp)
+            both = da * sig
+            dg = (both * up * (1.0 + gp * (1.0 - sig))).astype(bf16)
+            du = (both * gp).astype(bf16)
+            stage[0, slot, r, :] = dg
+            stage[1, slot, r, :] = du
+            acc[r, :] += nn(dg, w[p, :, :width]) + nn(du, w[p, :, width : 2 * width])
         out_copy(0, gg_hbm, p, slot).start()
         out_copy(1, ug_hbm, p, slot).start()
-        acc[...] += nn(dg, w[p, :, :width]) + nn(du, w[p, :, width : 2 * width])
         return 0
 
-    lax.fori_loop(0, pieces, backward, 0)
+    lax.fori_loop(0, steps, backward, 0)
 
     def tail(c, _):
         rows = pl.ds(pl.multiple_of(c * ROWS, ROWS), ROWS)
@@ -423,27 +481,34 @@
         return 0
 
     lax.fori_loop(0, tokens // ROWS, tail, 0)
-    for p in range(max(pieces - 2, 0), pieces):
+    chunk[...] = jnp.zeros_like(chunk)
+    room = chunk.shape[2]
+    each = 4 * width // pieces // room
+    for n in range(pieces * each):
+        j, lane = divmod(n * room, width)
+        chunk[n // each, n % each : n % each + 1, :] = small[j : j + 1, lane : lane + room]
+    for p in range(max(steps - 2, 0), steps):
         out_copy(0, gg_hbm, p, p % 2).wait()
         out_copy(1, ug_hbm, p, p % 2).wait()
 
 
-def ffn_layer(own, cot, norms, rel, w1, w_own, w2):
+def ffn_layer(own, cot, norms, rel, w1, w_own, w2, room):
     slots, tokens, cols = rel.shape
     width = own.shape[1]
     pieces, share = w_own.shape[:2]
     units = pieces * slots * share
+    pair = 2 if pieces % 2 == 0 else 1
     vm, hbm = pl.BlockSpec(memory_space=pltpu.VMEM), pl.BlockSpec(memory_space=pl.ANY)
     wide = jax.ShapeDtypeStruct((tokens, width), bf16)
     hidden = jax.ShapeDtypeStruct((tokens, units), bf16)
     return pl.pallas_call(
         functools.partial(ffn_kernel, slots=slots, pieces=pieces, share=share),
         out_shape=(wide, jax.ShapeDtypeStruct((tokens, width), f32), wide, wide, jax.ShapeDtypeStruct((width, tokens), bf16))
-        + (jax.ShapeDtypeStruct((slots, tokens, cols), bf16), jax.ShapeDtypeStruct((8, width), f32), hidden, hidden, hidden),
+        + (jax.ShapeDtypeStruct((slots, tokens, cols), bf16), jax.ShapeDtypeStruct((pieces, 16, room), f32), hidden, hidden, hidden),
         in_specs=[vm] * 7 + [hbm] * 3,
         out_specs=(vm,) * 7 + (hbm,) * 3,
         scratch_shapes=[
-            pltpu.VMEM((pieces, slots * share, 3 * width), bf16),
+            pltpu.VMEM((pieces // pair, pair * slots * share, 3 * width), bf16),
             pltpu.VMEM((pieces, slots, width // pieces, 256), bf16),
             pltpu.VMEM((slots, width, cols), bf16),
             pltpu.VMEM((tokens, units), f32),
@@ -452,7 +517,8 @@
             pltpu.VMEM((tokens, width), f32),
             pltpu.VMEM((tokens, 1), f32),
             pltpu.VMEM((tokens, width), f32),
-            pltpu.VMEM((2, 2, tokens, slots * share), bf16),
+            pltpu.VMEM((8, width), f32),
+            pltpu.VMEM((2, 2, tokens, pair * slots * share), bf16),
             pltpu.SemaphoreType.DMA((pieces,)),
             pltpu.SemaphoreType.DMA((pieces,)),
             pltpu.SemaphoreType.DMA,
@@ -467,51 +533,121 @@
 def wgrad_kernel(*refs, slots, share, add):
     gg, ug, act, brt, nlow, flow, rel, small = refs[1:9]
     got = refs[9] if add else None
-    out = refs[-1]
     width = nlow.shape[1]
     cols = rel.shape[2]
     edge = 3 * width + cols
-    room = out.shape[2] - edge
+    blk = slots * share
+    out = refs[-1] if add else refs[-1].at[0]
+    room = out.shape[1] - edge
 
     def put(rows, lanes, value):
         if add:
             value = value + got[0, rows, lanes].astype(f32)
-        out[0, rows, lanes] = value.astype(bf16)
-
-    every = slice(0, out.shape[1])
-    put(every, slice(0, width), tn(gg[...], nlow[...]))
-    put(every, slice(width, 2 * width), tn(ug[...], nlow[...]))
-    put(every, slice(2 * width, 3 * width), tn(act[...], flow[...]))
+        out[rows, lanes] = value.astype(bf16)
+
+    terms = [tn(gg[...], nlow[...]), tn(ug[...], nlow[...]), tn(act[...], flow[...])]
     for s in range(slots):
-        put(slice(s * share, (s + 1) * share), slice(3 * width, edge), nn(brt[...], rel[s]))
-        put(slice(s * share, (s + 1) * share), slice(edge, edge + room), jnp.concatenate([small[0], jnp.zeros((share - 16, room), f32)], axis=0))
-
-
-def wgrad(me, first, count, gg, ug, act, brt, nlow, flow, rel, small, got, pieces, share, span):
+        place = lax.rem(refs[0][1] - s + slots, slots)
+        rows = pl.ds(pl.multiple_of(place * share, 32 if share % 32 == 0 else 4), share)
+        for i in range(3):
+            put(rows, slice(i * width, (i + 1) * width), terms[i][s * share : (s + 1) * share])
+        put(rows, slice(3 * width, edge), nn(brt[...], rel[s]))
+        put(rows, slice(edge, edge + room), jnp.concatenate([small[0], jnp.zeros((share - 16, room), f32)], axis=0))
+    if add:
+        first, second, rest = refs[10:13]
+        top = first.shape[0]
+
+        @pl.when(pl.program_id(0) == 0)
+        def _():
+            first[...] = out[:top, :]
+
+        @pl.when(pl.program_id(0) == 1)
+        def _():
+            second[...] = out[:top, :]
+
+        rest[0] = out[top:, :]
+
+
+def wgrad(me, start, gg, ug, act, brt, nlow, flow, rel, small, got, pieces, share, span):
     slots = rel.shape[0]
     tokens, width = nlow.shape
     blk = slots * share
+    top = slots // 2 * share
 
     def piece(i, me):
-        return jnp.bitwise_xor(2 * i + first, me[0])
-
-    out_block = pl.BlockSpec((1, blk, span), lambda i, me: (i, 0, 0))
+        return jnp.bitwise_xor(2 * i + start, me[0])
+
+    def stay(array):
+        return pltpu.with_memory_space_constraint(array, pltpu.HBM)
+
+    both = pl.BlockSpec((1, blk, span), lambda i, me: (i, 0, 0))
     in_specs = [pl.BlockSpec((tokens, blk), lambda i, me: (0, piece(i, me)))] * 3
     in_specs += [pl.BlockSpec((width // pieces, tokens), lambda i, me: (piece(i, me), 0))]
     in_specs += [pl.BlockSpec((tokens, width), lambda i, me: (0, 0))] * 2
     in_specs += [pl.BlockSpec(rel.shape, lambda i, me: (0, 0, 0)), pl.BlockSpec((1,) + small.shape[1:], lambda i, me: (piece(i, me), 0, 0))]
-    args = [gg, ug, act, brt, nlow, flow, rel, small]
-    if got is not None:
-        in_specs.append(out_block)
+    args = [stay(gg), stay(ug), stay(act), brt, nlow, flow, rel, small]
+    if got is None:
+        out_shape, out_specs, scratch = jax.ShapeDtypeStruct((2, blk, span), bf16), both, []
+    else:
+        in_specs.append(both)
         args.append(got)
+        half = jax.ShapeDtypeStruct((top, span), bf16)
+        out_shape = (half, half, jax.ShapeDtypeStruct((2, blk - top, span), bf16))
+        fixed = pl.BlockSpec((top, span), lambda i, me: (0, 0))
+        out_specs = (fixed, fixed, pl.BlockSpec((1, blk - top, span), lambda i, me: (i, 0, 0)))
+        scratch = [pltpu.VMEM((blk, span), bf16)]
     return pl.pallas_call(
         functools.partial(wgrad_kernel, slots=slots, share=share, add=got is not None),
-        out_shape=jax.ShapeDtypeStruct((count, blk, span), bf16),
-        grid_spec=pltpu.PrefetchScalarGridSpec(num_scalar_prefetch=1, grid=(count,), in_specs=in_specs, out_specs=out_block),
+        out_shape=out_shape,
+        grid_spec=pltpu.PrefetchScalarGridSpec(num_scalar_prefetch=1, grid=(2,), in_specs=in_specs, out_specs=out_specs, scratch_shapes=scratch),
         compiler_params=pltpu.CompilerParams(vmem_limit_bytes=40 << 20),
-        cost_estimate=pl.CostEstimate(flops=count << 30, bytes_accessed=count * 5 << 20, transcendentals=0),
+        cost_estimate=pl.CostEstimate(flops=2 << 30, bytes_accessed=10 << 20, transcendentals=0),
         name="wgrad",
     )(me, *args)
+
+
+def final_ffn_kernel(gate, up, out):
+    out[:, 0, :] = gate[...].astype(f32).T
+    out[:, 1, :] = up[...].astype(f32).T
+
+
+def final_ffn(main, width, lanes):
+    units = main.shape[0]
+    steps = width // lanes
+    return pl.pallas_call(
+        final_ffn_kernel,
+        grid=(steps,),
+        out_shape=jax.ShapeDtypeStruct((width, 2, units), f32),
+        in_specs=[pl.BlockSpec((units, lanes), lambda i: (0, i)), pl.BlockSpec((units, lanes), lambda i: (0, i + steps))],
+        out_specs=pl.BlockSpec((lanes, 2, units), lambda i: (i, 0, 0)),
+        cost_estimate=pl.CostEstimate(flops=1 << 20, bytes_accessed=8 << 20, transcendentals=0),
+        name="final_ffn",
+    )(main, main)
+
+
+def final_qkv_kernel(query, key, value, out, *, heads):
+    cols = heads * HD
+    for k, source in enumerate((query, key)):
+        turned = source[...].astype(f32).T
+        for h in range(heads):
+            for half in range(2):
+                start = 128 * half + HALF * h
+                out[k, HD * h + HALF * half : HD * h + HALF * (half + 1), :] = turned[start : start + HALF, :]
+    out[2, :, :] = value[...].astype(f32).T[:cols]
+
+
+def final_qkv(main, start, heads, rows):
+    width = main.shape[0]
+    cols = heads * HD
+    return pl.pallas_call(
+        functools.partial(final_qkv_kernel, heads=heads),
+        grid=(width // rows,),
+        out_shape=jax.ShapeDtypeStruct((3, cols, width), f32),
+        in_specs=[pl.BlockSpec((rows, 256), lambda i, k=k: (i, start // 256 + k)) for k in range(3)],
+        out_specs=pl.BlockSpec((3, cols, rows), lambda i: (0, 0, i)),
+        cost_estimate=pl.CostEstimate(flops=1 << 20, bytes_accessed=4 << 20, transcendentals=0),
+        name="final_qkv",
+    )(main, main, main)
 
 
 ROPE_BASE = 1000.0
@@ -604,8 +740,9 @@
     row_lengths, gate_up_late, down_late = after(lengths[0], ones[-1]), after(w_gate_up, ones[-1]), after(w_down, ones[-1])
     w_own = jnp.concatenate([gate_up_late[:, 0].T, gate_up_late[:, 1].T, down_late], axis=1).reshape(pieces, share, 3 * width)
 
-    segment, position, lo, hi, base = doc_tables(row_lengths, seq, z * rows_here, rows_here)
-    info = jnp.stack([lo, hi, base, me]).astype(jnp.int32)
+    tables = doc_tables(row_lengths, seq, z * rows_here, rows_here)
+    segment, position = tables[:2]
+    info = make_info(tables, me)
     inverse = ROPE_BASE ** (-2.0 * lax.rem(jnp.arange(128), HALF).astype(f32) / HD)
     angles = position[:, None] * inverse[None, :]
     cosine, sine = jnp.cos(angles), jnp.sin(angles)
@@ -614,53 +751,52 @@
     saved = attn_fwd(info, toks, w1, cosine, sine, seg_col, docs, heads)
     rel = saved[4]
     norms = [v.reshape(1, width) for v in (norm1_scale, norm1_shift, norm2_scale, norm2_shift)]
-    layer_out, grad_one, nlow, flow, brt, back, small, act, gg, ug = ffn_layer(own, cotangent[0], norms, rel, w1, w_own, w2)
+    room = span - 3 * width - cols_here
+    layer_out, grad_one, nlow, flow, brt, back, chunk, act, gg, ug = ffn_layer(own, cotangent[0], norms, rel, w1, w_own, w2, room)
 
     half = tp_size // 2
 
-    def meet(one, two, bit):
-        return low_sum(one, flip(two, bit))
-
-    def reduce_slots(parts):
-        total = parts[0].astype(f32)
-        for s in range(1, tp_size):
-            total = total + shift(parts[s], -s).astype(f32)
-        return total.astype(bf16)
-
-    me_array = me.reshape(1).astype(jnp.int32)
-    room = span - 3 * width - cols_here
-    chunk = small[:4].reshape(pieces, 4 * width // pieces // room, room)
-    chunk = jnp.pad(chunk, ((0, 0), (0, 16 - chunk.shape[1]), (0, 0)))
+    me_array = jnp.stack([me, z]).astype(jnp.int32)
     fixed = (gg, ug, act, brt, nlow, flow, rel, chunk)
-    far_sent = wgrad(me_array, 5, 2, *fixed, None, pieces, share, span)
-    near_sent = wgrad(after(me_array, far_sent), 1, 2, *fixed, None, pieces, share, span)
-    far = wgrad(after(me_array, near_sent), 4, 2, *fixed, flip(far_sent, 1), pieces, share, span)
-    near = wgrad(after(me_array, far), 0, 2, *fixed, flip(near_sent, 1), pieces, share, span)
-    far, near = (v.reshape(2, tp_size, share, span) for v in (far, near))
-    far_a, far_b, near_a, near_b = far[:, :half], far[:, half:], near[:, :half], near[:, half:]
-    out_b, out_a = far_b, jnp.stack([near_a[1], far_a[1]])
-
-    back, out_a, out_b = lax.optimization_barrier((back, out_a, out_b))
-    next_b = meet(near_b, out_b, 4)
-    next_a = meet(jnp.stack([near_a[0], far_a[0]]), out_a, 2)
+    far_sent = wgrad(me_array, 5, *fixed, None, pieces, share, span)
+    near_sent = wgrad(after(me_array, far_sent), 1, *fixed, None, pieces, share, span)
+    far_keep, far_give, far_rest = wgrad(after(me_array, near_sent), 4, *fixed, flip(far_sent, 1), pieces, share, span)
+    near_keep, near_give, near_rest = wgrad(after(me_array, far_rest), 0, *fixed, flip(near_sent, 1), pieces, share, span)
+
+    back, far_give, far_rest, near_give = lax.optimization_barrier((back, far_give, far_rest, near_give))
+    got = [flip(far_give, 2), flip(far_rest, 4), flip(near_give, 2)]
     bwd = attn_bwd(info, toks, w1, cosine, sine, seg_col, saved, back, docs, heads, pieces)
+    got, bwd = lax.optimization_barrier((got, bwd))
     dw, dx = bwd[0], bwd[1:]
-    right, left = along(dx[1], 1), along(dx[3], -1)
-    across_half = lax.ppermute(dx[2], "tensor", rotate_axis(tp_size, half))
-    input_grad = grad_one + dx[0] + right.astype(f32) + left.astype(f32) + across_half.astype(f32)
-
-    last_b = meet(next_b[0], next_b[1], 2)
-    last_a = meet(next_a[0], next_a[1], 4)
-    last_a, last_b, right, left, across_half = lax.optimization_barrier((last_a, last_b, right, left, across_half))
-    share_two = reduce_slots([last_a[i] for i in range(half)] + [last_b[i] for i in range(tp_size - half)])
-
+    next_b = low_sum(near_rest, got[1])
+    got_a, got_b = flip(low_sum(far_keep, got[0]), 4), flip(next_b[1], 2)
+    next_a = low_sum(near_keep, got[2])
     pairs = dw.reshape((pieces // 2, 2) + dw.shape[1:])
-    pairs = meet(pairs[:, 0], pairs[:, 1], 1).reshape((2, 2) + dw.shape[1:])
-    next_a = meet(pairs[:, 0, :half], pairs[:, 1, :half], 2)
-    next_b = meet(pairs[0, :, half:], pairs[1, :, half:], 4)
-    last_a, last_b = meet(next_a[0], next_a[1], 4), meet(next_b[0], next_b[1], 2)
-    last_a, last_b, share_two = lax.optimization_barrier((last_a, last_b, share_two))
-    share_one = reduce_slots([last_a[i] for i in range(half)] + [last_b[i] for i in range(tp_size - half)])
+    got_pairs = flip(pairs[:, 1], 1)
+    from_left = lax.ppermute(dx[2], "tensor", [(i, i + 1) for i in range(half)])
+    from_right = lax.ppermute(dx[2], "tensor", [(i + half, i + half - 1) for i in range(half)])
+    got_a, got_b, got_pairs, from_left, from_right = lax.optimization_barrier((got_a, got_b, got_pairs, from_left, from_right))
+
+    def by_slot(low, high):
+        low, high = low.reshape(half, -1, low.shape[-1]), high.reshape(tp_size - half, -1, high.shape[-1])
+        return [low[i] for i in range(half)] + [high[i] for i in range(tp_size - half)]
+
+    parts_two = jnp.concatenate([low_sum(next_a, got_a), low_sum(next_b[0], got_b)], axis=0)
+    share_two = lax.psum_scatter(parts_two, "tensor", scatter_dimension=0, tiled=True)
+    pairs = low_sum(pairs[:, 0], got_pairs).reshape((2, 2) + dw.shape[1:])
+    got_a, got_b = flip(pairs[:, 1, :half], 2), flip(pairs[1, :, half:], 4)
+    near_right, near_left = low_sum(dx[1], from_left), low_sum(dx[3], from_right)
+    next_a, next_b = low_sum(pairs[:, 0, :half], got_a), low_sum(pairs[0, :, half:], got_b)
+    got_a, got_b = flip(next_a[1], 4), flip(next_b[1], 2)
+
+    def total(own_part, moved):
+        return functools.reduce(lambda x, y: x + y.astype(f32), moved, own_part.astype(f32)).astype(bf16)
+
+    parts_one = by_slot(low_sum(next_a[0], got_a), low_sum(next_b[0], got_b))
+    moved_one = [shift(parts_one[s], -s) for s in range(1, tp_size)]
+    share_one = total(parts_one[0], moved_one)
+    share_two, share_one, near_right, near_left = lax.optimization_barrier((share_two, share_one, near_right, near_left))
+    input_grad = grad_one + dx[0] + along(near_right, 1).astype(f32) + along(near_left, -1).astype(f32)
 
     def finish(array):
         if groups is not None:
@@ -668,18 +804,12 @@
             array = lax.psum(array.astype(f32), "dp", axis_index_groups=across).astype(bf16)
         return gather_dp(array)
 
-    main = finish(share_two).reshape(units, span).astype(f32)
-    down_sum = main[:, 2 * width : 3 * width]
-    out_sum = main[:, 3 * width : 3 * width + cols_here].T
-    gate_up_sum = jnp.stack([main[:, :width].T, main[:, width : 2 * width].T], axis=1)
-    q3 = finish(share_one).reshape(width, -1).astype(f32)
-
-    def rope_back(matrix):
-        halves = matrix.reshape(width, 2, 128)[:, :, : heads * HALF].reshape(width, 2, heads, HALF)
-        return halves.transpose(0, 2, 1, 3).reshape(width, cols_here)
-
-    qkv_sum = jnp.stack([rope_back(q3[:, :256]), rope_back(q3[:, 256:512]), q3[:, 512 : 512 + cols_here]], axis=1)
-    small_out = main.reshape(pieces, share, span)[:, : 4 * width // pieces // room, span - room :].reshape(4, width)
+    main = finish(jnp.concatenate([share_two, share_one], axis=1)).reshape(units, -1)
+    down_sum = main[:, 2 * width : 3 * width].astype(f32)
+    out_sum = main[:, 3 * width : 3 * width + cols_here].astype(f32).T
+    gate_up_sum = final_ffn(main, width, 128)
+    qkv_sum = final_qkv(main, span, heads, 256).transpose(2, 0, 1)
+    small_out = main.reshape(pieces, share, -1)[:, : 4 * width // pieces // room, span - room : span].astype(f32).reshape(4, width)
     return (
         layer_out[None],
         input_grad[None],

time: 547 us -> 449 us (0.82)
  starting transfers between devices: 110 us -> 61.8 us
  waiting for transfers between devices: 186 us -> 147 us
  local copies, waits for them, and re-layouts: 66.2 us -> 34.9 us
  Pallas kernels: 132 us -> 150 us
    ppermute x11 -> x12, starting transfers between devices: 65.5 us -> 5.71 us  [flip(): return lax.ppermute(array, 'dp', flip_axis(dp_size, bit))]
    all_gather x4 -> x3, waiting for transfers between devices: 46.4 us -> 13.1 us  [gather_dp(): return lax.all_gather(array, 'dp', axis=0, axis_index_groups=groups)]
    ppermute x12 -> x9, waiting for transfers between devices: 92.5 us -> 60 us  [shift(): return lax.ppermute(array, 'tensor', rotate_axis(tp_size, step))]
    ppermute x6, waiting for transfers between devices: 13.2 us -> 32.5 us  [along(): return lax.ppermute(array, 'tensor', line_axis(tp_size, step))]
    unnamed x74 -> x64, local copies, waits for them, and re-layouts: 27.8 us -> 10.5 us
    ppermute x1 -> x2, waiting for transfers between devices: 0.01 us -> 16.8 us  [the longest x1 16.8 us: body(): from_left = lax.ppermute(dx[2], 'tensor', [(i, i + 1) for i in range(half)])]
    ppermute x1 -> x2, starting transfers between devices: 2.11 us -> 18 us  [the longest x1 17.2 us: body(): from_left = lax.ppermute(dx[2], 'tensor', [(i, i + 1) for i in range(half)])]
    pallas_call x1, Pallas kernels: 40.8 us -> 52.7 us  [attn_bwd(): pl.pallas_call(functools.partial(attn_bwd_kernel, docs=docs, heads=heads,...]
  transfers between devices with their start and end apart: 34 -> 33, of which waited for: 19 -> 17; matrix products, arithmetic and copies ran while one was open for 8% -> 8% of each run, Pallas kernels for 15% -> 22%
where the time goes in v3:
time: 449 us; the launch traced here: 440 us
  Pallas kernels  150 us (33%)
  waiting for transfers between devices  147 us (33%)
  starting transfers between devices  61.8 us (14%)
  local copies, waits for them, and re-layouts  34.9 us (8%)
  other arithmetic  31.7 us (7%)
  between operations  15 us (3%)
    ppermute x9, waiting for transfers between devices, shift(): return lax.ppermute(array, 'tensor', rotate_axis(tp_size, step))  60 us
    pallas_call x1, Pallas kernels, attn_bwd(): pl.pallas_call(functools.partial(attn_bwd_kernel, docs=docs, heads=heads,...  52.7 us
    pallas_call x1, Pallas kernels, attn_fwd(): pl.pallas_call(functools.partial(attn_fwd_kernel, docs=docs, heads=heads,...  34 us
    pallas_call x1, Pallas kernels, ffn_layer(): pl.pallas_call(functools.partial(ffn_kernel, slots=slots, pieces=pieces,...  33 us
    ppermute x6, waiting for transfers between devices, along(): return lax.ppermute(array, 'tensor', line_axis(tp_size, step))  32.5 us
    ppermute x9, starting transfers between devices, shift(): return lax.ppermute(array, 'tensor', rotate_axis(tp_size, step))  22.3 us
    ppermute x12, waiting for transfers between devices, flip(): return lax.ppermute(array, 'dp', flip_axis(dp_size, bit))  21.7 us
    pallas_call x4, Pallas kernels, wgrad(): pl.pallas_call(functools.partial(wgrad_kernel, slots=slots, share=share,...  20.1 us
  transfers between devices with their start and end apart: 33, of which 17 were waited for; matrix products, arithmetic and copies ran while one was open for 8% of the time, Pallas kernels for 22%

profile of v3, /device:TPU:0, one launch (start us, length us, event | category | flops | bytes accessed | tf_op | source)
XLA Modules:
  0.0 440.4 jit_solution(7542770741551457867)
XLA Ops:
  8.3 1.1 constant_dynamic-slice_fusion.1
  10.8 2.9 constant_dynamic-slice_fusion.2
  14.5 4.1 collective-permute-start.2
  18.6 1.6 collective-permute-start.1
  20.1 2.2 collective-permute-start
  22.4 8.8 %collective-permute-done.2 = bf16[96,896]{1,0:T(8,128)(2,1)S(1)} collective-permute-done((bf16[96,896]{1,0:T(8,128)(2,1)S(1)}, bf16[96,896]{1,0:T(8,128)(2,1)S(1)}, u32[]{:S(2)}, u32[]{:S(2)}) %collective-permute-start.2) | collective-permute-done | bytes 172064 | tf_op jit(solution)/shard_map/ppermute | solution.py:710
  33.0 2.1 collective-permute-start.9
  35.2 2.7 collective-permute-start.8
  37.9 1.9 collective-permute-start.7
  39.8 6.4 %collective-permute-done.9 = bf16[96,2304]{1,0:T(8,128)(2,1)S(1)} collective-permute-done((bf16[96,2304]{1,0:T(8,128)(2,1)S(1)}, bf16[96,2304]{1,0:T(8,128)(2,1)S(1)}, u32[]{:S(2)}, u32[]{:S(2)}) %collective-permute-start.9) | collective-permute-done | bytes 442400 | tf_op jit(solution)/shard_map/ppermute | solution.py:710
  46.2 30.4 %collective-permute-done.8 = bf16[96,2304]{1,0:T(8,128)(2,1)S(1)} collective-permute-done((bf16[96,2304]{1,0:T(8,128)(2,1)S(1)}, bf16[96,2304]{1,0:T(8,128)(2,1)S(1)}, u32[]{:S(2)}, u32[]{:S(2)}) %collective-permute-start.8) | collective-permute-done | bytes 442400 | tf_op jit(solution)/shard_map/ppermute | solution.py:710
  76.6 1.1 pad_maximum_fusion.2
  81.0 1.3 collective-permute-start.5
  82.4 1.3 collective-permute-start.3
  84.7 1.3 fusion.13
  86.1 1.4 copy.87.refs_7_
  87.5 6.8 %copy.88 = bf16[768,2,768]{0,2,1:T(8,128)(2,1)} copy(bf16[768,2,768]{2,1,0:T(2,128)(2,1)} %param.17) | data formatting | bytes 4718592 | tf_op jit(solution)/shard_map/optimization_barrier | solution.py:669
  94.3 1.4 concatenate.23.info
  95.7 1.9 slice_bitcast_fusion.3
  97.7 1.9 pad_maximum_fusion
  99.6 4.6 %collective-permute-start.6 = (bf16[512,768]{1,0:T(8,128)(2,1)S(1)}, bf16[512,768]{1,0:T(8,128)(2,1)S(1)}, u32[]{:S(2)}, u32[]{:S(2)}) collective-permute-start(bf16[512,768]{1,0:T(8,128)(2,1)S(1)} %collective-permute-done.5.refs_3_), channel_id=1, source_target_pairs={{0,1},{1,2},{2,3},{4,5},{5,6},{6,7},{8,9},{9,10},{10,11},{12,13},{... | collective-permute-start | bytes 2359304 | tf_op jit(solution)/shard_map/ppermute | solution.py:713
  104.2 1.5 collective-permute-start.4
  105.8 5.6 %multiply_sine_fusion = (f32[2048,128]{1,0:T(8,128)}, f32[2048,128]{1,0:T(8,128)}) fusion(f32[128]{0:T(128)S(1)} %multiply_power_fusion, f32[2048]{0:T(1024)S(1)} %subtract_convert_fusion), kind=kLoop, calls=%fused_computation.15 | loop fusion | flops 262144 | bytes 2105856 | tf_op jit(solution)/shard_map/sin | solution.py:748
  111.4 8.9 %collective-permute-done.6 = bf16[512,768]{1,0:T(8,128)(2,1)S(1)} collective-permute-done((bf16[512,768]{1,0:T(8,128)(2,1)S(1)}, bf16[512,768]{1,0:T(8,128)(2,1)S(1)}, u32[]{:S(2)}, u32[]{:S(2)}) %collective-permute-start.6) | collective-permute-done | bytes 786464 | tf_op jit(solution)/shard_map/ppermute | solution.py:713
  120.3 4.2 collective-permute-done.4
  124.6 1.4 copy-done.12
  126.0 34.0 %attn_fwd.1 = (bf16[4,3,512,256]{3,2,1,0:T(8,128)(2,1)}, bf16[4,2048,256]{2,1,0:T(8,128)(2,1)}, bf16[4,2048,192]{2,1,0:T(8,128)(2,1)}, f32[4,8,512]{2,1,0:T(8,128)S(1)}, bf16[4,512,192]{2,1,0:T(8,128)(2,1)}) custom-call(s32[8]{0:T(128)S(1)} %concatenate.23.info, bf16[512,768]{1,0:T(8,128)(2,1)S(1)} %bitcast.119, bf16[512,768]{1,0:T(8,128)(2,1)S(1)} %copy-done.12, ...), custom_call_target="tpu_custom_call" | custom-call | flops 21474836480 | bytes 20971520 | tf_op jit(solution)/shard_map/attn_fwd/pallas_call | solution.py:149
  160.0 33.0 %ffn_layer.1 = (bf16[512,768]{1,0:T(8,128)(2,1)}, f32[512,768]{1,0:T(8,128)}, bf16[512,768]{1,0:T(8,128)(2,1)}, bf16[512,768]{1,0:T(8,128)(2,1)}, bf16[768,512]{...) custom-call(bf16[512,768]{1,0:T(8,128)(2,1)} %bitcast.115, ...), custom_call_target="tpu_custom_call" | custom-call | flops 17179869184 | bytes 31457280 | tf_op jit(solution)/shard_map/ffn_layer/pallas_call | solution.py:504
  193.0 1.1 copy-done.3
  194.1 1.1 copy-done.4
  195.3 1.1 copy-done.5
  197.2 4.5 %wgrad.4 = bf16[2,384,2560]{2,1,0:T(8,128)(2,1)S(1)} custom-call(s32[2]{0:T(128)S(1)} %pad_add_fusion.refs_0_, bf16[512,3072]{1,0:T(8,128)(2,1)} %get-tuple-element.78.refs_1_, bf16[512,3072]{1,0:T(8,128)(2,1)} %get-tuple-element.79.refs_2_, bf16[512,3072]{1,0:T(8,128)(2,1)} %get-tuple-element.80.refs_3_, bf16[768,512]{1,0:T(8,128)(2,1)S(1)} %copy-done.5, ...), custom_call_target="tpu_custom_call" | custom-call | flops 2147483648 | bytes 10485760 | tf_op jit(solution)/shard_map/wgrad/pallas_call | solution.py:599
  201.8 4.5 %wgrad.5 = bf16[2,384,2560]{2,1,0:T(8,128)(2,1)S(1)} custom-call(s32[2]{0:T(128)S(1)} %pad_add_fusion.refs_0_, bf16[512,3072]{1,0:T(8,128)(2,1)} %get-tuple-element.78.refs_1_, bf16[512,3072]{1,0:T(8,128)(2,1)} %get-tuple-element.79.refs_2_, bf16[512,3072]{1,0:T(8,128)(2,1)} %get-tuple-element.80.refs_3_, bf16[768,512]{1,0:T(8,128)(2,1)S(1)} %copy-done.5, ...), custom_call_target="tpu_custom_call" | custom-call | flops 2147483648 | bytes 10485760 | tf_op jit(solution)/shard_map/wgrad/pallas_call | solution.py:599
  206.9 1.7 collective-permute-done.10.refs_9_
  208.6 5.6 %wgrad.6 = (bf16[192,2560]{1,0:T(8,128)(2,1)S(1)}, bf16[192,2560]{1,0:T(8,128)(2,1)S(1)}, bf16[2,192,2560]{2,1,0:T(8,128)(2,1)}) custom-call(s32[2]{0:T(128)S(1)} %pad_add_fusion.refs_0_, bf16[512,3072]{1,0:T(8,128)(2,1)} %get-tuple-element.78.refs_1_, bf16[512,3072]{1,0:T(8,128)(2,1)} %get-tuple-element.79.refs_2_, ...), custom_call_target="tpu_custom_call" | custom-call | flops 2147483648 | bytes 10485760 | tf_op jit(solution)/shard_map/wgrad/pallas_call | solution.py:599
  214.2 5.5 %wgrad.7 = (bf16[192,2560]{1,0:T(8,128)(2,1)S(1)}, bf16[192,2560]{1,0:T(8,128)(2,1)}, bf16[2,192,2560]{2,1,0:T(8,128)(2,1)S(1)}) custom-call(s32[2]{0:T(128)S(1)} %pad_add_fusion.refs_0_, bf16[512,3072]{1,0:T(8,128)(2,1)} %get-tuple-element.78.refs_1_, bf16[512,3072]{1,0:T(8,128)(2,1)} %get-tuple-element.79.refs_2_, ...), custom_call_target="tpu_custom_call" | custom-call | flops 2147483648 | bytes 10485760 | tf_op jit(solution)/shard_map/wgrad/pallas_call | solution.py:599
  219.8 1.4 collective-permute-start.12
  221.8 52.7 %attn_bwd.1 = (bf16[8,4,96,768]{3,2,1,0:T(8,128)(2,1)}, f32[512,768]{1,0:T(8,128)}, bf16[512,768]{1,0:T(8,128)(2,1)}, bf16[512,768]{1,0:T(8,128)(2,1)}, bf16[512,768]{1,0:T(8,128)(2,1)}) custom-call(s32[8]{0:T(128)} %copy-done.8, bf16[512,768]{1,0:T(8,128)(2,1)} %bitcast.116, bf16[512,768]{1,0:T(8,128)(2,1)} %copy-done.11, bf16[512,768]{1,0:T(8,128)(2,1)} %copy-done.7, ...), custom_call_target="tpu_custom_call" | custom-call | flops 42949672960 | bytes 25165824 | tf_op jit(solution)/shard_map/attn_bwd/pallas_call | solution.py:283
  275.5 1.8 slice_bitcast_fusion.1
  277.4 2.0 add_convert_fusion
  281.6 17.2 %collective-permute-start.18 = (bf16[512,768]{1,0:T(8,128)(2,1)S(1)}, bf16[512,768]{1,0:T(8,128)(2,1)S(1)}, u32[]{:S(2)}, u32[]{:S(2)}) collective-permute-start(bf16[512,768]{1,0:T(8,128)(2,1)S(1)} %copy-done.29), channel_id=1, source_target_pairs={{0,1},{1,2},{4,5},{5,6},{8,9},{9,10},{12,13},{13,14},{16,17},{17,1... | collective-permute-start | bytes 2359304 | tf_op jit(solution)/shard_map/ppermute | solution.py:776
  298.9 16.8 %collective-permute-done.18 = bf16[512,768]{1,0:T(8,128)(2,1)S(1)} collective-permute-done((bf16[512,768]{1,0:T(8,128)(2,1)S(1)}, bf16[512,768]{1,0:T(8,128)(2,1)S(1)}, u32[]{:S(2)}, u32[]{:S(2)}) %collective-permute-start.18) | collective-permute-done | bytes 786464 | tf_op jit(solution)/shard_map/ppermute | solution.py:776
  316.0 1.6 add_convert_fusion.1
  317.6 1.4 pad_maximum_fusion.1
  319.0 2.4 fusion
  321.5 1.4 collective-permute-start.20
  323.2 12.7 %collective-permute-done.20 = bf16[2,2,96,768]{3,2,1,0:T(8,128)(2,1)S(1)} collective-permute-done((bf16[2,2,96,768]{3,2,1,0:T(8,128)(2,1)S(1)}, bf16[2,2,96,768]{3,2,1,0:T(8,128)(2,1)S(1)}, u32[]{:S(2)}, u32[]{:S(2)}) %collective-permute-start.20) | collective-permute-done | bytes 589856 | tf_op jit(solution)/shard_map/ppermute | solution.py:707
  335.9 1.4 collective-permute-done.23
  339.0 5.9 %collective-permute-done.24 = bf16[2,96,768]{2,1,0:T(8,128)(2,1)S(1)} collective-permute-done((bf16[2,96,768]{2,1,0:T(8,128)(2,1)S(1)}, bf16[2,96,768]{2,1,0:T(8,128)(2,1)S(1)}, u32[]{:S(2)}, u32[]{:S(2)}) %collective-permute-start.24) | collective-permute-done | bytes 294944 | tf_op jit(solution)/shard_map/ppermute | solution.py:707
  345.0 3.7 collective-permute-start.25
  348.8 3.9 collective-permute-start.22
  353.7 12.7 %collective-permute-done.25 = bf16[96,768]{1,0:T(8,128)(2,1)S(1)} collective-permute-done((bf16[96,768]{1,0:T(8,128)(2,1)S(1)}, bf16[96,768]{1,0:T(8,128)(2,1)S(1)}, u32[]{:S(2)}, u32[]{:S(2)}) %collective-permute-start.25) | collective-permute-done | bytes 147488 | tf_op jit(solution)/shard_map/ppermute | solution.py:710
  367.6 3.3 reduce-scatter.2.cloned.1.call-done
  370.9 1.9 pad_maximum_fusion.4
  372.8 5.6 %collective-permute-start.27 = (bf16[512,768]{1,0:T(8,128)(2,1)}, bf16[512,768]{1,0:T(8,128)(2,1)S(1)}, u32[]{:S(2)}, u32[]{:S(2)}) collective-permute-start(bf16[512,768]{1,0:T(8,128)(2,1)} %add_convert_fusion.5), channel_id=1, source_target_pairs={{0,1},{1,2},{2,3},{4,5},{5,6},{6,7},{8,9},{9,10},{10,11},{12,13},{... | collective-permute-start | bytes 2359304 | tf_op jit(solution)/shard_map/ppermute | solution.py:713
  378.5 1.3 collective-permute-start.28
  379.8 15.6 %collective-permute-done.27 = bf16[512,768]{1,0:T(8,128)(2,1)S(1)} collective-permute-done((bf16[512,768]{1,0:T(8,128)(2,1)}, bf16[512,768]{1,0:T(8,128)(2,1)S(1)}, u32[]{:S(2)}, u32[]{:S(2)}) %collective-permute-start.27) | collective-permute-done | bytes 786464 | tf_op jit(solution)/shard_map/ppermute | solution.py:713
  395.3 3.8 collective-permute-done.28
  399.2 2.9 add_bitcast_fusion
  402.1 13.0 %all-gather.11.cloned.1.call-done.query.key.value.gate.up = bf16[768,3328]{1,0:T(8,128)(2,1)} async-done(((bf16[96,3328]{1,0:T(8,128)(2,1)}), bf16[768,3328]{1,0:T(8,128)(2,1)}) %all-gather.11.cloned.1.call-update) | async-done | bytes 5111824 | tf_op jit(solution)/shard_map/all_gather | solution.py:716
  419.6 1.1 copy.95
  420.7 3.7 final_qkv.1
  424.4 2.8 slice_convert_fusion
  427.2 6.2 %final_ffn.1 = f32[768,2,768]{2,1,0:T(2,128)} custom-call(bf16[768,3328]{1,0:T(8,128)(2,1)} %all-gather.11.cloned.1.call-done.query.key.value.gate.up, bf16[768,3328]{1,0:T(8,128)(2,1)} %all-gather.11.cloned.1.call-done.query.key.value.gate.up), custom_call_target="tpu_custom_call" | custom-call | flops 1048576 | bytes 8388608 | tf_op jit(solution)/shard_map/final_ffn/pallas_call | solution.py:617
  (150 shorter events, 24.3 us)
Async XLA Ops:
  7.2 1.0 copy-start
  7.2 117.4 %all-gather.7.cloned.1.call-start = ((), (), s32[]{:S(2)}) async-start(), calls=%async_computation.2 | async-start | bytes 6193152 | tf_op jit(solution)/shard_map/all_gather | solution.py:716
  14.5 16.7 %collective-permute-start.2 = (bf16[96,896]{1,0:T(8,128)(2,1)S(1)}, bf16[96,896]{1,0:T(8,128)(2,1)S(1)}, u32[]{:S(2)}, u32[]{:S(2)}) collective-permute-start(bf16[96,896]{1,0:T(8,128)(2,1)S(1)} %pad_maximum_fusion.6), channel_id=1, source_target_pairs={{0,2},{1,3},{2,0},{3,1},{4,6},{5,7},{6,4},{7,5},{8,10},{9,11},{10,... | collective-permute-start | bytes 516104 | tf_op jit(solution)/shard_map/ppermute | solution.py:710
  18.6 12.6 %collective-permute-start.1 = (bf16[96,896]{1,0:T(8,128)(2,1)S(1)}, bf16[96,896]{1,0:T(8,128)(2,1)S(1)}, u32[]{:S(2)}, u32[]{:S(2)}) collective-permute-start(bf16[96,896]{1,0:T(8,128)(2,1)S(1)} %pad_maximum_fusion.6), channel_id=1, source_target_pairs={{0,1},{1,2},{2,3},{3,0},{4,5},{5,6},{6,7},{7,4},{8,9},{9,10},{10,1... | collective-permute-start | bytes 516104 | tf_op jit(solution)/shard_map/ppermute | solution.py:710
  20.1 11.8 %collective-permute-start = (bf16[96,896]{1,0:T(8,128)(2,1)S(1)}, bf16[96,896]{1,0:T(8,128)(2,1)S(1)}, u32[]{:S(2)}, u32[]{:S(2)}) collective-permute-start(bf16[96,896]{1,0:T(8,128)(2,1)S(1)} %pad_maximum_fusion.6), channel_id=1, source_target_pairs={{0,3},{1,0},{2,1},{3,2},{4,7},{5,4},{6,5},{7,6},{8,11},{9,8},{10,9... | collective-permute-start | bytes 516104 | tf_op jit(solution)/shard_map/ppermute | solution.py:710
  32.9 44.9 %copy-start.24 = (f32[768]{0:T(1024)S(1)}, f32[768]{0:T(1024)}, u32[]{:S(2)}) copy-start(f32[768]{0:T(1024)} %param.15) | copy-start | bytes 9220
  32.9 45.5 %copy-start.25 = (f32[768]{0:T(1024)S(1)}, f32[768]{0:T(1024)}, u32[]{:S(2)}) copy-start(f32[768]{0:T(1024)} %param.16) | copy-start | bytes 9220
  32.9 46.1 %copy-start.26 = (f32[768]{0:T(1024)S(1)}, f32[768]{0:T(1024)}, u32[]{:S(2)}) copy-start(f32[768]{0:T(1024)} %param.19) | copy-start | bytes 9220
  32.9 46.7 %copy-start.27 = (f32[768]{0:T(1024)S(1)}, f32[768]{0:T(1024)}, u32[]{:S(2)}) copy-start(f32[768]{0:T(1024)} %param.20) | copy-start | bytes 9220
  32.9 47.3 %copy-start.28 = (s32[1,24]{1,0:T(1,128)S(1)}, s32[1,24]{1,0:T(1,128)}, u32[]{:S(2)}) copy-start(s32[1,24]{1,0:T(1,128)} %param.12) | copy-start | bytes 292
  32.9 48.1 %copy-start.9 = (bf16[1,512,768]{2,1,0:T(8,128)(2,1)S(1)}, bf16[1,512,768]{2,1,0:T(8,128)(2,1)}, u32[]{:S(2)}) copy-start(bf16[1,512,768]{2,1,0:T(8,128)(2,1)} %param.11) | copy-start | bytes 2359300
  33.0 127.0 %all-gather.9.cloned.1.call-start = ((), (), s32[]{:S(2)}) async-start(), calls=%async_computation.3 | async-start | bytes 11943936 | tf_op jit(solution)/shard_map/all_gather | solution.py:716
  33.0 13.2 %collective-permute-start.9 = (bf16[96,2304]{1,0:T(8,128)(2,1)S(1)}, bf16[96,2304]{1,0:T(8,128)(2,1)S(1)}, u32[]{:S(2)}, u32[]{:S(2)}) collective-permute-start(bf16[96,2304]{1,0:T(8,128)(2,1)S(1)} %pad_maximum_fusion.5), channel_id=1, source_target_pairs={{0,3},{1,0},{2,1},{3,2},{4,7},{5,4},{6,5},{7,6},{8,11},{9,8},{10,9... | collective-permute-start | bytes 1327112 | tf_op jit(solution)/shard_map/ppermute | solution.py:710
  35.2 41.4 %collective-permute-start.8 = (bf16[96,2304]{1,0:T(8,128)(2,1)S(1)}, bf16[96,2304]{1,0:T(8,128)(2,1)S(1)}, u32[]{:S(2)}, u32[]{:S(2)}) collective-permute-start(bf16[96,2304]{1,0:T(8,128)(2,1)S(1)} %pad_maximum_fusion.5), channel_id=1, source_target_pairs={{0,2},{1,3},{2,0},{3,1},{4,6},{5,7},{6,4},{7,5},{8,10},{9,11},{10,... | collective-permute-start | bytes 1327112 | tf_op jit(solution)/shard_map/ppermute | solution.py:710
  37.9 38.7 %collective-permute-start.7 = (bf16[96,2304]{1,0:T(8,128)(2,1)S(1)}, bf16[96,2304]{1,0:T(8,128)(2,1)S(1)}, u32[]{:S(2)}, u32[]{:S(2)}) collective-permute-start(bf16[96,2304]{1,0:T(8,128)(2,1)S(1)} %pad_maximum_fusion.5), channel_id=1, source_target_pairs={{0,1},{1,2},{2,3},{3,0},{4,5},{5,6},{6,7},{7,4},{8,9},{9,10},{10,1... | collective-permute-start | bytes 1327112 | tf_op jit(solution)/shard_map/ppermute | solution.py:710
  77.8 293.1 %reduce-scatter.2.cloned.1.call-start = ((), (), s32[]{:S(2)}) async-start(), calls=%async_computation.1 | async-start | bytes 2457600 | tf_op jit(solution)/shard_map/reduce_scatter | solution.py:785
  81.0 18.6 %collective-permute-start.5 = (bf16[512,768]{1,0:T(8,128)(2,1)S(1)}, bf16[512,768]{1,0:T(8,128)(2,1)S(1)}, u32[]{:S(2)}, u32[]{:S(2)}) collective-permute-start(bf16[512,768]{1,0:T(8,128)(2,1)S(1)} %bitcast.117), channel_id=1, source_target_pairs={{0,1},{1,2},{2,3},{4,5},{5,6},{6,7},{8,9},{9,10},{10,11},{12,13},{... | collective-permute-start | bytes 2359304 | tf_op jit(solution)/shard_map/ppermute | solution.py:713
  82.4 21.8 %collective-permute-start.3 = (bf16[512,768]{1,0:T(8,128)(2,1)S(1)}, bf16[512,768]{1,0:T(8,128)(2,1)S(1)}, u32[]{:S(2)}, u32[]{:S(2)}) collective-permute-start(bf16[512,768]{1,0:T(8,128)(2,1)S(1)} %bitcast.118), channel_id=1, source_target_pairs={{1,0},{2,1},{3,2},{5,4},{6,5},{7,6},{9,8},{10,9},{11,10},{13,12},{... | collective-permute-start | bytes 2359304 | tf_op jit(solution)/shard_map/ppermute | solution.py:713
  95.7 28.9 %copy-start.8 = (s32[8]{0:T(128)}, s32[8]{0:T(128)S(1)}, u32[]{:S(2)}) copy-start(s32[8]{0:T(128)S(1)} %concatenate.23.info) | copy-start | bytes 100
  95.7 2.0 copy-start.15
  99.6 25.0 %copy-start.10 = (bf16[512,768]{1,0:T(8,128)(2,1)}, bf16[512,768]{1,0:T(8,128)(2,1)S(1)}, u32[]{:S(2)}) copy-start(bf16[512,768]{1,0:T(8,128)(2,1)S(1)} %collective-permute-done.5.refs_3_) | copy-start | bytes 2359300
  99.6 20.7 %collective-permute-start.6 = (bf16[512,768]{1,0:T(8,128)(2,1)S(1)}, bf16[512,768]{1,0:T(8,128)(2,1)S(1)}, u32[]{:S(2)}, u32[]{:S(2)}) collective-permute-start(bf16[512,768]{1,0:T(8,128)(2,1)S(1)} %collective-permute-done.5.refs_3_), channel_id=1, source_target_pairs={{0,1},{1,2},{2,3},{4,5},{5,6},{6,7},{8,9},{9,10},{10,11},{12,13},{... | collective-permute-start | bytes 2359304 | tf_op jit(solution)/shard_map/ppermute | solution.py:713
  104.2 16.1 %copy-start.11 = (bf16[512,768]{1,0:T(8,128)(2,1)}, bf16[512,768]{1,0:T(8,128)(2,1)S(1)}, u32[]{:S(2)}) copy-start(bf16[512,768]{1,0:T(8,128)(2,1)S(1)} %collective-permute-done.3.refs_1_) | copy-start | bytes 2359300
  104.2 20.2 %collective-permute-start.4 = (bf16[512,768]{1,0:T(8,128)(2,1)S(1)}, bf16[512,768]{1,0:T(8,128)(2,1)S(1)}, u32[]{:S(2)}, u32[]{:S(2)}) collective-permute-start(bf16[512,768]{1,0:T(8,128)(2,1)S(1)} %collective-permute-done.3.refs_1_), channel_id=1, source_target_pairs={{1,0},{2,1},{3,2},{5,4},{6,5},{7,6},{9,8},{10,9},{11,10},{13,12},{... | collective-permute-start | bytes 2359304 | tf_op jit(solution)/shard_map/ppermute | solution.py:713
  124.5 35.4 %copy-start.7 = (bf16[512,768]{1,0:T(8,128)(2,1)}, bf16[512,768]{1,0:T(8,128)(2,1)S(1)}, u32[]{:S(2)}) copy-start(bf16[512,768]{1,0:T(8,128)(2,1)S(1)} %broadcast_select_fusion.refs_2_) | copy-start | bytes 2359300
  124.6 1.4 copy-start.12
  159.9 33.1 %copy-start.13 = (f32[4,8,512]{2,1,0:T(8,128)}, f32[4,8,512]{2,1,0:T(8,128)S(1)}, u32[]{:S(2)}) copy-start(f32[4,8,512]{2,1,0:T(8,128)S(1)} %get-tuple-element.97.refs_11_) | copy-start | bytes 196612
  160.0 33.0 %copy-start.2 = (bf16[4,512,192]{2,1,0:T(8,128)(2,1)S(1)}, bf16[4,512,192]{2,1,0:T(8,128)(2,1)}, u32[]{:S(2)}) copy-start(bf16[4,512,192]{2,1,0:T(8,128)(2,1)} %get-tuple-element.70.refs_6_.refs_7_.refs_12_) | copy-start | bytes 2359300
  193.0 1.1 copy-start.3
  194.1 1.1 copy-start.4
  195.3 1.1 copy-start.5
  196.4 0.8 copy-start.6
  201.8 6.8 %collective-permute-start.10 = (bf16[2,384,2560]{2,1,0:T(8,128)(2,1)S(1)}, bf16[2,384,2560]{2,1,0:T(8,128)(2,1)S(1)}, u32[]{:S(2)}, u32[]{:S(2)}) collective-permute-start(bf16[2,384,2560]{2,1,0:T(8,128)(2,1)S(1)} %wgrad.4), channel_id=1, source_target_pairs={{0,4},{4,0},{8,12},{12,8},{16,20},{20,16},{24,28},{28,24},{1,5},{5... | collective-permute-start | bytes 11796488 | tf_op jit(solution)/shard_map/ppermute | solution.py:707
  206.4 7.9 %collective-permute-start.11 = (bf16[2,384,2560]{2,1,0:T(8,128)(2,1)S(1)}, bf16[2,384,2560]{2,1,0:T(8,128)(2,1)S(1)}, u32[]{:S(2)}, u32[]{:S(2)}) collective-permute-start(bf16[2,384,2560]{2,1,0:T(8,128)(2,1)S(1)} %wgrad.5), channel_id=1, source_target_pairs={{0,4},{4,0},{8,12},{12,8},{16,20},{20,16},{24,28},{28,24},{1,5},{5... | collective-permute-start | bytes 11796488 | tf_op jit(solution)/shard_map/ppermute | solution.py:707
  219.8 54.7 %collective-permute-start.12 = (bf16[192,2560]{1,0:T(8,128)(2,1)S(1)}, bf16[192,2560]{1,0:T(8,128)(2,1)S(1)}, u32[]{:S(2)}, u32[]{:S(2)}) collective-permute-start(bf16[192,2560]{1,0:T(8,128)(2,1)S(1)} %get-tuple-element.91), channel_id=1, source_target_pairs={{0,8},{4,12},{8,0},{12,4},{16,24},{20,28},{24,16},{28,20},{1,9},{5... | collective-permute-start | bytes 2949128 | tf_op jit(solution)/shard_map/ppermute | solution.py:707
  221.2 53.3 %collective-permute-start.14 = (bf16[192,2560]{1,0:T(8,128)(2,1)}, bf16[192,2560]{1,0:T(8,128)(2,1)}, u32[]{:S(2)}, u32[]{:S(2)}) collective-permute-start(bf16[192,2560]{1,0:T(8,128)(2,1)} %get-tuple-element.93), channel_id=1, source_target_pairs={{0,8},{4,12},{8,0},{12,4},{16,24},{20,28},{24,16},{28,20},{1,9},{5... | collective-permute-start | bytes 2949128 | tf_op jit(solution)/shard_map/ppermute | solution.py:707
  221.8 52.7 %collective-permute-start.13 = (bf16[2,192,2560]{2,1,0:T(8,128)(2,1)}, bf16[2,192,2560]{2,1,0:T(8,128)(2,1)}, u32[]{:S(2)}, u32[]{:S(2)}) collective-permute-start(bf16[2,192,2560]{2,1,0:T(8,128)(2,1)} %get-tuple-element.92), channel_id=1, source_target_pairs={{0,16},{4,20},{8,24},{12,28},{16,0},{20,4},{24,8},{28,12},{1,17},{... | collective-permute-start | bytes 5898248 | tf_op jit(solution)/shard_map/ppermute | solution.py:707
  274.5 1.0 copy-start.16
  277.3 38.4 %collective-permute-start.17 = (bf16[4,4,96,768]{3,2,1,0:T(8,128)(2,1)S(1)}, bf16[4,4,96,768]{3,2,1,0:T(8,128)(2,1)S(1)}, u32[]{:S(2)}, u32[]{:S(2)}) collective-permute-start(bf16[4,4,96,768]{3,2,1,0:T(8,128)(2,1)S(1)} %slice_bitcast_fusion.1), channel_id=1, source_target_pairs={{0,4},{4,0},{8,12},{12,8},{16,20},{20,16},{24,28},{28,24},{1,5},{5... | collective-permute-start | bytes 7077896 | tf_op jit(solution)/shard_map/ppermute | solution.py:707
  279.4 1.2 copy-start.17
  279.5 1.4 copy-start.29
  279.5 36.2 %collective-permute-start.16 = (bf16[192,2560]{1,0:T(8,128)(2,1)S(1)}, bf16[192,2560]{1,0:T(8,128)(2,1)S(1)}, u32[]{:S(2)}, u32[]{:S(2)}) collective-permute-start(bf16[192,2560]{1,0:T(8,128)(2,1)S(1)} %slice_bitcast_fusion.5), channel_id=1, source_target_pairs={{0,8},{4,12},{8,0},{12,4},{16,24},{20,28},{24,16},{28,20},{1,9},{5... | collective-permute-start | bytes 2949128 | tf_op jit(solution)/shard_map/ppermute | solution.py:707
  280.8 34.9 %collective-permute-start.15 = (bf16[192,2560]{1,0:T(8,128)(2,1)S(1)}, bf16[192,2560]{1,0:T(8,128)(2,1)S(1)}, u32[]{:S(2)}, u32[]{:S(2)}) collective-permute-start(bf16[192,2560]{1,0:T(8,128)(2,1)S(1)} %add_convert_fusion.2), channel_id=1, source_target_pairs={{0,16},{4,20},{8,24},{12,28},{16,0},{20,4},{24,8},{28,12},{1,17},{... | collective-permute-start | bytes 2949128 | tf_op jit(solution)/shard_map/ppermute | solution.py:707
  280.9 18.0 %collective-permute-start.19 = (bf16[512,768]{1,0:T(8,128)(2,1)S(1)}, bf16[512,768]{1,0:T(8,128)(2,1)S(1)}, u32[]{:S(2)}, u32[]{:S(2)}) collective-permute-start(bf16[512,768]{1,0:T(8,128)(2,1)S(1)} %copy-done.29), channel_id=1, source_target_pairs={{2,1},{3,2},{6,5},{7,6},{10,9},{11,10},{14,13},{15,14},{18,17},{19... | collective-permute-start | bytes 2359304 | tf_op jit(solution)/shard_map/ppermute | solution.py:777
  281.6 34.1 %collective-permute-start.18 = (bf16[512,768]{1,0:T(8,128)(2,1)S(1)}, bf16[512,768]{1,0:T(8,128)(2,1)S(1)}, u32[]{:S(2)}, u32[]{:S(2)}) collective-permute-start(bf16[512,768]{1,0:T(8,128)(2,1)S(1)} %copy-done.29), channel_id=1, source_target_pairs={{0,1},{1,2},{4,5},{5,6},{8,9},{9,10},{12,13},{13,14},{16,17},{17,1... | collective-permute-start | bytes 2359304 | tf_op jit(solution)/shard_map/ppermute | solution.py:776
  298.9 18.7 %copy-start.22 = (bf16[512,768]{1,0:T(8,128)(2,1)}, bf16[512,768]{1,0:T(8,128)(2,1)S(1)}, u32[]{:S(2)}) copy-start(bf16[512,768]{1,0:T(8,128)(2,1)S(1)} %collective-permute-done.19) | copy-start | bytes 2359300
  315.7 1.9 copy-start.20
  319.0 96.1 %all-gather.11.cloned.1.call-start = ((), (), s32[]{:S(2)}) async-start(), calls=%async_computation.4 | async-start | bytes 5750784 | tf_op jit(solution)/shard_map/all_gather | solution.py:716
  321.5 16.6 %copy-start.19 = (bf16[512,768]{1,0:T(8,128)(2,1)S(1)}, bf16[512,768]{1,0:T(8,128)(2,1)}, u32[]{:S(2)}) copy-start(bf16[512,768]{1,0:T(8,128)(2,1)} %get-tuple-element.118) | copy-start | bytes 2359300
  321.5 16.5 %copy-start.23 = (bf16[512,768]{1,0:T(8,128)(2,1)S(1)}, bf16[512,768]{1,0:T(8,128)(2,1)}, u32[]{:S(2)}) copy-start(bf16[512,768]{1,0:T(8,128)(2,1)} %copy-done.22) | copy-start | bytes 2359300
  321.5 14.4 %collective-permute-start.20 = (bf16[2,2,96,768]{3,2,1,0:T(8,128)(2,1)S(1)}, bf16[2,2,96,768]{3,2,1,0:T(8,128)(2,1)S(1)}, u32[]{:S(2)}, u32[]{:S(2)}) collective-permute-start(bf16[2,2,96,768]{3,2,1,0:T(8,128)(2,1)S(1)} %slice_bitcast_fusion.8), channel_id=1, source_target_pairs={{0,8},{4,12},{8,0},{12,4},{16,24},{20,28},{24,16},{28,20},{1,9},{5... | collective-permute-start | bytes 1769480 | tf_op jit(solution)/shard_map/ppermute | solution.py:707
  322.9 14.4 %collective-permute-start.23 = (bf16[2,2,96,768]{3,2,1,0:T(8,128)(2,1)S(1)}, bf16[2,2,96,768]{3,2,1,0:T(8,128)(2,1)S(1)}, u32[]{:S(2)}, u32[]{:S(2)}) collective-permute-start(bf16[2,2,96,768]{3,2,1,0:T(8,128)(2,1)S(1)} %slice_bitcast_fusion.6), channel_id=1, source_target_pairs={{0,16},{4,20},{8,24},{12,28},{16,0},{20,4},{24,8},{28,12},{1,17},{... | collective-permute-start | bytes 1769480 | tf_op jit(solution)/shard_map/ppermute | solution.py:707
  337.6 7.3 %collective-permute-start.24 = (bf16[2,96,768]{2,1,0:T(8,128)(2,1)S(1)}, bf16[2,96,768]{2,1,0:T(8,128)(2,1)S(1)}, u32[]{:S(2)}, u32[]{:S(2)}) collective-permute-start(bf16[2,96,768]{2,1,0:T(8,128)(2,1)S(1)} %slice_bitcast_fusion.10), channel_id=1, source_target_pairs={{0,8},{4,12},{8,0},{12,4},{16,24},{20,28},{24,16},{28,20},{1,9},{5... | collective-permute-start | bytes 884744 | tf_op jit(solution)/shard_map/ppermute | solution.py:707
  338.3 14.4 %copy-start.18 = (bf16[512,768]{1,0:T(8,128)(2,1)S(1)}, bf16[512,768]{1,0:T(8,128)(2,1)}, u32[]{:S(2)}) copy-start(bf16[512,768]{1,0:T(8,128)(2,1)} %get-tuple-element.116) | copy-start | bytes 2359300
  338.3 14.4 %copy-start.21 = (bf16[512,768]{1,0:T(8,128)(2,1)S(1)}, bf16[512,768]{1,0:T(8,128)(2,1)}, u32[]{:S(2)}) copy-start(bf16[512,768]{1,0:T(8,128)(2,1)} %copy-done.20) | copy-start | bytes 2359300
  338.3 10.4 %collective-permute-start.21 = (bf16[2,96,768]{2,1,0:T(8,128)(2,1)S(1)}, bf16[2,96,768]{2,1,0:T(8,128)(2,1)S(1)}, u32[]{:S(2)}, u32[]{:S(2)}) collective-permute-start(bf16[2,96,768]{2,1,0:T(8,128)(2,1)S(1)} %slice_bitcast_fusion.12), channel_id=1, source_target_pairs={{0,16},{4,20},{8,24},{12,28},{16,0},{20,4},{24,8},{28,12},{1,17},{... | collective-permute-start | bytes 884744 | tf_op jit(solution)/shard_map/ppermute | solution.py:707
  345.0 21.5 %collective-permute-start.25 = (bf16[96,768]{1,0:T(8,128)(2,1)S(1)}, bf16[96,768]{1,0:T(8,128)(2,1)S(1)}, u32[]{:S(2)}, u32[]{:S(2)}) collective-permute-start(bf16[96,768]{1,0:T(8,128)(2,1)S(1)} %get-tuple-element.187), channel_id=1, source_target_pairs={{0,2},{1,3},{2,0},{3,1},{4,6},{5,7},{6,4},{7,5},{8,10},{9,11},{10,... | collective-permute-start | bytes 442376 | tf_op jit(solution)/shard_map/ppermute | solution.py:710
  348.7 17.8 %collective-permute-start.26 = (bf16[96,768]{1,0:T(8,128)(2,1)S(1)}, bf16[96,768]{1,0:T(8,128)(2,1)S(1)}, u32[]{:S(2)}, u32[]{:S(2)}) collective-permute-start(bf16[96,768]{1,0:T(8,128)(2,1)S(1)} %get-tuple-element.188), channel_id=1, source_target_pairs={{0,1},{1,2},{2,3},{3,0},{4,5},{5,6},{6,7},{7,4},{8,9},{9,10},{10,1... | collective-permute-start | bytes 442376 | tf_op jit(solution)/shard_map/ppermute | solution.py:710
  348.8 50.4 %copy-start.14 = (f32[512,768]{1,0:T(8,128)S(1)}, f32[512,768]{1,0:T(8,128)}, u32[]{:S(2)}) copy-start(f32[512,768]{1,0:T(8,128)} %get-tuple-element.76) | copy-start | bytes 4718596
  348.8 18.7 %collective-permute-start.22 = (bf16[96,768]{1,0:T(8,128)(2,1)S(1)}, bf16[96,768]{1,0:T(8,128)(2,1)S(1)}, u32[]{:S(2)}, u32[]{:S(2)}) collective-permute-start(bf16[96,768]{1,0:T(8,128)(2,1)S(1)} %slice_bitcast_fusion.16), channel_id=1, source_target_pairs={{0,3},{1,0},{2,1},{3,2},{4,7},{5,4},{6,5},{7,6},{8,11},{9,8},{10,9... | collective-permute-start | bytes 442376 | tf_op jit(solution)/shard_map/ppermute | solution.py:710
  372.8 22.5 %collective-permute-start.27 = (bf16[512,768]{1,0:T(8,128)(2,1)}, bf16[512,768]{1,0:T(8,128)(2,1)S(1)}, u32[]{:S(2)}, u32[]{:S(2)}) collective-permute-start(bf16[512,768]{1,0:T(8,128)(2,1)} %add_convert_fusion.5), channel_id=1, source_target_pairs={{0,1},{1,2},{2,3},{4,5},{5,6},{6,7},{8,9},{9,10},{10,11},{12,13},{... | collective-permute-start | bytes 2359304 | tf_op jit(solution)/shard_map/ppermute | solution.py:713
  378.5 20.7 %collective-permute-start.28 = (bf16[512,768]{1,0:T(8,128)(2,1)S(1)}, bf16[512,768]{1,0:T(8,128)(2,1)S(1)}, u32[]{:S(2)}, u32[]{:S(2)}) collective-permute-start(bf16[512,768]{1,0:T(8,128)(2,1)S(1)} %add_convert_fusion.4), channel_id=1, source_target_pairs={{1,0},{2,1},{3,2},{5,4},{6,5},{7,6},{9,8},{10,9},{11,10},{13,12},{... | collective-permute-start | bytes 2359304 | tf_op jit(solution)/shard_map/ppermute | solution.py:713
  427.2 6.2 %copy-start.1 = (bf16[192,768]{1,0:T(8,128)(2,1)S(1)}, bf16[192,768]{1,0:T(8,128)(2,1)}, u32[]{:S(2)}) copy-start(bf16[192,768]{1,0:T(8,128)(2,1)} %param.14) | copy-start | bytes 884740
Sparse Core Ops, SparseCore 0:
  33.0 44.2 all-gather.6
  79.7 63.8 all-gather.8
  319.1 51.7 reduce-scatter.1
  373.2 41.8 all-gather.10

commit v4 on v3

--- a/solution.py
+++ b/solution.py
@@ -22,6 +22,10 @@
     return jnp.dot(a, b, preferred_element_type=f32)
 
 
+def stay(array):
+    return pltpu.with_memory_space_constraint(array, pltpu.HBM)
+
+
 def tile_rows(tile, base, count):
     return pl.ds(pl.multiple_of(lax.rem(tile - base + count, count) * TILE, TILE), TILE)
 
@@ -51,81 +55,104 @@
     lax.fori_loop(lo, hi, one, 0)
 
 
-def attn_fwd_kernel(info, *refs, docs, heads, slots):
-    toks = refs[:slots]
-    w, cos, sin, seg, qh, ka, va, lse, mixed, tok, vt, acc, top = refs[slots:]
-    here, width = toks[0].shape
-    seq = here * slots
-    count = seq // TILE
+def project_kernel(*refs, docs, heads, slot):
+    tok, w, cos, sin, seg = refs[:5]
+    outs = refs[5:] if slot == 0 else refs[8:]
+    ka, va, vt = outs[:3]
+    here, width = tok.shape
     used = heads * HALF
     cols = heads * HD
-    lo, hi, base = info[0], info[1], info[2]
-    tiles = here // TILE
-
-    @pl.when(pl.program_id(0) == 0)
-    def _():
-        for s in range(slots):
-            tok[s * here : (s + 1) * here, :] = toks[s][...]
-        r = lax.broadcasted_iota(jnp.int32, vt.shape, 0)
-        one = r == HD
-        for h in range(1, heads):
-            one = one | (r == 80 * h + HD)
-        vt[...] = jnp.where(one, 1.0, 0.0).astype(bf16)
+    lane = lax.broadcasted_iota(jnp.int32, (TILE, 128), 1)
+    filler = lax.broadcasted_iota(jnp.int32, (80 - HD, here), 0)
 
     def weight(start, stop):
         return w[:, 0, :, start:stop].reshape(width, stop - start)
 
-    lane = lax.broadcasted_iota(jnp.int32, (TILE, 128), 1)
-
-    def queries(c, _):
+    for h in range(heads):
+        vt[0, 0, 80 * h + HD : 80 * (h + 1), :] = jnp.where(filler == 0, 1.0, 0.0).astype(bf16)
+
+    def tile(c, _):
         rows = pl.ds(pl.multiple_of(c * TILE, TILE), TILE)
-        p = nn(tok[rows, :], weight(0, 256))
+        x = tok[rows, :]
         co, si = cos[rows, :], sin[rows, :]
         hit = (lane - used) == seg[rows, :]
-        ra = (p[:, :128] * co - p[:, 128:] * si).astype(bf16).astype(f32) * HD**-0.5
-        rb = (p[:, 128:] * co + p[:, :128] * si).astype(bf16).astype(f32) * HD**-0.5
+        if slot == 0:
+            p = nn(x, weight(0, 256))
+            ra = (p[:, :128] * co - p[:, 128:] * si).astype(bf16).astype(f32) * HD**-0.5
+            rb = (p[:, 128:] * co + p[:, :128] * si).astype(bf16).astype(f32) * HD**-0.5
+            for h in range(heads):
+                keep = (lane >= HALF * h) & (lane < HALF * (h + 1))
+                outs[3][0, h, rows, :128] = jnp.where(keep, ra, jnp.where(hit, -BIG, 0.0)).astype(bf16)
+                outs[3][0, h, rows, 128:] = jnp.where(keep, rb, 0.0).astype(bf16)
+        p = nn(x, weight(256, 512))
+        other = (lane >= used) & (lane < used + docs) & jnp.logical_not(hit)
+        ra, rb = p[:, :128] * co - p[:, 128:] * si, p[:, 128:] * co + p[:, :128] * si
+        ka[0, 0, rows, :128] = jnp.where(lane < used, ra, jnp.where(other, 1.0, 0.0)).astype(bf16)
+        ka[0, 0, rows, 128:] = rb.astype(bf16)
+        v = nn(x, weight(512 + cols, 512 + 2 * cols))
+        va[0, 0, rows, :] = v.astype(bf16)
+        turned = v.T.astype(bf16)
         for h in range(heads):
-            keep = (lane >= HALF * h) & (lane < HALF * (h + 1))
-            qh[0, h, rows, :128] = jnp.where(keep, ra, jnp.where(hit, -BIG, 0.0)).astype(bf16)
-            qh[0, h, rows, 128:] = jnp.where(keep, rb, 0.0).astype(bf16)
+            vt[0, 0, 80 * h : 80 * h + HD, rows] = turned[HD * h : HD * (h + 1), :]
         return 0
 
-    lax.fori_loop(0, here // TILE, queries, 0)
-
-    def keys(t, _):
-        rows = tile_rows(t, base, count)
-        x = tok[rows, :]
-        p = nn(x, weight(256, 512))
-        co, si = cos[rows, :], sin[rows, :]
-        other = (lane >= used) & (lane < used + docs) & ((lane - used) != seg[rows, :])
-        ra, rb = p[:, :128] * co - p[:, 128:] * si, p[:, 128:] * co + p[:, :128] * si
-        ka[0, rows, :128] = jnp.where(lane < used, ra, jnp.where(other, 1.0, 0.0)).astype(bf16)
-        ka[0, rows, 128:] = rb.astype(bf16)
-        v = nn(x, weight(512 + cols, 512 + 2 * cols))
-        va[0, rows, :] = v.astype(bf16)
-        vtt = v.T.astype(bf16)
-        for h in range(heads):
-            vt[80 * h : 80 * h + HD, rows] = vtt[HD * h : HD * (h + 1), :]
-        return 0
-
-    lax.fori_loop(lo, hi, keys, 0)
+    lax.fori_loop(0, here // TILE, tile, 0)
+
+
+def project(tok, w, cos, sin, seg, docs, heads, slot, slots, held=()):
+    here, width = tok.shape
+    cols = heads * HD
+    shapes = [(here, 256), (here, cols), (80 * heads, here)]
+    out_shape = [pltpu.HBM((slots, slots) + s, bf16) for s in shapes]
+    out_specs = [pl.BlockSpec((1, 1) + s, lambda g: (g, slot, 0, 0)) for s in shapes]
+    if slot == 0:
+        out_shape.append(pltpu.HBM((slots, heads, here, 256), bf16))
+        out_specs.append(pl.BlockSpec((1, heads, here, 256), lambda g: (g, 0, 0, 0)))
+    rows = pl.BlockSpec((here, cos.shape[1]), lambda g: (slot, 0))
+    return pl.pallas_call(
+        functools.partial(project_kernel, docs=docs, heads=heads, slot=slot),
+        grid=(slots,),
+        out_shape=tuple(out_shape),
+        in_specs=[
+            pl.BlockSpec((here, width), lambda g: (0, 0)),
+            pl.BlockSpec((w.shape[0], 1) + w.shape[2:], lambda g: (0, g, 0, 0)),
+            rows,
+            rows,
+            pl.BlockSpec((here, 1), lambda g: (slot, 0)),
+        ]
+        + [pl.BlockSpec(memory_space=pl.ANY)] * len(held),
+        out_specs=tuple(out_specs),
+        input_output_aliases={5 + n: n for n in range(len(held))},
+        compiler_params=pltpu.CompilerParams(vmem_limit_bytes=30 << 20),
+        cost_estimate=pl.CostEstimate(flops=2 << 30, bytes_accessed=8 << 20, transcendentals=0),
+        name="project",
+    )(tok, w, cos, sin, seg, *[stay(a) for a in held])
+
+
+def attn_fwd_kernel(info, seg, qh, ka, vt, lse, mixed, acc, top, *, docs, heads):
+    here = qh.shape[2]
+    tiles = here // TILE
+    count = ka.shape[1] * tiles
+    lo, hi, base = info[0], info[1], info[2]
     acc[...] = jnp.zeros_like(acc)
     top[...] = jnp.full_like(top, -3e38)
 
     def scan(t, mine):
-        rows = tile_rows(t, base, count)
-        kk = ka[0, rows, :]
+        c = lax.rem(t - base + count, count)
+        slot = c // tiles
+        rows = pl.ds(pl.multiple_of(lax.rem(c, tiles) * TILE, TILE), TILE)
+        kk = ka[0, slot, rows, :]
         scores = [nt(kk, qh[0, h, mine, :]) for h in range(heads)]
         olds = [top[h : h + 1, mine] for h in range(heads)]
         news = [jnp.maximum(olds[h], jnp.max(scores[h], axis=0, keepdims=True)) for h in range(heads)]
         probs = [jnp.exp(scores[h] - news[h]).astype(bf16) for h in range(heads)]
-        adds = [nn(vt[80 * h : 80 * h + 80, rows], probs[h]) for h in range(heads)]
+        adds = [nn(vt[0, slot, 80 * h : 80 * h + 80, rows], probs[h]) for h in range(heads)]
         for h in range(heads):
             top[h : h + 1, mine] = news[h]
             acc[h, :, mine] = acc[h, :, mine] * jnp.exp(olds[h] - news[h]) + adds[h]
 
     over_tiles(info, lo, hi, tiles, scan)
-    good = seg[:here, :] < docs - 1
+    good = seg[...] < docs - 1
     total = [jnp.where(top[h : h + 1, :] > -1e29, acc[h, HD : HD + 1, :], 1.0) for h in range(heads)]
     outs = jnp.concatenate([acc[h, :HD, :] / total[h] for h in range(heads)], axis=0).T
     mixed[0] = jnp.where(good, outs, 0.0).astype(bf16)
@@ -133,44 +160,38 @@
     lse[0] = jnp.concatenate(stats + [jnp.zeros((8 - heads, here), f32)], axis=0)
 
 
-def attn_fwd(info, toks, w, cos, sin, seg, docs, heads):
-    slots = len(toks)
-    here, width = toks[0].shape
-    seq = here * slots
+def attn_fwd(info, seg, qh, ka, vt, docs):
+    slots, heads, here = qh.shape[:3]
     cols = heads * HD
 
-    def whole(shape):
-        return pl.BlockSpec(shape, lambda g: (0,) * len(shape))
-
     def part(shape):
-        return pl.BlockSpec((1,) + shape, lambda g: (g,) + (0,) * len(shape))
-
-    shapes = [((heads, here, 256), bf16), ((seq, 256), bf16), ((seq, cols), bf16), ((8, here), f32), ((here, cols), bf16)]
+        return pl.BlockSpec((1,) + shape[1:], lambda g: (g,) + (0,) * (len(shape) - 1))
+
+    shapes = [((slots, 8, here), f32), ((slots, here, cols), bf16)]
     return pl.pallas_call(
-        functools.partial(attn_fwd_kernel, docs=docs, heads=heads, slots=slots),
+        functools.partial(attn_fwd_kernel, docs=docs, heads=heads),
         grid=(slots,),
-        out_shape=tuple(jax.ShapeDtypeStruct((slots,) + s, d) for s, d in shapes),
-        in_specs=[pl.BlockSpec(memory_space=pltpu.SMEM)]
-        + [whole((here, width))] * slots
-        + [pl.BlockSpec((w.shape[0], 1) + w.shape[2:], lambda g: (0, g, 0, 0)), whole(cos.shape), whole(sin.shape), whole(seg.shape)],
+        out_shape=tuple(jax.ShapeDtypeStruct(s, d) for s, d in shapes),
+        in_specs=[pl.BlockSpec(memory_space=pltpu.SMEM), pl.BlockSpec((here, 1), lambda g: (0, 0))] + [part(a.shape) for a in (qh, ka, vt)],
         out_specs=tuple(part(s) for s, _ in shapes),
-        scratch_shapes=[
-            pltpu.VMEM((seq, width), bf16),
-            pltpu.VMEM((80 * heads, seq), bf16),
-            pltpu.VMEM((heads, 80, here), f32),
-            pltpu.VMEM((8, here), f32),
-        ],
-        compiler_params=pltpu.CompilerParams(vmem_limit_bytes=50 << 20),
-        cost_estimate=pl.CostEstimate(flops=20 << 30, bytes_accessed=20 << 20, transcendentals=4 << 20),
+        scratch_shapes=[pltpu.VMEM((heads, 80, here), f32), pltpu.VMEM((8, here), f32)],
+        compiler_params=pltpu.CompilerParams(vmem_limit_bytes=40 << 20),
+        cost_estimate=pl.CostEstimate(flops=12 << 30, bytes_accessed=12 << 20, transcendentals=4 << 20),
         name="attn_fwd",
-    )(info, *toks, w, cos, sin, seg)
-
-
-def attn_bwd_kernel(info, *refs, docs, heads, slots, pieces):
+    )(info, seg, stay(qh), stay(ka), stay(vt))
+
+
+def attn_bwd_kernel(info, *refs, docs, heads, slots, pieces, start, stop):
     toks = refs[:slots]
     w, cos, sin, seg, qh, ka, va, lse, mixed, do = refs[slots : slots + 10]
-    dw, dx_out = refs[slots + 10], refs[slots + 11 : 2 * slots + 11]
-    tokt, dkv, dq, dqt, dwa, doh, delta, dka, dva = refs[2 * slots + 11 :]
+    refs = refs[slots + 10 :]
+    last = stop == slots
+    if start:
+        old_dkv, old_dq, refs = refs[0], refs[1], refs[2:]
+    dw, refs = refs[0], refs[1:]
+    if last:
+        dx_out, refs = refs[:slots], refs[slots:]
+    dkv, dq, tokt, dqt, dwa, doh, delta, dka, dva = refs
     here, width = toks[0].shape
     seq = here * slots
     count = seq // TILE
@@ -248,7 +269,13 @@
         p = jnp.bitwise_xor(me, r)
         dw[r, 0] = dwa[pl.ds(pl.multiple_of(p * share, 8), share), :].astype(bf16)
 
-    @pl.when(g == slots - 1)
+    if not last:
+        return
+
+    def key_grads(group, rows, cut):
+        return old_dkv[group, rows, cut] if group < start else dkv[group - start, rows, cut]
+
+    @pl.when(g == stop - start - 1)
     def _():
         for s in range(slots):
             dx_out[s][...] = jnp.zeros_like(dx_out[s])
@@ -259,41 +286,52 @@
             def _(s=s):
                 rows = slice(s * here, (s + 1) * here)
                 total = sum(
-                    nt(dkv[group, rows, :256], weight(group, 256, 512)) + nt(dkv[group, rows, 256:], weight(group, 512 + cols, 512 + 2 * cols))
+                    nt(key_grads(group, rows, slice(0, 256)), weight(group, 256, 512))
+                    + nt(key_grads(group, rows, slice(256, 256 + cols)), weight(group, 512 + cols, 512 + 2 * cols))
                     for group in range(slots)
                 )
                 if s == 0:
-                    total = total + sum(nt(dq[group], weight(group, 0, 256)) for group in range(slots))
+                    total = total + sum(nt(old_dq[group] if group < start else dq[group - start], weight(group, 0, 256)) for group in range(slots))
                 dx_out[s][...] = total.astype(dx_out[s].dtype)
 
 
-def attn_bwd(info, toks, w, cos, sin, seg, saved, do, docs, heads, pieces):
+def attn_bwd(info, toks, w, cos, sin, seg, saved, do, docs, heads, pieces, start, stop, carry=()):
     slots = len(toks)
     here, width = toks[0].shape
     seq = here * slots
     cols = heads * HD
     span = -(-(512 + cols) // 128) * 128
+    count = stop - start
+    last = stop == slots
 
     def whole(shape):
         return pl.BlockSpec(shape, lambda g: (0,) * len(shape))
 
     def part(array):
-        return pl.BlockSpec((1,) + array.shape[1:], lambda g: (g,) + (0,) * (array.ndim - 1))
-
+        return pl.BlockSpec((1,) + array.shape[1:], lambda g: (g + start,) + (0,) * (array.ndim - 1))
+
+    kept = [((count, seq, 256 + cols), bf16), ((count, here, 256), bf16)]
+    out_shape = [jax.ShapeDtypeStruct((pieces, count, width // pieces, span), bf16)]
+    out_specs = [pl.BlockSpec((pieces, 1, width // pieces, span), lambda g: (0, g, 0, 0))]
+    if last:
+        out_shape += [jax.ShapeDtypeStruct((here, width), f32)] + [jax.ShapeDtypeStruct((here, width), bf16)] * (slots - 1)
+        out_specs += [whole((here, width))] * slots
+    else:
+        out_shape += [jax.ShapeDtypeStruct(s, d) for s, d in kept]
+        out_specs += [whole(s) for s, _ in kept]
     return pl.pallas_call(
-        functools.partial(attn_bwd_kernel, docs=docs, heads=heads, slots=slots, pieces=pieces),
-        grid=(slots,),
-        out_shape=(jax.ShapeDtypeStruct((pieces, slots, width // pieces, span), bf16), jax.ShapeDtypeStruct((here, width), f32))
-        + (jax.ShapeDtypeStruct((here, width), bf16),) * (slots - 1),
+        functools.partial(attn_bwd_kernel, docs=docs, heads=heads, slots=slots, pieces=pieces, start=start, stop=stop),
+        grid=(count,),
+        out_shape=tuple(out_shape),
         in_specs=[pl.BlockSpec(memory_space=pltpu.SMEM)]
         + [whole((here, width))] * slots
         + [whole(w.shape), whole(cos.shape), whole(sin.shape), whole(seg.shape)]
-        + [part(a) for a in (*saved, do)],
-        out_specs=(pl.BlockSpec((pieces, 1, width // pieces, span), lambda g: (0, g, 0, 0)),) + (whole((here, width)),) * slots,
-        scratch_shapes=[
+        + [part(a) for a in (*saved, do)]
+        + [whole(a.shape) for a in carry],
+        out_specs=tuple(out_specs),
+        scratch_shapes=([pltpu.VMEM(s, d) for s, d in kept] if last else [])
+        + [
             pltpu.VMEM((width, seq), bf16),
-            pltpu.VMEM((slots, seq, 256 + cols), bf16),
-            pltpu.VMEM((slots, here, 256), bf16),
             pltpu.VMEM((256, here), f32),
             pltpu.VMEM((width, span), f32),
             pltpu.VMEM((heads, here, cols), bf16),
@@ -302,9 +340,9 @@
             pltpu.VMEM((TILE, cols), f32),
         ],
         compiler_params=pltpu.CompilerParams(vmem_limit_bytes=56 << 20),
-        cost_estimate=pl.CostEstimate(flops=40 << 30, bytes_accessed=24 << 20, transcendentals=4 << 20),
+        cost_estimate=pl.CostEstimate(flops=10 * count << 30, bytes_accessed=6 * count << 20, transcendentals=count << 20),
         name="attn_bwd",
-    )(info, *toks, w, cos, sin, seg, *saved, do)
+    )(info, *toks, w, cos, sin, seg, *saved, do, *carry)
 
 
 def doc_tables(lengths, seq, first, here):
@@ -577,9 +615,6 @@
     def piece(i, me):
         return jnp.bitwise_xor(2 * i + start, me[0])
 
-    def stay(array):
-        return pltpu.with_memory_space_constraint(array, pltpu.HBM)
-
     both = pl.BlockSpec((1, blk, span), lambda i, me: (i, 0, 0))
     in_specs = [pl.BlockSpec((tokens, blk), lambda i, me: (0, piece(i, me)))] * 3
     in_specs += [pl.BlockSpec((width // pieces, tokens), lambda i, me: (piece(i, me), 0))]
@@ -606,48 +641,67 @@
     )(me, *args)
 
 
-def final_ffn_kernel(gate, up, out):
-    out[:, 0, :] = gate[...].astype(f32).T
-    out[:, 1, :] = up[...].astype(f32).T
-
-
-def final_ffn(main, width, lanes):
-    units = main.shape[0]
-    steps = width // lanes
-    return pl.pallas_call(
-        final_ffn_kernel,
-        grid=(steps,),
-        out_shape=jax.ShapeDtypeStruct((width, 2, units), f32),
-        in_specs=[pl.BlockSpec((units, lanes), lambda i: (0, i)), pl.BlockSpec((units, lanes), lambda i: (0, i + steps))],
-        out_specs=pl.BlockSpec((lanes, 2, units), lambda i: (i, 0, 0)),
-        cost_estimate=pl.CostEstimate(flops=1 << 20, bytes_accessed=8 << 20, transcendentals=0),
-        name="final_ffn",
-    )(main, main)
-
-
-def final_qkv_kernel(query, key, value, out, *, heads):
+def final_kernel(gate, up, down, out_part, query, key, value, edge, gate_up_sum, down_sum, out_sum, qkv_sum, small_sum, *, heads, pieces, share, room):
     cols = heads * HD
+    gate_up_sum[:, 0, :] = gate[...].astype(f32).T
+    gate_up_sum[:, 1, :] = up[...].astype(f32).T
+    down_sum[...] = down[...].astype(f32)
+    out_sum[...] = out_part[...].astype(f32).T[:cols]
     for k, source in enumerate((query, key)):
         turned = source[...].astype(f32).T
         for h in range(heads):
             for half in range(2):
                 start = 128 * half + HALF * h
-                out[k, HD * h + HALF * half : HD * h + HALF * (half + 1), :] = turned[start : start + HALF, :]
-    out[2, :, :] = value[...].astype(f32).T[:cols]
-
-
-def final_qkv(main, start, heads, rows):
-    width = main.shape[0]
+                qkv_sum[k, HD * h + HALF * half : HD * h + HALF * (half + 1), :] = turned[start : start + HALF, :]
+    qkv_sum[2, :, :] = value[...].astype(f32).T[:cols]
+
+    @pl.when(pl.program_id(0) == 0)
+    def _():
+        width = small_sum.shape[1]
+        each = 4 * width // pieces // room
+        for n in range(pieces * each):
+            j, lane = divmod(n * room, width)
+            row = n // each * share + n % each
+            base = row // 16 * 16
+            block = edge[base : base + 16, 128 - room :].astype(f32)
+            small_sum[j : j + 1, lane : lane + room] = block[row - base : row - base + 1, :]
+
+
+def final_sums(main, width, span, heads, pieces):
+    units = main.shape[0]
+    lanes = 128
+    steps = width // lanes
     cols = heads * HD
+    room = span - 3 * width - cols
+    tall = units // steps
+
+    def band(first, size):
+        return pl.BlockSpec((tall, size), lambda i, n=first // size: (i, n))
+
+    in_specs = [pl.BlockSpec((units, lanes), lambda i: (0, i)), pl.BlockSpec((units, lanes), lambda i: (0, i + steps))]
+    in_specs += [band(2 * width, width), band(3 * width, 256)] + [band(span + 256 * k, 256) for k in range(3)]
+    in_specs += [pl.BlockSpec((units, lanes), lambda i: (0, span // lanes - 1))]
     return pl.pallas_call(
-        functools.partial(final_qkv_kernel, heads=heads),
-        grid=(width // rows,),
-        out_shape=jax.ShapeDtypeStruct((3, cols, width), f32),
-        in_specs=[pl.BlockSpec((rows, 256), lambda i, k=k: (i, start // 256 + k)) for k in range(3)],
-        out_specs=pl.BlockSpec((3, cols, rows), lambda i: (0, 0, i)),
-        cost_estimate=pl.CostEstimate(flops=1 << 20, bytes_accessed=4 << 20, transcendentals=0),
-        name="final_qkv",
-    )(main, main, main)
+        functools.partial(final_kernel, heads=heads, pieces=pieces, share=units // pieces, room=room),
+        grid=(steps,),
+        out_shape=(
+            jax.ShapeDtypeStruct((width, 2, units), f32),
+            jax.ShapeDtypeStruct((units, width), f32),
+            jax.ShapeDtypeStruct((cols, width), f32),
+            jax.ShapeDtypeStruct((3, cols, width), f32),
+            jax.ShapeDtypeStruct((4, width), f32),
+        ),
+        in_specs=in_specs,
+        out_specs=(
+            pl.BlockSpec((lanes, 2, units), lambda i: (i, 0, 0)),
+            pl.BlockSpec((tall, width), lambda i: (i, 0)),
+            pl.BlockSpec((cols, tall), lambda i: (0, i)),
+            pl.BlockSpec((3, cols, tall), lambda i: (0, 0, i)),
+            pl.BlockSpec((4, width), lambda i: (0, 0)),
+        ),
+        cost_estimate=pl.CostEstimate(flops=1 << 20, bytes_accessed=15 << 20, transcendentals=0),
+        name="final_sums",
+    )(*[main] * 8)
 
 
 ROPE_BASE = 1000.0
@@ -730,13 +784,6 @@
     piece_two = after(piece_two, *ones[1:])
     twos = [shift(piece_two, s) for s in range(1, tp_size)]
     w1 = gather_dp(jnp.stack(ones))
-    w2 = gather_dp(jnp.concatenate(twos, axis=0))
-
-    own_late = after(own, *ones[1:])
-    before, behind = along(own_late, 1), along(own_late, -1)
-    before2, behind2 = along(before, 1), along(behind, -1)
-    toks = [own, behind, jnp.where(z < tp_size // 2, behind2, before2), before]
-
     row_lengths, gate_up_late, down_late = after(lengths[0], ones[-1]), after(w_gate_up, ones[-1]), after(w_down, ones[-1])
     w_own = jnp.concatenate([gate_up_late[:, 0].T, gate_up_late[:, 1].T, down_late], axis=1).reshape(pieces, share, 3 * width)
 
@@ -748,8 +795,22 @@
     cosine, sine = jnp.cos(angles), jnp.sin(angles)
     seg_col = segment[:, None]
 
-    saved = attn_fwd(info, toks, w1, cosine, sine, seg_col, docs, heads)
-    rel = saved[4]
+    twos, cosine, sine, seg_col, info, w_own = lax.optimization_barrier((twos, cosine, sine, seg_col, info, w_own))
+    w2 = gather_dp(jnp.concatenate(twos, axis=0))
+
+    own_late = after(own, *ones[1:])
+    before, behind = along(own_late, 1), along(own_late, -1)
+
+    *held, qh = project(own, w1, cosine, sine, seg_col, docs, heads, 0, tp_size)
+    held, before, behind = lax.optimization_barrier((held, before, behind))
+    before2, behind2 = along(before, 1), along(behind, -1)
+    held = project(behind, w1, cosine, sine, seg_col, docs, heads, 1, tp_size, held)
+    held = project(before, w1, cosine, sine, seg_col, docs, heads, 3, tp_size, held)
+    held, behind2, before2 = lax.optimization_barrier((held, behind2, before2))
+    toks = [own, behind, jnp.where(z < tp_size // 2, behind2, before2), before]
+    held = project(toks[2], w1, cosine, sine, seg_col, docs, heads, 2, tp_size, held)
+    lse, rel = attn_fwd(info, seg_col, qh, held[0], held[2], docs)
+    saved = (qh, held[0].reshape(tp_size, seq, -1), held[1].reshape(tp_size, seq, -1), lse, rel)
     norms = [v.reshape(1, width) for v in (norm1_scale, norm1_shift, norm2_scale, norm2_shift)]
     room = span - 3 * width - cols_here
     layer_out, grad_one, nlow, flow, brt, back, chunk, act, gg, ug = ffn_layer(own, cotangent[0], norms, rel, w1, w_own, w2, room)
@@ -765,37 +826,45 @@
 
     back, far_give, far_rest, near_give = lax.optimization_barrier((back, far_give, far_rest, near_give))
     got = [flip(far_give, 2), flip(far_rest, 4), flip(near_give, 2)]
-    bwd = attn_bwd(info, toks, w1, cosine, sine, seg_col, saved, back, docs, heads, pieces)
-    got, bwd = lax.optimization_barrier((got, bwd))
-    dw, dx = bwd[0], bwd[1:]
+    backward = functools.partial(attn_bwd, info, toks, w1, cosine, sine, seg_col, saved)
+    cut = tp_size - 1
+    dw_low, *carry = backward(back, docs, heads, pieces, 0, cut)
+    got, dw_low, carry, back_late = lax.optimization_barrier((got, dw_low, carry, back))
     next_b = low_sum(near_rest, got[1])
-    got_a, got_b = flip(low_sum(far_keep, got[0]), 4), flip(next_b[1], 2)
-    next_a = low_sum(near_keep, got[2])
-    pairs = dw.reshape((pieces // 2, 2) + dw.shape[1:])
-    got_pairs = flip(pairs[:, 1], 1)
-    from_left = lax.ppermute(dx[2], "tensor", [(i, i + 1) for i in range(half)])
-    from_right = lax.ppermute(dx[2], "tensor", [(i + half, i + half - 1) for i in range(half)])
-    got_a, got_b, got_pairs, from_left, from_right = lax.optimization_barrier((got_a, got_b, got_pairs, from_left, from_right))
+    give_a, next_a = low_sum(far_keep, got[0]), low_sum(near_keep, got[2])
+    back_late, next_a, give_a, next_b = lax.optimization_barrier((back_late, next_a, give_a, next_b))
+    got_a, got_b, got_low = flip(give_a, 4), flip(next_b[1], 2), flip(dw_low.reshape((pieces // 2, 2) + dw_low.shape[1:])[:, 1], 1)
+    dw_high, *dx = backward(back_late, docs, heads, pieces, cut, tp_size, carry)
+    got_a, got_b, got_low, dw_high, dx = lax.optimization_barrier((got_a, got_b, got_low, dw_high, dx))
+    parts_two = jnp.concatenate([low_sum(next_a, got_a), low_sum(next_b[0], got_b)], axis=0)
+    share_two = lax.psum_scatter(parts_two, "tensor", scatter_dimension=0, tiled=True)
+
+    def pairs_of(array):
+        return array.reshape((pieces // 2, 2) + array.shape[1:])
+
+    got_high = flip(pairs_of(dw_high)[:, 1], 1)
+    low = low_sum(pairs_of(dw_low)[:, 0], got_low).reshape((2, 2) + dw_low.shape[1:])
+    got_a = flip(low[:, 1, :half], 2)
+    high = low_sum(pairs_of(dw_high)[:, 0], got_high).reshape((2, 2) + dw_high.shape[1:])
+    high = jnp.concatenate([low[:, :, half:], high], axis=2)
+    got_b = flip(high[1], 4)
+    next_a, next_b = low_sum(low[:, 0, :half], got_a), low_sum(high[0], got_b)
+    got_a, got_b = flip(next_a[1], 4), flip(next_b[1], 2)
 
     def by_slot(low, high):
         low, high = low.reshape(half, -1, low.shape[-1]), high.reshape(tp_size - half, -1, high.shape[-1])
         return [low[i] for i in range(half)] + [high[i] for i in range(tp_size - half)]
 
-    parts_two = jnp.concatenate([low_sum(next_a, got_a), low_sum(next_b[0], got_b)], axis=0)
-    share_two = lax.psum_scatter(parts_two, "tensor", scatter_dimension=0, tiled=True)
-    pairs = low_sum(pairs[:, 0], got_pairs).reshape((2, 2) + dw.shape[1:])
-    got_a, got_b = flip(pairs[:, 1, :half], 2), flip(pairs[1, :, half:], 4)
-    near_right, near_left = low_sum(dx[1], from_left), low_sum(dx[3], from_right)
-    next_a, next_b = low_sum(pairs[:, 0, :half], got_a), low_sum(pairs[0, :, half:], got_b)
-    got_a, got_b = flip(next_a[1], 4), flip(next_b[1], 2)
-
     def total(own_part, moved):
         return functools.reduce(lambda x, y: x + y.astype(f32), moved, own_part.astype(f32)).astype(bf16)
 
     parts_one = by_slot(low_sum(next_a[0], got_a), low_sum(next_b[0], got_b))
     moved_one = [shift(parts_one[s], -s) for s in range(1, tp_size)]
     share_one = total(parts_one[0], moved_one)
-    share_two, share_one, near_right, near_left = lax.optimization_barrier((share_two, share_one, near_right, near_left))
+    share_two, share_one, dx = lax.optimization_barrier((share_two, share_one, dx))
+    from_left = lax.ppermute(dx[2], "tensor", [(i, i + 1) for i in range(half)])
+    from_right = lax.ppermute(dx[2], "tensor", [(i + half, i + half - 1) for i in range(half)])
+    near_right, near_left = low_sum(dx[1], from_left), low_sum(dx[3], from_right)
     input_grad = grad_one + dx[0] + along(near_right, 1).astype(f32) + along(near_left, -1).astype(f32)
 
     def finish(array):
@@ -805,11 +874,8 @@
         return gather_dp(array)
 
     main = finish(jnp.concatenate([share_two, share_one], axis=1)).reshape(units, -1)
-    down_sum = main[:, 2 * width : 3 * width].astype(f32)
-    out_sum = main[:, 3 * width : 3 * width + cols_here].astype(f32).T
-    gate_up_sum = final_ffn(main, width, 128)
-    qkv_sum = final_qkv(main, span, heads, 256).transpose(2, 0, 1)
-    small_out = main.reshape(pieces, share, -1)[:, : 4 * width // pieces // room, span - room : span].astype(f32).reshape(4, width)
+    gate_up_sum, down_sum, out_sum, qkv_turned, small_out = final_sums(main, width, span, heads, pieces)
+    qkv_sum = qkv_turned.transpose(2, 0, 1)
     return (
         layer_out[None],
         input_grad[None],

time: 449 us -> 427 us (0.951)
  waiting for transfers between devices: 147 us -> 117 us
  Pallas kernels: 150 us -> 168 us
  other arithmetic: 31.7 us -> 24.4 us
  starting transfers between devices: 61.8 us -> 55.4 us
    ppermute x1, starting transfers between devices: 17.2 us -> 1.47 us  [body(): from_left = lax.ppermute(dx[2], 'tensor', [(i, i + 1) for i in range(half)])]
    all_gather x3, waiting for transfers between devices: 13.1 us -> 0.02 us  [gather_dp(): return lax.all_gather(array, 'dp', axis=0, axis_index_groups=groups)]
    ppermute x6, waiting for transfers between devices: 32.5 us -> 19.8 us  [along(): return lax.ppermute(array, 'tensor', line_axis(tp_size, step))]
    pallas_call x1 -> x2, Pallas kernels: 52.7 us -> 62.6 us  [attn_bwd(): pl.pallas_call(functools.partial(attn_bwd_kernel, docs=docs, heads=heads,...]
    pallas_call x3 -> x6, Pallas kernels: 43.8 us -> 52.7 us  [the longest x4 25.6 us: project(): pl.pallas_call(functools.partial(project_kernel, docs=docs, heads=heads,...]
    unnamed x64 -> x71, local copies, waits for them, and re-layouts: 10.5 us -> 18.9 us
    ppermute x12 -> x13, waiting for transfers between devices: 21.7 us -> 28.4 us  [flip(): return lax.ppermute(array, 'dp', flip_axis(dp_size, bit))]
    ppermute x9, waiting for transfers between devices: 60 us -> 53.3 us  [shift(): return lax.ppermute(array, 'tensor', rotate_axis(tp_size, step))]
  transfers between devices with their start and end apart: 33 -> 34, of which waited for: 17 -> 15; matrix products, arithmetic and copies ran while one was open for 8% -> 7% of each run, Pallas kernels for 22% -> 28%
where the time goes in v4:
time: 427 us; the launch traced here: 419 us
  Pallas kernels  168 us (39%)
  waiting for transfers between devices  117 us (27%)
  starting transfers between devices  55.4 us (13%)
  local copies, waits for them, and re-layouts  39 us (9%)
  other arithmetic  24.4 us (6%)
  between operations  14.8 us (3%)
    pallas_call x2, Pallas kernels, attn_bwd(): pl.pallas_call(functools.partial(attn_bwd_kernel, docs=docs, heads=heads,...  62.6 us
    ppermute x9, waiting for transfers between devices, shift(): return lax.ppermute(array, 'tensor', rotate_axis(tp_size, step))  53.3 us
    pallas_call x1, Pallas kernels, ffn_layer(): pl.pallas_call(functools.partial(ffn_kernel, slots=slots, pieces=pieces,...  33 us
    ppermute x13, waiting for transfers between devices, flip(): return lax.ppermute(array, 'dp', flip_axis(dp_size, bit))  28.4 us
    pallas_call x4, Pallas kernels, project(): pl.pallas_call(functools.partial(project_kernel, docs=docs, heads=heads,...  25.6 us
    ppermute x9, starting transfers between devices, shift(): return lax.ppermute(array, 'tensor', rotate_axis(tp_size, step))  21.2 us
    ppermute x6, starting transfers between devices, along(): return lax.ppermute(array, 'tensor', line_axis(tp_size, step))  20.9 us
    pallas_call x4, Pallas kernels, wgrad(): pl.pallas_call(functools.partial(wgrad_kernel, slots=slots, share=share,...  20.2 us
  transfers between devices with their start and end apart: 34, of which 15 were waited for; matrix products, arithmetic and copies ran while one was open for 7% of the time, Pallas kernels for 28%

profile of v4, /device:TPU:0, one launch (start us, length us, event | category | flops | bytes accessed | tf_op | source)
XLA Modules:
  0.0 419.0 jit_solution(14725138810770066993)
XLA Ops:
  10.8 2.9 constant_dynamic-slice_fusion.2
  14.5 5.1 %collective-permute-start.2 = (bf16[96,896]{1,0:T(8,128)(2,1)S(1)}, bf16[96,896]{1,0:T(8,128)(2,1)S(1)}, u32[]{:S(2)}, u32[]{:S(2)}) collective-permute-start(bf16[96,896]{1,0:T(8,128)(2,1)S(1)} %pad_maximum_fusion.7), channel_id=1, source_target_pairs={{0,3},{1,0},{2,1},{3,2},{4,7},{5,4},{6,5},{7,6},{8,11},{9,8},{10,9... | collective-permute-start | bytes 516104 | tf_op jit(solution)/shard_map/ppermute | solution.py:764
  20.6 3.8 collective-permute-done.2
  24.4 9.8 %collective-permute-done.1 = bf16[96,896]{1,0:T(8,128)(2,1)S(1)} collective-permute-done((bf16[96,896]{1,0:T(8,128)(2,1)S(1)}, bf16[96,896]{1,0:T(8,128)(2,1)S(1)}, u32[]{:S(2)}, u32[]{:S(2)}) %collective-permute-start.1) | collective-permute-done | bytes 172064 | tf_op jit(solution)/shard_map/ppermute | solution.py:764
  37.0 2.0 collective-permute-start.4
  39.0 1.9 collective-permute-start.3
  40.9 5.7 %copy.117 = bf16[768,2,768]{0,2,1:T(8,128)(2,1)S(1)} copy(bf16[768,2,768]{2,1,0:T(2,128)(2,1)} %param.17) | data formatting | bytes 4718592 | tf_op jit(solution)/shard_map/optimization_barrier | solution.py:723
  47.6 1.3 fusion.17
  48.9 1.4 concatenate.26.info
  50.7 3.7 multiply_sine_fusion
  54.4 2.1 pad_maximum_fusion
  56.5 20.5 %collective-permute-done.4 = bf16[96,2304]{1,0:T(8,128)(2,1)} collective-permute-done((bf16[96,2304]{1,0:T(8,128)(2,1)S(1)}, bf16[96,2304]{1,0:T(8,128)(2,1)}, u32[]{:S(2)}, u32[]{:S(2)}) %collective-permute-start.4) | collective-permute-done | bytes 442400 | tf_op jit(solution)/shard_map/ppermute | solution.py:764
  77.0 2.3 pad_maximum_fusion.2
  79.4 1.3 collective-permute-start.7
  80.7 5.4 %collective-permute-start.6 = (bf16[512,768]{1,0:T(8,128)(2,1)}, bf16[512,768]{1,0:T(8,128)(2,1)}, u32[]{:S(2)}, u32[]{:S(2)}) collective-permute-start(bf16[512,768]{1,0:T(8,128)(2,1)} %bitcast.refs_0_), channel_id=1, source_target_pairs={{0,1},{1,2},{2,3},{4,5},{5,6},{6,7},{8,9},{9,10},{10,11},{12,13},{... | collective-permute-start | bytes 2359304 | tf_op jit(solution)/shard_map/ppermute | solution.py:767
  86.5 3.5 copy-done.2
  90.0 7.3 %project.4 = (bf16[4,4,512,256]{3,2,1,0:T(8,128)(2,1)}, bf16[4,4,512,192]{3,2,1,0:T(8,128)(2,1)}, bf16[4,4,240,512]{3,2,1,0:T(8,128)(2,1)}, bf16[4,3,512,256]{3,2,1,0:T(8,128)(2,1)}) custom-call(bf16[512,768]{1,0:T(8,128)(2,1)} %bitcast.refs_0_, bf16[8,4,96,896]{3,2,1,0:T(8,128)(2,1)S(1)} %bitcast.130, f32[2048,128]{1,0:T(8,128)S(1)} %get-tuple-element.119.refs_2_.refs_5_, ...), custom_call_target="tpu_custom_call" | custom-call | flops 2147483648 | bytes 8388608 | tf_op jit(solution)/shard_map/project/pallas_call | solution.py:112
  97.3 2.3 collective-permute-done.7.refs_0_.refs_1_
  99.6 1.2 collective-permute-done.6.refs_0_.refs_3_
  100.8 5.3 %collective-permute-start.9 = (bf16[512,768]{1,0:T(8,128)(2,1)}, bf16[512,768]{1,0:T(8,128)(2,1)}, u32[]{:S(2)}, u32[]{:S(2)}) collective-permute-start(bf16[512,768]{1,0:T(8,128)(2,1)} %collective-permute-done.6.refs_0_.refs_3_), channel_id=1, source_target_pairs={{0,1},{1,2},{2,3},{4,5},{5,6},{6,7},{8,9},{9,10},{10,11},{12,13},{... | collective-permute-start | bytes 2359304 | tf_op jit(solution)/shard_map/ppermute | solution.py:767
  106.1 1.7 collective-permute-start.8
  110.2 3.9 copy-done.3
  114.1 6.4 %project.5 = (bf16[4,4,512,256]{3,2,1,0:T(8,128)(2,1)}, bf16[4,4,512,192]{3,2,1,0:T(8,128)(2,1)}, bf16[4,4,240,512]{3,2,1,0:T(8,128)(2,1)}) custom-call(bf16[512,768]{1,0:T(8,128)(2,1)} %collective-permute-done.7.refs_0_.refs_1_, bf16[8,4,96,896]{3,2,1,0:T(8,128)(2,1)S(1)} %bitcast.131, ...), custom_call_target="tpu_custom_call", output_to_operand_aliasing={{0}: (5, {}), {1}: (6, {}), {2}: (7, {})} | custom-call | flops 2147483648 | bytes 8388608 | tf_op jit(solution)/shard_map/project/pallas_call | solution.py:112
  120.5 6.5 %project.6 = (bf16[4,4,512,256]{3,2,1,0:T(8,128)(2,1)}, bf16[4,4,512,192]{3,2,1,0:T(8,128)(2,1)}, bf16[4,4,240,512]{3,2,1,0:T(8,128)(2,1)}) custom-call(bf16[512,768]{1,0:T(8,128)(2,1)} %collective-permute-done.6.refs_0_.refs_3_, bf16[8,4,96,896]{3,2,1,0:T(8,128)(2,1)S(1)} %bitcast.132, ...), custom_call_target="tpu_custom_call", output_to_operand_aliasing={{0}: (5, {}), {1}: (6, {}), {2}: (7, {})} | custom-call | flops 2147483648 | bytes 8388608 | tf_op jit(solution)/shard_map/project/pallas_call | solution.py:112
  127.0 1.2 broadcast_select_fusion.refs_0_.refs_2_
  128.3 5.4 %project.7 = (bf16[4,4,512,256]{3,2,1,0:T(8,128)(2,1)}, bf16[4,4,512,192]{3,2,1,0:T(8,128)(2,1)}, bf16[4,4,240,512]{3,2,1,0:T(8,128)(2,1)}) custom-call(bf16[512,768]{1,0:T(8,128)(2,1)S(1)} %broadcast_select_fusion.refs_0_.refs_2_, bf16[8,4,96,896]{3,2,1,0:T(8,128)(2,1)S(1)} %bitcast.133, ...), custom_call_target="tpu_custom_call", output_to_operand_aliasing={{0}: (5, {}), {1}: (6, {}), {2}: (7, {})} | custom-call | flops 2147483648 | bytes 8388608 | tf_op jit(solution)/shard_map/project/pallas_call | solution.py:112
  133.7 18.7 %attn_fwd.1 = (f32[4,8,512]{2,1,0:T(8,128)S(1)}, bf16[4,512,192]{2,1,0:T(8,128)(2,1)S(1)}) custom-call(s32[8]{0:T(128)S(1)} %concatenate.26.info, s32[2048,1]{1,0:T(8,128)S(1)} %copy.123.refs_4_.seg.refs_7_, bf16[4,3,512,256]{3,2,1,0:T(8,128)(2,1)} %get-tuple-element.121.qh.refs_8_, bf16[4,4,512,256]{3,2,1,0:T(8,128)(2,1)} %get-tuple-element.142.ka, ...), custom_call_target="tpu_custom_call" | custom-call | flops 12884901888 | bytes 12582912 | tf_op jit(solution)/shard_map/attn_fwd/pallas_call | solution.py:171
  154.1 33.0 %ffn_layer.1 = (bf16[512,768]{1,0:T(8,128)(2,1)}, f32[512,768]{1,0:T(8,128)}, bf16[512,768]{1,0:T(8,128)(2,1)}, bf16[512,768]{1,0:T(8,128)(2,1)}, bf16[768,512]{...) custom-call(bf16[512,768]{1,0:T(8,128)(2,1)} %bitcast.refs_0_, ...), custom_call_target="tpu_custom_call" | custom-call | flops 17179869184 | bytes 31457280 | tf_op jit(solution)/shard_map/ffn_layer/pallas_call | solution.py:542
  188.3 1.1 copy-done.10
  189.4 1.1 copy-done.11
  191.4 4.5 %wgrad.4 = bf16[2,384,2560]{2,1,0:T(8,128)(2,1)S(1)} custom-call(s32[2]{0:T(128)S(1)} %get-tuple-element.163.refs_0_, bf16[512,3072]{1,0:T(8,128)(2,1)} %get-tuple-element.152.refs_1_, bf16[512,3072]{1,0:T(8,128)(2,1)} %get-tuple-element.153.refs_2_, bf16[512,3072]{1,0:T(8,128)(2,1)} %get-tuple-element.154.refs_3_, bf16[768,512]{1,0:T(8,128)(2,1)S(1)} %copy-done.11, ...), custom_call_target="tpu_custom_call" | custom-call | flops 2147483648 | bytes 10485760 | tf_op jit(solution)/shard_map/wgrad/pallas_call | solution.py:634
  196.0 4.5 %wgrad.5 = bf16[2,384,2560]{2,1,0:T(8,128)(2,1)S(1)} custom-call(s32[2]{0:T(128)S(1)} %get-tuple-element.163.refs_0_, bf16[512,3072]{1,0:T(8,128)(2,1)} %get-tuple-element.152.refs_1_, bf16[512,3072]{1,0:T(8,128)(2,1)} %get-tuple-element.153.refs_2_, bf16[512,3072]{1,0:T(8,128)(2,1)} %get-tuple-element.154.refs_3_, bf16[768,512]{1,0:T(8,128)(2,1)S(1)} %copy-done.11, ...), custom_call_target="tpu_custom_call" | custom-call | flops 2147483648 | bytes 10485760 | tf_op jit(solution)/shard_map/wgrad/pallas_call | solution.py:634
  201.0 1.7 collective-permute-done.10.refs_9_
  202.7 5.7 %wgrad.6 = (bf16[192,2560]{1,0:T(8,128)(2,1)S(1)}, bf16[192,2560]{1,0:T(8,128)(2,1)S(1)}, bf16[2,192,2560]{2,1,0:T(8,128)(2,1)}) custom-call(s32[2]{0:T(128)S(1)} %get-tuple-element.163.refs_0_, bf16[512,3072]{1,0:T(8,128)(2,1)} %get-tuple-element.152.refs_1_, bf16[512,3072]{1,0:T(8,128)(2,1)} %get-tuple-element.153.refs_2_, ...), custom_call_target="tpu_custom_call" | custom-call | flops 2147483648 | bytes 10485760 | tf_op jit(solution)/shard_map/wgrad/pallas_call | solution.py:634
  208.5 5.5 %wgrad.7 = (bf16[192,2560]{1,0:T(8,128)(2,1)S(1)}, bf16[192,2560]{1,0:T(8,128)(2,1)}, bf16[2,192,2560]{2,1,0:T(8,128)(2,1)S(1)}) custom-call(s32[2]{0:T(128)S(1)} %get-tuple-element.163.refs_0_, bf16[512,3072]{1,0:T(8,128)(2,1)} %get-tuple-element.152.refs_1_, bf16[512,3072]{1,0:T(8,128)(2,1)} %get-tuple-element.153.refs_2_, ...), custom_call_target="tpu_custom_call" | custom-call | flops 2147483648 | bytes 10485760 | tf_op jit(solution)/shard_map/wgrad/pallas_call | solution.py:634
  213.9 1.8 collective-permute-start.12
  216.0 1.4 collective-permute-start.13
  217.4 36.4 %attn_bwd.2 = (bf16[8,3,96,768]{3,2,1,0:T(8,128)(2,1)}, bf16[3,2048,448]{2,1,0:T(8,128)(2,1)}, bf16[3,512,256]{2,1,0:T(8,128)(2,1)}) custom-call(s32[8]{0:T(128)} %copy-done.14, bf16[512,768]{1,0:T(8,128)(2,1)} %bitcast.refs_0_, bf16[512,768]{1,0:T(8,128)(2,1)} %collective-permute-done.7.refs_0_.refs_1_, bf16[512,768]{1,0:T(8,128)(2,1)} %copy-done.12, ...), custom_call_target="tpu_custom_call" | custom-call | flops 32212254720 | bytes 18874368 | tf_op jit(solution)/shard_map/attn_bwd/pallas_call | solution.py:322
  253.8 5.0 %collective-permute-done.14 = bf16[192,2560]{1,0:T(8,128)(2,1)S(1)} collective-permute-done((bf16[192,2560]{1,0:T(8,128)(2,1)}, bf16[192,2560]{1,0:T(8,128)(2,1)S(1)}, u32[]{:S(2)}, u32[]{:S(2)}) %collective-permute-start.14) | collective-permute-done | bytes 983072 | tf_op jit(solution)/shard_map/ppermute | solution.py:761
  258.8 1.8 collective-permute-done.13
  260.6 1.6 slice_bitcast_fusion.1
  262.3 2.1 add_convert_fusion
  266.9 1.7 collective-permute-start.16
  268.9 26.2 %attn_bwd.3 = (bf16[8,1,96,768]{3,2,1,0:T(8,128)(2,1)}, f32[512,768]{1,0:T(8,128)}, bf16[512,768]{1,0:T(8,128)(2,1)}, bf16[512,768]{1,0:T(8,128)(2,1)}, bf16[512,768]{1,0:T(8,128)(2,1)}) custom-call(s32[8]{0:T(128)} %copy-done.14, bf16[512,768]{1,0:T(8,128)(2,1)} %bitcast.refs_0_, bf16[512,768]{1,0:T(8,128)(2,1)} %collective-permute-done.7.refs_0_.refs_1_, ...), custom_call_target="tpu_custom_call" | custom-call | flops 10737418240 | bytes 6291456 | tf_op jit(solution)/shard_map/attn_bwd/pallas_call | solution.py:322
  297.4 1.4 pad_maximum_fusion.1
  300.2 2.5 fusion
  302.8 1.8 collective-permute-start.18
  305.1 13.4 %collective-permute-done.18 = bf16[2,2,96,768]{3,2,1,0:T(8,128)(2,1)S(1)} collective-permute-done((bf16[2,2,96,768]{3,2,1,0:T(8,128)(2,1)S(1)}, bf16[2,2,96,768]{3,2,1,0:T(8,128)(2,1)S(1)}, u32[]{:S(2)}, u32[]{:S(2)}) %collective-permute-start.18) | collective-permute-done | bytes 589856 | tf_op jit(solution)/shard_map/ppermute | solution.py:761
  318.7 1.8 collective-permute-start.19
  321.1 6.5 %collective-permute-done.19 = bf16[2,96,768]{2,1,0:T(8,128)(2,1)S(1)} collective-permute-done((bf16[2,96,768]{2,1,0:T(8,128)(2,1)S(1)}, bf16[2,96,768]{2,1,0:T(8,128)(2,1)S(1)}, u32[]{:S(2)}, u32[]{:S(2)}) %collective-permute-start.19) | collective-permute-done | bytes 294944 | tf_op jit(solution)/shard_map/ppermute | solution.py:761
  327.6 4.3 %collective-permute-start.20 = (bf16[96,768]{1,0:T(8,128)(2,1)S(1)}, bf16[96,768]{1,0:T(8,128)(2,1)S(1)}, u32[]{:S(2)}, u32[]{:S(2)}) collective-permute-start(bf16[96,768]{1,0:T(8,128)(2,1)S(1)} %slice_bitcast_fusion.15), channel_id=1, source_target_pairs={{0,3},{1,0},{2,1},{3,2},{4,7},{5,4},{6,5},{7,6},{8,11},{9,8},{10,9... | collective-permute-start | bytes 442376 | tf_op jit(solution)/shard_map/ppermute | solution.py:764
  332.1 5.4 %collective-permute-start.24 = (bf16[96,768]{1,0:T(8,128)(2,1)S(1)}, bf16[96,768]{1,0:T(8,128)(2,1)S(1)}, u32[]{:S(2)}, u32[]{:S(2)}) collective-permute-start(bf16[96,768]{1,0:T(8,128)(2,1)S(1)} %get-tuple-element.227), channel_id=1, source_target_pairs={{0,2},{1,3},{2,0},{3,1},{4,6},{5,7},{6,4},{7,5},{8,10},{9,11},{10,... | collective-permute-start | bytes 442376 | tf_op jit(solution)/shard_map/ppermute | solution.py:764
  338.0 7.0 %collective-permute-done.20 = bf16[96,768]{1,0:T(8,128)(2,1)S(1)} collective-permute-done((bf16[96,768]{1,0:T(8,128)(2,1)S(1)}, bf16[96,768]{1,0:T(8,128)(2,1)S(1)}, u32[]{:S(2)}, u32[]{:S(2)}) %collective-permute-start.20) | collective-permute-done | bytes 147488 | tf_op jit(solution)/shard_map/ppermute | solution.py:764
  345.0 12.2 %collective-permute-done.24 = bf16[96,768]{1,0:T(8,128)(2,1)S(1)} collective-permute-done((bf16[96,768]{1,0:T(8,128)(2,1)S(1)}, bf16[96,768]{1,0:T(8,128)(2,1)S(1)}, u32[]{:S(2)}, u32[]{:S(2)}) %collective-permute-start.24) | collective-permute-done | bytes 147488 | tf_op jit(solution)/shard_map/ppermute | solution.py:764
  357.3 2.0 pad_maximum_fusion.4
  360.2 1.5 collective-permute-start.26
  361.9 1.3 collective-permute-start.29
  363.2 15.3 %collective-permute-done.26 = bf16[512,768]{1,0:T(8,128)(2,1)S(1)} collective-permute-done((bf16[512,768]{1,0:T(8,128)(2,1)S(1)}, bf16[512,768]{1,0:T(8,128)(2,1)S(1)}, u32[]{:S(2)}, u32[]{:S(2)}) %collective-permute-start.26) | collective-permute-done | bytes 786464 | tf_op jit(solution)/shard_map/ppermute | solution.py:865
  378.7 5.9 %collective-permute-start.27 = (bf16[512,768]{1,0:T(8,128)(2,1)S(1)}, bf16[512,768]{1,0:T(8,128)(2,1)S(1)}, u32[]{:S(2)}, u32[]{:S(2)}) collective-permute-start(bf16[512,768]{1,0:T(8,128)(2,1)S(1)} %add_convert_fusion.5), channel_id=1, source_target_pairs={{0,1},{1,2},{2,3},{4,5},{5,6},{6,7},{8,9},{9,10},{10,11},{12,13},{... | collective-permute-start | bytes 2359304 | tf_op jit(solution)/shard_map/ppermute | solution.py:767
  384.6 14.9 %collective-permute-done.29 = bf16[512,768]{1,0:T(8,128)(2,1)S(1)} collective-permute-done((bf16[512,768]{1,0:T(8,128)(2,1)S(1)}, bf16[512,768]{1,0:T(8,128)(2,1)S(1)}, u32[]{:S(2)}, u32[]{:S(2)}) %collective-permute-start.29) | collective-permute-done | bytes 786464 | tf_op jit(solution)/shard_map/ppermute | solution.py:767
  399.5 1.4 collective-permute-done.27
  400.9 1.4 add_bitcast_fusion
  402.3 8.4 %final_sums.1 = (f32[768,2,768]{2,1,0:T(2,128)}, f32[768,768]{1,0:T(8,128)}, f32[192,768]{1,0:T(8,128)}, f32[3,192,768]{2,1,0:T(8,128)}, f32[4,768]{1,0:T(4,128)}) custom-call(bf16[768,3328]{1,0:T(8,128)(2,1)} %all-gather.11.cloned.1.call-done.gate.up.down.out_part.query.key.value.edge, ...), custom_call_target="tpu_custom_call" | custom-call | flops 1048576 | bytes 15728640 | tf_op jit(solution)/shard_map/final_sums/pallas_call | solution.py:684
  410.7 1.5 slice_reduce_fusion
  (161 shorter events, 26.6 us)
Async XLA Ops:
  7.2 79.3 %all-gather.7.cloned.1.call-start = ((), (), s32[]{:S(2)}) async-start(), calls=%async_computation.2 | async-start | bytes 6193152 | tf_op jit(solution)/shard_map/all_gather | solution.py:770
  14.0 21.2 %copy-start.32 = (s32[1,24]{1,0:T(1,128)S(1)}, s32[1,24]{1,0:T(1,128)}, u32[]{:S(2)}) copy-start(s32[1,24]{1,0:T(1,128)} %param.12) | copy-start | bytes 292
  14.5 9.9 %collective-permute-start.2 = (bf16[96,896]{1,0:T(8,128)(2,1)S(1)}, bf16[96,896]{1,0:T(8,128)(2,1)S(1)}, u32[]{:S(2)}, u32[]{:S(2)}) collective-permute-start(bf16[96,896]{1,0:T(8,128)(2,1)S(1)} %pad_maximum_fusion.7), channel_id=1, source_target_pairs={{0,3},{1,0},{2,1},{3,2},{4,7},{5,4},{6,5},{7,6},{8,11},{9,8},{10,9... | collective-permute-start | bytes 516104 | tf_op jit(solution)/shard_map/ppermute | solution.py:764
  19.6 14.6 %collective-permute-start.1 = (bf16[96,896]{1,0:T(8,128)(2,1)S(1)}, bf16[96,896]{1,0:T(8,128)(2,1)S(1)}, u32[]{:S(2)}, u32[]{:S(2)}) collective-permute-start(bf16[96,896]{1,0:T(8,128)(2,1)S(1)} %pad_maximum_fusion.7), channel_id=1, source_target_pairs={{0,2},{1,3},{2,0},{3,1},{4,6},{5,7},{6,4},{7,5},{8,10},{9,11},{10,... | collective-permute-start | bytes 516104 | tf_op jit(solution)/shard_map/ppermute | solution.py:764
  19.6 14.6 %collective-permute-start = (bf16[96,896]{1,0:T(8,128)(2,1)S(1)}, bf16[96,896]{1,0:T(8,128)(2,1)S(1)}, u32[]{:S(2)}, u32[]{:S(2)}) collective-permute-start(bf16[96,896]{1,0:T(8,128)(2,1)S(1)} %pad_maximum_fusion.7), channel_id=1, source_target_pairs={{0,1},{1,2},{2,3},{3,0},{4,5},{5,6},{6,7},{7,4},{8,9},{9,10},{10,1... | collective-permute-start | bytes 516104 | tf_op jit(solution)/shard_map/ppermute | solution.py:764
  35.1 118.9 %all-gather.9.cloned.1.call-start = ((), (), s32[]{:S(2)}) async-start(), calls=%async_computation.3 | async-start | bytes 11943936 | tf_op jit(solution)/shard_map/all_gather | solution.py:770
  36.0 20.5 %collective-permute-start.5 = (bf16[96,2304]{1,0:T(8,128)(2,1)S(1)}, bf16[96,2304]{1,0:T(8,128)(2,1)S(1)}, u32[]{:S(2)}, u32[]{:S(2)}) collective-permute-start(bf16[96,2304]{1,0:T(8,128)(2,1)S(1)} %pad_maximum_fusion.6), channel_id=1, source_target_pairs={{0,3},{1,0},{2,1},{3,2},{4,7},{5,4},{6,5},{7,6},{8,11},{9,8},{10,9... | collective-permute-start | bytes 1327112 | tf_op jit(solution)/shard_map/ppermute | solution.py:764
  37.0 40.0 %collective-permute-start.4 = (bf16[96,2304]{1,0:T(8,128)(2,1)S(1)}, bf16[96,2304]{1,0:T(8,128)(2,1)}, u32[]{:S(2)}, u32[]{:S(2)}) collective-permute-start(bf16[96,2304]{1,0:T(8,128)(2,1)S(1)} %pad_maximum_fusion.6), channel_id=1, source_target_pairs={{0,2},{1,3},{2,0},{3,1},{4,6},{5,7},{6,4},{7,5},{8,10},{9,11},{10,... | collective-permute-start | bytes 1327112 | tf_op jit(solution)/shard_map/ppermute | solution.py:764
  39.0 38.0 %collective-permute-start.3 = (bf16[96,2304]{1,0:T(8,128)(2,1)S(1)}, bf16[96,2304]{1,0:T(8,128)(2,1)}, u32[]{:S(2)}, u32[]{:S(2)}) collective-permute-start(bf16[96,2304]{1,0:T(8,128)(2,1)S(1)} %pad_maximum_fusion.6), channel_id=1, source_target_pairs={{0,1},{1,2},{2,3},{3,0},{4,5},{5,6},{6,7},{7,4},{8,9},{9,10},{10,1... | collective-permute-start | bytes 1327112 | tf_op jit(solution)/shard_map/ppermute | solution.py:764
  50.2 83.5 %copy-start.14 = (s32[8]{0:T(128)}, s32[8]{0:T(128)S(1)}, u32[]{:S(2)}) copy-start(s32[8]{0:T(128)S(1)} %concatenate.26.info) | copy-start | bytes 100
  50.7 3.7 copy-start.18
  54.4 73.9 %copy-start.4 = (f32[2048,128]{1,0:T(8,128)}, f32[2048,128]{1,0:T(8,128)S(1)}, u32[]{:S(2)}) copy-start(f32[2048,128]{1,0:T(8,128)S(1)} %get-tuple-element.120.refs_3_.refs_6_) | copy-start | bytes 3145732
  54.4 73.9 %copy-start.5 = (f32[2048,128]{1,0:T(8,128)}, f32[2048,128]{1,0:T(8,128)S(1)}, u32[]{:S(2)}) copy-start(f32[2048,128]{1,0:T(8,128)S(1)} %get-tuple-element.119.refs_2_.refs_5_) | copy-start | bytes 3145732
  79.3 278.0 %reduce-scatter.2.cloned.1.call-start = ((), (), s32[]{:S(2)}) async-start(), calls=%async_computation.1 | async-start | bytes 2457600 | tf_op jit(solution)/shard_map/reduce_scatter | solution.py:840
  79.4 20.3 %collective-permute-start.7 = (bf16[512,768]{1,0:T(8,128)(2,1)}, bf16[512,768]{1,0:T(8,128)(2,1)}, u32[]{:S(2)}, u32[]{:S(2)}) collective-permute-start(bf16[512,768]{1,0:T(8,128)(2,1)} %bitcast.refs_0_), channel_id=1, source_target_pairs={{1,0},{2,1},{3,2},{5,4},{6,5},{7,6},{9,8},{10,9},{11,10},{13,12},{... | collective-permute-start | bytes 2359304 | tf_op jit(solution)/shard_map/ppermute | solution.py:767
  80.7 20.1 %collective-permute-start.6 = (bf16[512,768]{1,0:T(8,128)(2,1)}, bf16[512,768]{1,0:T(8,128)(2,1)}, u32[]{:S(2)}, u32[]{:S(2)}) collective-permute-start(bf16[512,768]{1,0:T(8,128)(2,1)} %bitcast.refs_0_), channel_id=1, source_target_pairs={{0,1},{1,2},{2,3},{4,5},{5,6},{6,7},{8,9},{9,10},{10,11},{12,13},{... | collective-permute-start | bytes 2359304 | tf_op jit(solution)/shard_map/ppermute | solution.py:767
  86.5 47.3 %copy-start.6 = (s32[2048,1]{1,0:T(8,128)}, s32[2048,1]{1,0:T(8,128)S(1)}, u32[]{:S(2)}) copy-start(s32[2048,1]{1,0:T(8,128)S(1)} %copy.123.refs_4_.seg.refs_7_) | copy-start | bytes 24580
  86.5 3.5 copy-start.2
  90.0 17.8 %copy-start.28 = (f32[768]{0:T(1024)S(1)}, f32[768]{0:T(1024)}, u32[]{:S(2)}) copy-start(f32[768]{0:T(1024)} %param.15) | copy-start | bytes 9220
  90.0 18.4 %copy-start.29 = (f32[768]{0:T(1024)S(1)}, f32[768]{0:T(1024)}, u32[]{:S(2)}) copy-start(f32[768]{0:T(1024)} %param.16) | copy-start | bytes 9220
  90.0 19.0 %copy-start.30 = (f32[768]{0:T(1024)S(1)}, f32[768]{0:T(1024)}, u32[]{:S(2)}) copy-start(f32[768]{0:T(1024)} %param.19) | copy-start | bytes 9220
  90.0 19.6 %copy-start.31 = (f32[768]{0:T(1024)S(1)}, f32[768]{0:T(1024)}, u32[]{:S(2)}) copy-start(f32[768]{0:T(1024)} %param.20) | copy-start | bytes 9220
  100.8 26.2 %collective-permute-start.9 = (bf16[512,768]{1,0:T(8,128)(2,1)}, bf16[512,768]{1,0:T(8,128)(2,1)}, u32[]{:S(2)}, u32[]{:S(2)}) collective-permute-start(bf16[512,768]{1,0:T(8,128)(2,1)} %collective-permute-done.6.refs_0_.refs_3_), channel_id=1, source_target_pairs={{0,1},{1,2},{2,3},{4,5},{5,6},{6,7},{8,9},{9,10},{10,11},{12,13},{... | collective-permute-start | bytes 2359304 | tf_op jit(solution)/shard_map/ppermute | solution.py:767
  106.1 20.9 %collective-permute-start.8 = (bf16[512,768]{1,0:T(8,128)(2,1)}, bf16[512,768]{1,0:T(8,128)(2,1)}, u32[]{:S(2)}, u32[]{:S(2)}) collective-permute-start(bf16[512,768]{1,0:T(8,128)(2,1)} %collective-permute-done.7.refs_0_.refs_1_), channel_id=1, source_target_pairs={{1,0},{2,1},{3,2},{5,4},{6,5},{7,6},{9,8},{10,9},{11,10},{13,12},{... | collective-permute-start | bytes 2359304 | tf_op jit(solution)/shard_map/ppermute | solution.py:767
  110.2 3.9 copy-start.3
  128.3 5.4 %copy-start.12 = (bf16[512,768]{1,0:T(8,128)(2,1)}, bf16[512,768]{1,0:T(8,128)(2,1)S(1)}, u32[]{:S(2)}) copy-start(bf16[512,768]{1,0:T(8,128)(2,1)S(1)} %broadcast_select_fusion.refs_0_.refs_2_) | copy-start | bytes 2359300
  152.4 1.1 copy-start.7
  154.1 33.0 %copy-start.8 = (bf16[4,512,192]{2,1,0:T(8,128)(2,1)S(1)}, bf16[4,512,192]{2,1,0:T(8,128)(2,1)}, u32[]{:S(2)}) copy-start(bf16[4,512,192]{2,1,0:T(8,128)(2,1)} %copy-done.7) | copy-start | bytes 2359300
  187.1 1.1 copy-start.9
  188.3 1.1 copy-start.10
  189.4 1.1 copy-start.11
  195.9 6.8 %collective-permute-start.10 = (bf16[2,384,2560]{2,1,0:T(8,128)(2,1)S(1)}, bf16[2,384,2560]{2,1,0:T(8,128)(2,1)S(1)}, u32[]{:S(2)}, u32[]{:S(2)}) collective-permute-start(bf16[2,384,2560]{2,1,0:T(8,128)(2,1)S(1)} %wgrad.4), channel_id=1, source_target_pairs={{0,4},{4,0},{8,12},{12,8},{16,20},{20,16},{24,28},{28,24},{1,5},{5... | collective-permute-start | bytes 11796488 | tf_op jit(solution)/shard_map/ppermute | solution.py:761
  200.4 8.0 %collective-permute-start.11 = (bf16[2,384,2560]{2,1,0:T(8,128)(2,1)S(1)}, bf16[2,384,2560]{2,1,0:T(8,128)(2,1)S(1)}, u32[]{:S(2)}, u32[]{:S(2)}) collective-permute-start(bf16[2,384,2560]{2,1,0:T(8,128)(2,1)S(1)} %wgrad.5), channel_id=1, source_target_pairs={{0,4},{4,0},{8,12},{12,8},{16,20},{20,16},{24,28},{28,24},{1,5},{5... | collective-permute-start | bytes 11796488 | tf_op jit(solution)/shard_map/ppermute | solution.py:761
  213.9 39.9 %collective-permute-start.12 = (bf16[192,2560]{1,0:T(8,128)(2,1)S(1)}, bf16[192,2560]{1,0:T(8,128)(2,1)S(1)}, u32[]{:S(2)}, u32[]{:S(2)}) collective-permute-start(bf16[192,2560]{1,0:T(8,128)(2,1)S(1)} %get-tuple-element.165), channel_id=1, source_target_pairs={{0,8},{4,12},{8,0},{12,4},{16,24},{20,28},{24,16},{28,20},{1,9},{5... | collective-permute-start | bytes 2949128 | tf_op jit(solution)/shard_map/ppermute | solution.py:761
  215.7 43.1 %collective-permute-start.14 = (bf16[192,2560]{1,0:T(8,128)(2,1)}, bf16[192,2560]{1,0:T(8,128)(2,1)S(1)}, u32[]{:S(2)}, u32[]{:S(2)}) collective-permute-start(bf16[192,2560]{1,0:T(8,128)(2,1)} %get-tuple-element.167), channel_id=1, source_target_pairs={{0,8},{4,12},{8,0},{12,4},{16,24},{20,28},{24,16},{28,20},{1,9},{5... | collective-permute-start | bytes 2949128 | tf_op jit(solution)/shard_map/ppermute | solution.py:761
  216.0 44.7 %collective-permute-start.13 = (bf16[2,192,2560]{2,1,0:T(8,128)(2,1)}, bf16[2,192,2560]{2,1,0:T(8,128)(2,1)}, u32[]{:S(2)}, u32[]{:S(2)}) collective-permute-start(bf16[2,192,2560]{2,1,0:T(8,128)(2,1)} %get-tuple-element.166), channel_id=1, source_target_pairs={{0,16},{4,20},{8,24},{12,28},{16,0},{20,4},{24,8},{28,12},{1,17},{... | collective-permute-start | bytes 5898248 | tf_op jit(solution)/shard_map/ppermute | solution.py:761
  253.8 8.5 %copy-start.22 = (bf16[192,2560]{1,0:T(8,128)(2,1)}, bf16[192,2560]{1,0:T(8,128)(2,1)S(1)}, u32[]{:S(2)}) copy-start(bf16[192,2560]{1,0:T(8,128)(2,1)S(1)} %collective-permute-done.12) | copy-start | bytes 2949124
  258.8 1.8 copy-start.24
  262.2 32.8 %collective-permute-start.17 = (bf16[4,3,96,768]{3,2,1,0:T(8,128)(2,1)S(1)}, bf16[4,3,96,768]{3,2,1,0:T(8,128)(2,1)}, u32[]{:S(2)}, u32[]{:S(2)}) collective-permute-start(bf16[4,3,96,768]{3,2,1,0:T(8,128)(2,1)S(1)} %slice_bitcast_fusion.1), channel_id=1, source_target_pairs={{0,4},{4,0},{8,12},{12,8},{16,20},{20,16},{24,28},{28,24},{1,5},{5... | collective-permute-start | bytes 5308424 | tf_op jit(solution)/shard_map/ppermute | solution.py:761
  262.3 2.1 copy-start.23
  264.4 1.2 copy-start.25
  266.9 28.2 %collective-permute-start.16 = (bf16[192,2560]{1,0:T(8,128)(2,1)}, bf16[192,2560]{1,0:T(8,128)(2,1)S(1)}, u32[]{:S(2)}, u32[]{:S(2)}) collective-permute-start(bf16[192,2560]{1,0:T(8,128)(2,1)} %slice_bitcast_fusion.4), channel_id=1, source_target_pairs={{0,8},{4,12},{8,0},{12,4},{16,24},{20,28},{24,16},{28,20},{1,9},{5... | collective-permute-start | bytes 2949128 | tf_op jit(solution)/shard_map/ppermute | solution.py:761
  268.6 26.5 %collective-permute-start.15 = (bf16[192,2560]{1,0:T(8,128)(2,1)S(1)}, bf16[192,2560]{1,0:T(8,128)(2,1)S(1)}, u32[]{:S(2)}, u32[]{:S(2)}) collective-permute-start(bf16[192,2560]{1,0:T(8,128)(2,1)S(1)} %add_convert_fusion.2), channel_id=1, source_target_pairs={{0,16},{4,20},{8,24},{12,28},{16,0},{20,4},{24,8},{28,12},{1,17},{... | collective-permute-start | bytes 2949128 | tf_op jit(solution)/shard_map/ppermute | solution.py:761
  296.0 1.2 copy-start.21
  298.8 1.3 copy-start.19
  298.9 103.5 %all-gather.11.cloned.1.call-start = ((), (), s32[]{:S(2)}) async-start(), calls=%async_computation.4 | async-start | bytes 5750784 | tf_op jit(solution)/shard_map/all_gather | solution.py:770
  300.1 4.4 %collective-permute-start.21 = (bf16[4,1,96,768]{3,2,0,1:T(8,128)(2,1)S(1)}, bf16[4,1,96,768]{3,2,0,1:T(8,128)(2,1)S(1)}, u32[]{:S(2)}, u32[]{:S(2)}) collective-permute-start(bf16[4,1,96,768]{3,2,0,1:T(8,128)(2,1)S(1)} %slice_bitcast_fusion.5), channel_id=1, source_target_pairs={{0,4},{4,0},{8,12},{12,8},{16,20},{20,16},{24,28},{28,24},{1,5},{5... | collective-permute-start | bytes 1769480 | tf_op jit(solution)/shard_map/ppermute | solution.py:761
  302.8 15.8 %collective-permute-start.18 = (bf16[2,2,96,768]{3,2,1,0:T(8,128)(2,1)S(1)}, bf16[2,2,96,768]{3,2,1,0:T(8,128)(2,1)S(1)}, u32[]{:S(2)}, u32[]{:S(2)}) collective-permute-start(bf16[2,2,96,768]{3,2,1,0:T(8,128)(2,1)S(1)} %slice_bitcast_fusion.7), channel_id=1, source_target_pairs={{0,8},{4,12},{8,0},{12,4},{16,24},{20,28},{24,16},{28,20},{1,9},{5... | collective-permute-start | bytes 1769480 | tf_op jit(solution)/shard_map/ppermute | solution.py:761
  304.8 15.7 %collective-permute-start.22 = (bf16[2,2,96,768]{3,2,1,0:T(8,128)(2,1)S(1)}, bf16[2,2,96,768]{3,2,1,0:T(8,128)(2,1)S(1)}, u32[]{:S(2)}, u32[]{:S(2)}) collective-permute-start(bf16[2,2,96,768]{3,2,1,0:T(8,128)(2,1)S(1)} %fusion.7), channel_id=1, source_target_pairs={{0,16},{4,20},{8,24},{12,28},{16,0},{20,4},{24,8},{28,12},{1,17},{... | collective-permute-start | bytes 1769480 | tf_op jit(solution)/shard_map/ppermute | solution.py:761
  318.7 8.8 %collective-permute-start.19 = (bf16[2,96,768]{2,1,0:T(8,128)(2,1)S(1)}, bf16[2,96,768]{2,1,0:T(8,128)(2,1)S(1)}, u32[]{:S(2)}, u32[]{:S(2)}) collective-permute-start(bf16[2,96,768]{2,1,0:T(8,128)(2,1)S(1)} %slice_bitcast_fusion.11), channel_id=1, source_target_pairs={{0,16},{4,20},{8,24},{12,28},{16,0},{20,4},{24,8},{28,12},{1,17},{... | collective-permute-start | bytes 884744 | tf_op jit(solution)/shard_map/ppermute | solution.py:761
  320.7 11.2 %collective-permute-start.23 = (bf16[2,96,768]{2,1,0:T(8,128)(2,1)S(1)}, bf16[2,96,768]{2,1,0:T(8,128)(2,1)S(1)}, u32[]{:S(2)}, u32[]{:S(2)}) collective-permute-start(bf16[2,96,768]{2,1,0:T(8,128)(2,1)S(1)} %slice_bitcast_fusion.9), channel_id=1, source_target_pairs={{0,8},{4,12},{8,0},{12,4},{16,24},{20,28},{24,16},{28,20},{1,9},{5... | collective-permute-start | bytes 884744 | tf_op jit(solution)/shard_map/ppermute | solution.py:761
  327.6 31.7 %copy-start.33 = (bf16[512,768]{1,0:T(8,128)(2,1)S(1)}, bf16[512,768]{1,0:T(8,128)(2,1)}, u32[]{:S(2)}) copy-start(bf16[512,768]{1,0:T(8,128)(2,1)} %get-tuple-element.203) | copy-start | bytes 2359300
  327.6 34.1 %copy-start.27 = (bf16[512,768]{1,0:T(8,128)(2,1)S(1)}, bf16[512,768]{1,0:T(8,128)(2,1)}, u32[]{:S(2)}) copy-start(bf16[512,768]{1,0:T(8,128)(2,1)} %get-tuple-element.204) | copy-start | bytes 2359300
  327.6 17.4 %collective-permute-start.20 = (bf16[96,768]{1,0:T(8,128)(2,1)S(1)}, bf16[96,768]{1,0:T(8,128)(2,1)S(1)}, u32[]{:S(2)}, u32[]{:S(2)}) collective-permute-start(bf16[96,768]{1,0:T(8,128)(2,1)S(1)} %slice_bitcast_fusion.15), channel_id=1, source_target_pairs={{0,3},{1,0},{2,1},{3,2},{4,7},{5,4},{6,5},{7,6},{8,11},{9,8},{10,9... | collective-permute-start | bytes 442376 | tf_op jit(solution)/shard_map/ppermute | solution.py:764
  332.1 25.2 %collective-permute-start.24 = (bf16[96,768]{1,0:T(8,128)(2,1)S(1)}, bf16[96,768]{1,0:T(8,128)(2,1)S(1)}, u32[]{:S(2)}, u32[]{:S(2)}) collective-permute-start(bf16[96,768]{1,0:T(8,128)(2,1)S(1)} %get-tuple-element.227), channel_id=1, source_target_pairs={{0,2},{1,3},{2,0},{3,1},{4,6},{5,7},{6,4},{7,5},{8,10},{9,11},{10,... | collective-permute-start | bytes 442376 | tf_op jit(solution)/shard_map/ppermute | solution.py:764
  337.5 19.7 %collective-permute-start.25 = (bf16[96,768]{1,0:T(8,128)(2,1)S(1)}, bf16[96,768]{1,0:T(8,128)(2,1)S(1)}, u32[]{:S(2)}, u32[]{:S(2)}) collective-permute-start(bf16[96,768]{1,0:T(8,128)(2,1)S(1)} %get-tuple-element.228), channel_id=1, source_target_pairs={{0,1},{1,2},{2,3},{3,0},{4,5},{5,6},{6,7},{7,4},{8,9},{9,10},{10,1... | collective-permute-start | bytes 442376 | tf_op jit(solution)/shard_map/ppermute | solution.py:764
  357.3 21.2 %copy-start.26 = (bf16[512,768]{1,0:T(8,128)(2,1)S(1)}, bf16[512,768]{1,0:T(8,128)(2,1)}, u32[]{:S(2)}) copy-start(bf16[512,768]{1,0:T(8,128)(2,1)} %get-tuple-element.202) | copy-start | bytes 2359300
  359.3 41.5 %copy-start.16 = (f32[512,768]{1,0:T(8,128)S(1)}, f32[512,768]{1,0:T(8,128)}, u32[]{:S(2)}) copy-start(f32[512,768]{1,0:T(8,128)} %get-tuple-element.150) | copy-start | bytes 4718596
  359.3 41.5 %copy-start.17 = (f32[512,768]{1,0:T(8,128)S(1)}, f32[512,768]{1,0:T(8,128)}, u32[]{:S(2)}) copy-start(f32[512,768]{1,0:T(8,128)} %get-tuple-element.201) | copy-start | bytes 4718596
  359.4 2.3 collective-permute-start.28
  360.2 18.3 %collective-permute-start.26 = (bf16[512,768]{1,0:T(8,128)(2,1)S(1)}, bf16[512,768]{1,0:T(8,128)(2,1)S(1)}, u32[]{:S(2)}, u32[]{:S(2)}) collective-permute-start(bf16[512,768]{1,0:T(8,128)(2,1)S(1)} %copy-done.33), channel_id=1, source_target_pairs={{0,1},{1,2},{4,5},{5,6},{8,9},{9,10},{12,13},{13,14},{16,17},{17,1... | collective-permute-start | bytes 2359304 | tf_op jit(solution)/shard_map/ppermute | solution.py:865
  361.9 37.6 %collective-permute-start.29 = (bf16[512,768]{1,0:T(8,128)(2,1)S(1)}, bf16[512,768]{1,0:T(8,128)(2,1)S(1)}, u32[]{:S(2)}, u32[]{:S(2)}) collective-permute-start(bf16[512,768]{1,0:T(8,128)(2,1)S(1)} %add_convert_fusion.4), channel_id=1, source_target_pairs={{1,0},{2,1},{3,2},{5,4},{6,5},{7,6},{9,8},{10,9},{11,10},{13,12},{... | collective-permute-start | bytes 2359304 | tf_op jit(solution)/shard_map/ppermute | solution.py:767
  378.7 22.2 %collective-permute-start.27 = (bf16[512,768]{1,0:T(8,128)(2,1)S(1)}, bf16[512,768]{1,0:T(8,128)(2,1)S(1)}, u32[]{:S(2)}, u32[]{:S(2)}) collective-permute-start(bf16[512,768]{1,0:T(8,128)(2,1)S(1)} %add_convert_fusion.5), channel_id=1, source_target_pairs={{0,1},{1,2},{2,3},{4,5},{5,6},{6,7},{8,9},{9,10},{10,11},{12,13},{... | collective-permute-start | bytes 2359304 | tf_op jit(solution)/shard_map/ppermute | solution.py:767
  402.3 9.9 %copy-start.1 = (bf16[192,768]{1,0:T(8,128)(2,1)S(1)}, bf16[192,768]{1,0:T(8,128)(2,1)}, u32[]{:S(2)}) copy-start(bf16[192,768]{1,0:T(8,128)(2,1)} %param.14) | copy-start | bytes 884740
  (4 other events, 3.4 us)
Sparse Core Ops, SparseCore 0:
  35.3 42.2 all-gather.6
  80.0 63.8 all-gather.8
  299.0 53.4 reduce-scatter.1
  359.4 38.6 all-gather.10

commit v5 on v4

--- a/solution.py
+++ b/solution.py
@@ -123,7 +123,7 @@
         + [pl.BlockSpec(memory_space=pl.ANY)] * len(held),
         out_specs=tuple(out_specs),
         input_output_aliases={5 + n: n for n in range(len(held))},
-        compiler_params=pltpu.CompilerParams(vmem_limit_bytes=30 << 20),
+        compiler_params=pltpu.CompilerParams(vmem_limit_bytes=20 << 20),
         cost_estimate=pl.CostEstimate(flops=2 << 30, bytes_accessed=8 << 20, transcendentals=0),
         name="project",
     )(tok, w, cos, sin, seg, *[stay(a) for a in held])
@@ -175,23 +175,16 @@
         in_specs=[pl.BlockSpec(memory_space=pltpu.SMEM), pl.BlockSpec((here, 1), lambda g: (0, 0))] + [part(a.shape) for a in (qh, ka, vt)],
         out_specs=tuple(part(s) for s, _ in shapes),
         scratch_shapes=[pltpu.VMEM((heads, 80, here), f32), pltpu.VMEM((8, here), f32)],
-        compiler_params=pltpu.CompilerParams(vmem_limit_bytes=40 << 20),
+        compiler_params=pltpu.CompilerParams(vmem_limit_bytes=24 << 20),
         cost_estimate=pl.CostEstimate(flops=12 << 30, bytes_accessed=12 << 20, transcendentals=4 << 20),
         name="attn_fwd",
     )(info, seg, stay(qh), stay(ka), stay(vt))
 
 
-def attn_bwd_kernel(info, *refs, docs, heads, slots, pieces, start, stop):
+def attn_bwd_kernel(info, *refs, docs, heads, slots, pieces):
     toks = refs[:slots]
-    w, cos, sin, seg, qh, ka, va, lse, mixed, do = refs[slots : slots + 10]
-    refs = refs[slots + 10 :]
-    last = stop == slots
-    if start:
-        old_dkv, old_dq, refs = refs[0], refs[1], refs[2:]
-    dw, refs = refs[0], refs[1:]
-    if last:
-        dx_out, refs = refs[:slots], refs[slots:]
-    dkv, dq, tokt, dqt, dwa, doh, delta, dka, dva = refs
+    cos, sin, seg, qh, ka, va, lse, mixed, do = refs[slots : slots + 9]
+    dw, dkv, dq, tokt, dqt, dwa, doh, delta, dka, dva = refs[slots + 9 :]
     here, width = toks[0].shape
     seq = here * slots
     count = seq // TILE
@@ -210,9 +203,6 @@
                 tokt[:, start : start + TILE] = toks[s][c * TILE : (c + 1) * TILE, :].astype(f32).T.astype(bf16)
 
     g = pl.program_id(0)
-
-    def weight(group, start, stop):
-        return w[:, group, :, start:stop].reshape(width, stop - start)
 
     wlane = lax.broadcasted_iota(jnp.int32, (here, cols), 1)
     lane = lax.broadcasted_iota(jnp.int32, (TILE, 128), 1)
@@ -269,40 +259,14 @@
         p = jnp.bitwise_xor(me, r)
         dw[r, 0] = dwa[pl.ds(pl.multiple_of(p * share, 8), share), :].astype(bf16)
 
-    if not last:
-        return
-
-    def key_grads(group, rows, cut):
-        return old_dkv[group, rows, cut] if group < start else dkv[group - start, rows, cut]
-
-    @pl.when(g == stop - start - 1)
-    def _():
-        for s in range(slots):
-            dx_out[s][...] = jnp.zeros_like(dx_out[s])
-        for s in range(slots):
-            begin = lax.rem(base + s * tiles, count)
-
-            @pl.when((begin + tiles > lo) & (begin < hi))
-            def _(s=s):
-                rows = slice(s * here, (s + 1) * here)
-                total = sum(
-                    nt(key_grads(group, rows, slice(0, 256)), weight(group, 256, 512))
-                    + nt(key_grads(group, rows, slice(256, 256 + cols)), weight(group, 512 + cols, 512 + 2 * cols))
-                    for group in range(slots)
-                )
-                if s == 0:
-                    total = total + sum(nt(old_dq[group] if group < start else dq[group - start], weight(group, 0, 256)) for group in range(slots))
-                dx_out[s][...] = total.astype(dx_out[s].dtype)
-
-
-def attn_bwd(info, toks, w, cos, sin, seg, saved, do, docs, heads, pieces, start, stop, carry=()):
+
+def attn_bwd(info, toks, cos, sin, seg, saved, do, docs, heads, pieces, start, stop):
     slots = len(toks)
     here, width = toks[0].shape
     seq = here * slots
     cols = heads * HD
     span = -(-(512 + cols) // 128) * 128
     count = stop - start
-    last = stop == slots
 
     def whole(shape):
         return pl.BlockSpec(shape, lambda g: (0,) * len(shape))
@@ -311,26 +275,16 @@
         return pl.BlockSpec((1,) + array.shape[1:], lambda g: (g + start,) + (0,) * (array.ndim - 1))
 
     kept = [((count, seq, 256 + cols), bf16), ((count, here, 256), bf16)]
-    out_shape = [jax.ShapeDtypeStruct((pieces, count, width // pieces, span), bf16)]
-    out_specs = [pl.BlockSpec((pieces, 1, width // pieces, span), lambda g: (0, g, 0, 0))]
-    if last:
-        out_shape += [jax.ShapeDtypeStruct((here, width), f32)] + [jax.ShapeDtypeStruct((here, width), bf16)] * (slots - 1)
-        out_specs += [whole((here, width))] * slots
-    else:
-        out_shape += [jax.ShapeDtypeStruct(s, d) for s, d in kept]
-        out_specs += [whole(s) for s, _ in kept]
     return pl.pallas_call(
-        functools.partial(attn_bwd_kernel, docs=docs, heads=heads, slots=slots, pieces=pieces, start=start, stop=stop),
+        functools.partial(attn_bwd_kernel, docs=docs, heads=heads, slots=slots, pieces=pieces),
         grid=(count,),
-        out_shape=tuple(out_shape),
+        out_shape=(jax.ShapeDtypeStruct((pieces, count, width // pieces, span), bf16),) + tuple(jax.ShapeDtypeStruct(s, d) for s, d in kept),
         in_specs=[pl.BlockSpec(memory_space=pltpu.SMEM)]
         + [whole((here, width))] * slots
-        + [whole(w.shape), whole(cos.shape), whole(sin.shape), whole(seg.shape)]
-        + [part(a) for a in (*saved, do)]
-        + [whole(a.shape) for a in carry],
-        out_specs=tuple(out_specs),
-        scratch_shapes=([pltpu.VMEM(s, d) for s, d in kept] if last else [])
-        + [
+        + [whole(cos.shape), whole(sin.shape), pl.BlockSpec((here, 1), lambda g: (0, 0))]
+        + [part(a) for a in (*saved, do)],
+        out_specs=(pl.BlockSpec((pieces, 1, width // pieces, span), lambda g: (0, g, 0, 0)),) + tuple(whole(s) for s, _ in kept),
+        scratch_shapes=[
             pltpu.VMEM((width, seq), bf16),
             pltpu.VMEM((256, here), f32),
             pltpu.VMEM((width, span), f32),
@@ -339,10 +293,71 @@
             pltpu.VMEM((TILE, 256), f32),
             pltpu.VMEM((TILE, cols), f32),
         ],
-        compiler_params=pltpu.CompilerParams(vmem_limit_bytes=56 << 20),
+        compiler_params=pltpu.CompilerParams(vmem_limit_bytes=40 << 20),
         cost_estimate=pl.CostEstimate(flops=10 * count << 30, bytes_accessed=6 * count << 20, transcendentals=count << 20),
         name="attn_bwd",
-    )(info, *toks, w, cos, sin, seg, *saved, do, *carry)
+    )(info, *toks, cos, sin, seg, *saved, do)
+
+
+def token_grads_kernel(info, w, *refs, cols, split):
+    dkv, dq, (own, rest) = refs[:split], refs[split : 2 * split], refs[2 * split :]
+    here = rest.shape[1]
+    width = own.shape[1]
+    tiles = here // TILE
+    count = pl.num_programs(0) * tiles
+    s = pl.program_id(0)
+    begin = lax.rem(info[2] + s * tiles, count)
+    live = (begin + tiles > info[0]) & (begin < info[1])
+
+    def weight(group, start, stop):
+        return w[:, group, :, start:stop].reshape(width, stop - start)
+
+    def keys():
+        total, group = jnp.zeros((here, width), f32), 0
+        for part in dkv:
+            for n in range(part.shape[0]):
+                total = total + nt(part[n, :, :256], weight(group, 256, 512)) + nt(part[n, :, 256:], weight(group, 512 + cols, 512 + 2 * cols))
+                group += 1
+        return total
+
+    @pl.when(jnp.logical_not(live))
+    def _():
+        rest[0] = jnp.zeros((here, width), bf16)
+
+    @pl.when(live)
+    def _():
+        rest[0] = keys().astype(bf16)
+
+    @pl.when(s == 0)
+    def _():
+        total, group = jnp.where(live, keys(), 0.0), 0
+        for part in dq:
+            for n in range(part.shape[0]):
+                total = total + nt(part[n], weight(group, 0, 256))
+                group += 1
+        own[...] = total
+
+
+def token_grads(info, w, dkv, dq, cols, slots):
+    width = w.shape[0] * w.shape[2]
+    here = dq[0].shape[1]
+
+    def slot(array):
+        return pl.BlockSpec((array.shape[0], here, array.shape[2]), lambda s: (0, s, 0))
+
+    def whole(shape):
+        return pl.BlockSpec(shape, lambda s: (0,) * len(shape))
+
+    return pl.pallas_call(
+        functools.partial(token_grads_kernel, cols=cols, split=len(dkv)),
+        grid=(slots,),
+        out_shape=(jax.ShapeDtypeStruct((here, width), f32), jax.ShapeDtypeStruct((slots, here, width), bf16)),
+        in_specs=[pl.BlockSpec(memory_space=pltpu.SMEM), whole(w.shape)] + [slot(a) for a in dkv] + [whole(a.shape) for a in dq],
+        out_specs=(whole((here, width)), pl.BlockSpec((1, here, width), lambda s: (s, 0, 0))),
+        compiler_params=pltpu.CompilerParams(vmem_limit_bytes=40 << 20),
+        cost_estimate=pl.CostEstimate(flops=8 << 30, bytes_accessed=20 << 20, transcendentals=0),
+        name="token_grads",
+    )(info, w, *dkv, *dq)
 
 
 def doc_tables(lengths, seq, first, here):
@@ -635,7 +650,7 @@
         functools.partial(wgrad_kernel, slots=slots, share=share, add=got is not None),
         out_shape=out_shape,
         grid_spec=pltpu.PrefetchScalarGridSpec(num_scalar_prefetch=1, grid=(2,), in_specs=in_specs, out_specs=out_specs, scratch_shapes=scratch),
-        compiler_params=pltpu.CompilerParams(vmem_limit_bytes=40 << 20),
+        compiler_params=pltpu.CompilerParams(vmem_limit_bytes=24 << 20),
         cost_estimate=pl.CostEstimate(flops=2 << 30, bytes_accessed=10 << 20, transcendentals=0),
         name="wgrad",
     )(me, *args)
@@ -824,18 +839,18 @@
     far_keep, far_give, far_rest = wgrad(after(me_array, near_sent), 4, *fixed, flip(far_sent, 1), pieces, share, span)
     near_keep, near_give, near_rest = wgrad(after(me_array, far_rest), 0, *fixed, flip(near_sent, 1), pieces, share, span)
 
-    back, far_give, far_rest, near_give = lax.optimization_barrier((back, far_give, far_rest, near_give))
+    back, near_give = lax.optimization_barrier((back, near_give))
     got = [flip(far_give, 2), flip(far_rest, 4), flip(near_give, 2)]
-    backward = functools.partial(attn_bwd, info, toks, w1, cosine, sine, seg_col, saved)
+    backward = functools.partial(attn_bwd, info, toks, cosine, sine, seg_col, saved)
     cut = tp_size - 1
-    dw_low, *carry = backward(back, docs, heads, pieces, 0, cut)
-    got, dw_low, carry, back_late = lax.optimization_barrier((got, dw_low, carry, back))
+    dw_low, kv_low, q_low = backward(back, docs, heads, pieces, 0, cut)
+    got, dw_low, back_late = lax.optimization_barrier((got, dw_low, back))
     next_b = low_sum(near_rest, got[1])
     give_a, next_a = low_sum(far_keep, got[0]), low_sum(near_keep, got[2])
     back_late, next_a, give_a, next_b = lax.optimization_barrier((back_late, next_a, give_a, next_b))
     got_a, got_b, got_low = flip(give_a, 4), flip(next_b[1], 2), flip(dw_low.reshape((pieces // 2, 2) + dw_low.shape[1:])[:, 1], 1)
-    dw_high, *dx = backward(back_late, docs, heads, pieces, cut, tp_size, carry)
-    got_a, got_b, got_low, dw_high, dx = lax.optimization_barrier((got_a, got_b, got_low, dw_high, dx))
+    dw_high, kv_high, q_high = backward(back_late, docs, heads, pieces, cut, tp_size)
+    got_a, got_b, got_low, dw_high, kv_high = lax.optimization_barrier((got_a, got_b, got_low, dw_high, kv_high))
     parts_two = jnp.concatenate([low_sum(next_a, got_a), low_sum(next_b[0], got_b)], axis=0)
     share_two = lax.psum_scatter(parts_two, "tensor", scatter_dimension=0, tiled=True)
 
@@ -843,6 +858,7 @@
         return array.reshape((pieces // 2, 2) + array.shape[1:])
 
     got_high = flip(pairs_of(dw_high)[:, 1], 1)
+    dx_own, dx = token_grads(info, w1, (kv_low, kv_high), (q_low, q_high), cols_here, tp_size)
     low = low_sum(pairs_of(dw_low)[:, 0], got_low).reshape((2, 2) + dw_low.shape[1:])
     got_a = flip(low[:, 1, :half], 2)
     high = low_sum(pairs_of(dw_high)[:, 0], got_high).reshape((2, 2) + dw_high.shape[1:])
@@ -860,12 +876,12 @@
 
     parts_one = by_slot(low_sum(next_a[0], got_a), low_sum(next_b[0], got_b))
     moved_one = [shift(parts_one[s], -s) for s in range(1, tp_size)]
+    moved_one, dx = lax.optimization_barrier((moved_one, dx))
     share_one = total(parts_one[0], moved_one)
-    share_two, share_one, dx = lax.optimization_barrier((share_two, share_one, dx))
     from_left = lax.ppermute(dx[2], "tensor", [(i, i + 1) for i in range(half)])
     from_right = lax.ppermute(dx[2], "tensor", [(i + half, i + half - 1) for i in range(half)])
     near_right, near_left = low_sum(dx[1], from_left), low_sum(dx[3], from_right)
-    input_grad = grad_one + dx[0] + along(near_right, 1).astype(f32) + along(near_left, -1).astype(f32)
+    from_before, from_behind = along(near_right, 1), along(near_left, -1)
 
     def finish(array):
         if groups is not None:
@@ -876,6 +892,8 @@
     main = finish(jnp.concatenate([share_two, share_one], axis=1)).reshape(units, -1)
     gate_up_sum, down_sum, out_sum, qkv_turned, small_out = final_sums(main, width, span, heads, pieces)
     qkv_sum = qkv_turned.transpose(2, 0, 1)
+    from_before, from_behind, small_out = lax.optimization_barrier((from_before, from_behind, small_out))
+    input_grad = grad_one + dx_own + from_before.astype(f32) + from_behind.astype(f32)
     return (
         layer_out[None],
         input_grad[None],

time: 427 us -> 416 us (0.974)
  Pallas kernels: 168 us -> 159 us
  starting transfers between devices: 55.4 us -> 49.7 us
    pallas_call x2, Pallas kernels: 62.6 us -> 44.6 us  [attn_bwd(): pl.pallas_call(functools.partial(attn_bwd_kernel, docs=docs, heads=heads,...]
    ppermute x6, waiting for transfers between devices: 19.8 us -> 3.76 us  [along(): return lax.ppermute(array, 'tensor', line_axis(tp_size, step))]
    ppermute x13, waiting for transfers between devices: 28.4 us -> 43.4 us  [flip(): return lax.ppermute(array, 'dp', flip_axis(dp_size, bit))]
    all_gather x3, waiting for transfers between devices: 0.02 us -> 11.7 us  [gather_dp(): return lax.all_gather(array, 'dp', axis=0, axis_index_groups=groups)]
    pallas_call x0 -> x1, Pallas kernels: none -> 10 us  [token_grads(): pl.pallas_call(functools.partial(token_grads_kernel, cols=cols, split=len...]
    ppermute x9, waiting for transfers between devices: 53.3 us -> 43.6 us  [shift(): return lax.ppermute(array, 'tensor', rotate_axis(tp_size, step))]
  transfers between devices with their start and end apart: 34 -> 34, of which waited for: 15 -> 18; matrix products, arithmetic and copies ran while one was open for 7% -> 7% of each run, Pallas kernels for 28% -> 30%
where the time goes in v5:
time: 416 us; the launch traced here: 408 us
  Pallas kernels  159 us (38%)
  waiting for transfers between devices  119 us (29%)
  starting transfers between devices  49.7 us (12%)
  local copies, waits for them, and re-layouts  37.8 us (9%)
  other arithmetic  26.4 us (6%)
  between operations  15 us (4%)
    pallas_call x2, Pallas kernels, attn_bwd(): pl.pallas_call(functools.partial(attn_bwd_kernel, docs=docs, heads=heads,...  44.6 us
    ppermute x9, waiting for transfers between devices, shift(): return lax.ppermute(array, 'tensor', rotate_axis(tp_size, step))  43.6 us
    ppermute x13, waiting for transfers between devices, flip(): return lax.ppermute(array, 'dp', flip_axis(dp_size, bit))  43.4 us
    pallas_call x1, Pallas kernels, ffn_layer(): pl.pallas_call(functools.partial(ffn_kernel, slots=slots, pieces=pieces,...  33 us
    pallas_call x4, Pallas kernels, project(): pl.pallas_call(functools.partial(project_kernel, docs=docs, heads=heads,...  25.7 us
    ppermute x6, starting transfers between devices, along(): return lax.ppermute(array, 'tensor', line_axis(tp_size, step))  21 us
    pallas_call x4, Pallas kernels, wgrad(): pl.pallas_call(functools.partial(wgrad_kernel, slots=slots, share=share,...  18.9 us
    pallas_call x1, Pallas kernels, attn_fwd(): pl.pallas_call(functools.partial(attn_fwd_kernel, docs=docs, heads=heads)...  18.7 us
  transfers between devices with their start and end apart: 34, of which 18 were waited for; matrix products, arithmetic and copies ran while one was open for 7% of the time, Pallas kernels for 30%

profile of v5, /device:TPU:0, one launch (start us, length us, event | category | flops | bytes accessed | tf_op | source)
XLA Modules:
  0.0 407.6 jit_solution(14408423230467039737)
XLA Ops:
  10.8 3.0 constant_dynamic-slice_fusion.2
  14.5 5.1 %collective-permute-start.2 = (bf16[96,896]{1,0:T(8,128)(2,1)S(1)}, bf16[96,896]{1,0:T(8,128)(2,1)S(1)}, u32[]{:S(2)}, u32[]{:S(2)}) collective-permute-start(bf16[96,896]{1,0:T(8,128)(2,1)S(1)} %pad_maximum_fusion.7), channel_id=1, source_target_pairs={{0,3},{1,0},{2,1},{3,2},{4,7},{5,4},{6,5},{7,6},{8,11},{9,8},{10,9... | collective-permute-start | bytes 516104 | tf_op jit(solution)/shard_map/ppermute | solution.py:779
  20.6 3.8 collective-permute-done.2
  24.5 9.8 %collective-permute-done.1 = bf16[96,896]{1,0:T(8,128)(2,1)S(1)} collective-permute-done((bf16[96,896]{1,0:T(8,128)(2,1)S(1)}, bf16[96,896]{1,0:T(8,128)(2,1)S(1)}, u32[]{:S(2)}, u32[]{:S(2)}) %collective-permute-start.1) | collective-permute-done | bytes 172064 | tf_op jit(solution)/shard_map/ppermute | solution.py:779
  37.0 2.0 collective-permute-start.4
  39.0 1.9 collective-permute-start.3
  41.0 5.6 %copy.117 = bf16[768,2,768]{0,2,1:T(8,128)(2,1)S(1)} copy(bf16[768,2,768]{2,1,0:T(2,128)(2,1)} %param.17) | data formatting | bytes 4718592 | tf_op jit(solution)/shard_map/optimization_barrier | solution.py:738
  47.6 1.3 fusion.19
  48.9 1.4 concatenate.26.info
  50.7 3.7 multiply_sine_fusion
  54.4 2.0 pad_maximum_fusion
  56.4 20.7 %collective-permute-done.4 = bf16[96,2304]{1,0:T(8,128)(2,1)} collective-permute-done((bf16[96,2304]{1,0:T(8,128)(2,1)S(1)}, bf16[96,2304]{1,0:T(8,128)(2,1)}, u32[]{:S(2)}, u32[]{:S(2)}) %collective-permute-start.4) | collective-permute-done | bytes 442400 | tf_op jit(solution)/shard_map/ppermute | solution.py:779
  77.0 2.3 pad_maximum_fusion.2
  79.4 1.3 collective-permute-start.7
  80.7 5.4 %collective-permute-start.6 = (bf16[512,768]{1,0:T(8,128)(2,1)}, bf16[512,768]{1,0:T(8,128)(2,1)}, u32[]{:S(2)}, u32[]{:S(2)}) collective-permute-start(bf16[512,768]{1,0:T(8,128)(2,1)} %bitcast.refs_0_), channel_id=1, source_target_pairs={{0,1},{1,2},{2,3},{4,5},{5,6},{6,7},{8,9},{9,10},{10,11},{12,13},{... | collective-permute-start | bytes 2359304 | tf_op jit(solution)/shard_map/ppermute | solution.py:782
  86.5 3.2 copy-done.2
  89.8 7.3 %project.4 = (bf16[4,4,512,256]{3,2,1,0:T(8,128)(2,1)}, bf16[4,4,512,192]{3,2,1,0:T(8,128)(2,1)}, bf16[4,4,240,512]{3,2,1,0:T(8,128)(2,1)}, bf16[4,3,512,256]{3,2,1,0:T(8,128)(2,1)}) custom-call(bf16[512,768]{1,0:T(8,128)(2,1)} %bitcast.refs_0_, bf16[8,4,96,896]{3,2,1,0:T(8,128)(2,1)S(1)} %bitcast.136, f32[2048,128]{1,0:T(8,128)S(1)} %get-tuple-element.113.refs_2_.refs_4_, ...), custom_call_target="tpu_custom_call" | custom-call | flops 2147483648 | bytes 8388608 | tf_op jit(solution)/shard_map/project/pallas_call | solution.py:112
  97.1 2.6 collective-permute-done.7.refs_0_.refs_1_
  99.7 1.2 collective-permute-done.6.refs_0_.refs_3_
  100.8 5.3 %collective-permute-start.9 = (bf16[512,768]{1,0:T(8,128)(2,1)}, bf16[512,768]{1,0:T(8,128)(2,1)}, u32[]{:S(2)}, u32[]{:S(2)}) collective-permute-start(bf16[512,768]{1,0:T(8,128)(2,1)} %collective-permute-done.6.refs_0_.refs_3_), channel_id=1, source_target_pairs={{0,1},{1,2},{2,3},{4,5},{5,6},{6,7},{8,9},{9,10},{10,11},{12,13},{... | collective-permute-start | bytes 2359304 | tf_op jit(solution)/shard_map/ppermute | solution.py:782
  106.1 1.5 collective-permute-start.8
  110.0 3.6 copy-done.3
  113.6 6.4 %project.5 = (bf16[4,4,512,256]{3,2,1,0:T(8,128)(2,1)}, bf16[4,4,512,192]{3,2,1,0:T(8,128)(2,1)}, bf16[4,4,240,512]{3,2,1,0:T(8,128)(2,1)}) custom-call(bf16[512,768]{1,0:T(8,128)(2,1)} %collective-permute-done.7.refs_0_.refs_1_, bf16[8,4,96,896]{3,2,1,0:T(8,128)(2,1)S(1)} %bitcast.137, ...), custom_call_target="tpu_custom_call", output_to_operand_aliasing={{0}: (5, {}), {1}: (6, {}), {2}: (7, {})} | custom-call | flops 2147483648 | bytes 8388608 | tf_op jit(solution)/shard_map/project/pallas_call | solution.py:112
  120.0 6.5 %project.6 = (bf16[4,4,512,256]{3,2,1,0:T(8,128)(2,1)}, bf16[4,4,512,192]{3,2,1,0:T(8,128)(2,1)}, bf16[4,4,240,512]{3,2,1,0:T(8,128)(2,1)}) custom-call(bf16[512,768]{1,0:T(8,128)(2,1)} %collective-permute-done.6.refs_0_.refs_3_, bf16[8,4,96,896]{3,2,1,0:T(8,128)(2,1)S(1)} %bitcast.138, ...), custom_call_target="tpu_custom_call", output_to_operand_aliasing={{0}: (5, {}), {1}: (6, {}), {2}: (7, {})} | custom-call | flops 2147483648 | bytes 8388608 | tf_op jit(solution)/shard_map/project/pallas_call | solution.py:112
  126.5 1.2 broadcast_select_fusion.refs_0_.refs_2_
  127.7 5.4 %project.7 = (bf16[4,4,512,256]{3,2,1,0:T(8,128)(2,1)}, bf16[4,4,512,192]{3,2,1,0:T(8,128)(2,1)}, bf16[4,4,240,512]{3,2,1,0:T(8,128)(2,1)}) custom-call(bf16[512,768]{1,0:T(8,128)(2,1)S(1)} %broadcast_select_fusion.refs_0_.refs_2_, bf16[8,4,96,896]{3,2,1,0:T(8,128)(2,1)S(1)} %bitcast.139, ...), custom_call_target="tpu_custom_call", output_to_operand_aliasing={{0}: (5, {}), {1}: (6, {}), {2}: (7, {})} | custom-call | flops 2147483648 | bytes 8388608 | tf_op jit(solution)/shard_map/project/pallas_call | solution.py:112
  133.2 18.7 %attn_fwd.1 = (f32[4,8,512]{2,1,0:T(8,128)S(1)}, bf16[4,512,192]{2,1,0:T(8,128)(2,1)S(1)}) custom-call(s32[8]{0:T(128)S(1)} %concatenate.26.info, s32[2048,1]{1,0:T(8,128)S(1)} %copy.123.refs_4_.seg.refs_6_, bf16[4,3,512,256]{3,2,1,0:T(8,128)(2,1)} %get-tuple-element.115.qh.refs_7_, bf16[4,4,512,256]{3,2,1,0:T(8,128)(2,1)} %get-tuple-element.136.ka, ...), custom_call_target="tpu_custom_call" | custom-call | flops 12884901888 | bytes 12582912 | tf_op jit(solution)/shard_map/attn_fwd/pallas_call | solution.py:171
  152.8 33.0 %ffn_layer.1 = (bf16[512,768]{1,0:T(8,128)(2,1)}, f32[512,768]{1,0:T(8,128)}, bf16[512,768]{1,0:T(8,128)(2,1)}, bf16[512,768]{1,0:T(8,128)(2,1)}, bf16[768,512]{...) custom-call(bf16[512,768]{1,0:T(8,128)(2,1)} %bitcast.refs_0_, ...), custom_call_target="tpu_custom_call" | custom-call | flops 17179869184 | bytes 31457280 | tf_op jit(solution)/shard_map/ffn_layer/pallas_call | solution.py:557
  185.8 1.2 copy-done.5
  187.0 1.1 copy-done.7
  191.3 4.5 %wgrad.4 = bf16[2,384,2560]{2,1,0:T(8,128)(2,1)S(1)} custom-call(s32[2]{0:T(128)S(1)} %get-tuple-element.158.refs_0_, bf16[512,3072]{1,0:T(8,128)(2,1)} %get-tuple-element.148.refs_1_, bf16[512,3072]{1,0:T(8,128)(2,1)} %get-tuple-element.149.refs_2_, bf16[512,3072]{1,0:T(8,128)(2,1)} %get-tuple-element.150.refs_3_, bf16[768,512]{1,0:T(8,128)(2,1)S(1)} %copy-done.9, ...), custom_call_target="tpu_custom_call" | custom-call | flops 2147483648 | bytes 10485760 | tf_op jit(solution)/shard_map/wgrad/pallas_call | solution.py:649
  195.8 4.5 %wgrad.5 = bf16[2,384,2560]{2,1,0:T(8,128)(2,1)S(1)} custom-call(s32[2]{0:T(128)S(1)} %get-tuple-element.158.refs_0_, bf16[512,3072]{1,0:T(8,128)(2,1)} %get-tuple-element.148.refs_1_, bf16[512,3072]{1,0:T(8,128)(2,1)} %get-tuple-element.149.refs_2_, bf16[512,3072]{1,0:T(8,128)(2,1)} %get-tuple-element.150.refs_3_, bf16[768,512]{1,0:T(8,128)(2,1)S(1)} %copy-done.9, ...), custom_call_target="tpu_custom_call" | custom-call | flops 2147483648 | bytes 10485760 | tf_op jit(solution)/shard_map/wgrad/pallas_call | solution.py:649
  200.9 1.7 collective-permute-done.10.refs_9_
  202.6 4.8 %wgrad.6 = (bf16[192,2560]{1,0:T(8,128)(2,1)S(1)}, bf16[192,2560]{1,0:T(8,128)(2,1)S(1)}, bf16[2,192,2560]{2,1,0:T(8,128)(2,1)S(1)}) custom-call(s32[2]{0:T(128)S(1)} %get-tuple-element.158.refs_0_, bf16[512,3072]{1,0:T(8,128)(2,1)} %get-tuple-element.148.refs_1_, bf16[512,3072]{1,0:T(8,128)(2,1)} %get-tuple-element.149.refs_2_, ...), custom_call_target="tpu_custom_call" | custom-call | flops 2147483648 | bytes 10485760 | tf_op jit(solution)/shard_map/wgrad/pallas_call | solution.py:649
  208.2 5.1 %wgrad.7 = (bf16[192,2560]{1,0:T(8,128)(2,1)S(1)}, bf16[192,2560]{1,0:T(8,128)(2,1)S(1)}, bf16[2,192,2560]{2,1,0:T(8,128)(2,1)S(1)}) custom-call(s32[2]{0:T(128)S(1)} %get-tuple-element.158.refs_0_, bf16[512,3072]{1,0:T(8,128)(2,1)} %get-tuple-element.148.refs_1_, bf16[512,3072]{1,0:T(8,128)(2,1)} %get-tuple-element.149.refs_2_, ...), custom_call_target="tpu_custom_call" | custom-call | flops 2147483648 | bytes 10485760 | tf_op jit(solution)/shard_map/wgrad/pallas_call | solution.py:649
  214.2 1.2 collective-permute-start.12
  215.5 32.5 %attn_bwd.2 = (bf16[8,3,96,768]{3,2,1,0:T(8,128)(2,1)}, bf16[3,2048,448]{2,1,0:T(8,128)(2,1)}, bf16[3,512,256]{2,1,0:T(8,128)(2,1)S(1)}) custom-call(s32[8]{0:T(128)S(1)} %concatenate.26.info, bf16[512,768]{1,0:T(8,128)(2,1)} %bitcast.refs_0_, bf16[512,768]{1,0:T(8,128)(2,1)} %collective-permute-done.7.refs_0_.refs_1_, bf16[512,768]{1,0:T(8,128)(2,1)S(1)} %copy-done.11, ...), custom_call_target="tpu_custom_call" | custom-call | flops 32212254720 | bytes 18874368 | tf_op jit(solution)/shard_map/attn_bwd/pallas_call | solution.py:278
  248.0 10.3 %collective-permute-done.12 = bf16[192,2560]{1,0:T(8,128)(2,1)S(1)} collective-permute-done((bf16[192,2560]{1,0:T(8,128)(2,1)S(1)}, bf16[192,2560]{1,0:T(8,128)(2,1)S(1)}, u32[]{:S(2)}, u32[]{:S(2)}) %collective-permute-start.12) | collective-permute-done | bytes 983072 | tf_op jit(solution)/shard_map/ppermute | solution.py:776
  258.3 1.6 slice_bitcast_fusion.1
  260.0 2.0 add_convert_fusion
  264.0 12.1 %attn_bwd.3 = (bf16[8,1,96,768]{3,2,1,0:T(8,128)(2,1)S(1)}, bf16[1,2048,448]{2,1,0:T(8,128)(2,1)S(1)}, bf16[1,512,256]{2,1,0:T(8,128)(2,1)S(1)}) custom-call(s32[8]{0:T(128)S(1)} %concatenate.26.info, bf16[512,768]{1,0:T(8,128)(2,1)} %bitcast.refs_0_, bf16[512,768]{1,0:T(8,128)(2,1)} %collective-permute-done.7.refs_0_.refs_1_, ...), custom_call_target="tpu_custom_call" | custom-call | flops 10737418240 | bytes 6291456 | tf_op jit(solution)/shard_map/attn_bwd/pallas_call | solution.py:278
  276.1 10.6 %collective-permute-done.16 = bf16[192,2560]{1,0:T(8,128)(2,1)S(1)} collective-permute-done((bf16[192,2560]{1,0:T(8,128)(2,1)S(1)}, bf16[192,2560]{1,0:T(8,128)(2,1)S(1)}, u32[]{:S(2)}, u32[]{:S(2)}) %collective-permute-start.16) | collective-permute-done | bytes 983072 | tf_op jit(solution)/shard_map/ppermute | solution.py:776
  288.5 1.4 pad_maximum_fusion.1
  289.9 1.2 copy-done.15
  291.7 2.1 fusion
  293.8 1.3 collective-permute-start.18
  296.1 13.1 %collective-permute-done.18 = bf16[2,2,96,768]{3,2,1,0:T(8,128)(2,1)S(1)} collective-permute-done((bf16[2,2,96,768]{3,2,1,0:T(8,128)(2,1)S(1)}, bf16[2,2,96,768]{3,2,1,0:T(8,128)(2,1)S(1)}, u32[]{:S(2)}, u32[]{:S(2)}) %collective-permute-start.18) | collective-permute-done | bytes 589856 | tf_op jit(solution)/shard_map/ppermute | solution.py:776
  311.5 6.1 %collective-permute-done.19 = bf16[2,96,768]{2,1,0:T(8,128)(2,1)S(1)} collective-permute-done((bf16[2,96,768]{2,1,0:T(8,128)(2,1)S(1)}, bf16[2,96,768]{2,1,0:T(8,128)(2,1)S(1)}, u32[]{:S(2)}, u32[]{:S(2)}) %collective-permute-start.19) | collective-permute-done | bytes 294944 | tf_op jit(solution)/shard_map/ppermute | solution.py:776
  317.8 5.7 %collective-permute-start.20 = (bf16[96,768]{1,0:T(8,128)(2,1)S(1)}, bf16[96,768]{1,0:T(8,128)(2,1)S(1)}, u32[]{:S(2)}, u32[]{:S(2)}) collective-permute-start(bf16[96,768]{1,0:T(8,128)(2,1)S(1)} %slice_bitcast_fusion.17), channel_id=1, source_target_pairs={{0,3},{1,0},{2,1},{3,2},{4,7},{5,4},{6,5},{7,6},{8,11},{9,8},{10,9... | collective-permute-start | bytes 442376 | tf_op jit(solution)/shard_map/ppermute | solution.py:779
  323.6 1.5 collective-permute-start.25
  325.5 10.0 %token_grads.1 = (f32[512,768]{1,0:T(8,128)S(1)}, bf16[4,512,768]{2,1,0:T(8,128)(2,1)S(1)}) custom-call(s32[8]{0:T(128)S(1)} %concatenate.26.info, bf16[8,4,96,896]{3,2,1,0:T(8,128)(2,1)S(1)} %bitcast.142, bf16[3,2048,448]{2,1,0:T(8,128)(2,1)} %get-tuple-element.161.refs_0_, bf16[1,2048,448]{2,1,0:T(8,128)(2,1)S(1)} %copy-done.19, ...), custom_call_target="tpu_custom_call" | custom-call | flops 8589934592 | bytes 20971520 | tf_op jit(solution)/shard_map/token_grads/pallas_call | solution.py:351
  335.5 1.2 copy-done.12
  336.8 2.2 collective-permute-done.25
  339.0 7.0 %collective-permute-done.24 = bf16[96,768]{1,0:T(8,128)(2,1)S(1)} collective-permute-done((bf16[96,768]{1,0:T(8,128)(2,1)S(1)}, bf16[96,768]{1,0:T(8,128)(2,1)S(1)}, u32[]{:S(2)}, u32[]{:S(2)}) %collective-permute-start.24) | collective-permute-done | bytes 147488 | tf_op jit(solution)/shard_map/ppermute | solution.py:779
  346.2 1.9 pad_maximum_fusion.4
  348.9 1.3 collective-permute-start.26
  350.2 16.8 %collective-permute-done.26 = bf16[512,768]{1,0:T(8,128)(2,1)S(1)} collective-permute-done((bf16[512,768]{1,0:T(8,128)(2,1)S(1)}, bf16[512,768]{1,0:T(8,128)(2,1)S(1)}, u32[]{:S(2)}, u32[]{:S(2)}) %collective-permute-start.26) | collective-permute-done | bytes 786464 | tf_op jit(solution)/shard_map/ppermute | solution.py:881
  367.1 1.6 fusion.2
  368.6 1.3 collective-permute-start.29
  369.9 6.2 %collective-permute-start.27 = (bf16[512,768]{1,0:T(8,128)(2,1)}, bf16[512,768]{1,0:T(8,128)(2,1)}, u32[]{:S(2)}, u32[]{:S(2)}) collective-permute-start(bf16[512,768]{1,0:T(8,128)(2,1)} %get-tuple-element.209), channel_id=1, source_target_pairs={{0,1},{1,2},{2,3},{4,5},{5,6},{6,7},{8,9},{9,10},{10,11},{12,13},{... | collective-permute-start | bytes 2359304 | tf_op jit(solution)/shard_map/ppermute | solution.py:782
  376.2 11.7 %all-gather.11.cloned.1.call-done.gate.up.down.out_part.query.key.value.edge = bf16[768,3328]{1,0:T(8,128)(2,1)} async-done(((bf16[96,3328]{1,0:T(8,128)(2,1)}), bf16[768,3328]{1,0:T(8,128)(2,1)}) %all-gather.11.cloned.1.call-update) | async-done | bytes 5111824 | tf_op jit(solution)/shard_map/all_gather | solution.py:785
  387.8 8.4 %final_sums.1 = (f32[768,2,768]{2,1,0:T(2,128)}, f32[768,768]{1,0:T(8,128)}, f32[192,768]{1,0:T(8,128)}, f32[3,192,768]{2,1,0:T(8,128)}, f32[4,768]{1,0:T(4,128)}) custom-call(bf16[768,3328]{1,0:T(8,128)(2,1)} %all-gather.11.cloned.1.call-done.gate.up.down.out_part.query.key.value.edge, ...), custom_call_target="tpu_custom_call" | custom-call | flops 1048576 | bytes 15728640 | tf_op jit(solution)/shard_map/final_sums/pallas_call | solution.py:699
  396.2 1.5 slice_reduce_fusion
  397.7 2.9 add_bitcast_fusion
  (163 shorter events, 27.8 us)
Async XLA Ops:
  7.2 79.3 %all-gather.7.cloned.1.call-start = ((), (), s32[]{:S(2)}) async-start(), calls=%async_computation.2 | async-start | bytes 6193152 | tf_op jit(solution)/shard_map/all_gather | solution.py:785
  14.1 21.2 %copy-start.31 = (s32[1,24]{1,0:T(1,128)S(1)}, s32[1,24]{1,0:T(1,128)}, u32[]{:S(2)}) copy-start(s32[1,24]{1,0:T(1,128)} %param.12) | copy-start | bytes 292
  14.5 9.9 %collective-permute-start.2 = (bf16[96,896]{1,0:T(8,128)(2,1)S(1)}, bf16[96,896]{1,0:T(8,128)(2,1)S(1)}, u32[]{:S(2)}, u32[]{:S(2)}) collective-permute-start(bf16[96,896]{1,0:T(8,128)(2,1)S(1)} %pad_maximum_fusion.7), channel_id=1, source_target_pairs={{0,3},{1,0},{2,1},{3,2},{4,7},{5,4},{6,5},{7,6},{8,11},{9,8},{10,9... | collective-permute-start | bytes 516104 | tf_op jit(solution)/shard_map/ppermute | solution.py:779
  19.6 14.6 %collective-permute-start.1 = (bf16[96,896]{1,0:T(8,128)(2,1)S(1)}, bf16[96,896]{1,0:T(8,128)(2,1)S(1)}, u32[]{:S(2)}, u32[]{:S(2)}) collective-permute-start(bf16[96,896]{1,0:T(8,128)(2,1)S(1)} %pad_maximum_fusion.7), channel_id=1, source_target_pairs={{0,2},{1,3},{2,0},{3,1},{4,6},{5,7},{6,4},{7,5},{8,10},{9,11},{10,... | collective-permute-start | bytes 516104 | tf_op jit(solution)/shard_map/ppermute | solution.py:779
  19.6 14.6 %collective-permute-start = (bf16[96,896]{1,0:T(8,128)(2,1)S(1)}, bf16[96,896]{1,0:T(8,128)(2,1)S(1)}, u32[]{:S(2)}, u32[]{:S(2)}) collective-permute-start(bf16[96,896]{1,0:T(8,128)(2,1)S(1)} %pad_maximum_fusion.7), channel_id=1, source_target_pairs={{0,1},{1,2},{2,3},{3,0},{4,5},{5,6},{6,7},{7,4},{8,9},{9,10},{10,1... | collective-permute-start | bytes 516104 | tf_op jit(solution)/shard_map/ppermute | solution.py:779
  35.2 117.6 %all-gather.9.cloned.1.call-start = ((), (), s32[]{:S(2)}) async-start(), calls=%async_computation.3 | async-start | bytes 11943936 | tf_op jit(solution)/shard_map/all_gather | solution.py:785
  36.1 20.3 %collective-permute-start.5 = (bf16[96,2304]{1,0:T(8,128)(2,1)S(1)}, bf16[96,2304]{1,0:T(8,128)(2,1)S(1)}, u32[]{:S(2)}, u32[]{:S(2)}) collective-permute-start(bf16[96,2304]{1,0:T(8,128)(2,1)S(1)} %pad_maximum_fusion.6), channel_id=1, source_target_pairs={{0,3},{1,0},{2,1},{3,2},{4,7},{5,4},{6,5},{7,6},{8,11},{9,8},{10,9... | collective-permute-start | bytes 1327112 | tf_op jit(solution)/shard_map/ppermute | solution.py:779
  37.0 40.0 %collective-permute-start.4 = (bf16[96,2304]{1,0:T(8,128)(2,1)S(1)}, bf16[96,2304]{1,0:T(8,128)(2,1)}, u32[]{:S(2)}, u32[]{:S(2)}) collective-permute-start(bf16[96,2304]{1,0:T(8,128)(2,1)S(1)} %pad_maximum_fusion.6), channel_id=1, source_target_pairs={{0,2},{1,3},{2,0},{3,1},{4,6},{5,7},{6,4},{7,5},{8,10},{9,11},{10,... | collective-permute-start | bytes 1327112 | tf_op jit(solution)/shard_map/ppermute | solution.py:779
  39.0 38.0 %collective-permute-start.3 = (bf16[96,2304]{1,0:T(8,128)(2,1)S(1)}, bf16[96,2304]{1,0:T(8,128)(2,1)}, u32[]{:S(2)}, u32[]{:S(2)}) collective-permute-start(bf16[96,2304]{1,0:T(8,128)(2,1)S(1)} %pad_maximum_fusion.6), channel_id=1, source_target_pairs={{0,1},{1,2},{2,3},{3,0},{4,5},{5,6},{6,7},{7,4},{8,9},{9,10},{10,1... | collective-permute-start | bytes 1327112 | tf_op jit(solution)/shard_map/ppermute | solution.py:779
  50.7 3.7 copy-start.26
  79.4 266.8 %reduce-scatter.2.cloned.1.call-start = ((), (), s32[]{:S(2)}) async-start(), calls=%async_computation.1 | async-start | bytes 2457600 | tf_op jit(solution)/shard_map/reduce_scatter | solution.py:855
  79.4 20.3 %collective-permute-start.7 = (bf16[512,768]{1,0:T(8,128)(2,1)}, bf16[512,768]{1,0:T(8,128)(2,1)}, u32[]{:S(2)}, u32[]{:S(2)}) collective-permute-start(bf16[512,768]{1,0:T(8,128)(2,1)} %bitcast.refs_0_), channel_id=1, source_target_pairs={{1,0},{2,1},{3,2},{5,4},{6,5},{7,6},{9,8},{10,9},{11,10},{13,12},{... | collective-permute-start | bytes 2359304 | tf_op jit(solution)/shard_map/ppermute | solution.py:782
  80.7 20.1 %collective-permute-start.6 = (bf16[512,768]{1,0:T(8,128)(2,1)}, bf16[512,768]{1,0:T(8,128)(2,1)}, u32[]{:S(2)}, u32[]{:S(2)}) collective-permute-start(bf16[512,768]{1,0:T(8,128)(2,1)} %bitcast.refs_0_), channel_id=1, source_target_pairs={{0,1},{1,2},{2,3},{4,5},{5,6},{6,7},{8,9},{9,10},{10,11},{12,13},{... | collective-permute-start | bytes 2359304 | tf_op jit(solution)/shard_map/ppermute | solution.py:782
  86.5 3.2 copy-start.2
  89.8 17.8 %copy-start.27 = (f32[768]{0:T(1024)S(1)}, f32[768]{0:T(1024)}, u32[]{:S(2)}) copy-start(f32[768]{0:T(1024)} %param.15) | copy-start | bytes 9220
  89.8 18.4 %copy-start.28 = (f32[768]{0:T(1024)S(1)}, f32[768]{0:T(1024)}, u32[]{:S(2)}) copy-start(f32[768]{0:T(1024)} %param.16) | copy-start | bytes 9220
  89.8 19.0 %copy-start.29 = (f32[768]{0:T(1024)S(1)}, f32[768]{0:T(1024)}, u32[]{:S(2)}) copy-start(f32[768]{0:T(1024)} %param.19) | copy-start | bytes 9220
  89.8 19.6 %copy-start.30 = (f32[768]{0:T(1024)S(1)}, f32[768]{0:T(1024)}, u32[]{:S(2)}) copy-start(f32[768]{0:T(1024)} %param.20) | copy-start | bytes 9220
  100.8 25.6 %collective-permute-start.9 = (bf16[512,768]{1,0:T(8,128)(2,1)}, bf16[512,768]{1,0:T(8,128)(2,1)}, u32[]{:S(2)}, u32[]{:S(2)}) collective-permute-start(bf16[512,768]{1,0:T(8,128)(2,1)} %collective-permute-done.6.refs_0_.refs_3_), channel_id=1, source_target_pairs={{0,1},{1,2},{2,3},{4,5},{5,6},{6,7},{8,9},{9,10},{10,11},{12,13},{... | collective-permute-start | bytes 2359304 | tf_op jit(solution)/shard_map/ppermute | solution.py:782
  106.1 20.3 %collective-permute-start.8 = (bf16[512,768]{1,0:T(8,128)(2,1)}, bf16[512,768]{1,0:T(8,128)(2,1)}, u32[]{:S(2)}, u32[]{:S(2)}) collective-permute-start(bf16[512,768]{1,0:T(8,128)(2,1)} %collective-permute-done.7.refs_0_.refs_1_), channel_id=1, source_target_pairs={{1,0},{2,1},{3,2},{5,4},{6,5},{7,6},{9,8},{10,9},{11,10},{13,12},{... | collective-permute-start | bytes 2359304 | tf_op jit(solution)/shard_map/ppermute | solution.py:782
  110.0 3.6 copy-start.3
  127.7 5.5 %copy-start.10 = (bf16[512,768]{1,0:T(8,128)(2,1)}, bf16[512,768]{1,0:T(8,128)(2,1)S(1)}, u32[]{:S(2)}) copy-start(bf16[512,768]{1,0:T(8,128)(2,1)S(1)} %broadcast_select_fusion.refs_0_.refs_2_) | copy-start | bytes 2359300
  185.8 1.2 copy-start.5
  187.0 1.1 copy-start.7
  188.2 1.1 copy-start.8
  195.8 6.8 %collective-permute-start.10 = (bf16[2,384,2560]{2,1,0:T(8,128)(2,1)S(1)}, bf16[2,384,2560]{2,1,0:T(8,128)(2,1)S(1)}, u32[]{:S(2)}, u32[]{:S(2)}) collective-permute-start(bf16[2,384,2560]{2,1,0:T(8,128)(2,1)S(1)} %wgrad.4), channel_id=1, source_target_pairs={{0,4},{4,0},{8,12},{12,8},{16,20},{20,16},{24,28},{28,24},{1,5},{5... | collective-permute-start | bytes 11796488 | tf_op jit(solution)/shard_map/ppermute | solution.py:776
  200.3 7.9 %collective-permute-start.11 = (bf16[2,384,2560]{2,1,0:T(8,128)(2,1)S(1)}, bf16[2,384,2560]{2,1,0:T(8,128)(2,1)S(1)}, u32[]{:S(2)}, u32[]{:S(2)}) collective-permute-start(bf16[2,384,2560]{2,1,0:T(8,128)(2,1)S(1)} %wgrad.5), channel_id=1, source_target_pairs={{0,4},{4,0},{8,12},{12,8},{16,20},{20,16},{24,28},{28,24},{1,5},{5... | collective-permute-start | bytes 11796488 | tf_op jit(solution)/shard_map/ppermute | solution.py:776
  207.5 8.0 %copy-start.6 = (bf16[4,512,192]{2,1,0:T(8,128)(2,1)S(1)}, bf16[4,512,192]{2,1,0:T(8,128)(2,1)}, u32[]{:S(2)}) copy-start(bf16[4,512,192]{2,1,0:T(8,128)(2,1)} %copy-done.4) | copy-start | bytes 2359300
  207.5 8.0 %copy-start.11 = (bf16[512,768]{1,0:T(8,128)(2,1)S(1)}, bf16[512,768]{1,0:T(8,128)(2,1)}, u32[]{:S(2)}) copy-start(bf16[512,768]{1,0:T(8,128)(2,1)} %copy-done.10) | copy-start | bytes 2359300
  207.5 8.0 %copy-start.17 = (bf16[4,3,512,256]{3,2,1,0:T(8,128)(2,1)S(1)}, bf16[4,3,512,256]{3,2,1,0:T(8,128)(2,1)}, u32[]{:S(2)}) copy-start(bf16[4,3,512,256]{3,2,1,0:T(8,128)(2,1)} %get-tuple-element.115.qh.refs_7_) | copy-start | bytes 9437188
  207.5 8.0 %copy-start.22 = (bf16[4,512,192]{2,1,0:T(8,128)(2,1)S(1)}, bf16[4,512,192]{2,1,0:T(8,128)(2,1)}, u32[]{:S(2)}) copy-start(bf16[4,512,192]{2,1,0:T(8,128)(2,1)} %get-tuple-element.175.refs_12_) | copy-start | bytes 2359300
  207.5 50.8 %collective-permute-start.13 = (bf16[2,192,2560]{2,1,0:T(8,128)(2,1)S(1)}, bf16[2,192,2560]{2,1,0:T(8,128)(2,1)}, u32[]{:S(2)}, u32[]{:S(2)}) collective-permute-start(bf16[2,192,2560]{2,1,0:T(8,128)(2,1)S(1)} %get-tuple-element.157), channel_id=1, source_target_pairs={{0,16},{4,20},{8,24},{12,28},{16,0},{20,4},{24,8},{28,12},{1,17},{... | collective-permute-start | bytes 5898248 | tf_op jit(solution)/shard_map/ppermute | solution.py:776
  213.4 34.6 %collective-permute-start.14 = (bf16[192,2560]{1,0:T(8,128)(2,1)S(1)}, bf16[192,2560]{1,0:T(8,128)(2,1)S(1)}, u32[]{:S(2)}, u32[]{:S(2)}) collective-permute-start(bf16[192,2560]{1,0:T(8,128)(2,1)S(1)} %get-tuple-element.163), channel_id=1, source_target_pairs={{0,8},{4,12},{8,0},{12,4},{16,24},{20,28},{24,16},{28,20},{1,9},{5... | collective-permute-start | bytes 2949128 | tf_op jit(solution)/shard_map/ppermute | solution.py:776
  214.2 44.1 %collective-permute-start.12 = (bf16[192,2560]{1,0:T(8,128)(2,1)S(1)}, bf16[192,2560]{1,0:T(8,128)(2,1)S(1)}, u32[]{:S(2)}, u32[]{:S(2)}) collective-permute-start(bf16[192,2560]{1,0:T(8,128)(2,1)S(1)} %get-tuple-element.162), channel_id=1, source_target_pairs={{0,8},{4,12},{8,0},{12,4},{16,24},{20,28},{24,16},{28,20},{1,9},{5... | collective-permute-start | bytes 2949128 | tf_op jit(solution)/shard_map/ppermute | solution.py:776
  248.0 14.0 %copy-start.20 = (bf16[3,512,256]{2,1,0:T(8,128)(2,1)}, bf16[3,512,256]{2,1,0:T(8,128)(2,1)S(1)}, u32[]{:S(2)}) copy-start(bf16[3,512,256]{2,1,0:T(8,128)(2,1)S(1)} %get-tuple-element.179.refs_2_) | copy-start | bytes 2359300
  259.9 27.4 %collective-permute-start.17 = (bf16[4,3,96,768]{3,2,1,0:T(8,128)(2,1)S(1)}, bf16[4,3,96,768]{3,2,1,0:T(8,128)(2,1)S(1)}, u32[]{:S(2)}, u32[]{:S(2)}) collective-permute-start(bf16[4,3,96,768]{3,2,1,0:T(8,128)(2,1)S(1)} %slice_bitcast_fusion.1), channel_id=1, source_target_pairs={{0,4},{4,0},{8,12},{12,8},{16,20},{20,16},{24,28},{28,24},{1,5},{5... | collective-permute-start | bytes 5308424 | tf_op jit(solution)/shard_map/ppermute | solution.py:776
  262.5 24.2 %collective-permute-start.16 = (bf16[192,2560]{1,0:T(8,128)(2,1)S(1)}, bf16[192,2560]{1,0:T(8,128)(2,1)S(1)}, u32[]{:S(2)}, u32[]{:S(2)}) collective-permute-start(bf16[192,2560]{1,0:T(8,128)(2,1)S(1)} %slice_bitcast_fusion.4), channel_id=1, source_target_pairs={{0,8},{4,12},{8,0},{12,4},{16,24},{20,28},{24,16},{28,20},{1,9},{5... | collective-permute-start | bytes 2949128 | tf_op jit(solution)/shard_map/ppermute | solution.py:776
  263.4 23.9 %collective-permute-start.15 = (bf16[192,2560]{1,0:T(8,128)(2,1)S(1)}, bf16[192,2560]{1,0:T(8,128)(2,1)S(1)}, u32[]{:S(2)}, u32[]{:S(2)}) collective-permute-start(bf16[192,2560]{1,0:T(8,128)(2,1)S(1)} %add_convert_fusion.2), channel_id=1, source_target_pairs={{0,16},{4,20},{8,24},{12,28},{16,0},{20,4},{24,8},{28,12},{1,17},{... | collective-permute-start | bytes 2949128 | tf_op jit(solution)/shard_map/ppermute | solution.py:776
  276.1 11.6 %copy-start.14 = (bf16[8,1,96,768]{3,2,1,0:T(8,128)(2,1)}, bf16[8,1,96,768]{3,2,1,0:T(8,128)(2,1)S(1)}, u32[]{:S(2)}) copy-start(bf16[8,1,96,768]{3,2,1,0:T(8,128)(2,1)S(1)} %get-tuple-element.183) | copy-start | bytes 3538948
  276.1 11.6 %copy-start.18 = (bf16[1,2048,448]{2,1,0:T(8,128)(2,1)}, bf16[1,2048,448]{2,1,0:T(8,128)(2,1)S(1)}, u32[]{:S(2)}) copy-start(bf16[1,2048,448]{2,1,0:T(8,128)(2,1)S(1)} %get-tuple-element.178.refs_1_) | copy-start | bytes 5505028
  287.3 1.2 copy-start.23
  289.9 1.3 copy-start.15
  289.9 1.8 copy-start.24
  289.9 98.0 %all-gather.11.cloned.1.call-start = ((), (), s32[]{:S(2)}) async-start(), calls=%async_computation.4 | async-start | bytes 5750784 | tf_op jit(solution)/shard_map/all_gather | solution.py:785
  291.2 4.0 collective-permute-start.21
  291.7 33.8 %slice-start = ((s8[5505024]{0:T(1024)(128)(4,1)}), s8[4194304]{0:T(1024)(128)(4,1)S(1)}, s32[]{:S(2)}) async-start(s8[5505024]{0:T(1024)(128)(4,1)} %bitcast.140), calls=%async_computation.5 | async-start | bytes 8388608
  293.8 15.4 %collective-permute-start.18 = (bf16[2,2,96,768]{3,2,1,0:T(8,128)(2,1)S(1)}, bf16[2,2,96,768]{3,2,1,0:T(8,128)(2,1)S(1)}, u32[]{:S(2)}, u32[]{:S(2)}) collective-permute-start(bf16[2,2,96,768]{3,2,1,0:T(8,128)(2,1)S(1)} %slice_bitcast_fusion.8), channel_id=1, source_target_pairs={{0,8},{4,12},{8,0},{12,4},{16,24},{20,28},{24,16},{28,20},{1,9},{5... | collective-permute-start | bytes 1769480 | tf_op jit(solution)/shard_map/ppermute | solution.py:776
  295.3 30.1 %slice-start.1 = ((s8[5505024]{0:T(1024)(128)(4,1)}), s8[1310720]{0:T(1024)(128)(4,1)S(1)}, s32[]{:S(2)}) async-start(s8[5505024]{0:T(1024)(128)(4,1)} %bitcast.140), calls=%async_computation.6 | async-start | bytes 2621440
  295.4 15.1 %collective-permute-start.22 = (bf16[2,2,96,768]{3,2,1,0:T(8,128)(2,1)S(1)}, bf16[2,2,96,768]{3,2,1,0:T(8,128)(2,1)S(1)}, u32[]{:S(2)}, u32[]{:S(2)}) collective-permute-start(bf16[2,2,96,768]{3,2,1,0:T(8,128)(2,1)S(1)} %fusion.9), channel_id=1, source_target_pairs={{0,16},{4,20},{8,24},{12,28},{16,0},{20,4},{24,8},{28,12},{1,17},{... | collective-permute-start | bytes 1769480 | tf_op jit(solution)/shard_map/ppermute | solution.py:776
  309.4 8.3 %collective-permute-start.19 = (bf16[2,96,768]{2,1,0:T(8,128)(2,1)S(1)}, bf16[2,96,768]{2,1,0:T(8,128)(2,1)S(1)}, u32[]{:S(2)}, u32[]{:S(2)}) collective-permute-start(bf16[2,96,768]{2,1,0:T(8,128)(2,1)S(1)} %slice_bitcast_fusion.12), channel_id=1, source_target_pairs={{0,16},{4,20},{8,24},{12,28},{16,0},{20,4},{24,8},{28,12},{1,17},{... | collective-permute-start | bytes 884744 | tf_op jit(solution)/shard_map/ppermute | solution.py:776
  310.6 14.9 %copy-start.19 = (bf16[1,2048,448]{2,1,0:T(8,128)(2,1)S(1)}, bf16[1,2048,448]{2,1,0:T(8,128)(2,1)}, u32[]{:S(2)}) copy-start(bf16[1,2048,448]{2,1,0:T(8,128)(2,1)} %copy-done.18) | copy-start | bytes 5505028
  310.6 14.8 %copy-start.21 = (bf16[3,512,256]{2,1,0:T(8,128)(2,1)S(1)}, bf16[3,512,256]{2,1,0:T(8,128)(2,1)}, u32[]{:S(2)}) copy-start(bf16[3,512,256]{2,1,0:T(8,128)(2,1)} %copy-done.20) | copy-start | bytes 2359300
  310.7 12.8 %collective-permute-start.23 = (bf16[2,96,768]{2,1,0:T(8,128)(2,1)S(1)}, bf16[2,96,768]{2,1,0:T(8,128)(2,1)S(1)}, u32[]{:S(2)}, u32[]{:S(2)}) collective-permute-start(bf16[2,96,768]{2,1,0:T(8,128)(2,1)S(1)} %slice_bitcast_fusion.10), channel_id=1, source_target_pairs={{0,8},{4,12},{8,0},{12,4},{16,24},{20,28},{24,16},{28,20},{1,9},{5... | collective-permute-start | bytes 884744 | tf_op jit(solution)/shard_map/ppermute | solution.py:776
  317.8 19.1 %collective-permute-start.20 = (bf16[96,768]{1,0:T(8,128)(2,1)S(1)}, bf16[96,768]{1,0:T(8,128)(2,1)S(1)}, u32[]{:S(2)}, u32[]{:S(2)}) collective-permute-start(bf16[96,768]{1,0:T(8,128)(2,1)S(1)} %slice_bitcast_fusion.17), channel_id=1, source_target_pairs={{0,3},{1,0},{2,1},{3,2},{4,7},{5,4},{6,5},{7,6},{8,11},{9,8},{10,9... | collective-permute-start | bytes 442376 | tf_op jit(solution)/shard_map/ppermute | solution.py:779
  323.6 15.4 %collective-permute-start.25 = (bf16[96,768]{1,0:T(8,128)(2,1)S(1)}, bf16[96,768]{1,0:T(8,128)(2,1)S(1)}, u32[]{:S(2)}, u32[]{:S(2)}) collective-permute-start(bf16[96,768]{1,0:T(8,128)(2,1)S(1)} %get-tuple-element.217), channel_id=1, source_target_pairs={{0,1},{1,2},{2,3},{3,0},{4,5},{5,6},{6,7},{7,4},{8,9},{9,10},{10,1... | collective-permute-start | bytes 442376 | tf_op jit(solution)/shard_map/ppermute | solution.py:779
  325.1 21.0 %collective-permute-start.24 = (bf16[96,768]{1,0:T(8,128)(2,1)S(1)}, bf16[96,768]{1,0:T(8,128)(2,1)S(1)}, u32[]{:S(2)}, u32[]{:S(2)}) collective-permute-start(bf16[96,768]{1,0:T(8,128)(2,1)S(1)} %get-tuple-element.218), channel_id=1, source_target_pairs={{0,2},{1,3},{2,0},{3,1},{4,6},{5,7},{6,4},{7,5},{8,10},{9,11},{10,... | collective-permute-start | bytes 442376 | tf_op jit(solution)/shard_map/ppermute | solution.py:779
  335.5 1.2 copy-start.12
  348.2 2.1 collective-permute-start.28
  348.9 18.2 %collective-permute-start.26 = (bf16[512,768]{1,0:T(8,128)(2,1)S(1)}, bf16[512,768]{1,0:T(8,128)(2,1)S(1)}, u32[]{:S(2)}, u32[]{:S(2)}) collective-permute-start(bf16[512,768]{1,0:T(8,128)(2,1)S(1)} %slice_bitcast_fusion.5), channel_id=1, source_target_pairs={{0,1},{1,2},{4,5},{5,6},{8,9},{9,10},{12,13},{13,14},{16,17},{17,1... | collective-permute-start | bytes 2359304 | tf_op jit(solution)/shard_map/ppermute | solution.py:881
  368.6 27.6 %collective-permute-start.29 = (bf16[512,768]{1,0:T(8,128)(2,1)}, bf16[512,768]{1,0:T(8,128)(2,1)}, u32[]{:S(2)}, u32[]{:S(2)}) collective-permute-start(bf16[512,768]{1,0:T(8,128)(2,1)} %get-tuple-element.208), channel_id=1, source_target_pairs={{1,0},{2,1},{3,2},{5,4},{6,5},{7,6},{9,8},{10,9},{11,10},{13,12},{... | collective-permute-start | bytes 2359304 | tf_op jit(solution)/shard_map/ppermute | solution.py:782
  369.9 27.8 %copy-start.13 = (f32[512,768]{1,0:T(8,128)S(1)}, f32[512,768]{1,0:T(8,128)}, u32[]{:S(2)}) copy-start(f32[512,768]{1,0:T(8,128)} %copy-done.12) | copy-start | bytes 4718596
  369.9 27.8 %copy-start.25 = (f32[512,768]{1,0:T(8,128)S(1)}, f32[512,768]{1,0:T(8,128)}, u32[]{:S(2)}) copy-start(f32[512,768]{1,0:T(8,128)} %get-tuple-element.144) | copy-start | bytes 4718596
  369.9 26.3 %collective-permute-start.27 = (bf16[512,768]{1,0:T(8,128)(2,1)}, bf16[512,768]{1,0:T(8,128)(2,1)}, u32[]{:S(2)}, u32[]{:S(2)}) collective-permute-start(bf16[512,768]{1,0:T(8,128)(2,1)} %get-tuple-element.209), channel_id=1, source_target_pairs={{0,1},{1,2},{2,3},{4,5},{5,6},{6,7},{8,9},{9,10},{10,11},{12,13},{... | collective-permute-start | bytes 2359304 | tf_op jit(solution)/shard_map/ppermute | solution.py:782
  397.7 2.9 copy-start.1
  (4 other events, 3.9 us)
Sparse Core Ops, SparseCore 0:
  35.3 42.3 all-gather.6
  80.1 63.8 all-gather.8
  290.0 52.8 reduce-scatter.1
  348.2 39.5 all-gather.10

commit v6 on v5

--- a/solution.py
+++ b/solution.py
@@ -577,7 +577,7 @@
             pltpu.SemaphoreType.DMA,
             pltpu.SemaphoreType.DMA((2, 2)),
         ],
-        compiler_params=pltpu.CompilerParams(vmem_limit_bytes=60 << 20),
+        compiler_params=pltpu.CompilerParams(vmem_limit_bytes=50 << 20),
         cost_estimate=pl.CostEstimate(flops=16 << 30, bytes_accessed=30 << 20, transcendentals=3 << 20),
         name="ffn_layer",
     )(own, cot, *norms, rel, w1, w_own, w2)

time: 416 us -> 409 us (0.983)
  local copies, waits for them, and re-layouts: 37.8 us -> 30.6 us
    unnamed x71 -> x65, local copies, waits for them, and re-layouts: 18.5 us -> 13.6 us
  transfers between devices with their start and end apart: 34 -> 34, of which waited for: 18 -> 16; matrix products, arithmetic and copies ran while one was open for 7% -> 6% of each run, Pallas kernels for 30% -> 31%
where the time goes in v6:
time: 409 us; the launch traced here: 401 us
  Pallas kernels  160 us (39%)
  waiting for transfers between devices  118 us (29%)
  starting transfers between devices  52.8 us (13%)
  local copies, waits for them, and re-layouts  30.6 us (7%)
  other arithmetic  24.9 us (6%)
  between operations  15 us (4%)
    pallas_call x2, Pallas kernels, attn_bwd(): pl.pallas_call(functools.partial(attn_bwd_kernel, docs=docs, heads=heads,...  44.7 us
    ppermute x9, waiting for transfers between devices, shift(): return lax.ppermute(array, 'tensor', rotate_axis(tp_size, step))  42.4 us
    ppermute x13, waiting for transfers between devices, flip(): return lax.ppermute(array, 'dp', flip_axis(dp_size, bit))  42.2 us
    pallas_call x1, Pallas kernels, ffn_layer(): pl.pallas_call(functools.partial(ffn_kernel, slots=slots, pieces=pieces,...  32.1 us
    pallas_call x4, Pallas kernels, project(): pl.pallas_call(functools.partial(project_kernel, docs=docs, heads=heads,...  25.8 us
    ppermute x6, starting transfers between devices, along(): return lax.ppermute(array, 'tensor', line_axis(tp_size, step))  21 us
    pallas_call x4, Pallas kernels, wgrad(): pl.pallas_call(functools.partial(wgrad_kernel, slots=slots, share=share,...  20.6 us
    ppermute x9, starting transfers between devices, shift(): return lax.ppermute(array, 'tensor', rotate_axis(tp_size, step))  19.3 us
  transfers between devices with their start and end apart: 34, of which 16 were waited for; matrix products, arithmetic and copies ran while one was open for 6% of the time, Pallas kernels for 31%

profile of v6, /device:TPU:0, one launch (start us, length us, event | category | flops | bytes accessed | tf_op | source)
XLA Modules:
  0.0 401.4 jit_solution(2126011944059768847)
XLA Ops:
  10.8 3.0 constant_dynamic-slice_fusion.2
  14.5 5.1 %collective-permute-start.2 = (bf16[96,896]{1,0:T(8,128)(2,1)S(1)}, bf16[96,896]{1,0:T(8,128)(2,1)S(1)}, u32[]{:S(2)}, u32[]{:S(2)}) collective-permute-start(bf16[96,896]{1,0:T(8,128)(2,1)S(1)} %pad_maximum_fusion.7), channel_id=1, source_target_pairs={{0,3},{1,0},{2,1},{3,2},{4,7},{5,4},{6,5},{7,6},{8,11},{9,8},{10,9... | collective-permute-start | bytes 516104 | tf_op jit(solution)/shard_map/ppermute | solution.py:779
  20.6 3.8 collective-permute-done.2
  24.5 9.8 %collective-permute-done.1 = bf16[96,896]{1,0:T(8,128)(2,1)S(1)} collective-permute-done((bf16[96,896]{1,0:T(8,128)(2,1)S(1)}, bf16[96,896]{1,0:T(8,128)(2,1)S(1)}, u32[]{:S(2)}, u32[]{:S(2)}) %collective-permute-start.1) | collective-permute-done | bytes 172064 | tf_op jit(solution)/shard_map/ppermute | solution.py:779
  37.0 2.0 collective-permute-start.4
  39.0 1.9 collective-permute-start.3
  41.0 5.6 %copy.117 = bf16[768,2,768]{0,2,1:T(8,128)(2,1)S(1)} copy(bf16[768,2,768]{2,1,0:T(2,128)(2,1)} %param.17) | data formatting | bytes 4718592 | tf_op jit(solution)/shard_map/optimization_barrier | solution.py:738
  47.6 1.3 fusion.19
  48.9 1.4 concatenate.26.info
  50.7 3.7 multiply_sine_fusion
  54.4 2.0 pad_maximum_fusion
  56.4 20.6 %collective-permute-done.4 = bf16[96,2304]{1,0:T(8,128)(2,1)} collective-permute-done((bf16[96,2304]{1,0:T(8,128)(2,1)S(1)}, bf16[96,2304]{1,0:T(8,128)(2,1)}, u32[]{:S(2)}, u32[]{:S(2)}) %collective-permute-start.4) | collective-permute-done | bytes 442400 | tf_op jit(solution)/shard_map/ppermute | solution.py:779
  77.0 2.3 pad_maximum_fusion.2
  79.4 1.3 collective-permute-start.7
  80.7 5.5 %collective-permute-start.6 = (bf16[512,768]{1,0:T(8,128)(2,1)}, bf16[512,768]{1,0:T(8,128)(2,1)}, u32[]{:S(2)}, u32[]{:S(2)}) collective-permute-start(bf16[512,768]{1,0:T(8,128)(2,1)} %bitcast.refs_0_), channel_id=1, source_target_pairs={{0,1},{1,2},{2,3},{4,5},{5,6},{6,7},{8,9},{9,10},{10,11},{12,13},{... | collective-permute-start | bytes 2359304 | tf_op jit(solution)/shard_map/ppermute | solution.py:782
  86.6 3.2 copy-done.2
  89.8 7.3 %project.4 = (bf16[4,4,512,256]{3,2,1,0:T(8,128)(2,1)}, bf16[4,4,512,192]{3,2,1,0:T(8,128)(2,1)}, bf16[4,4,240,512]{3,2,1,0:T(8,128)(2,1)}, bf16[4,3,512,256]{3,2,1,0:T(8,128)(2,1)}) custom-call(bf16[512,768]{1,0:T(8,128)(2,1)} %bitcast.refs_0_, bf16[8,4,96,896]{3,2,1,0:T(8,128)(2,1)S(1)} %bitcast.136, f32[2048,128]{1,0:T(8,128)S(1)} %get-tuple-element.113.refs_2_.refs_4_, ...), custom_call_target="tpu_custom_call" | custom-call | flops 2147483648 | bytes 8388608 | tf_op jit(solution)/shard_map/project/pallas_call | solution.py:112
  97.2 2.5 collective-permute-done.7.refs_0_.refs_1_
  100.8 5.3 %collective-permute-start.9 = (bf16[512,768]{1,0:T(8,128)(2,1)}, bf16[512,768]{1,0:T(8,128)(2,1)}, u32[]{:S(2)}, u32[]{:S(2)}) collective-permute-start(bf16[512,768]{1,0:T(8,128)(2,1)} %collective-permute-done.6.refs_0_.refs_3_), channel_id=1, source_target_pairs={{0,1},{1,2},{2,3},{4,5},{5,6},{6,7},{8,9},{9,10},{10,11},{12,13},{... | collective-permute-start | bytes 2359304 | tf_op jit(solution)/shard_map/ppermute | solution.py:782
  106.1 1.5 collective-permute-start.8
  107.7 2.6 copy-done.3
  110.2 6.5 %project.5 = (bf16[4,4,512,256]{3,2,1,0:T(8,128)(2,1)}, bf16[4,4,512,192]{3,2,1,0:T(8,128)(2,1)}, bf16[4,4,240,512]{3,2,1,0:T(8,128)(2,1)}) custom-call(bf16[512,768]{1,0:T(8,128)(2,1)} %collective-permute-done.7.refs_0_.refs_1_, bf16[8,4,96,896]{3,2,1,0:T(8,128)(2,1)S(1)} %bitcast.137, ...), custom_call_target="tpu_custom_call", output_to_operand_aliasing={{0}: (5, {}), {1}: (6, {}), {2}: (7, {})} | custom-call | flops 2147483648 | bytes 8388608 | tf_op jit(solution)/shard_map/project/pallas_call | solution.py:112
  116.8 6.5 %project.6 = (bf16[4,4,512,256]{3,2,1,0:T(8,128)(2,1)}, bf16[4,4,512,192]{3,2,1,0:T(8,128)(2,1)}, bf16[4,4,240,512]{3,2,1,0:T(8,128)(2,1)}) custom-call(bf16[512,768]{1,0:T(8,128)(2,1)} %collective-permute-done.6.refs_0_.refs_3_, bf16[8,4,96,896]{3,2,1,0:T(8,128)(2,1)S(1)} %bitcast.138, ...), custom_call_target="tpu_custom_call", output_to_operand_aliasing={{0}: (5, {}), {1}: (6, {}), {2}: (7, {})} | custom-call | flops 2147483648 | bytes 8388608 | tf_op jit(solution)/shard_map/project/pallas_call | solution.py:112
  123.2 1.7 collective-permute-done.8
  124.9 1.2 broadcast_select_fusion.refs_0_.refs_2_
  126.1 5.4 %project.7 = (bf16[4,4,512,256]{3,2,1,0:T(8,128)(2,1)}, bf16[4,4,512,192]{3,2,1,0:T(8,128)(2,1)}, bf16[4,4,240,512]{3,2,1,0:T(8,128)(2,1)}) custom-call(bf16[512,768]{1,0:T(8,128)(2,1)S(1)} %broadcast_select_fusion.refs_0_.refs_2_, bf16[8,4,96,896]{3,2,1,0:T(8,128)(2,1)S(1)} %bitcast.139, ...), custom_call_target="tpu_custom_call", output_to_operand_aliasing={{0}: (5, {}), {1}: (6, {}), {2}: (7, {})} | custom-call | flops 2147483648 | bytes 8388608 | tf_op jit(solution)/shard_map/project/pallas_call | solution.py:112
  131.6 18.7 %attn_fwd.1 = (f32[4,8,512]{2,1,0:T(8,128)S(1)}, bf16[4,512,192]{2,1,0:T(8,128)(2,1)S(1)}) custom-call(s32[8]{0:T(128)S(1)} %concatenate.26.info, s32[2048,1]{1,0:T(8,128)S(1)} %copy.123.refs_4_.seg.refs_6_, bf16[4,3,512,256]{3,2,1,0:T(8,128)(2,1)} %get-tuple-element.115.qh.refs_7_, bf16[4,4,512,256]{3,2,1,0:T(8,128)(2,1)} %get-tuple-element.136.ka, ...), custom_call_target="tpu_custom_call" | custom-call | flops 12884901888 | bytes 12582912 | tf_op jit(solution)/shard_map/attn_fwd/pallas_call | solution.py:171
  152.4 32.1 %ffn_layer.1 = (bf16[512,768]{1,0:T(8,128)(2,1)}, f32[512,768]{1,0:T(8,128)}, bf16[512,768]{1,0:T(8,128)(2,1)S(1)}, bf16[512,768]{1,0:T(8,128)(2,1)S(1)}, bf16[7...) custom-call(bf16[512,768]{1,0:T(8,128)(2,1)} %bitcast.refs_0_, ...), custom_call_target="tpu_custom_call" | custom-call | flops 17179869184 | bytes 31457280 | tf_op jit(solution)/shard_map/ffn_layer/pallas_call | solution.py:557
  184.6 4.5 %wgrad.4 = bf16[2,384,2560]{2,1,0:T(8,128)(2,1)S(1)} custom-call(s32[2]{0:T(128)S(1)} %get-tuple-element.158.refs_0_, bf16[512,3072]{1,0:T(8,128)(2,1)} %get-tuple-element.148.refs_1_, bf16[512,3072]{1,0:T(8,128)(2,1)} %get-tuple-element.149.refs_2_, bf16[512,3072]{1,0:T(8,128)(2,1)} %get-tuple-element.150.refs_3_, ...), custom_call_target="tpu_custom_call" | custom-call | flops 2147483648 | bytes 10485760 | tf_op jit(solution)/shard_map/wgrad/pallas_call | solution.py:649
  189.1 4.5 %wgrad.5 = bf16[2,384,2560]{2,1,0:T(8,128)(2,1)S(1)} custom-call(s32[2]{0:T(128)S(1)} %get-tuple-element.158.refs_0_, bf16[512,3072]{1,0:T(8,128)(2,1)} %get-tuple-element.148.refs_1_, bf16[512,3072]{1,0:T(8,128)(2,1)} %get-tuple-element.149.refs_2_, bf16[512,3072]{1,0:T(8,128)(2,1)} %get-tuple-element.150.refs_3_, ...), custom_call_target="tpu_custom_call" | custom-call | flops 2147483648 | bytes 10485760 | tf_op jit(solution)/shard_map/wgrad/pallas_call | solution.py:649
  194.2 1.7 collective-permute-done.10.refs_9_
  195.9 5.8 %wgrad.6 = (bf16[192,2560]{1,0:T(8,128)(2,1)S(1)}, bf16[192,2560]{1,0:T(8,128)(2,1)S(1)}, bf16[2,192,2560]{2,1,0:T(8,128)(2,1)}) custom-call(s32[2]{0:T(128)S(1)} %get-tuple-element.158.refs_0_, bf16[512,3072]{1,0:T(8,128)(2,1)} %get-tuple-element.148.refs_1_, bf16[512,3072]{1,0:T(8,128)(2,1)} %get-tuple-element.149.refs_2_, ...), custom_call_target="tpu_custom_call" | custom-call | flops 2147483648 | bytes 10485760 | tf_op jit(solution)/shard_map/wgrad/pallas_call | solution.py:649
  201.8 5.8 %wgrad.7 = (bf16[192,2560]{1,0:T(8,128)(2,1)S(1)}, bf16[192,2560]{1,0:T(8,128)(2,1)}, bf16[2,192,2560]{2,1,0:T(8,128)(2,1)S(1)}) custom-call(s32[2]{0:T(128)S(1)} %get-tuple-element.158.refs_0_, bf16[512,3072]{1,0:T(8,128)(2,1)} %get-tuple-element.148.refs_1_, bf16[512,3072]{1,0:T(8,128)(2,1)} %get-tuple-element.149.refs_2_, ...), custom_call_target="tpu_custom_call" | custom-call | flops 2147483648 | bytes 10485760 | tf_op jit(solution)/shard_map/wgrad/pallas_call | solution.py:649
  207.6 2.1 collective-permute-start.14
  209.7 32.5 %attn_bwd.2 = (bf16[8,3,96,768]{3,2,1,0:T(8,128)(2,1)}, bf16[3,2048,448]{2,1,0:T(8,128)(2,1)}, bf16[3,512,256]{2,1,0:T(8,128)(2,1)S(1)}) custom-call(s32[8]{0:T(128)S(1)} %concatenate.26.info, bf16[512,768]{1,0:T(8,128)(2,1)} %bitcast.refs_0_, bf16[512,768]{1,0:T(8,128)(2,1)} %collective-permute-done.7.refs_0_.refs_1_, bf16[512,768]{1,0:T(8,128)(2,1)S(1)} %copy-done.7, ...), custom_call_target="tpu_custom_call" | custom-call | flops 32212254720 | bytes 18874368 | tf_op jit(solution)/shard_map/attn_bwd/pallas_call | solution.py:278
  242.3 10.5 %collective-permute-done.12 = bf16[192,2560]{1,0:T(8,128)(2,1)S(1)} collective-permute-done((bf16[192,2560]{1,0:T(8,128)(2,1)S(1)}, bf16[192,2560]{1,0:T(8,128)(2,1)S(1)}, u32[]{:S(2)}, u32[]{:S(2)}) %collective-permute-start.12) | collective-permute-done | bytes 983072 | tf_op jit(solution)/shard_map/ppermute | solution.py:776
  252.7 1.6 slice_bitcast_fusion.1
  255.4 1.8 collective-permute-start.16
  258.4 12.1 %attn_bwd.3 = (bf16[8,1,96,768]{3,2,1,0:T(8,128)(2,1)S(1)}, bf16[1,2048,448]{2,1,0:T(8,128)(2,1)S(1)}, bf16[1,512,256]{2,1,0:T(8,128)(2,1)S(1)}) custom-call(s32[8]{0:T(128)S(1)} %concatenate.26.info, bf16[512,768]{1,0:T(8,128)(2,1)} %bitcast.refs_0_, bf16[512,768]{1,0:T(8,128)(2,1)} %collective-permute-done.7.refs_0_.refs_1_, ...), custom_call_target="tpu_custom_call" | custom-call | flops 10737418240 | bytes 6291456 | tf_op jit(solution)/shard_map/attn_bwd/pallas_call | solution.py:278
  270.5 9.1 %collective-permute-done.16 = bf16[192,2560]{1,0:T(8,128)(2,1)S(1)} collective-permute-done((bf16[192,2560]{1,0:T(8,128)(2,1)S(1)}, bf16[192,2560]{1,0:T(8,128)(2,1)S(1)}, u32[]{:S(2)}, u32[]{:S(2)}) %collective-permute-start.16) | collective-permute-done | bytes 983072 | tf_op jit(solution)/shard_map/ppermute | solution.py:776
  279.6 1.5 collective-permute-done.15
  281.1 1.2 copy-done.20
  282.8 1.4 pad_maximum_fusion.1
  286.0 2.1 fusion
  288.9 1.3 collective-permute-start.22
  290.2 13.3 %collective-permute-done.18 = bf16[2,2,96,768]{3,2,1,0:T(8,128)(2,1)S(1)} collective-permute-done((bf16[2,2,96,768]{3,2,1,0:T(8,128)(2,1)S(1)}, bf16[2,2,96,768]{3,2,1,0:T(8,128)(2,1)S(1)}, u32[]{:S(2)}, u32[]{:S(2)}) %collective-permute-start.18) | collective-permute-done | bytes 589856 | tf_op jit(solution)/shard_map/ppermute | solution.py:776
  303.7 1.2 collective-permute-start.19
  305.9 6.1 %collective-permute-done.19 = bf16[2,96,768]{2,1,0:T(8,128)(2,1)S(1)} collective-permute-done((bf16[2,96,768]{2,1,0:T(8,128)(2,1)S(1)}, bf16[2,96,768]{2,1,0:T(8,128)(2,1)S(1)}, u32[]{:S(2)}, u32[]{:S(2)}) %collective-permute-start.19) | collective-permute-done | bytes 294944 | tf_op jit(solution)/shard_map/ppermute | solution.py:776
  312.1 2.8 collective-permute-start.20
  315.0 2.5 collective-permute-start.25
  317.6 3.0 collective-permute-start.24
  320.5 10.0 %token_grads.1 = (f32[512,768]{1,0:T(8,128)S(1)}, bf16[4,512,768]{2,1,0:T(8,128)(2,1)S(1)}) custom-call(s32[8]{0:T(128)S(1)} %concatenate.26.info, bf16[8,4,96,896]{3,2,1,0:T(8,128)(2,1)S(1)} %bitcast.142, bf16[3,2048,448]{2,1,0:T(8,128)(2,1)} %get-tuple-element.161.refs_0_, bf16[1,2048,448]{2,1,0:T(8,128)(2,1)S(1)} %copy-done.15, ...), custom_call_target="tpu_custom_call" | custom-call | flops 8589934592 | bytes 20971520 | tf_op jit(solution)/shard_map/token_grads/pallas_call | solution.py:351
  331.7 2.4 collective-permute-done.25
  334.1 5.8 %collective-permute-done.24 = bf16[96,768]{1,0:T(8,128)(2,1)S(1)} collective-permute-done((bf16[96,768]{1,0:T(8,128)(2,1)S(1)}, bf16[96,768]{1,0:T(8,128)(2,1)S(1)}, u32[]{:S(2)}, u32[]{:S(2)}) %collective-permute-start.24) | collective-permute-done | bytes 147488 | tf_op jit(solution)/shard_map/ppermute | solution.py:779
  340.0 1.9 pad_maximum_fusion.4
  342.7 1.9 collective-permute-start.26
  344.7 16.4 %collective-permute-done.26 = bf16[512,768]{1,0:T(8,128)(2,1)S(1)} collective-permute-done((bf16[512,768]{1,0:T(8,128)(2,1)S(1)}, bf16[512,768]{1,0:T(8,128)(2,1)S(1)}, u32[]{:S(2)}, u32[]{:S(2)}) %collective-permute-start.26) | collective-permute-done | bytes 786464 | tf_op jit(solution)/shard_map/ppermute | solution.py:881
  361.1 1.6 fusion.2
  362.7 1.3 collective-permute-start.29
  364.0 6.2 %collective-permute-start.27 = (bf16[512,768]{1,0:T(8,128)(2,1)}, bf16[512,768]{1,0:T(8,128)(2,1)}, u32[]{:S(2)}, u32[]{:S(2)}) collective-permute-start(bf16[512,768]{1,0:T(8,128)(2,1)} %get-tuple-element.209), channel_id=1, source_target_pairs={{0,1},{1,2},{2,3},{4,5},{5,6},{6,7},{8,9},{9,10},{10,11},{12,13},{... | collective-permute-start | bytes 2359304 | tf_op jit(solution)/shard_map/ppermute | solution.py:782
  370.2 11.5 %all-gather.11.cloned.1.call-done.gate.up.down.out_part.query.key.value.edge = bf16[768,3328]{1,0:T(8,128)(2,1)} async-done(((bf16[96,3328]{1,0:T(8,128)(2,1)}), bf16[768,3328]{1,0:T(8,128)(2,1)}) %all-gather.11.cloned.1.call-update) | async-done | bytes 5111824 | tf_op jit(solution)/shard_map/all_gather | solution.py:785
  381.7 8.4 %final_sums.1 = (f32[768,2,768]{2,1,0:T(2,128)}, f32[768,768]{1,0:T(8,128)}, f32[192,768]{1,0:T(8,128)}, f32[3,192,768]{2,1,0:T(8,128)}, f32[4,768]{1,0:T(4,128)}) custom-call(bf16[768,3328]{1,0:T(8,128)(2,1)} %all-gather.11.cloned.1.call-done.gate.up.down.out_part.query.key.value.edge, ...), custom_call_target="tpu_custom_call" | custom-call | flops 1048576 | bytes 15728640 | tf_op jit(solution)/shard_map/final_sums/pallas_call | solution.py:699
  390.0 1.5 slice_reduce_fusion
  391.5 2.9 add_bitcast_fusion
  (157 shorter events, 22.5 us)
Async XLA Ops:
  7.2 79.4 %all-gather.7.cloned.1.call-start = ((), (), s32[]{:S(2)}) async-start(), calls=%async_computation.2 | async-start | bytes 6193152 | tf_op jit(solution)/shard_map/all_gather | solution.py:785
  14.1 21.2 %copy-start.28 = (s32[1,24]{1,0:T(1,128)S(1)}, s32[1,24]{1,0:T(1,128)}, u32[]{:S(2)}) copy-start(s32[1,24]{1,0:T(1,128)} %param.12) | copy-start | bytes 292
  14.5 9.9 %collective-permute-start.2 = (bf16[96,896]{1,0:T(8,128)(2,1)S(1)}, bf16[96,896]{1,0:T(8,128)(2,1)S(1)}, u32[]{:S(2)}, u32[]{:S(2)}) collective-permute-start(bf16[96,896]{1,0:T(8,128)(2,1)S(1)} %pad_maximum_fusion.7), channel_id=1, source_target_pairs={{0,3},{1,0},{2,1},{3,2},{4,7},{5,4},{6,5},{7,6},{8,11},{9,8},{10,9... | collective-permute-start | bytes 516104 | tf_op jit(solution)/shard_map/ppermute | solution.py:779
  19.6 14.6 %collective-permute-start.1 = (bf16[96,896]{1,0:T(8,128)(2,1)S(1)}, bf16[96,896]{1,0:T(8,128)(2,1)S(1)}, u32[]{:S(2)}, u32[]{:S(2)}) collective-permute-start(bf16[96,896]{1,0:T(8,128)(2,1)S(1)} %pad_maximum_fusion.7), channel_id=1, source_target_pairs={{0,2},{1,3},{2,0},{3,1},{4,6},{5,7},{6,4},{7,5},{8,10},{9,11},{10,... | collective-permute-start | bytes 516104 | tf_op jit(solution)/shard_map/ppermute | solution.py:779
  19.6 14.6 %collective-permute-start = (bf16[96,896]{1,0:T(8,128)(2,1)S(1)}, bf16[96,896]{1,0:T(8,128)(2,1)S(1)}, u32[]{:S(2)}, u32[]{:S(2)}) collective-permute-start(bf16[96,896]{1,0:T(8,128)(2,1)S(1)} %pad_maximum_fusion.7), channel_id=1, source_target_pairs={{0,1},{1,2},{2,3},{3,0},{4,5},{5,6},{6,7},{7,4},{8,9},{9,10},{10,1... | collective-permute-start | bytes 516104 | tf_op jit(solution)/shard_map/ppermute | solution.py:779
  35.2 116.1 %all-gather.9.cloned.1.call-start = ((), (), s32[]{:S(2)}) async-start(), calls=%async_computation.3 | async-start | bytes 11943936 | tf_op jit(solution)/shard_map/all_gather | solution.py:785
  36.1 20.3 %collective-permute-start.5 = (bf16[96,2304]{1,0:T(8,128)(2,1)S(1)}, bf16[96,2304]{1,0:T(8,128)(2,1)S(1)}, u32[]{:S(2)}, u32[]{:S(2)}) collective-permute-start(bf16[96,2304]{1,0:T(8,128)(2,1)S(1)} %pad_maximum_fusion.6), channel_id=1, source_target_pairs={{0,3},{1,0},{2,1},{3,2},{4,7},{5,4},{6,5},{7,6},{8,11},{9,8},{10,9... | collective-permute-start | bytes 1327112 | tf_op jit(solution)/shard_map/ppermute | solution.py:779
  37.0 40.0 %collective-permute-start.4 = (bf16[96,2304]{1,0:T(8,128)(2,1)S(1)}, bf16[96,2304]{1,0:T(8,128)(2,1)}, u32[]{:S(2)}, u32[]{:S(2)}) collective-permute-start(bf16[96,2304]{1,0:T(8,128)(2,1)S(1)} %pad_maximum_fusion.6), channel_id=1, source_target_pairs={{0,2},{1,3},{2,0},{3,1},{4,6},{5,7},{6,4},{7,5},{8,10},{9,11},{10,... | collective-permute-start | bytes 1327112 | tf_op jit(solution)/shard_map/ppermute | solution.py:779
  39.0 38.0 %collective-permute-start.3 = (bf16[96,2304]{1,0:T(8,128)(2,1)S(1)}, bf16[96,2304]{1,0:T(8,128)(2,1)}, u32[]{:S(2)}, u32[]{:S(2)}) collective-permute-start(bf16[96,2304]{1,0:T(8,128)(2,1)S(1)} %pad_maximum_fusion.6), channel_id=1, source_target_pairs={{0,1},{1,2},{2,3},{3,0},{4,5},{5,6},{6,7},{7,4},{8,9},{9,10},{10,1... | collective-permute-start | bytes 1327112 | tf_op jit(solution)/shard_map/ppermute | solution.py:779
  50.7 3.7 copy-start.23
  79.4 260.6 %reduce-scatter.2.cloned.1.call-start = ((), (), s32[]{:S(2)}) async-start(), calls=%async_computation.1 | async-start | bytes 2457600 | tf_op jit(solution)/shard_map/reduce_scatter | solution.py:855
  79.4 20.3 %collective-permute-start.7 = (bf16[512,768]{1,0:T(8,128)(2,1)}, bf16[512,768]{1,0:T(8,128)(2,1)}, u32[]{:S(2)}, u32[]{:S(2)}) collective-permute-start(bf16[512,768]{1,0:T(8,128)(2,1)} %bitcast.refs_0_), channel_id=1, source_target_pairs={{1,0},{2,1},{3,2},{5,4},{6,5},{7,6},{9,8},{10,9},{11,10},{13,12},{... | collective-permute-start | bytes 2359304 | tf_op jit(solution)/shard_map/ppermute | solution.py:782
  80.7 20.1 %collective-permute-start.6 = (bf16[512,768]{1,0:T(8,128)(2,1)}, bf16[512,768]{1,0:T(8,128)(2,1)}, u32[]{:S(2)}, u32[]{:S(2)}) collective-permute-start(bf16[512,768]{1,0:T(8,128)(2,1)} %bitcast.refs_0_), channel_id=1, source_target_pairs={{0,1},{1,2},{2,3},{4,5},{5,6},{6,7},{8,9},{9,10},{10,11},{12,13},{... | collective-permute-start | bytes 2359304 | tf_op jit(solution)/shard_map/ppermute | solution.py:782
  86.6 3.2 copy-start.2
  89.8 17.8 %copy-start.24 = (f32[768]{0:T(1024)S(1)}, f32[768]{0:T(1024)}, u32[]{:S(2)}) copy-start(f32[768]{0:T(1024)} %param.15) | copy-start | bytes 9220
  89.8 17.8 %copy-start.25 = (f32[768]{0:T(1024)S(1)}, f32[768]{0:T(1024)}, u32[]{:S(2)}) copy-start(f32[768]{0:T(1024)} %param.16) | copy-start | bytes 9220
  89.8 17.8 %copy-start.26 = (f32[768]{0:T(1024)S(1)}, f32[768]{0:T(1024)}, u32[]{:S(2)}) copy-start(f32[768]{0:T(1024)} %param.19) | copy-start | bytes 9220
  89.8 17.8 %copy-start.27 = (f32[768]{0:T(1024)S(1)}, f32[768]{0:T(1024)}, u32[]{:S(2)}) copy-start(f32[768]{0:T(1024)} %param.20) | copy-start | bytes 9220
  100.8 22.4 %collective-permute-start.9 = (bf16[512,768]{1,0:T(8,128)(2,1)}, bf16[512,768]{1,0:T(8,128)(2,1)}, u32[]{:S(2)}, u32[]{:S(2)}) collective-permute-start(bf16[512,768]{1,0:T(8,128)(2,1)} %collective-permute-done.6.refs_0_.refs_3_), channel_id=1, source_target_pairs={{0,1},{1,2},{2,3},{4,5},{5,6},{6,7},{8,9},{9,10},{10,11},{12,13},{... | collective-permute-start | bytes 2359304 | tf_op jit(solution)/shard_map/ppermute | solution.py:782
  106.1 18.8 %collective-permute-start.8 = (bf16[512,768]{1,0:T(8,128)(2,1)}, bf16[512,768]{1,0:T(8,128)(2,1)}, u32[]{:S(2)}, u32[]{:S(2)}) collective-permute-start(bf16[512,768]{1,0:T(8,128)(2,1)} %collective-permute-done.7.refs_0_.refs_1_), channel_id=1, source_target_pairs={{1,0},{2,1},{3,2},{5,4},{6,5},{7,6},{9,8},{10,9},{11,10},{13,12},{... | collective-permute-start | bytes 2359304 | tf_op jit(solution)/shard_map/ppermute | solution.py:782
  107.7 2.6 copy-start.3
  126.1 5.4 %copy-start.6 = (bf16[512,768]{1,0:T(8,128)(2,1)}, bf16[512,768]{1,0:T(8,128)(2,1)S(1)}, u32[]{:S(2)}) copy-start(bf16[512,768]{1,0:T(8,128)(2,1)S(1)} %broadcast_select_fusion.refs_0_.refs_2_) | copy-start | bytes 2359300
  150.3 1.0 copy-start.4
  151.3 1.1 copy-start.13
  152.4 32.1 %copy-start.5 = (bf16[4,512,192]{2,1,0:T(8,128)(2,1)S(1)}, bf16[4,512,192]{2,1,0:T(8,128)(2,1)}, u32[]{:S(2)}) copy-start(bf16[4,512,192]{2,1,0:T(8,128)(2,1)} %copy-done.4) | copy-start | bytes 2359300
  189.1 6.8 %collective-permute-start.10 = (bf16[2,384,2560]{2,1,0:T(8,128)(2,1)S(1)}, bf16[2,384,2560]{2,1,0:T(8,128)(2,1)S(1)}, u32[]{:S(2)}, u32[]{:S(2)}) collective-permute-start(bf16[2,384,2560]{2,1,0:T(8,128)(2,1)S(1)} %wgrad.4), channel_id=1, source_target_pairs={{0,4},{4,0},{8,12},{12,8},{16,20},{20,16},{24,28},{28,24},{1,5},{5... | collective-permute-start | bytes 11796488 | tf_op jit(solution)/shard_map/ppermute | solution.py:776
  193.6 8.1 %collective-permute-start.11 = (bf16[2,384,2560]{2,1,0:T(8,128)(2,1)S(1)}, bf16[2,384,2560]{2,1,0:T(8,128)(2,1)S(1)}, u32[]{:S(2)}, u32[]{:S(2)}) collective-permute-start(bf16[2,384,2560]{2,1,0:T(8,128)(2,1)S(1)} %wgrad.5), channel_id=1, source_target_pairs={{0,4},{4,0},{8,12},{12,8},{16,20},{20,16},{24,28},{28,24},{1,5},{5... | collective-permute-start | bytes 11796488 | tf_op jit(solution)/shard_map/ppermute | solution.py:776
  201.7 8.0 %copy-start.7 = (bf16[512,768]{1,0:T(8,128)(2,1)S(1)}, bf16[512,768]{1,0:T(8,128)(2,1)}, u32[]{:S(2)}) copy-start(bf16[512,768]{1,0:T(8,128)(2,1)} %copy-done.6) | copy-start | bytes 2359300
  201.7 8.0 %copy-start.12 = (bf16[4,3,512,256]{3,2,1,0:T(8,128)(2,1)S(1)}, bf16[4,3,512,256]{3,2,1,0:T(8,128)(2,1)}, u32[]{:S(2)}) copy-start(bf16[4,3,512,256]{3,2,1,0:T(8,128)(2,1)} %get-tuple-element.115.qh.refs_7_) | copy-start | bytes 9437188
  201.7 8.0 %copy-start.18 = (bf16[4,512,192]{2,1,0:T(8,128)(2,1)S(1)}, bf16[4,512,192]{2,1,0:T(8,128)(2,1)}, u32[]{:S(2)}) copy-start(bf16[4,512,192]{2,1,0:T(8,128)(2,1)} %get-tuple-element.175.refs_12_) | copy-start | bytes 2359300
  201.7 51.0 %collective-permute-start.13 = (bf16[2,192,2560]{2,1,0:T(8,128)(2,1)}, bf16[2,192,2560]{2,1,0:T(8,128)(2,1)S(1)}, u32[]{:S(2)}, u32[]{:S(2)}) collective-permute-start(bf16[2,192,2560]{2,1,0:T(8,128)(2,1)} %get-tuple-element.157), channel_id=1, source_target_pairs={{0,16},{4,20},{8,24},{12,28},{16,0},{20,4},{24,8},{28,12},{1,17},{... | collective-permute-start | bytes 5898248 | tf_op jit(solution)/shard_map/ppermute | solution.py:776
  207.6 34.7 %collective-permute-start.14 = (bf16[192,2560]{1,0:T(8,128)(2,1)}, bf16[192,2560]{1,0:T(8,128)(2,1)S(1)}, u32[]{:S(2)}, u32[]{:S(2)}) collective-permute-start(bf16[192,2560]{1,0:T(8,128)(2,1)} %get-tuple-element.163), channel_id=1, source_target_pairs={{0,8},{4,12},{8,0},{12,4},{16,24},{20,28},{24,16},{28,20},{1,9},{5... | collective-permute-start | bytes 2949128 | tf_op jit(solution)/shard_map/ppermute | solution.py:776
  209.7 43.1 %collective-permute-start.12 = (bf16[192,2560]{1,0:T(8,128)(2,1)S(1)}, bf16[192,2560]{1,0:T(8,128)(2,1)S(1)}, u32[]{:S(2)}, u32[]{:S(2)}) collective-permute-start(bf16[192,2560]{1,0:T(8,128)(2,1)S(1)} %get-tuple-element.162), channel_id=1, source_target_pairs={{0,8},{4,12},{8,0},{12,4},{16,24},{20,28},{24,16},{28,20},{1,9},{5... | collective-permute-start | bytes 2949128 | tf_op jit(solution)/shard_map/ppermute | solution.py:776
  242.2 12.6 %copy-start.16 = (bf16[3,512,256]{2,1,0:T(8,128)(2,1)}, bf16[3,512,256]{2,1,0:T(8,128)(2,1)S(1)}, u32[]{:S(2)}) copy-start(bf16[3,512,256]{2,1,0:T(8,128)(2,1)S(1)} %get-tuple-element.179.refs_2_) | copy-start | bytes 2359300
  254.3 26.8 %collective-permute-start.17 = (bf16[4,3,96,768]{3,2,1,0:T(8,128)(2,1)S(1)}, bf16[4,3,96,768]{3,2,1,0:T(8,128)(2,1)S(1)}, u32[]{:S(2)}, u32[]{:S(2)}) collective-permute-start(bf16[4,3,96,768]{3,2,1,0:T(8,128)(2,1)S(1)} %slice_bitcast_fusion.1), channel_id=1, source_target_pairs={{0,4},{4,0},{8,12},{12,8},{16,20},{20,16},{24,28},{28,24},{1,5},{5... | collective-permute-start | bytes 5308424 | tf_op jit(solution)/shard_map/ppermute | solution.py:776
  255.1 3.3 copy-start.19
  255.4 24.2 %collective-permute-start.16 = (bf16[192,2560]{1,0:T(8,128)(2,1)S(1)}, bf16[192,2560]{1,0:T(8,128)(2,1)S(1)}, u32[]{:S(2)}, u32[]{:S(2)}) collective-permute-start(bf16[192,2560]{1,0:T(8,128)(2,1)S(1)} %slice_bitcast_fusion.4), channel_id=1, source_target_pairs={{0,8},{4,12},{8,0},{12,4},{16,24},{20,28},{24,16},{28,20},{1,9},{5... | collective-permute-start | bytes 2949128 | tf_op jit(solution)/shard_map/ppermute | solution.py:776
  257.2 23.9 %collective-permute-start.15 = (bf16[192,2560]{1,0:T(8,128)(2,1)S(1)}, bf16[192,2560]{1,0:T(8,128)(2,1)S(1)}, u32[]{:S(2)}, u32[]{:S(2)}) collective-permute-start(bf16[192,2560]{1,0:T(8,128)(2,1)S(1)} %add_convert_fusion.2), channel_id=1, source_target_pairs={{0,16},{4,20},{8,24},{12,28},{16,0},{20,4},{24,8},{28,12},{1,17},{... | collective-permute-start | bytes 2949128 | tf_op jit(solution)/shard_map/ppermute | solution.py:776
  270.5 12.3 %copy-start.10 = (bf16[8,1,96,768]{3,2,1,0:T(8,128)(2,1)}, bf16[8,1,96,768]{3,2,1,0:T(8,128)(2,1)S(1)}, u32[]{:S(2)}) copy-start(bf16[8,1,96,768]{3,2,1,0:T(8,128)(2,1)S(1)} %get-tuple-element.183) | copy-start | bytes 3538948
  270.5 12.3 %copy-start.14 = (bf16[1,2048,448]{2,1,0:T(8,128)(2,1)}, bf16[1,2048,448]{2,1,0:T(8,128)(2,1)S(1)}, u32[]{:S(2)}) copy-start(bf16[1,2048,448]{2,1,0:T(8,128)(2,1)S(1)} %get-tuple-element.178.refs_1_) | copy-start | bytes 5505028
  281.1 1.2 copy-start.20
  284.2 1.3 copy-start.11
  284.2 1.8 copy-start.21
  284.2 97.5 %all-gather.11.cloned.1.call-start = ((), (), s32[]{:S(2)}) async-start(), calls=%async_computation.4 | async-start | bytes 5750784 | tf_op jit(solution)/shard_map/all_gather | solution.py:785
  285.5 3.1 collective-permute-start.21
  286.0 34.5 %slice-start = ((s8[5505024]{0:T(1024)(128)(4,1)}), s8[4194304]{0:T(1024)(128)(4,1)S(1)}, s32[]{:S(2)}) async-start(s8[5505024]{0:T(1024)(128)(4,1)} %bitcast.140), calls=%async_computation.5 | async-start | bytes 8388608
  288.2 15.4 %collective-permute-start.18 = (bf16[2,2,96,768]{3,2,1,0:T(8,128)(2,1)S(1)}, bf16[2,2,96,768]{3,2,1,0:T(8,128)(2,1)S(1)}, u32[]{:S(2)}, u32[]{:S(2)}) collective-permute-start(bf16[2,2,96,768]{3,2,1,0:T(8,128)(2,1)S(1)} %slice_bitcast_fusion.8), channel_id=1, source_target_pairs={{0,8},{4,12},{8,0},{12,4},{16,24},{20,28},{24,16},{28,20},{1,9},{5... | collective-permute-start | bytes 1769480 | tf_op jit(solution)/shard_map/ppermute | solution.py:776
  288.8 31.7 %slice-start.1 = ((s8[5505024]{0:T(1024)(128)(4,1)}), s8[1310720]{0:T(1024)(128)(4,1)S(1)}, s32[]{:S(2)}) async-start(s8[5505024]{0:T(1024)(128)(4,1)} %bitcast.140), calls=%async_computation.6 | async-start | bytes 2621440
  288.9 16.0 %collective-permute-start.22 = (bf16[2,2,96,768]{3,2,1,0:T(8,128)(2,1)S(1)}, bf16[2,2,96,768]{3,2,1,0:T(8,128)(2,1)S(1)}, u32[]{:S(2)}, u32[]{:S(2)}) collective-permute-start(bf16[2,2,96,768]{3,2,1,0:T(8,128)(2,1)S(1)} %fusion.9), channel_id=1, source_target_pairs={{0,16},{4,20},{8,24},{12,28},{16,0},{20,4},{24,8},{28,12},{1,17},{... | collective-permute-start | bytes 1769480 | tf_op jit(solution)/shard_map/ppermute | solution.py:776
  303.7 8.3 %collective-permute-start.19 = (bf16[2,96,768]{2,1,0:T(8,128)(2,1)S(1)}, bf16[2,96,768]{2,1,0:T(8,128)(2,1)S(1)}, u32[]{:S(2)}, u32[]{:S(2)}) collective-permute-start(bf16[2,96,768]{2,1,0:T(8,128)(2,1)S(1)} %slice_bitcast_fusion.12), channel_id=1, source_target_pairs={{0,16},{4,20},{8,24},{12,28},{16,0},{20,4},{24,8},{28,12},{1,17},{... | collective-permute-start | bytes 884744 | tf_op jit(solution)/shard_map/ppermute | solution.py:776
  305.0 15.5 %copy-start.15 = (bf16[1,2048,448]{2,1,0:T(8,128)(2,1)S(1)}, bf16[1,2048,448]{2,1,0:T(8,128)(2,1)}, u32[]{:S(2)}) copy-start(bf16[1,2048,448]{2,1,0:T(8,128)(2,1)} %copy-done.14) | copy-start | bytes 5505028
  305.1 15.5 %copy-start.17 = (bf16[3,512,256]{2,1,0:T(8,128)(2,1)S(1)}, bf16[3,512,256]{2,1,0:T(8,128)(2,1)}, u32[]{:S(2)}) copy-start(bf16[3,512,256]{2,1,0:T(8,128)(2,1)} %copy-done.16) | copy-start | bytes 2359300
  305.1 9.8 %collective-permute-start.23 = (bf16[2,96,768]{2,1,0:T(8,128)(2,1)S(1)}, bf16[2,96,768]{2,1,0:T(8,128)(2,1)S(1)}, u32[]{:S(2)}, u32[]{:S(2)}) collective-permute-start(bf16[2,96,768]{2,1,0:T(8,128)(2,1)S(1)} %slice_bitcast_fusion.10), channel_id=1, source_target_pairs={{0,8},{4,12},{8,0},{12,4},{16,24},{20,28},{24,16},{28,20},{1,9},{5... | collective-permute-start | bytes 884744 | tf_op jit(solution)/shard_map/ppermute | solution.py:776
  312.1 19.7 %collective-permute-start.20 = (bf16[96,768]{1,0:T(8,128)(2,1)S(1)}, bf16[96,768]{1,0:T(8,128)(2,1)S(1)}, u32[]{:S(2)}, u32[]{:S(2)}) collective-permute-start(bf16[96,768]{1,0:T(8,128)(2,1)S(1)} %slice_bitcast_fusion.17), channel_id=1, source_target_pairs={{0,3},{1,0},{2,1},{3,2},{4,7},{5,4},{6,5},{7,6},{8,11},{9,8},{10,9... | collective-permute-start | bytes 442376 | tf_op jit(solution)/shard_map/ppermute | solution.py:779
  315.0 19.1 %collective-permute-start.25 = (bf16[96,768]{1,0:T(8,128)(2,1)S(1)}, bf16[96,768]{1,0:T(8,128)(2,1)S(1)}, u32[]{:S(2)}, u32[]{:S(2)}) collective-permute-start(bf16[96,768]{1,0:T(8,128)(2,1)S(1)} %get-tuple-element.217), channel_id=1, source_target_pairs={{0,1},{1,2},{2,3},{3,0},{4,5},{5,6},{6,7},{7,4},{8,9},{9,10},{10,1... | collective-permute-start | bytes 442376 | tf_op jit(solution)/shard_map/ppermute | solution.py:779
  317.6 22.3 %collective-permute-start.24 = (bf16[96,768]{1,0:T(8,128)(2,1)S(1)}, bf16[96,768]{1,0:T(8,128)(2,1)S(1)}, u32[]{:S(2)}, u32[]{:S(2)}) collective-permute-start(bf16[96,768]{1,0:T(8,128)(2,1)S(1)} %get-tuple-element.218), channel_id=1, source_target_pairs={{0,2},{1,3},{2,0},{3,1},{4,6},{5,7},{6,4},{7,5},{8,10},{9,11},{10,... | collective-permute-start | bytes 442376 | tf_op jit(solution)/shard_map/ppermute | solution.py:779
  330.6 1.2 copy-start.8
  342.0 2.7 collective-permute-start.28
  342.7 18.4 %collective-permute-start.26 = (bf16[512,768]{1,0:T(8,128)(2,1)S(1)}, bf16[512,768]{1,0:T(8,128)(2,1)S(1)}, u32[]{:S(2)}, u32[]{:S(2)}) collective-permute-start(bf16[512,768]{1,0:T(8,128)(2,1)S(1)} %slice_bitcast_fusion.5), channel_id=1, source_target_pairs={{0,1},{1,2},{4,5},{5,6},{8,9},{9,10},{12,13},{13,14},{16,17},{17,1... | collective-permute-start | bytes 2359304 | tf_op jit(solution)/shard_map/ppermute | solution.py:881
  362.7 27.4 %collective-permute-start.29 = (bf16[512,768]{1,0:T(8,128)(2,1)}, bf16[512,768]{1,0:T(8,128)(2,1)}, u32[]{:S(2)}, u32[]{:S(2)}) collective-permute-start(bf16[512,768]{1,0:T(8,128)(2,1)} %get-tuple-element.208), channel_id=1, source_target_pairs={{1,0},{2,1},{3,2},{5,4},{6,5},{7,6},{9,8},{10,9},{11,10},{13,12},{... | collective-permute-start | bytes 2359304 | tf_op jit(solution)/shard_map/ppermute | solution.py:782
  363.9 27.6 %copy-start.9 = (f32[512,768]{1,0:T(8,128)S(1)}, f32[512,768]{1,0:T(8,128)}, u32[]{:S(2)}) copy-start(f32[512,768]{1,0:T(8,128)} %copy-done.8) | copy-start | bytes 4718596
  364.0 27.6 %copy-start.22 = (f32[512,768]{1,0:T(8,128)S(1)}, f32[512,768]{1,0:T(8,128)}, u32[]{:S(2)}) copy-start(f32[512,768]{1,0:T(8,128)} %get-tuple-element.144) | copy-start | bytes 4718596
  364.0 26.1 %collective-permute-start.27 = (bf16[512,768]{1,0:T(8,128)(2,1)}, bf16[512,768]{1,0:T(8,128)(2,1)}, u32[]{:S(2)}, u32[]{:S(2)}) collective-permute-start(bf16[512,768]{1,0:T(8,128)(2,1)} %get-tuple-element.209), channel_id=1, source_target_pairs={{0,1},{1,2},{2,3},{4,5},{5,6},{6,7},{8,9},{9,10},{10,11},{12,13},{... | collective-permute-start | bytes 2359304 | tf_op jit(solution)/shard_map/ppermute | solution.py:782
  391.5 2.9 copy-start.1
  (1 other events, 1.0 us)
Sparse Core Ops, SparseCore 0:
  35.3 42.3 all-gather.6
  80.1 63.8 all-gather.8
  284.3 51.0 reduce-scatter.1
  342.1 39.5 all-gather.10

commit v7 on v6

--- a/solution.py
+++ b/solution.py
@@ -684,7 +684,7 @@
 
 def final_sums(main, width, span, heads, pieces):
     units = main.shape[0]
-    lanes = 128
+    lanes = 256
     steps = width // lanes
     cols = heads * HD
     room = span - 3 * width - cols
@@ -695,7 +695,7 @@
 
     in_specs = [pl.BlockSpec((units, lanes), lambda i: (0, i)), pl.BlockSpec((units, lanes), lambda i: (0, i + steps))]
     in_specs += [band(2 * width, width), band(3 * width, 256)] + [band(span + 256 * k, 256) for k in range(3)]
-    in_specs += [pl.BlockSpec((units, lanes), lambda i: (0, span // lanes - 1))]
+    in_specs += [pl.BlockSpec((units, 128), lambda i: (0, span // 128 - 1))]
     return pl.pallas_call(
         functools.partial(final_kernel, heads=heads, pieces=pieces, share=units // pieces, room=room),
         grid=(steps,),

time: 409 us -> 409 us (level)
  Pallas kernels: 160 us -> 141 us
  waiting for transfers between devices: 118 us -> 129 us
  starting transfers between devices: 52.8 us -> 59.8 us
    ppermute x13, waiting for transfers between devices: 42.2 us -> 52.6 us  [flip(): return lax.ppermute(array, 'dp', flip_axis(dp_size, bit))]
    pallas_call x2, Pallas kernels: 44.7 us -> 34.6 us  [attn_bwd(): pl.pallas_call(functools.partial(attn_bwd_kernel, docs=docs, heads=heads,...]
    ppermute x13, starting transfers between devices: 9.63 us -> 17 us  [flip(): return lax.ppermute(array, 'dp', flip_axis(dp_size, bit))]
    pallas_call x1, Pallas kernels: 18.7 us -> 11.7 us  [attn_fwd(): pl.pallas_call(functools.partial(attn_fwd_kernel, docs=docs, heads=heads)...]
  transfers between devices with their start and end apart: 34 -> 34, of which waited for: 16 -> 16; matrix products, arithmetic and copies ran while one was open for 6% -> 6% of each run, Pallas kernels for 31% -> 26%
where the time goes in v7:
time: 409 us; the launch traced here: 400 us
  Pallas kernels  141 us (34%)
  waiting for transfers between devices  129 us (32%)
  starting transfers between devices  59.8 us (15%)
  local copies, waits for them, and re-layouts  30.6 us (7%)
  other arithmetic  24.9 us (6%)
  between operations  15 us (4%)
    ppermute x13, waiting for transfers between devices, flip(): return lax.ppermute(array, 'dp', flip_axis(dp_size, bit))  52.6 us
    ppermute x9, waiting for transfers between devices, shift(): return lax.ppermute(array, 'tensor', rotate_axis(tp_size, step))  42.9 us
    pallas_call x2, Pallas kernels, attn_bwd(): pl.pallas_call(functools.partial(attn_bwd_kernel, docs=docs, heads=heads,...  34.6 us
    pallas_call x1, Pallas kernels, ffn_layer(): pl.pallas_call(functools.partial(ffn_kernel, slots=slots, pieces=pieces,...  32.1 us
    pallas_call x4, Pallas kernels, project(): pl.pallas_call(functools.partial(project_kernel, docs=docs, heads=heads,...  25.8 us
    ppermute x6, starting transfers between devices, along(): return lax.ppermute(array, 'tensor', line_axis(tp_size, step))  21 us
    pallas_call x4, Pallas kernels, wgrad(): pl.pallas_call(functools.partial(wgrad_kernel, slots=slots, share=share,...  20.2 us
    ppermute x9, starting transfers between devices, shift(): return lax.ppermute(array, 'tensor', rotate_axis(tp_size, step))  19 us
  transfers between devices with their start and end apart: 34, of which 16 were waited for; matrix products, arithmetic and copies ran while one was open for 6% of the time, Pallas kernels for 26%

profile of v7, /device:TPU:0, one launch (start us, length us, event | category | flops | bytes accessed | tf_op | source)
XLA Modules:
  0.0 400.5 jit_solution(6610614282909367085)
XLA Ops:
  10.8 3.0 constant_dynamic-slice_fusion.2
  14.5 5.1 %collective-permute-start.2 = (bf16[96,896]{1,0:T(8,128)(2,1)S(1)}, bf16[96,896]{1,0:T(8,128)(2,1)S(1)}, u32[]{:S(2)}, u32[]{:S(2)}) collective-permute-start(bf16[96,896]{1,0:T(8,128)(2,1)S(1)} %pad_maximum_fusion.7), channel_id=1, source_target_pairs={{0,3},{1,0},{2,1},{3,2},{4,7},{5,4},{6,5},{7,6},{8,11},{9,8},{10,9... | collective-permute-start | bytes 516104 | tf_op jit(solution)/shard_map/ppermute | solution.py:779
  20.6 3.8 collective-permute-done.2
  24.5 9.8 %collective-permute-done.1 = bf16[96,896]{1,0:T(8,128)(2,1)S(1)} collective-permute-done((bf16[96,896]{1,0:T(8,128)(2,1)S(1)}, bf16[96,896]{1,0:T(8,128)(2,1)S(1)}, u32[]{:S(2)}, u32[]{:S(2)}) %collective-permute-start.1) | collective-permute-done | bytes 172064 | tf_op jit(solution)/shard_map/ppermute | solution.py:779
  37.0 2.0 collective-permute-start.4
  39.0 1.9 collective-permute-start.3
  41.0 5.6 %copy.117 = bf16[768,2,768]{0,2,1:T(8,128)(2,1)S(1)} copy(bf16[768,2,768]{2,1,0:T(2,128)(2,1)} %param.17) | data formatting | bytes 4718592 | tf_op jit(solution)/shard_map/optimization_barrier | solution.py:738
  47.6 1.3 fusion.19
  48.9 1.4 concatenate.26.info
  50.7 3.7 multiply_sine_fusion
  54.4 2.0 pad_maximum_fusion
  56.4 20.6 %collective-permute-done.4 = bf16[96,2304]{1,0:T(8,128)(2,1)} collective-permute-done((bf16[96,2304]{1,0:T(8,128)(2,1)S(1)}, bf16[96,2304]{1,0:T(8,128)(2,1)}, u32[]{:S(2)}, u32[]{:S(2)}) %collective-permute-start.4) | collective-permute-done | bytes 442400 | tf_op jit(solution)/shard_map/ppermute | solution.py:779
  77.0 2.3 pad_maximum_fusion.2
  79.4 1.3 collective-permute-start.7
  80.7 5.5 %collective-permute-start.6 = (bf16[512,768]{1,0:T(8,128)(2,1)}, bf16[512,768]{1,0:T(8,128)(2,1)}, u32[]{:S(2)}, u32[]{:S(2)}) collective-permute-start(bf16[512,768]{1,0:T(8,128)(2,1)} %bitcast.refs_0_), channel_id=1, source_target_pairs={{0,1},{1,2},{2,3},{4,5},{5,6},{6,7},{8,9},{9,10},{10,11},{12,13},{... | collective-permute-start | bytes 2359304 | tf_op jit(solution)/shard_map/ppermute | solution.py:782
  86.6 3.2 copy-done.2
  89.8 7.3 %project.4 = (bf16[4,4,512,256]{3,2,1,0:T(8,128)(2,1)}, bf16[4,4,512,192]{3,2,1,0:T(8,128)(2,1)}, bf16[4,4,240,512]{3,2,1,0:T(8,128)(2,1)}, bf16[4,3,512,256]{3,2,1,0:T(8,128)(2,1)}) custom-call(bf16[512,768]{1,0:T(8,128)(2,1)} %bitcast.refs_0_, bf16[8,4,96,896]{3,2,1,0:T(8,128)(2,1)S(1)} %bitcast.136, f32[2048,128]{1,0:T(8,128)S(1)} %get-tuple-element.113.refs_2_.refs_4_, ...), custom_call_target="tpu_custom_call" | custom-call | flops 2147483648 | bytes 8388608 | tf_op jit(solution)/shard_map/project/pallas_call | solution.py:112
  97.2 2.5 collective-permute-done.7.refs_0_.refs_1_
  100.8 5.3 %collective-permute-start.9 = (bf16[512,768]{1,0:T(8,128)(2,1)}, bf16[512,768]{1,0:T(8,128)(2,1)}, u32[]{:S(2)}, u32[]{:S(2)}) collective-permute-start(bf16[512,768]{1,0:T(8,128)(2,1)} %collective-permute-done.6.refs_0_.refs_3_), channel_id=1, source_target_pairs={{0,1},{1,2},{2,3},{4,5},{5,6},{6,7},{8,9},{9,10},{10,11},{12,13},{... | collective-permute-start | bytes 2359304 | tf_op jit(solution)/shard_map/ppermute | solution.py:782
  106.1 1.5 collective-permute-start.8
  107.7 2.6 copy-done.3
  110.2 6.5 %project.5 = (bf16[4,4,512,256]{3,2,1,0:T(8,128)(2,1)}, bf16[4,4,512,192]{3,2,1,0:T(8,128)(2,1)}, bf16[4,4,240,512]{3,2,1,0:T(8,128)(2,1)}) custom-call(bf16[512,768]{1,0:T(8,128)(2,1)} %collective-permute-done.7.refs_0_.refs_1_, bf16[8,4,96,896]{3,2,1,0:T(8,128)(2,1)S(1)} %bitcast.137, ...), custom_call_target="tpu_custom_call", output_to_operand_aliasing={{0}: (5, {}), {1}: (6, {}), {2}: (7, {})} | custom-call | flops 2147483648 | bytes 8388608 | tf_op jit(solution)/shard_map/project/pallas_call | solution.py:112
  116.8 6.5 %project.6 = (bf16[4,4,512,256]{3,2,1,0:T(8,128)(2,1)}, bf16[4,4,512,192]{3,2,1,0:T(8,128)(2,1)}, bf16[4,4,240,512]{3,2,1,0:T(8,128)(2,1)}) custom-call(bf16[512,768]{1,0:T(8,128)(2,1)} %collective-permute-done.6.refs_0_.refs_3_, bf16[8,4,96,896]{3,2,1,0:T(8,128)(2,1)S(1)} %bitcast.138, ...), custom_call_target="tpu_custom_call", output_to_operand_aliasing={{0}: (5, {}), {1}: (6, {}), {2}: (7, {})} | custom-call | flops 2147483648 | bytes 8388608 | tf_op jit(solution)/shard_map/project/pallas_call | solution.py:112
  123.2 1.7 collective-permute-done.8
  124.9 1.2 broadcast_select_fusion.refs_0_.refs_2_
  126.1 5.4 %project.7 = (bf16[4,4,512,256]{3,2,1,0:T(8,128)(2,1)}, bf16[4,4,512,192]{3,2,1,0:T(8,128)(2,1)}, bf16[4,4,240,512]{3,2,1,0:T(8,128)(2,1)}) custom-call(bf16[512,768]{1,0:T(8,128)(2,1)S(1)} %broadcast_select_fusion.refs_0_.refs_2_, bf16[8,4,96,896]{3,2,1,0:T(8,128)(2,1)S(1)} %bitcast.139, ...), custom_call_target="tpu_custom_call", output_to_operand_aliasing={{0}: (5, {}), {1}: (6, {}), {2}: (7, {})} | custom-call | flops 2147483648 | bytes 8388608 | tf_op jit(solution)/shard_map/project/pallas_call | solution.py:112
  131.6 11.7 %attn_fwd.1 = (f32[4,8,512]{2,1,0:T(8,128)S(1)}, bf16[4,512,192]{2,1,0:T(8,128)(2,1)S(1)}) custom-call(s32[8]{0:T(128)S(1)} %concatenate.26.info, s32[2048,1]{1,0:T(8,128)S(1)} %copy.123.refs_4_.seg.refs_6_, bf16[4,3,512,256]{3,2,1,0:T(8,128)(2,1)} %get-tuple-element.115.qh.refs_7_, bf16[4,4,512,256]{3,2,1,0:T(8,128)(2,1)} %get-tuple-element.136.ka, ...), custom_call_target="tpu_custom_call" | custom-call | flops 12884901888 | bytes 12582912 | tf_op jit(solution)/shard_map/attn_fwd/pallas_call | solution.py:171
  145.3 32.1 %ffn_layer.1 = (bf16[512,768]{1,0:T(8,128)(2,1)}, f32[512,768]{1,0:T(8,128)}, bf16[512,768]{1,0:T(8,128)(2,1)S(1)}, bf16[512,768]{1,0:T(8,128)(2,1)S(1)}, bf16[7...) custom-call(bf16[512,768]{1,0:T(8,128)(2,1)} %bitcast.refs_0_, ...), custom_call_target="tpu_custom_call" | custom-call | flops 17179869184 | bytes 31457280 | tf_op jit(solution)/shard_map/ffn_layer/pallas_call | solution.py:557
  177.5 4.5 %wgrad.4 = bf16[2,384,2560]{2,1,0:T(8,128)(2,1)S(1)} custom-call(s32[2]{0:T(128)S(1)} %get-tuple-element.158.refs_0_, bf16[512,3072]{1,0:T(8,128)(2,1)} %get-tuple-element.148.refs_1_, bf16[512,3072]{1,0:T(8,128)(2,1)} %get-tuple-element.149.refs_2_, bf16[512,3072]{1,0:T(8,128)(2,1)} %get-tuple-element.150.refs_3_, ...), custom_call_target="tpu_custom_call" | custom-call | flops 2147483648 | bytes 10485760 | tf_op jit(solution)/shard_map/wgrad/pallas_call | solution.py:649
  182.0 3.4 collective-permute-start.10
  185.4 4.5 %wgrad.5 = bf16[2,384,2560]{2,1,0:T(8,128)(2,1)S(1)} custom-call(s32[2]{0:T(128)S(1)} %get-tuple-element.158.refs_0_, bf16[512,3072]{1,0:T(8,128)(2,1)} %get-tuple-element.148.refs_1_, bf16[512,3072]{1,0:T(8,128)(2,1)} %get-tuple-element.149.refs_2_, bf16[512,3072]{1,0:T(8,128)(2,1)} %get-tuple-element.150.refs_3_, ...), custom_call_target="tpu_custom_call" | custom-call | flops 2147483648 | bytes 10485760 | tf_op jit(solution)/shard_map/wgrad/pallas_call | solution.py:649
  190.0 1.8 collective-permute-done.10.refs_9_
  191.8 5.8 %wgrad.6 = (bf16[192,2560]{1,0:T(8,128)(2,1)S(1)}, bf16[192,2560]{1,0:T(8,128)(2,1)S(1)}, bf16[2,192,2560]{2,1,0:T(8,128)(2,1)}) custom-call(s32[2]{0:T(128)S(1)} %get-tuple-element.158.refs_0_, bf16[512,3072]{1,0:T(8,128)(2,1)} %get-tuple-element.148.refs_1_, bf16[512,3072]{1,0:T(8,128)(2,1)} %get-tuple-element.149.refs_2_, ...), custom_call_target="tpu_custom_call" | custom-call | flops 2147483648 | bytes 10485760 | tf_op jit(solution)/shard_map/wgrad/pallas_call | solution.py:649
  197.6 1.3 collective-permute-start.13
  198.9 5.5 %wgrad.7 = (bf16[192,2560]{1,0:T(8,128)(2,1)S(1)}, bf16[192,2560]{1,0:T(8,128)(2,1)}, bf16[2,192,2560]{2,1,0:T(8,128)(2,1)S(1)}) custom-call(s32[2]{0:T(128)S(1)} %get-tuple-element.158.refs_0_, bf16[512,3072]{1,0:T(8,128)(2,1)} %get-tuple-element.148.refs_1_, bf16[512,3072]{1,0:T(8,128)(2,1)} %get-tuple-element.149.refs_2_, ...), custom_call_target="tpu_custom_call" | custom-call | flops 2147483648 | bytes 10485760 | tf_op jit(solution)/shard_map/wgrad/pallas_call | solution.py:649
  204.4 5.4 %collective-permute-start.14 = (bf16[192,2560]{1,0:T(8,128)(2,1)}, bf16[192,2560]{1,0:T(8,128)(2,1)S(1)}, u32[]{:S(2)}, u32[]{:S(2)}) collective-permute-start(bf16[192,2560]{1,0:T(8,128)(2,1)} %get-tuple-element.163), channel_id=1, source_target_pairs={{0,8},{4,12},{8,0},{12,4},{16,24},{20,28},{24,16},{28,20},{1,9},{5... | collective-permute-start | bytes 2949128 | tf_op jit(solution)/shard_map/ppermute | solution.py:776
  209.9 25.0 %attn_bwd.2 = (bf16[8,3,96,768]{3,2,1,0:T(8,128)(2,1)}, bf16[3,2048,448]{2,1,0:T(8,128)(2,1)}, bf16[3,512,256]{2,1,0:T(8,128)(2,1)S(1)}) custom-call(s32[8]{0:T(128)S(1)} %concatenate.26.info, bf16[512,768]{1,0:T(8,128)(2,1)} %bitcast.refs_0_, bf16[512,768]{1,0:T(8,128)(2,1)} %collective-permute-done.7.refs_0_.refs_1_, bf16[512,768]{1,0:T(8,128)(2,1)S(1)} %copy-done.7, ...), custom_call_target="tpu_custom_call" | custom-call | flops 32212254720 | bytes 18874368 | tf_op jit(solution)/shard_map/attn_bwd/pallas_call | solution.py:278
  234.9 18.0 %collective-permute-done.12 = bf16[192,2560]{1,0:T(8,128)(2,1)S(1)} collective-permute-done((bf16[192,2560]{1,0:T(8,128)(2,1)S(1)}, bf16[192,2560]{1,0:T(8,128)(2,1)S(1)}, u32[]{:S(2)}, u32[]{:S(2)}) %collective-permute-start.12) | collective-permute-done | bytes 983072 | tf_op jit(solution)/shard_map/ppermute | solution.py:776
  252.9 1.6 slice_bitcast_fusion.1
  255.6 1.8 collective-permute-start.16
  258.5 9.6 %attn_bwd.3 = (bf16[8,1,96,768]{3,2,1,0:T(8,128)(2,1)S(1)}, bf16[1,2048,448]{2,1,0:T(8,128)(2,1)S(1)}, bf16[1,512,256]{2,1,0:T(8,128)(2,1)S(1)}) custom-call(s32[8]{0:T(128)S(1)} %concatenate.26.info, bf16[512,768]{1,0:T(8,128)(2,1)} %bitcast.refs_0_, bf16[512,768]{1,0:T(8,128)(2,1)} %collective-permute-done.7.refs_0_.refs_1_, ...), custom_call_target="tpu_custom_call" | custom-call | flops 10737418240 | bytes 6291456 | tf_op jit(solution)/shard_map/attn_bwd/pallas_call | solution.py:278
  268.2 11.6 %collective-permute-done.16 = bf16[192,2560]{1,0:T(8,128)(2,1)S(1)} collective-permute-done((bf16[192,2560]{1,0:T(8,128)(2,1)S(1)}, bf16[192,2560]{1,0:T(8,128)(2,1)S(1)}, u32[]{:S(2)}, u32[]{:S(2)}) %collective-permute-start.16) | collective-permute-done | bytes 983072 | tf_op jit(solution)/shard_map/ppermute | solution.py:776
  279.8 1.5 collective-permute-done.15
  281.3 1.2 copy-done.20
  283.0 1.4 pad_maximum_fusion.1
  286.2 2.1 fusion
  290.2 13.5 %collective-permute-done.18 = bf16[2,2,96,768]{3,2,1,0:T(8,128)(2,1)S(1)} collective-permute-done((bf16[2,2,96,768]{3,2,1,0:T(8,128)(2,1)S(1)}, bf16[2,2,96,768]{3,2,1,0:T(8,128)(2,1)S(1)}, u32[]{:S(2)}, u32[]{:S(2)}) %collective-permute-start.18) | collective-permute-done | bytes 589856 | tf_op jit(solution)/shard_map/ppermute | solution.py:776
  306.0 6.1 %collective-permute-done.19 = bf16[2,96,768]{2,1,0:T(8,128)(2,1)S(1)} collective-permute-done((bf16[2,96,768]{2,1,0:T(8,128)(2,1)S(1)}, bf16[2,96,768]{2,1,0:T(8,128)(2,1)S(1)}, u32[]{:S(2)}, u32[]{:S(2)}) %collective-permute-start.19) | collective-permute-done | bytes 294944 | tf_op jit(solution)/shard_map/ppermute | solution.py:776
  312.3 2.7 collective-permute-start.20
  315.0 2.5 collective-permute-start.25
  317.6 2.8 collective-permute-start.24
  320.4 9.5 %token_grads.1 = (f32[512,768]{1,0:T(8,128)S(1)}, bf16[4,512,768]{2,1,0:T(8,128)(2,1)S(1)}) custom-call(s32[8]{0:T(128)S(1)} %concatenate.26.info, bf16[8,4,96,896]{3,2,1,0:T(8,128)(2,1)S(1)} %bitcast.142, bf16[3,2048,448]{2,1,0:T(8,128)(2,1)} %get-tuple-element.161.refs_0_, bf16[1,2048,448]{2,1,0:T(8,128)(2,1)S(1)} %copy-done.15, ...), custom_call_target="tpu_custom_call" | custom-call | flops 8589934592 | bytes 20971520 | tf_op jit(solution)/shard_map/token_grads/pallas_call | solution.py:351
  331.0 2.9 collective-permute-done.25
  334.0 5.8 %collective-permute-done.24 = bf16[96,768]{1,0:T(8,128)(2,1)S(1)} collective-permute-done((bf16[96,768]{1,0:T(8,128)(2,1)S(1)}, bf16[96,768]{1,0:T(8,128)(2,1)S(1)}, u32[]{:S(2)}, u32[]{:S(2)}) %collective-permute-start.24) | collective-permute-done | bytes 147488 | tf_op jit(solution)/shard_map/ppermute | solution.py:779
  339.8 1.9 pad_maximum_fusion.4
  342.5 1.9 collective-permute-start.26
  344.5 16.4 %collective-permute-done.26 = bf16[512,768]{1,0:T(8,128)(2,1)S(1)} collective-permute-done((bf16[512,768]{1,0:T(8,128)(2,1)S(1)}, bf16[512,768]{1,0:T(8,128)(2,1)S(1)}, u32[]{:S(2)}, u32[]{:S(2)}) %collective-permute-start.26) | collective-permute-done | bytes 786464 | tf_op jit(solution)/shard_map/ppermute | solution.py:881
  360.9 1.6 fusion.2
  362.5 1.3 collective-permute-start.29
  363.8 6.2 %collective-permute-start.27 = (bf16[512,768]{1,0:T(8,128)(2,1)}, bf16[512,768]{1,0:T(8,128)(2,1)}, u32[]{:S(2)}, u32[]{:S(2)}) collective-permute-start(bf16[512,768]{1,0:T(8,128)(2,1)} %get-tuple-element.209), channel_id=1, source_target_pairs={{0,1},{1,2},{2,3},{4,5},{5,6},{6,7},{8,9},{9,10},{10,11},{12,13},{... | collective-permute-start | bytes 2359304 | tf_op jit(solution)/shard_map/ppermute | solution.py:782
  370.0 11.5 %all-gather.11.cloned.1.call-done.gate.up.down.out_part.query.key.value.edge = bf16[768,3328]{1,0:T(8,128)(2,1)} async-done(((bf16[96,3328]{1,0:T(8,128)(2,1)}), bf16[768,3328]{1,0:T(8,128)(2,1)}) %all-gather.11.cloned.1.call-update) | async-done | bytes 5111824 | tf_op jit(solution)/shard_map/all_gather | solution.py:785
  381.5 7.6 %final_sums.1 = (f32[768,2,768]{2,1,0:T(2,128)}, f32[768,768]{1,0:T(8,128)}, f32[192,768]{1,0:T(8,128)}, f32[3,192,768]{2,1,0:T(8,128)}, f32[4,768]{1,0:T(4,128)}) custom-call(bf16[768,3328]{1,0:T(8,128)(2,1)} %all-gather.11.cloned.1.call-done.gate.up.down.out_part.query.key.value.edge, ...), custom_call_target="tpu_custom_call" | custom-call | flops 1048576 | bytes 15728640 | tf_op jit(solution)/shard_map/final_sums/pallas_call | solution.py:699
  389.1 1.5 slice_reduce_fusion
  390.6 2.9 add_bitcast_fusion
  (157 shorter events, 24.3 us)
Async XLA Ops:
  7.2 79.4 %all-gather.7.cloned.1.call-start = ((), (), s32[]{:S(2)}) async-start(), calls=%async_computation.2 | async-start | bytes 6193152 | tf_op jit(solution)/shard_map/all_gather | solution.py:785
  14.1 21.2 %copy-start.28 = (s32[1,24]{1,0:T(1,128)S(1)}, s32[1,24]{1,0:T(1,128)}, u32[]{:S(2)}) copy-start(s32[1,24]{1,0:T(1,128)} %param.12) | copy-start | bytes 292
  14.5 9.9 %collective-permute-start.2 = (bf16[96,896]{1,0:T(8,128)(2,1)S(1)}, bf16[96,896]{1,0:T(8,128)(2,1)S(1)}, u32[]{:S(2)}, u32[]{:S(2)}) collective-permute-start(bf16[96,896]{1,0:T(8,128)(2,1)S(1)} %pad_maximum_fusion.7), channel_id=1, source_target_pairs={{0,3},{1,0},{2,1},{3,2},{4,7},{5,4},{6,5},{7,6},{8,11},{9,8},{10,9... | collective-permute-start | bytes 516104 | tf_op jit(solution)/shard_map/ppermute | solution.py:779
  19.6 14.6 %collective-permute-start.1 = (bf16[96,896]{1,0:T(8,128)(2,1)S(1)}, bf16[96,896]{1,0:T(8,128)(2,1)S(1)}, u32[]{:S(2)}, u32[]{:S(2)}) collective-permute-start(bf16[96,896]{1,0:T(8,128)(2,1)S(1)} %pad_maximum_fusion.7), channel_id=1, source_target_pairs={{0,2},{1,3},{2,0},{3,1},{4,6},{5,7},{6,4},{7,5},{8,10},{9,11},{10,... | collective-permute-start | bytes 516104 | tf_op jit(solution)/shard_map/ppermute | solution.py:779
  19.6 14.6 %collective-permute-start = (bf16[96,896]{1,0:T(8,128)(2,1)S(1)}, bf16[96,896]{1,0:T(8,128)(2,1)S(1)}, u32[]{:S(2)}, u32[]{:S(2)}) collective-permute-start(bf16[96,896]{1,0:T(8,128)(2,1)S(1)} %pad_maximum_fusion.7), channel_id=1, source_target_pairs={{0,1},{1,2},{2,3},{3,0},{4,5},{5,6},{6,7},{7,4},{8,9},{9,10},{10,1... | collective-permute-start | bytes 516104 | tf_op jit(solution)/shard_map/ppermute | solution.py:779
  35.2 109.0 %all-gather.9.cloned.1.call-start = ((), (), s32[]{:S(2)}) async-start(), calls=%async_computation.3 | async-start | bytes 11943936 | tf_op jit(solution)/shard_map/all_gather | solution.py:785
  36.1 20.3 %collective-permute-start.5 = (bf16[96,2304]{1,0:T(8,128)(2,1)S(1)}, bf16[96,2304]{1,0:T(8,128)(2,1)S(1)}, u32[]{:S(2)}, u32[]{:S(2)}) collective-permute-start(bf16[96,2304]{1,0:T(8,128)(2,1)S(1)} %pad_maximum_fusion.6), channel_id=1, source_target_pairs={{0,3},{1,0},{2,1},{3,2},{4,7},{5,4},{6,5},{7,6},{8,11},{9,8},{10,9... | collective-permute-start | bytes 1327112 | tf_op jit(solution)/shard_map/ppermute | solution.py:779
  37.0 40.0 %collective-permute-start.4 = (bf16[96,2304]{1,0:T(8,128)(2,1)S(1)}, bf16[96,2304]{1,0:T(8,128)(2,1)}, u32[]{:S(2)}, u32[]{:S(2)}) collective-permute-start(bf16[96,2304]{1,0:T(8,128)(2,1)S(1)} %pad_maximum_fusion.6), channel_id=1, source_target_pairs={{0,2},{1,3},{2,0},{3,1},{4,6},{5,7},{6,4},{7,5},{8,10},{9,11},{10,... | collective-permute-start | bytes 1327112 | tf_op jit(solution)/shard_map/ppermute | solution.py:779
  39.0 38.0 %collective-permute-start.3 = (bf16[96,2304]{1,0:T(8,128)(2,1)S(1)}, bf16[96,2304]{1,0:T(8,128)(2,1)}, u32[]{:S(2)}, u32[]{:S(2)}) collective-permute-start(bf16[96,2304]{1,0:T(8,128)(2,1)S(1)} %pad_maximum_fusion.6), channel_id=1, source_target_pairs={{0,1},{1,2},{2,3},{3,0},{4,5},{5,6},{6,7},{7,4},{8,9},{9,10},{10,1... | collective-permute-start | bytes 1327112 | tf_op jit(solution)/shard_map/ppermute | solution.py:779
  50.7 3.7 copy-start.23
  79.4 260.5 %reduce-scatter.2.cloned.1.call-start = ((), (), s32[]{:S(2)}) async-start(), calls=%async_computation.1 | async-start | bytes 2457600 | tf_op jit(solution)/shard_map/reduce_scatter | solution.py:855
  79.4 20.3 %collective-permute-start.7 = (bf16[512,768]{1,0:T(8,128)(2,1)}, bf16[512,768]{1,0:T(8,128)(2,1)}, u32[]{:S(2)}, u32[]{:S(2)}) collective-permute-start(bf16[512,768]{1,0:T(8,128)(2,1)} %bitcast.refs_0_), channel_id=1, source_target_pairs={{1,0},{2,1},{3,2},{5,4},{6,5},{7,6},{9,8},{10,9},{11,10},{13,12},{... | collective-permute-start | bytes 2359304 | tf_op jit(solution)/shard_map/ppermute | solution.py:782
  80.7 20.1 %collective-permute-start.6 = (bf16[512,768]{1,0:T(8,128)(2,1)}, bf16[512,768]{1,0:T(8,128)(2,1)}, u32[]{:S(2)}, u32[]{:S(2)}) collective-permute-start(bf16[512,768]{1,0:T(8,128)(2,1)} %bitcast.refs_0_), channel_id=1, source_target_pairs={{0,1},{1,2},{2,3},{4,5},{5,6},{6,7},{8,9},{9,10},{10,11},{12,13},{... | collective-permute-start | bytes 2359304 | tf_op jit(solution)/shard_map/ppermute | solution.py:782
  86.6 3.2 copy-start.2
  89.8 17.8 %copy-start.24 = (f32[768]{0:T(1024)S(1)}, f32[768]{0:T(1024)}, u32[]{:S(2)}) copy-start(f32[768]{0:T(1024)} %param.15) | copy-start | bytes 9220
  89.8 17.8 %copy-start.25 = (f32[768]{0:T(1024)S(1)}, f32[768]{0:T(1024)}, u32[]{:S(2)}) copy-start(f32[768]{0:T(1024)} %param.16) | copy-start | bytes 9220
  89.8 17.8 %copy-start.26 = (f32[768]{0:T(1024)S(1)}, f32[768]{0:T(1024)}, u32[]{:S(2)}) copy-start(f32[768]{0:T(1024)} %param.19) | copy-start | bytes 9220
  89.8 17.8 %copy-start.27 = (f32[768]{0:T(1024)S(1)}, f32[768]{0:T(1024)}, u32[]{:S(2)}) copy-start(f32[768]{0:T(1024)} %param.20) | copy-start | bytes 9220
  100.8 22.4 %collective-permute-start.9 = (bf16[512,768]{1,0:T(8,128)(2,1)}, bf16[512,768]{1,0:T(8,128)(2,1)}, u32[]{:S(2)}, u32[]{:S(2)}) collective-permute-start(bf16[512,768]{1,0:T(8,128)(2,1)} %collective-permute-done.6.refs_0_.refs_3_), channel_id=1, source_target_pairs={{0,1},{1,2},{2,3},{4,5},{5,6},{6,7},{8,9},{9,10},{10,11},{12,13},{... | collective-permute-start | bytes 2359304 | tf_op jit(solution)/shard_map/ppermute | solution.py:782
  106.1 18.8 %collective-permute-start.8 = (bf16[512,768]{1,0:T(8,128)(2,1)}, bf16[512,768]{1,0:T(8,128)(2,1)}, u32[]{:S(2)}, u32[]{:S(2)}) collective-permute-start(bf16[512,768]{1,0:T(8,128)(2,1)} %collective-permute-done.7.refs_0_.refs_1_), channel_id=1, source_target_pairs={{1,0},{2,1},{3,2},{5,4},{6,5},{7,6},{9,8},{10,9},{11,10},{13,12},{... | collective-permute-start | bytes 2359304 | tf_op jit(solution)/shard_map/ppermute | solution.py:782
  107.7 2.6 copy-start.3
  126.1 5.4 %copy-start.6 = (bf16[512,768]{1,0:T(8,128)(2,1)}, bf16[512,768]{1,0:T(8,128)(2,1)S(1)}, u32[]{:S(2)}) copy-start(bf16[512,768]{1,0:T(8,128)(2,1)S(1)} %broadcast_select_fusion.refs_0_.refs_2_) | copy-start | bytes 2359300
  143.2 1.0 copy-start.4
  144.2 1.1 copy-start.13
  145.3 32.1 %copy-start.5 = (bf16[4,512,192]{2,1,0:T(8,128)(2,1)S(1)}, bf16[4,512,192]{2,1,0:T(8,128)(2,1)}, u32[]{:S(2)}) copy-start(bf16[4,512,192]{2,1,0:T(8,128)(2,1)} %copy-done.4) | copy-start | bytes 2359300
  182.0 9.8 %collective-permute-start.10 = (bf16[2,384,2560]{2,1,0:T(8,128)(2,1)S(1)}, bf16[2,384,2560]{2,1,0:T(8,128)(2,1)S(1)}, u32[]{:S(2)}, u32[]{:S(2)}) collective-permute-start(bf16[2,384,2560]{2,1,0:T(8,128)(2,1)S(1)} %wgrad.4), channel_id=1, source_target_pairs={{0,4},{4,0},{8,12},{12,8},{16,20},{20,16},{24,28},{28,24},{1,5},{5... | collective-permute-start | bytes 11796488 | tf_op jit(solution)/shard_map/ppermute | solution.py:776
  189.9 9.0 %collective-permute-start.11 = (bf16[2,384,2560]{2,1,0:T(8,128)(2,1)S(1)}, bf16[2,384,2560]{2,1,0:T(8,128)(2,1)S(1)}, u32[]{:S(2)}, u32[]{:S(2)}) collective-permute-start(bf16[2,384,2560]{2,1,0:T(8,128)(2,1)S(1)} %wgrad.5), channel_id=1, source_target_pairs={{0,4},{4,0},{8,12},{12,8},{16,20},{20,16},{24,28},{28,24},{1,5},{5... | collective-permute-start | bytes 11796488 | tf_op jit(solution)/shard_map/ppermute | solution.py:776
  197.6 12.3 %copy-start.7 = (bf16[512,768]{1,0:T(8,128)(2,1)S(1)}, bf16[512,768]{1,0:T(8,128)(2,1)}, u32[]{:S(2)}) copy-start(bf16[512,768]{1,0:T(8,128)(2,1)} %copy-done.6) | copy-start | bytes 2359300
  197.6 12.3 %copy-start.12 = (bf16[4,3,512,256]{3,2,1,0:T(8,128)(2,1)S(1)}, bf16[4,3,512,256]{3,2,1,0:T(8,128)(2,1)}, u32[]{:S(2)}) copy-start(bf16[4,3,512,256]{3,2,1,0:T(8,128)(2,1)} %get-tuple-element.115.qh.refs_7_) | copy-start | bytes 9437188
  197.6 12.3 %copy-start.18 = (bf16[4,512,192]{2,1,0:T(8,128)(2,1)S(1)}, bf16[4,512,192]{2,1,0:T(8,128)(2,1)}, u32[]{:S(2)}) copy-start(bf16[4,512,192]{2,1,0:T(8,128)(2,1)} %get-tuple-element.175.refs_12_) | copy-start | bytes 2359300
  197.6 55.3 %collective-permute-start.13 = (bf16[2,192,2560]{2,1,0:T(8,128)(2,1)}, bf16[2,192,2560]{2,1,0:T(8,128)(2,1)S(1)}, u32[]{:S(2)}, u32[]{:S(2)}) collective-permute-start(bf16[2,192,2560]{2,1,0:T(8,128)(2,1)} %get-tuple-element.157), channel_id=1, source_target_pairs={{0,16},{4,20},{8,24},{12,28},{16,0},{20,4},{24,8},{28,12},{1,17},{... | collective-permute-start | bytes 5898248 | tf_op jit(solution)/shard_map/ppermute | solution.py:776
  204.4 30.4 %collective-permute-start.14 = (bf16[192,2560]{1,0:T(8,128)(2,1)}, bf16[192,2560]{1,0:T(8,128)(2,1)S(1)}, u32[]{:S(2)}, u32[]{:S(2)}) collective-permute-start(bf16[192,2560]{1,0:T(8,128)(2,1)} %get-tuple-element.163), channel_id=1, source_target_pairs={{0,8},{4,12},{8,0},{12,4},{16,24},{20,28},{24,16},{28,20},{1,9},{5... | collective-permute-start | bytes 2949128 | tf_op jit(solution)/shard_map/ppermute | solution.py:776
  209.8 43.1 %collective-permute-start.12 = (bf16[192,2560]{1,0:T(8,128)(2,1)S(1)}, bf16[192,2560]{1,0:T(8,128)(2,1)S(1)}, u32[]{:S(2)}, u32[]{:S(2)}) collective-permute-start(bf16[192,2560]{1,0:T(8,128)(2,1)S(1)} %get-tuple-element.162), channel_id=1, source_target_pairs={{0,8},{4,12},{8,0},{12,4},{16,24},{20,28},{24,16},{28,20},{1,9},{5... | collective-permute-start | bytes 2949128 | tf_op jit(solution)/shard_map/ppermute | solution.py:776
  234.8 20.2 %copy-start.16 = (bf16[3,512,256]{2,1,0:T(8,128)(2,1)}, bf16[3,512,256]{2,1,0:T(8,128)(2,1)S(1)}, u32[]{:S(2)}) copy-start(bf16[3,512,256]{2,1,0:T(8,128)(2,1)S(1)} %get-tuple-element.179.refs_2_) | copy-start | bytes 2359300
  254.5 26.8 %collective-permute-start.17 = (bf16[4,3,96,768]{3,2,1,0:T(8,128)(2,1)S(1)}, bf16[4,3,96,768]{3,2,1,0:T(8,128)(2,1)S(1)}, u32[]{:S(2)}, u32[]{:S(2)}) collective-permute-start(bf16[4,3,96,768]{3,2,1,0:T(8,128)(2,1)S(1)} %slice_bitcast_fusion.1), channel_id=1, source_target_pairs={{0,4},{4,0},{8,12},{12,8},{16,20},{20,16},{24,28},{28,24},{1,5},{5... | collective-permute-start | bytes 5308424 | tf_op jit(solution)/shard_map/ppermute | solution.py:776
  255.3 3.3 copy-start.19
  255.6 24.2 %collective-permute-start.16 = (bf16[192,2560]{1,0:T(8,128)(2,1)S(1)}, bf16[192,2560]{1,0:T(8,128)(2,1)S(1)}, u32[]{:S(2)}, u32[]{:S(2)}) collective-permute-start(bf16[192,2560]{1,0:T(8,128)(2,1)S(1)} %slice_bitcast_fusion.4), channel_id=1, source_target_pairs={{0,8},{4,12},{8,0},{12,4},{16,24},{20,28},{24,16},{28,20},{1,9},{5... | collective-permute-start | bytes 2949128 | tf_op jit(solution)/shard_map/ppermute | solution.py:776
  257.4 23.9 %collective-permute-start.15 = (bf16[192,2560]{1,0:T(8,128)(2,1)S(1)}, bf16[192,2560]{1,0:T(8,128)(2,1)S(1)}, u32[]{:S(2)}, u32[]{:S(2)}) collective-permute-start(bf16[192,2560]{1,0:T(8,128)(2,1)S(1)} %add_convert_fusion.2), channel_id=1, source_target_pairs={{0,16},{4,20},{8,24},{12,28},{16,0},{20,4},{24,8},{28,12},{1,17},{... | collective-permute-start | bytes 2949128 | tf_op jit(solution)/shard_map/ppermute | solution.py:776
  268.1 14.8 %copy-start.10 = (bf16[8,1,96,768]{3,2,1,0:T(8,128)(2,1)}, bf16[8,1,96,768]{3,2,1,0:T(8,128)(2,1)S(1)}, u32[]{:S(2)}) copy-start(bf16[8,1,96,768]{3,2,1,0:T(8,128)(2,1)S(1)} %get-tuple-element.183) | copy-start | bytes 3538948
  268.2 14.8 %copy-start.14 = (bf16[1,2048,448]{2,1,0:T(8,128)(2,1)}, bf16[1,2048,448]{2,1,0:T(8,128)(2,1)S(1)}, u32[]{:S(2)}) copy-start(bf16[1,2048,448]{2,1,0:T(8,128)(2,1)S(1)} %get-tuple-element.178.refs_1_) | copy-start | bytes 5505028
  281.3 1.2 copy-start.20
  284.4 1.3 copy-start.11
  284.4 1.8 copy-start.21
  284.4 97.1 %all-gather.11.cloned.1.call-start = ((), (), s32[]{:S(2)}) async-start(), calls=%async_computation.4 | async-start | bytes 5750784 | tf_op jit(solution)/shard_map/all_gather | solution.py:785
  285.7 3.1 collective-permute-start.21
  286.2 34.1 %slice-start = ((s8[5505024]{0:T(1024)(128)(4,1)}), s8[4194304]{0:T(1024)(128)(4,1)S(1)}, s32[]{:S(2)}) async-start(s8[5505024]{0:T(1024)(128)(4,1)} %bitcast.140), calls=%async_computation.5 | async-start | bytes 8388608
  288.3 15.4 %collective-permute-start.18 = (bf16[2,2,96,768]{3,2,1,0:T(8,128)(2,1)S(1)}, bf16[2,2,96,768]{3,2,1,0:T(8,128)(2,1)S(1)}, u32[]{:S(2)}, u32[]{:S(2)}) collective-permute-start(bf16[2,2,96,768]{3,2,1,0:T(8,128)(2,1)S(1)} %slice_bitcast_fusion.8), channel_id=1, source_target_pairs={{0,8},{4,12},{8,0},{12,4},{16,24},{20,28},{24,16},{28,20},{1,9},{5... | collective-permute-start | bytes 1769480 | tf_op jit(solution)/shard_map/ppermute | solution.py:776
  289.0 31.4 %slice-start.1 = ((s8[5505024]{0:T(1024)(128)(4,1)}), s8[1310720]{0:T(1024)(128)(4,1)S(1)}, s32[]{:S(2)}) async-start(s8[5505024]{0:T(1024)(128)(4,1)} %bitcast.140), calls=%async_computation.6 | async-start | bytes 2621440
  289.0 16.0 %collective-permute-start.22 = (bf16[2,2,96,768]{3,2,1,0:T(8,128)(2,1)S(1)}, bf16[2,2,96,768]{3,2,1,0:T(8,128)(2,1)S(1)}, u32[]{:S(2)}, u32[]{:S(2)}) collective-permute-start(bf16[2,2,96,768]{3,2,1,0:T(8,128)(2,1)S(1)} %fusion.9), channel_id=1, source_target_pairs={{0,16},{4,20},{8,24},{12,28},{16,0},{20,4},{24,8},{28,12},{1,17},{... | collective-permute-start | bytes 1769480 | tf_op jit(solution)/shard_map/ppermute | solution.py:776
  303.9 8.3 %collective-permute-start.19 = (bf16[2,96,768]{2,1,0:T(8,128)(2,1)S(1)}, bf16[2,96,768]{2,1,0:T(8,128)(2,1)S(1)}, u32[]{:S(2)}, u32[]{:S(2)}) collective-permute-start(bf16[2,96,768]{2,1,0:T(8,128)(2,1)S(1)} %slice_bitcast_fusion.12), channel_id=1, source_target_pairs={{0,16},{4,20},{8,24},{12,28},{16,0},{20,4},{24,8},{28,12},{1,17},{... | collective-permute-start | bytes 884744 | tf_op jit(solution)/shard_map/ppermute | solution.py:776
  305.2 15.1 %copy-start.15 = (bf16[1,2048,448]{2,1,0:T(8,128)(2,1)S(1)}, bf16[1,2048,448]{2,1,0:T(8,128)(2,1)}, u32[]{:S(2)}) copy-start(bf16[1,2048,448]{2,1,0:T(8,128)(2,1)} %copy-done.14) | copy-start | bytes 5505028
  305.2 15.1 %copy-start.17 = (bf16[3,512,256]{2,1,0:T(8,128)(2,1)S(1)}, bf16[3,512,256]{2,1,0:T(8,128)(2,1)}, u32[]{:S(2)}) copy-start(bf16[3,512,256]{2,1,0:T(8,128)(2,1)} %copy-done.16) | copy-start | bytes 2359300
  305.3 9.7 %collective-permute-start.23 = (bf16[2,96,768]{2,1,0:T(8,128)(2,1)S(1)}, bf16[2,96,768]{2,1,0:T(8,128)(2,1)S(1)}, u32[]{:S(2)}, u32[]{:S(2)}) collective-permute-start(bf16[2,96,768]{2,1,0:T(8,128)(2,1)S(1)} %slice_bitcast_fusion.10), channel_id=1, source_target_pairs={{0,8},{4,12},{8,0},{12,4},{16,24},{20,28},{24,16},{28,20},{1,9},{5... | collective-permute-start | bytes 884744 | tf_op jit(solution)/shard_map/ppermute | solution.py:776
  312.3 18.8 %collective-permute-start.20 = (bf16[96,768]{1,0:T(8,128)(2,1)S(1)}, bf16[96,768]{1,0:T(8,128)(2,1)S(1)}, u32[]{:S(2)}, u32[]{:S(2)}) collective-permute-start(bf16[96,768]{1,0:T(8,128)(2,1)S(1)} %slice_bitcast_fusion.17), channel_id=1, source_target_pairs={{0,3},{1,0},{2,1},{3,2},{4,7},{5,4},{6,5},{7,6},{8,11},{9,8},{10,9... | collective-permute-start | bytes 442376 | tf_op jit(solution)/shard_map/ppermute | solution.py:779
  315.0 18.9 %collective-permute-start.25 = (bf16[96,768]{1,0:T(8,128)(2,1)S(1)}, bf16[96,768]{1,0:T(8,128)(2,1)S(1)}, u32[]{:S(2)}, u32[]{:S(2)}) collective-permute-start(bf16[96,768]{1,0:T(8,128)(2,1)S(1)} %get-tuple-element.217), channel_id=1, source_target_pairs={{0,1},{1,2},{2,3},{3,0},{4,5},{5,6},{6,7},{7,4},{8,9},{9,10},{10,1... | collective-permute-start | bytes 442376 | tf_op jit(solution)/shard_map/ppermute | solution.py:779
  317.6 22.2 %collective-permute-start.24 = (bf16[96,768]{1,0:T(8,128)(2,1)S(1)}, bf16[96,768]{1,0:T(8,128)(2,1)S(1)}, u32[]{:S(2)}, u32[]{:S(2)}) collective-permute-start(bf16[96,768]{1,0:T(8,128)(2,1)S(1)} %get-tuple-element.218), channel_id=1, source_target_pairs={{0,2},{1,3},{2,0},{3,1},{4,6},{5,7},{6,4},{7,5},{8,10},{9,11},{10,... | collective-permute-start | bytes 442376 | tf_op jit(solution)/shard_map/ppermute | solution.py:779
  329.9 1.2 copy-start.8
  341.8 2.7 collective-permute-start.28
  342.5 18.4 %collective-permute-start.26 = (bf16[512,768]{1,0:T(8,128)(2,1)S(1)}, bf16[512,768]{1,0:T(8,128)(2,1)S(1)}, u32[]{:S(2)}, u32[]{:S(2)}) collective-permute-start(bf16[512,768]{1,0:T(8,128)(2,1)S(1)} %slice_bitcast_fusion.5), channel_id=1, source_target_pairs={{0,1},{1,2},{4,5},{5,6},{8,9},{9,10},{12,13},{13,14},{16,17},{17,1... | collective-permute-start | bytes 2359304 | tf_op jit(solution)/shard_map/ppermute | solution.py:881
  362.5 26.6 %collective-permute-start.29 = (bf16[512,768]{1,0:T(8,128)(2,1)}, bf16[512,768]{1,0:T(8,128)(2,1)}, u32[]{:S(2)}, u32[]{:S(2)}) collective-permute-start(bf16[512,768]{1,0:T(8,128)(2,1)} %get-tuple-element.208), channel_id=1, source_target_pairs={{1,0},{2,1},{3,2},{5,4},{6,5},{7,6},{9,8},{10,9},{11,10},{13,12},{... | collective-permute-start | bytes 2359304 | tf_op jit(solution)/shard_map/ppermute | solution.py:782
  363.8 26.8 %copy-start.9 = (f32[512,768]{1,0:T(8,128)S(1)}, f32[512,768]{1,0:T(8,128)}, u32[]{:S(2)}) copy-start(f32[512,768]{1,0:T(8,128)} %copy-done.8) | copy-start | bytes 4718596
  363.8 26.8 %copy-start.22 = (f32[512,768]{1,0:T(8,128)S(1)}, f32[512,768]{1,0:T(8,128)}, u32[]{:S(2)}) copy-start(f32[512,768]{1,0:T(8,128)} %get-tuple-element.144) | copy-start | bytes 4718596
  363.8 25.3 %collective-permute-start.27 = (bf16[512,768]{1,0:T(8,128)(2,1)}, bf16[512,768]{1,0:T(8,128)(2,1)}, u32[]{:S(2)}, u32[]{:S(2)}) collective-permute-start(bf16[512,768]{1,0:T(8,128)(2,1)} %get-tuple-element.209), channel_id=1, source_target_pairs={{0,1},{1,2},{2,3},{4,5},{5,6},{6,7},{8,9},{9,10},{10,11},{12,13},{... | collective-permute-start | bytes 2359304 | tf_op jit(solution)/shard_map/ppermute | solution.py:782
  390.6 2.9 copy-start.1
  (1 other events, 1.0 us)
Sparse Core Ops, SparseCore 0:
  35.3 42.3 all-gather.6
  80.1 63.8 all-gather.8
  284.5 50.7 reduce-scatter.1
  341.9 39.5 all-gather.10
